TPU v7x, 256 devices: a whole 4x4x8 slice. The times are simulated.
256 devices in a mesh: seq: 16 (over z, x_lo), head: 8 (over y, x_hi), pair: 2 (over core).
Axes of the slice: x: 4 (x_hi: 2, x_lo: 2; x = x_hi * 2 + x_lo), y: 4, z: 8, core: 2. Of those that a mesh axis runs over, the one named last changes fastest.
Arguments:
- queries: bfloat16 [12288, 5120], P(('pair', 'seq'), 'head'), parts along dimension 0, may hold values from -12 to 12
- keys: bfloat16 [12288, 5120], P(('pair', 'seq'), 'head'), parts along dimension 0, may hold values from -12 to 12
- values: bfloat16 [12288, 5120], P(('pair', 'seq'), 'head'), parts along dimension 0, may hold values from -6 to 6
- cross_query: bfloat16 [12288, 5120], P(('pair', 'seq'), 'head'), parts along dimension 0, may hold values from -12 to 12
- text_keys: bfloat16 [1024, 5120], P('pair', 'head'), parts along dimension 0, may hold values from -12 to 12
- text_values: bfloat16 [1024, 5120], P('pair', 'head'), parts along dimension 0, may hold values from -6 to 6
- out_weight: bfloat16 [5120, 5120], P('head'), may hold values from -0.078125 to 0.078125
- block_list: int32 [48, 18], replicated, may hold values from 0 to 47, as said below
- block_count: int32 [48], replicated, may hold values from 6 to 18, as said below
Outputs:
- block_stream: bfloat16 [12288, 5120], P(('pair', 'seq'), 'head'), parts along dimension 0
- cross_heads: bfloat16 [12288, 5120], P(('pair', 'seq'), 'head'), parts along dimension 0
There are 2 independent parts, one for each index of `pair`. A program takes and returns all parts, laid end to end along the dimension named above; an argument that names none is the same for every part. Nothing has to cross between parts.
Inputs may be any that keep to these rules, and one draw needn't show every extreme that they name: `block_list`: each row holds 18 distinct key blocks; its first block_count entries include every block of frame groups f - 1, f and f + 1 (those that exist) and of group 0, with f = row // 3 and a frame group being 3 consecutive blocks. `block_count`: some row uses all 18 entries.
All inputs are finite; a program needn't handle non-finite values.
Results may differ from a plain program's by a relative error of at most 0.029.
Values may be sent and summed in bfloat16 or wider, within the bound.
No kernel may reach another device: no remote copies, remote signals or barrier semaphores. Data moves between devices by JAX's collectives and lax.ppermute only.
A program may use at most 128 MiB of HBM per device.

v0:
```python
import functools
import math

import jax
import jax.numpy as jnp
from jax import lax
from jax.experimental import pallas as pl
from jax.experimental.pallas import tpu as pltpu
from jax.sharding import PartitionSpec as P

DH = 128
BLK = 128
FB = 3
ROWS = FB * BLK
MAX_EXTRA = 12
MAX_NEAR = 3
GROUPS = ((0, 1, 2), (3, 4))
IN_FLIGHT = 2
NEG = -1e30
LOG2E = math.log2(math.e)
TO_EXP2 = DH ** (-0.5) * LOG2E
NT = (((1,), (1,)), ((), ()))
SMEM = pl.BlockSpec(memory_space=pltpu.SMEM)
VMEM = pl.BlockSpec(memory_space=pltpu.VMEM)


def plan_kernel(last, seq_ref, list_ref, count_ref, blocks_out, count_out, near_out):
    side = seq_ref[0] % 2
    for which in range(2):
        frame = seq_ref[0] + which * (1 - 2 * side)
        found = jnp.int32(0)
        for w in range(MAX_NEAR):
            near_out[which * (MAX_NEAR + 1) + w] = 0
        for key_frame in (frame - 1, frame, frame + 1, 0):
            here = (key_frame % 2 == side) & (key_frame >= 0) & (key_frame <= last)
            if isinstance(key_frame, int):
                here &= frame > 1
            near_out[which * (MAX_NEAR + 1) + found] = jnp.where(here, key_frame // 2, 0)
            found += here.astype(jnp.int32)
        near_out[which * (MAX_NEAR + 1) + MAX_NEAR] = found
        for r in range(FB):
            row, out = frame * FB + r, which * FB + r
            for e in range(MAX_EXTRA + 1):
                blocks_out[out, e] = 0

            def one(j, extras, row=row, out=out, frame=frame):
                block = list_ref[row, j]
                key_frame = lax.div(block, FB)
                far = (jnp.abs(key_frame - frame) > 1) & (key_frame > 0) & (key_frame % 2 == side)
                blocks_out[out, extras] = jnp.where(
                    far, lax.div(key_frame, 2) * FB + block - key_frame * FB, 0
                )
                return extras + far.astype(jnp.int32)

            extras = lax.fori_loop(0, count_ref[row], one, jnp.int32(0))
            count_out[out] = extras


def plan(frames, seq, block_list, block_count):
    return pl.pallas_call(
        functools.partial(plan_kernel, frames - 1),
        out_shape=[
            jax.ShapeDtypeStruct((2 * FB, MAX_EXTRA + 1), jnp.int32),
            jax.ShapeDtypeStruct((2 * FB,), jnp.int32),
            jax.ShapeDtypeStruct((2 * (MAX_NEAR + 1),), jnp.int32),
        ],
        in_specs=[SMEM] * 3,
        out_specs=[SMEM] * 3,
        compiler_params=pltpu.CompilerParams(vmem_limit_bytes=1 << 20),
        cost_estimate=pl.CostEstimate(flops=1000, bytes_accessed=8000, transcendentals=0),
        name="plan",
    )(seq, block_list, block_count)


def pack_kernel(k_ref, v_ref, *outs):
    for heads, out in zip(GROUPS, outs):
        for n, head in enumerate(heads):
            columns = slice(head * DH, (head + 1) * DH)
            out[2 * n * ROWS : (2 * n + 1) * ROWS, :] = k_ref[:, columns]
            out[(2 * n + 1) * ROWS : (2 * n + 2) * ROWS, :] = v_ref[:, columns]


def pack(keys, values):
    return pl.pallas_call(
        pack_kernel,
        out_shape=[jax.ShapeDtypeStruct((2 * ROWS * len(heads), DH), jnp.bfloat16) for heads in GROUPS],
        in_specs=[VMEM, VMEM],
        out_specs=[VMEM] * len(GROUPS),
        compiler_params=pltpu.CompilerParams(vmem_limit_bytes=6 << 20),
        cost_estimate=pl.CostEstimate(flops=0, bytes_accessed=4 * keys.size * 2, transcendentals=0),
        name="pack",
    )(keys, values)


def attend_lanes(lanes, near_ref, blocks_ref, count_ref, q_s, o_s, lse_s, k_s, v_s, near_s, far_s, top_s, sum_s):
    frames = sorted({which for _, which in lanes}, key=str) if all(isinstance(w, int) for _, w in lanes) else [lanes[0][1]]
    nears = near_ref[frames[0] * (MAX_NEAR + 1) + MAX_NEAR]
    most = count_ref[frames[0] * FB]
    for which in frames:
        nears = jnp.maximum(nears, near_ref[which * (MAX_NEAR + 1) + MAX_NEAR])
        for r in range(FB):
            most = jnp.maximum(most, count_ref[which * FB + r])
    pairs = lax.div(most + 1, 2)

    def near_rows(which, w):
        return pl.ds(pl.multiple_of(near_ref[which * (MAX_NEAR + 1) + w] * ROWS, ROWS), ROWS)

    def far_rows(which, r, e):
        return pl.ds(pl.multiple_of(blocks_ref[which * FB + r, e] * BLK, BLK), BLK)

    top_s[...] = jnp.full_like(top_s, NEG)

    def near_scores(w, carry):
        for lane, (n, which) in enumerate(lanes):
            score = lax.dot_general(
                q_s[2 * n + which], k_s[n, near_rows(which, w), :], NT, preferred_element_type=jnp.float32
            )
            if len(frames) > 1:
                score = jnp.where(w < near_ref[which * (MAX_NEAR + 1) + MAX_NEAR], score, NEG)
            near_s[lane, w] = score
            best = jnp.maximum(jnp.maximum(score[:, :BLK], score[:, BLK : 2 * BLK]), score[:, 2 * BLK :])
            top_s[lane] = jnp.maximum(top_s[lane], best)
        return carry

    lax.fori_loop(0, nears, near_scores, 0)

    def far_scores(i, carry):
        for lane, (n, which) in enumerate(lanes):
            for r in range(FB):
                rows = slice(r * BLK, (r + 1) * BLK)
                best = top_s[lane, rows, :]
                for j in range(2):
                    e = 2 * i + j
                    score = lax.dot_general(
                        q_s[2 * n + which, rows, :], k_s[n, far_rows(which, r, e), :], NT, preferred_element_type=jnp.float32
                    )
                    score = jnp.where(e < count_ref[which * FB + r], score, NEG)
                    far_s[lane, r, e] = score
                    best = jnp.maximum(best, score)
                top_s[lane, rows, :] = best
        return carry

    lax.fori_loop(0, pairs, far_scores, 0)
    for lane in range(len(lanes)):
        top_s[lane] = jnp.broadcast_to(jnp.max(top_s[lane], axis=1, keepdims=True) * TO_EXP2, (ROWS, BLK))
    sum_s[...] = jnp.zeros_like(sum_s)

    def near_weights(w, carry):
        for lane, (n, which) in enumerate(lanes):
            top = top_s[lane]
            weights = [jnp.exp2(near_s[lane, w, :, c * BLK : (c + 1) * BLK] * TO_EXP2 - top) for c in range(FB)]
            weight = jnp.concatenate([p.astype(jnp.bfloat16) for p in weights], axis=1)
            sum_s[lane] += jnp.dot(weight, v_s[n, near_rows(which, w), :], preferred_element_type=jnp.float32)
        return carry

    lax.fori_loop(0, nears, near_weights, 0)

    def far_weights(i, carry):
        for lane, (n, which) in enumerate(lanes):
            for r in range(FB):
                rows = slice(r * BLK, (r + 1) * BLK)
                top = top_s[lane, rows, :]
                part = None
                for j in range(2):
                    weight = jnp.exp2(far_s[lane, r, 2 * i + j] * TO_EXP2 - top).astype(jnp.bfloat16)
                    value = v_s[n, far_rows(which, r, 2 * i + j), :]
                    added = jnp.dot(weight, value, preferred_element_type=jnp.float32)
                    part = added if part is None else part + added
                sum_s[lane, rows, :] += part
        return carry

    lax.fori_loop(0, pairs, far_weights, 0)
    for lane, (n, which) in enumerate(lanes):
        total = sum_s[lane, :, DH:]
        o_s[2 * n + which] = sum_s[lane, :, :DH] / total
        lse_s[2 * n + which] = top_s[lane] + jnp.log(total) * LOG2E


def attend_kernel(heads, first, planes, seq_ref, near_ref, blocks_ref, count_ref, q_ref, q_other_ref, *refs):
    piece_refs = refs[:planes]
    keep_o, keep_lse, send = refs[planes : planes + 3]
    q_s, o_s, lse_s, k_s, v_s, near_s, far_s, top_s, sum_s = refs[planes + 3 :]
    z = lax.div(seq_ref[0], 2)
    v_s[:, :, DH:] = jnp.ones((len(heads), planes * ROWS, DH), jnp.bfloat16)
    for d, piece in enumerate(piece_refs):
        rows = pl.ds(pl.multiple_of(lax.rem(z + planes - d, planes) * ROWS, ROWS), ROWS)
        for n in range(len(heads)):
            at = 2 * (first + n) * ROWS
            k_s[n, rows, :] = piece[at : at + ROWS, :]
            v_s[n, rows, 0:DH] = piece[at + ROWS : at + 2 * ROWS, :]
    for n, head in enumerate(heads):
        columns = slice(head * DH, (head + 1) * DH)
        q_s[2 * n] = q_ref[:, columns]
        q_s[2 * n + 1] = q_other_ref[:, columns]
    tables = (near_ref, blocks_ref, count_ref, q_s, o_s, lse_s, k_s, v_s, near_s, far_s, top_s, sum_s)
    if len(heads) == 1:
        attend_lanes([(0, 0), (0, 1)], *tables)
    else:

        def one(which, carry):
            attend_lanes([(n, which) for n in range(len(heads))], *tables)
            return carry

        lax.fori_loop(0, 2, one, 0)
    lane = lax.broadcasted_iota(jnp.int32, (ROWS, DH), 1)
    for n in range(len(heads)):
        rows = slice(n * ROWS, (n + 1) * ROWS)
        keep_o[rows, :] = o_s[2 * n]
        keep_lse[rows, :] = lse_s[2 * n]
        send[2 * n * ROWS : (2 * n + 1) * ROWS, :] = o_s[2 * n + 1].astype(jnp.bfloat16)
        left = lse_s[2 * n + 1]
        packed = jnp.zeros((ROWS, DH), jnp.float32)
        for term in range(3):
            piece = left.astype(jnp.bfloat16).astype(jnp.float32)
            packed = jnp.where(lane == term, piece, packed)
            left = left - piece
        send[(2 * n + 1) * ROWS : (2 * n + 2) * ROWS, :] = packed.astype(jnp.bfloat16)


def attend(heads, first, queries, queries_other, pieces, seq, near, blocks, counts):
    planes, held = len(pieces), len(heads)
    lanes = max(held, 2)
    tokens = planes * ROWS
    each = pltpu.VMEM((2 * held, ROWS, DH), jnp.float32)
    elements = held * ROWS * 18 * BLK
    return pl.pallas_call(
        functools.partial(attend_kernel, heads, first, planes),
        out_shape=[
            jax.ShapeDtypeStruct((held * ROWS, DH), jnp.float32),
            jax.ShapeDtypeStruct((held * ROWS, DH), jnp.float32),
            jax.ShapeDtypeStruct((2 * held * ROWS, DH), jnp.bfloat16),
        ],
        in_specs=[SMEM] * 4 + [VMEM] * (2 + planes),
        out_specs=[VMEM] * 3,
        scratch_shapes=[
            pltpu.VMEM((2 * held, ROWS, DH), jnp.bfloat16),
            each,
            each,
            pltpu.VMEM((held, tokens, DH), jnp.bfloat16),
            pltpu.VMEM((held, tokens, 2 * DH), jnp.bfloat16),
            pltpu.VMEM((lanes, MAX_NEAR, ROWS, ROWS), jnp.float32),
            pltpu.VMEM((lanes, FB, MAX_EXTRA, BLK, BLK), jnp.float32),
            pltpu.VMEM((lanes, ROWS, BLK), jnp.float32),
            pltpu.VMEM((lanes, ROWS, 2 * DH), jnp.float32),
        ],
        compiler_params=pltpu.CompilerParams(vmem_limit_bytes=(36 if held > 2 else 24) << 20),
        cost_estimate=pl.CostEstimate(
            flops=40 * elements * DH, bytes_accessed=4 * held * tokens * DH, transcendentals=elements
        ),
        name="attend",
    )(seq, near, blocks, counts, queries, queries_other, *pieces)


def merge_kernel(*refs):
    out_ref, parts = refs[-1], refs[:-1]
    column = 0
    for o_ref, lse_ref, got_ref in zip(parts[0::3], parts[1::3], parts[2::3]):
        for n in range(o_ref.shape[0] // ROWS):
            rows = slice(n * ROWS, (n + 1) * ROWS)
            other_o = got_ref[2 * n * ROWS : (2 * n + 1) * ROWS, :].astype(jnp.float32)
            packed = got_ref[(2 * n + 1) * ROWS : (2 * n + 2) * ROWS, :].astype(jnp.float32)
            other_lse = jnp.sum(packed, axis=1, keepdims=True)
            lse = lse_ref[rows, :]
            top = jnp.maximum(lse, other_lse)
            mine, other = jnp.exp2(lse - top), jnp.exp2(other_lse - top)
            out = ((o_ref[rows, :] * mine + other_o * other) / (mine + other)).astype(out_ref.dtype)
            out_ref[:, column : column + DH] = out
            column += DH


def merge(*parts):
    size = sum(part.size for part in parts[0::3])
    return pl.pallas_call(
        merge_kernel,
        out_shape=jax.ShapeDtypeStruct((ROWS, size // ROWS), jnp.bfloat16),
        in_specs=[VMEM] * len(parts),
        out_specs=VMEM,
        compiler_params=pltpu.CompilerParams(vmem_limit_bytes=10 << 20),
        cost_estimate=pl.CostEstimate(flops=8 * size, bytes_accessed=30 * size, transcendentals=2 * size),
        name="merge",
    )(*parts)


def tile_kernel(count, y_ref, pair_ref, weight_ref, *refs):
    outs, sems = refs[:-1], refs[-1]
    width = outs[0].shape[1]
    copies = []
    for n, out in enumerate(outs):
        block = pair_ref[0] if n < count else 1 - pair_ref[0]
        start = pl.multiple_of((lax.rem(y_ref[0] + n, count) * 2 + block) * width, width)
        copies.append(pltpu.make_async_copy(weight_ref.at[:, pl.ds(start, width)], out, sems.at[n]))
    for copy in copies:
        copy.start()
    for copy in copies:
        copy.wait()


def tile(y, pair, weight, count):
    stay = pl.BlockSpec(memory_space=pl.ANY)
    shape = (weight.shape[0], weight.shape[1] // (2 * count))
    return pl.pallas_call(
        functools.partial(tile_kernel, count),
        out_shape=[jax.ShapeDtypeStruct(shape, weight.dtype)] * (count + 1),
        in_specs=[SMEM, SMEM, stay],
        out_specs=[stay] * (count + 1),
        scratch_shapes=[pltpu.SemaphoreType.DMA((count + 1,))],
        compiler_params=pltpu.CompilerParams(vmem_limit_bytes=1 << 20),
        cost_estimate=pl.CostEstimate(flops=0, bytes_accessed=4 * weight.size, transcendentals=0),
        name="tile",
    )(y, pair, weight)


def cross_kernel(q_ref, k_ref, v_ref, o_ref):
    def one(h, carry):
        columns = pl.ds(pl.multiple_of(h * DH, DH), DH)
        score = lax.dot_general(q_ref[:, columns], k_ref[:, columns], NT, preferred_element_type=jnp.float32)
        top = jnp.max(score, axis=1, keepdims=True) * TO_EXP2
        weight = jnp.exp2(score * TO_EXP2 - top)
        total = jnp.sum(weight, axis=1, keepdims=True)
        part = jnp.dot(weight.astype(jnp.bfloat16), v_ref[:, columns], preferred_element_type=jnp.float32)
        o_ref[:, columns] = (part / total).astype(o_ref.dtype)
        return carry

    lax.fori_loop(0, q_ref.shape[1] // DH, one, 0)


def cross(cross_query, text_keys, text_values):
    elements = cross_query.shape[0] * cross_query.shape[1] // DH * text_keys.shape[0]
    return pl.pallas_call(
        cross_kernel,
        out_shape=jax.ShapeDtypeStruct(cross_query.shape, jnp.bfloat16),
        in_specs=[VMEM] * 3,
        out_specs=VMEM,
        compiler_params=pltpu.CompilerParams(vmem_limit_bytes=8 << 20),
        cost_estimate=pl.CostEstimate(
            flops=40 * elements * DH, bytes_accessed=4 * cross_query.size, transcendentals=elements
        ),
        name="cross",
    )(cross_query, text_keys, text_values)


def project_kernel(first, sources, last, *refs):
    keep_ref = refs[0] if last else None
    refs = refs[1:] if last else refs
    heads, weights, refs = refs[:sources], refs[sources : 3 * sources], refs[3 * sources :]
    depth = heads[0].shape[1]
    rows = slice(first * DH, first * DH + depth)
    total_ref = refs[-1]
    for block in range(2):
        total = refs[0][block] if len(refs) > 1 + 2 * last else None
        for head_ref, weight_ref in zip(heads, weights[block::2]):
            part = jnp.dot(head_ref[...], weight_ref[rows, :], preferred_element_type=jnp.float32)
            total = part if total is None else total + part
        total_ref[block] = total
    if last:
        refs[-3][...] = total_ref[keep_ref[0]]
        refs[-2][...] = total_ref[1 - keep_ref[0]].astype(jnp.bfloat16)


def project(first, heads, weights, before=None, keep=None):
    rows, depth = heads[0].shape
    width = weights[0].shape[1]
    given = [*heads, *weights] + ([] if before is None else [before])
    both = jax.ShapeDtypeStruct((2, rows, width), jnp.float32)
    split = [jax.ShapeDtypeStruct((rows, width), dtype) for dtype in (jnp.float32, jnp.bfloat16)]
    last = keep is not None
    return pl.pallas_call(
        functools.partial(project_kernel, first, len(heads), last),
        out_shape=split if last else both,
        in_specs=[SMEM] * last + [VMEM] * len(given),
        out_specs=[VMEM] * 2 if last else VMEM,
        scratch_shapes=[pltpu.VMEM(both.shape, both.dtype)] if last else [],
        compiler_params=pltpu.CompilerParams(vmem_limit_bytes=22 << 20),
        cost_estimate=pl.CostEstimate(
            flops=4 * len(heads) * rows * depth * width,
            bytes_accessed=2 * len(heads) * depth * (rows + 2 * width),
            transcendentals=0,
        ),
        name="project",
    )(*([keep] if last else []), *given)


def body(n_seq, n_head, queries, keys, values, cross_query, text_keys, text_values, out_weight, block_list, block_count):
    n_z, n_y = n_seq // 2, n_head // 2
    seq = lax.axis_index("seq").reshape(1)
    head = lax.axis_index("head").reshape(1)
    pair = lax.axis_index("pair").reshape(1)
    cross_heads = cross(cross_query, text_keys, text_values)
    swap = [(s, s ^ 1) for s in range(n_seq)]

    def to_other(array):
        return lax.ppermute(array, "seq", swap)

    def z_shift(step):
        return [(s, (s // 2 + step) % n_z * 2 + s % 2) for s in range(n_seq)]

    def y_shift(step):
        return [(g, (g // 2 + step) % n_y * 2 + g % 2) for g in range(n_head)]

    held = [{0: array} for array in pack(keys, values)]
    sent = {1: [], -1: []}

    def hop(way, group, step, after=None):
        done = sent[way]
        array = held[group][way * (step - 1) % n_z]
        if len(done) >= IN_FLIGHT:
            at, where = done[-IN_FLIGHT]
            array, held[at][where] = lax.optimization_barrier((array, held[at][where]))
        if after is not None:
            array, after[0] = lax.optimization_barrier((array, after[0]))
        place = way * step % n_z
        held[group][place] = lax.ppermute(array, "seq", z_shift(way))
        done.append((group, place))

    def partial(group, start, stop):
        pieces = [held[group][d] for d in range(n_z)]
        return list(attend(GROUPS[group][start:stop], start, queries, queries_other, pieces, seq, near, blocks, counts))

    def join(part):
        return merge(*part[:2], to_other(part[2]))

    def along_y(array):
        return [array] + [lax.ppermute(array, "head", y_shift(-dy)) for dy in range(1, n_y)]

    for group in (0, 1):
        hop(1, group, 1)
        hop(-1, group, 1)
    queries_other = to_other(queries)
    early = list(plan(n_seq, seq, block_list, block_count))
    tiles = list(tile(lax.div(head, 2), pair, out_weight, n_y))
    early[0], tiles[0] = lax.optimization_barrier((early[0], tiles[0]))
    hop(1, 0, 2, early)
    hop(-1, 0, 2)
    blocks, counts, near = early
    tiles[1:n_y] = [lax.ppermute(tiles[dy], "head", y_shift(dy)) for dy in range(1, n_y)][::-1]
    hop(1, 0, 3)
    hop(-1, 0, 3)
    far_tiles = [lax.optimization_barrier(tuple(tiles[1:n_y]))]
    hop(1, 0, 4, far_tiles)
    hop(-1, 1, 2)
    weights = [tiles[0], tiles[n_y]]
    for mine in far_tiles[0]:
        weights += [mine, lax.ppermute(mine, "pair", [(0, 1), (1, 0)])]
    hop(1, 1, 2)
    hop(-1, 1, 3)
    most = partial(0, 0, 3)
    hop(1, 1, 3, most)
    hop(-1, 1, 4, most)
    before = project(GROUPS[0][0], along_y(join(most)), weights)
    one, two = partial(1, 0, 1), partial(1, 1, 2)
    before = project(GROUPS[1][0], along_y(join(one)), weights, before)
    keep_block = (lax.rem(head, 2) != pair).astype(jnp.int32)
    keep, send = project(GROUPS[1][1], along_y(join(two)), weights, before, keep_block)
    got = lax.ppermute(send, "head", [(g, g ^ 1) for g in range(n_head)])
    return (keep + got.astype(jnp.float32)).astype(jnp.bfloat16), cross_heads


def solution(mesh):
    rows = P(("pair", "seq"), "head")
    text = P("pair", "head")
    return jax.shard_map(
        functools.partial(body, mesh.shape["seq"], mesh.shape["head"]),
        mesh=mesh,
        in_specs=(rows, rows, rows, rows, text, text, P("head", None), P(), P()),
        out_specs=(rows, rows),
        check_vma=False,
    )
```

profile of v0, /device:TPU:4, one launch (start us, length us, event | category | flops | bytes accessed | tf_op | source)
XLA Modules:
  0.0 187.9 jit_solution(3402684147054210866)
XLA Ops:
  0.6 1.0 copy-done.1
  1.7 1.0 copy-done.2
  2.9 2.0 %collective-permute-start = (bf16[2304,128]{1,0:T(8,128)(2,1)S(1)}, bf16[2304,128]{1,0:T(8,128)(2,1)S(1)}, u32[]{:S(2)}, u32[]{:S(2)}) collective-permute-start(bf16[2304,128]{1,0:T(8,128)(2,1)S(1)} %get-tuple-element.58.refs_0_), channel_id=1, source_target_pairs={{0,32},{16,48},{32,64},{48,80},{64,96},{80,112},{96,128},{112,144}... | collective-permute-start | bytes 1769480 | tf_op jit(solution)/shard_map/ppermute | solution.py:412
  4.9 4.0 %collective-permute-start.10 = (bf16[2304,128]{1,0:T(8,128)(2,1)S(1)}, bf16[2304,128]{1,0:T(8,128)(2,1)S(1)}, u32[]{:S(2)}, u32[]{:S(2)}) collective-permute-start(bf16[2304,128]{1,0:T(8,128)(2,1)S(1)} %get-tuple-element.58.refs_0_), channel_id=1, source_target_pairs={{0,224},{16,240},{32,0},{48,16},{64,32},{80,48},{96,64},{112,80},{... | collective-permute-start | bytes 1769480 | tf_op jit(solution)/shard_map/ppermute | solution.py:412
  8.9 0.8 copy.11.list_ref
  9.7 0.7 copy-done.3
  10.3 3.0 %plan.1 = (s32[6,13]{1,0:T(8,128)S(1)}, s32[6]{0:T(128)S(1)}, s32[8]{0:T(128)S(1)}) custom-call(s32[1]{0:T(128)} %bitcast.2.seq_ref, s32[48,18]{1,0:T(8,128)S(1)} %copy.11.list_ref, s32[48]{0:T(128)S(1)} %copy-done.3), custom_call_target="tpu_custom_call" | custom-call | flops 1000 | bytes 8000 | tf_op jit(solution)/shard_map/plan/pallas_call | solution.py:60
  13.3 2.9 %copy-done = bf16[640,5120]{1,0:T(8,128)(2,1)S(1)} copy-done((bf16[640,5120]{1,0:T(8,128)(2,1)S(1)}, bf16[640,5120]{1,0:T(8,128)(2,1)}, u32[]{:S(2)}) %copy-start) | copy-done | bytes 6553624
  16.8 5.3 %collective-permute-done.refs_1_ = bf16[2304,128]{1,0:T(8,128)(2,1)S(1)} collective-permute-done((bf16[2304,128]{1,0:T(8,128)(2,1)S(1)}, bf16[2304,128]{1,0:T(8,128)(2,1)S(1)}, u32[]{:S(2)}, u32[]{:S(2)}) %collective-permute-start) | collective-permute-done | bytes 589856 | tf_op jit(solution)/shard_map/ppermute | solution.py:412
  22.1 3.0 %collective-permute-start.6 = (bf16[640,640]{1,0:T(8,128)(2,1)S(1)}, bf16[640,640]{1,0:T(8,128)(2,1)S(1)}, u32[]{:S(2)}, u32[]{:S(2)}) collective-permute-start(bf16[640,640]{1,0:T(8,128)(2,1)S(1)} %get-tuple-element.71), channel_id=1, source_target_pairs={{0,12},{2,14},{4,0},{6,2},{8,4},{10,6},{12,8},{14,10},{1,13},{3,15... | collective-permute-start | bytes 2457608 | tf_op jit(solution)/shard_map/ppermute | solution.py:435
  25.2 3.3 %collective-permute-start.11 = (bf16[2304,128]{1,0:T(8,128)(2,1)S(1)}, bf16[2304,128]{1,0:T(8,128)(2,1)S(1)}, u32[]{:S(2)}, u32[]{:S(2)}) collective-permute-start(bf16[2304,128]{1,0:T(8,128)(2,1)S(1)} %collective-permute-done.10.refs_7_), channel_id=1, source_target_pairs={{0,224},{16,240},{32,0},{48,16},{64,32},{80,48},{96,64},{112,80},{... | collective-permute-start | bytes 1769480 | tf_op jit(solution)/shard_map/ppermute | solution.py:412
  28.4 2.0 %collective-permute-start.12 = (bf16[1536,128]{1,0:T(8,128)(2,1)S(1)}, bf16[1536,128]{1,0:T(8,128)(2,1)S(1)}, u32[]{:S(2)}, u32[]{:S(2)}) collective-permute-start(bf16[1536,128]{1,0:T(8,128)(2,1)S(1)} %get-tuple-element.65.refs_0_), channel_id=1, source_target_pairs={{0,224},{16,240},{32,0},{48,16},{64,32},{80,48},{96,64},{112,80},{... | collective-permute-start | bytes 1179656 | tf_op jit(solution)/shard_map/ppermute | solution.py:412
  30.4 15.9 %collective-permute-done.3.refs_1_ = bf16[1536,128]{1,0:T(8,128)(2,1)S(1)} collective-permute-done((bf16[1536,128]{1,0:T(8,128)(2,1)S(1)}, bf16[1536,128]{1,0:T(8,128)(2,1)S(1)}, u32[]{:S(2)}, u32[]{:S(2)}) %collective-permute-start.3) | collective-permute-done | bytes 393248 | tf_op jit(solution)/shard_map/ppermute | solution.py:412
  46.3 3.2 %collective-permute-start.7 = (bf16[640,640]{1,0:T(8,128)(2,1)S(1)}, bf16[640,640]{1,0:T(8,128)(2,1)S(1)}, u32[]{:S(2)}, u32[]{:S(2)}) collective-permute-start(bf16[640,640]{1,0:T(8,128)(2,1)S(1)} %get-tuple-element.72), channel_id=1, source_target_pairs={{0,8},{2,10},{4,12},{6,14},{8,0},{10,2},{12,4},{14,6},{1,9},{3,11}... | collective-permute-start | bytes 2457608 | tf_op jit(solution)/shard_map/ppermute | solution.py:435
  49.5 0.7 collective-permute-start.8
  50.2 1.0 collective-permute-start.4
  51.2 2.2 %collective-permute-start.14 = (bf16[2304,128]{1,0:T(8,128)(2,1)S(1)}, bf16[2304,128]{1,0:T(8,128)(2,1)S(1)}, u32[]{:S(2)}, u32[]{:S(2)}) collective-permute-start(bf16[2304,128]{1,0:T(8,128)(2,1)S(1)} %collective-permute-done.11.refs_6_), channel_id=1, source_target_pairs={{0,224},{16,240},{32,0},{48,16},{64,32},{80,48},{96,64},{112,80},{... | collective-permute-start | bytes 1769480 | tf_op jit(solution)/shard_map/ppermute | solution.py:412
  54.0 15.0 %collective-permute-done.7.refs_8_.refs_9_ = bf16[640,640]{1,0:T(8,128)(2,1)S(1)} collective-permute-done((bf16[640,640]{1,0:T(8,128)(2,1)S(1)}, bf16[640,640]{1,0:T(8,128)(2,1)S(1)}, u32[]{:S(2)}, u32[]{:S(2)}) %collective-permute-start.7) | collective-permute-done | bytes 819232 | tf_op jit(solution)/shard_map/ppermute | solution.py:435
  69.0 14.8 %collective-permute-done.8.refs_10_.refs_11_ = bf16[640,640]{1,0:T(8,128)(2,1)S(1)} collective-permute-done((bf16[640,640]{1,0:T(8,128)(2,1)S(1)}, bf16[640,640]{1,0:T(8,128)(2,1)S(1)}, u32[]{:S(2)}, u32[]{:S(2)}) %collective-permute-start.8) | collective-permute-done | bytes 819232 | tf_op jit(solution)/shard_map/ppermute | solution.py:435
  83.9 1.3 collective-permute-start.1
  85.1 3.1 %collective-permute-start.16 = (bf16[1536,128]{1,0:T(8,128)(2,1)S(1)}, bf16[1536,128]{1,0:T(8,128)(2,1)S(1)}, u32[]{:S(2)}, u32[]{:S(2)}) collective-permute-start(bf16[1536,128]{1,0:T(8,128)(2,1)S(1)} %collective-permute-done.13.refs_6_), channel_id=1, source_target_pairs={{0,224},{16,240},{32,0},{48,16},{64,32},{80,48},{96,64},{112,80},{... | collective-permute-start | bytes 1179656 | tf_op jit(solution)/shard_map/ppermute | solution.py:412
  88.3 8.0 %collective-permute-done.16.refs_5_ = bf16[1536,128]{1,0:T(8,128)(2,1)S(1)} collective-permute-done((bf16[1536,128]{1,0:T(8,128)(2,1)S(1)}, bf16[1536,128]{1,0:T(8,128)(2,1)S(1)}, u32[]{:S(2)}, u32[]{:S(2)}) %collective-permute-start.16) | collective-permute-done | bytes 393248 | tf_op jit(solution)/shard_map/ppermute | solution.py:412
  96.3 12.4 %collective-permute-done.5.refs_2_ = bf16[1536,128]{1,0:T(8,128)(2,1)S(1)} collective-permute-done((bf16[1536,128]{1,0:T(8,128)(2,1)S(1)}, bf16[1536,128]{1,0:T(8,128)(2,1)S(1)}, u32[]{:S(2)}, u32[]{:S(2)}) %collective-permute-start.5) | collective-permute-done | bytes 393248 | tf_op jit(solution)/shard_map/ppermute | solution.py:412
  108.7 9.3 %attend.3 = (f32[1152,128]{1,0:T(8,128)S(1)}, f32[1152,128]{1,0:T(8,128)S(1)}, bf16[2304,128]{1,0:T(8,128)(2,1)S(1)}) custom-call(s32[1]{0:T(128)} %bitcast.2.seq_ref, s32[8]{0:T(128)S(1)} %get-tuple-element.57.near_ref, s32[6,13]{1,0:T(8,128)S(1)} %get-tuple-element.63.blocks_ref, s32[6]{0:T(128)S(1)} %get-tuple-element.64.count_ref, ...), custom_call_target="tpu_custom_call" | custom-call | flops 13589544960 | bytes 4718592 | tf_op jit(solution)/shard_map/attend/pallas_call | solution.py:226
  118.1 1.0 collective-permute-start.15
  119.0 2.3 %collective-permute-start.17 = (bf16[1536,128]{1,0:T(8,128)(2,1)S(1)}, bf16[1536,128]{1,0:T(8,128)(2,1)S(1)}, u32[]{:S(2)}, u32[]{:S(2)}) collective-permute-start(bf16[1536,128]{1,0:T(8,128)(2,1)S(1)} %collective-permute-done.16.refs_5_), channel_id=1, source_target_pairs={{0,224},{16,240},{32,0},{48,16},{64,32},{80,48},{96,64},{112,80},{... | collective-permute-start | bytes 1179656 | tf_op jit(solution)/shard_map/ppermute | solution.py:412
  121.9 7.7 %collective-permute-done.15.refs_3_ = bf16[1536,128]{1,0:T(8,128)(2,1)S(1)} collective-permute-done((bf16[1536,128]{1,0:T(8,128)(2,1)S(1)}, bf16[1536,128]{1,0:T(8,128)(2,1)S(1)}, u32[]{:S(2)}, u32[]{:S(2)}) %collective-permute-start.15) | collective-permute-done | bytes 393248 | tf_op jit(solution)/shard_map/ppermute | solution.py:412
  129.5 2.3 %collective-permute-start.29 = (bf16[2304,128]{1,0:T(8,128)(2,1)S(1)}, bf16[2304,128]{1,0:T(8,128)(2,1)S(1)}, u32[]{:S(2)}, u32[]{:S(2)}) collective-permute-start(bf16[2304,128]{1,0:T(8,128)(2,1)S(1)} %get-tuple-element.109), channel_id=1, source_target_pairs={{0,16},{16,0},{32,48},{48,32},{64,80},{80,64},{96,112},{112,96},{1... | collective-permute-start | bytes 1769480 | tf_op jit(solution)/shard_map/ppermute | solution.py:392
  131.9 4.2 %attend.5 = (f32[384,128]{1,0:T(8,128)S(1)}, f32[384,128]{1,0:T(8,128)S(1)}, bf16[768,128]{1,0:T(8,128)(2,1)S(1)}) custom-call(s32[1]{0:T(128)} %bitcast.2.seq_ref, s32[8]{0:T(128)S(1)} %get-tuple-element.57.near_ref, s32[6,13]{1,0:T(8,128)S(1)} %get-tuple-element.63.blocks_ref, s32[6]{0:T(128)S(1)} %get-tuple-element.64.count_ref, ...), custom_call_target="tpu_custom_call" | custom-call | flops 4529848320 | bytes 1572864 | tf_op jit(solution)/shard_map/attend/pallas_call | solution.py:226
  136.2 4.3 %attend.4 = (f32[384,128]{1,0:T(8,128)S(1)}, f32[384,128]{1,0:T(8,128)S(1)}, bf16[768,128]{1,0:T(8,128)(2,1)S(1)}) custom-call(s32[1]{0:T(128)} %bitcast.2.seq_ref, s32[8]{0:T(128)S(1)} %get-tuple-element.57.near_ref, s32[6,13]{1,0:T(8,128)S(1)} %get-tuple-element.63.blocks_ref, s32[6]{0:T(128)S(1)} %get-tuple-element.64.count_ref, ...), custom_call_target="tpu_custom_call" | custom-call | flops 4529848320 | bytes 1572864 | tf_op jit(solution)/shard_map/attend/pallas_call | solution.py:226
  140.5 5.6 %collective-permute-done.29.refs_2_ = bf16[2304,128]{1,0:T(8,128)(2,1)S(1)} collective-permute-done((bf16[2304,128]{1,0:T(8,128)(2,1)S(1)}, bf16[2304,128]{1,0:T(8,128)(2,1)S(1)}, u32[]{:S(2)}, u32[]{:S(2)}) %collective-permute-start.29) | collective-permute-done | bytes 589856 | tf_op jit(solution)/shard_map/ppermute | solution.py:392
  146.1 2.0 %collective-permute-start.18 = (bf16[768,128]{1,0:T(8,128)(2,1)S(1)}, bf16[768,128]{1,0:T(8,128)(2,1)S(1)}, u32[]{:S(2)}, u32[]{:S(2)}) collective-permute-start(bf16[768,128]{1,0:T(8,128)(2,1)S(1)} %get-tuple-element.98), channel_id=1, source_target_pairs={{0,16},{16,0},{32,48},{48,32},{64,80},{80,64},{96,112},{112,96},{1... | collective-permute-start | bytes 589832 | tf_op jit(solution)/shard_map/ppermute | solution.py:392
  148.6 0.7 collective-permute-start.31
  149.9 0.8 collective-permute-start.32
  150.8 1.2 collective-permute-done.18.refs_2_
  152.0 1.5 collective-permute-start.26
  153.7 2.1 %collective-permute-start.19 = (bf16[384,128]{1,0:T(8,128)(2,1)S(1)}, bf16[384,128]{1,0:T(8,128)(2,1)S(1)}, u32[]{:S(2)}, u32[]{:S(2)}) collective-permute-start(bf16[384,128]{1,0:T(8,128)(2,1)S(1)} %merge.3.refs_1_), channel_id=1, source_target_pairs={{0,12},{2,14},{4,0},{6,2},{8,4},{10,6},{12,8},{14,10},{1,13},{3,15... | collective-permute-start | bytes 294920 | tf_op jit(solution)/shard_map/ppermute | solution.py:423
  155.8 7.9 %collective-permute-done.26.refs_1_ = bf16[384,128]{1,0:T(8,128)(2,1)S(1)} collective-permute-done((bf16[384,128]{1,0:T(8,128)(2,1)S(1)}, bf16[384,128]{1,0:T(8,128)(2,1)S(1)}, u32[]{:S(2)}, u32[]{:S(2)}) %collective-permute-start.26) | collective-permute-done | bytes 98336 | tf_op jit(solution)/shard_map/ppermute | solution.py:423
  164.0 2.9 %collective-permute-start.21 = (bf16[384,128]{1,0:T(8,128)(2,1)S(1)}, bf16[384,128]{1,0:T(8,128)(2,1)S(1)}, u32[]{:S(2)}, u32[]{:S(2)}) collective-permute-start(bf16[384,128]{1,0:T(8,128)(2,1)S(1)} %merge.3.refs_1_), channel_id=1, source_target_pairs={{0,4},{2,6},{4,8},{6,10},{8,12},{10,14},{12,0},{14,2},{1,5},{3,7},... | collective-permute-start | bytes 294920 | tf_op jit(solution)/shard_map/ppermute | solution.py:423
  168.1 2.4 %project.3.refs_12_ = f32[2,384,640]{2,1,0:T(8,128)S(1)} custom-call(bf16[384,384]{1,0:T(8,128)(2,1)S(1)} %merge.5.refs_0_, bf16[384,384]{1,0:T(8,128)(2,1)S(1)} %collective-permute-done.30.refs_1_, bf16[384,384]{1,0:T(8,128)(2,1)S(1)} %collective-permute-done.31.refs_2_, bf16[384,384]{1,0:T(8,128)(2,1)S(1)} %collective-permute-done.32.refs_3_, ...), custom_call_target="tpu_custom_call" | custom-call | flops 1509949440 | bytes 5111808 | tf_op jit(solution)/shard_map/project/pallas_call | solution.py:367
  170.5 2.6 %collective-permute-done.27.refs_2_ = bf16[384,128]{1,0:T(8,128)(2,1)S(1)} collective-permute-done((bf16[384,128]{1,0:T(8,128)(2,1)S(1)}, bf16[384,128]{1,0:T(8,128)(2,1)S(1)}, u32[]{:S(2)}, u32[]{:S(2)}) %collective-permute-start.27) | collective-permute-done | bytes 98336 | tf_op jit(solution)/shard_map/ppermute | solution.py:423
  173.1 1.0 collective-permute-done.28.refs_3_
  174.0 1.2 project.4.refs_13_
  175.3 1.3 project.5
  176.6 0.9 collective-permute-start.33
  177.4 4.1 %cross.1 = bf16[384,640]{1,0:T(8,128)(2,1)} custom-call(bf16[384,640]{1,0:T(8,128)(2,1)S(1)} %copy-done.7, bf16[512,640]{1,0:T(8,128)(2,1)S(1)} %copy-done.4, bf16[512,640]{1,0:T(8,128)(2,1)S(1)} %copy-done.5), custom_call_target="tpu_custom_call" | custom-call | flops 5033164800 | bytes 983040 | tf_op jit(solution)/shard_map/cross/pallas_call | solution.py:329
  181.6 5.4 %collective-permute-done.33 = bf16[384,640]{1,0:T(8,128)(2,1)S(1)} collective-permute-done((bf16[384,640]{1,0:T(8,128)(2,1)S(1)}, bf16[384,640]{1,0:T(8,128)(2,1)S(1)}, u32[]{:S(2)}, u32[]{:S(2)}) %collective-permute-start.33) | collective-permute-done | bytes 491552 | tf_op jit(solution)/shard_map/ppermute | solution.py:454
  187.0 0.9 add_convert_fusion
  (51 shorter events, 4.9 us)
Async XLA Ops:
  0.6 1.0 copy-start.1
  1.7 1.0 copy-start.2
  2.9 19.3 %collective-permute-start = (bf16[2304,128]{1,0:T(8,128)(2,1)S(1)}, bf16[2304,128]{1,0:T(8,128)(2,1)S(1)}, u32[]{:S(2)}, u32[]{:S(2)}) collective-permute-start(bf16[2304,128]{1,0:T(8,128)(2,1)S(1)} %get-tuple-element.58.refs_0_), channel_id=1, source_target_pairs={{0,32},{16,48},{32,64},{48,80},{64,96},{80,112},{96,128},{112,144}... | collective-permute-start | bytes 1769480 | tf_op jit(solution)/shard_map/ppermute | solution.py:412
  4.9 20.3 %collective-permute-start.10 = (bf16[2304,128]{1,0:T(8,128)(2,1)S(1)}, bf16[2304,128]{1,0:T(8,128)(2,1)S(1)}, u32[]{:S(2)}, u32[]{:S(2)}) collective-permute-start(bf16[2304,128]{1,0:T(8,128)(2,1)S(1)} %get-tuple-element.58.refs_0_), channel_id=1, source_target_pairs={{0,224},{16,240},{32,0},{48,16},{64,32},{80,48},{96,64},{112,80},{... | collective-permute-start | bytes 1769480 | tf_op jit(solution)/shard_map/ppermute | solution.py:412
  9.7 0.7 copy-start.3
  13.3 2.9 %copy-start = (bf16[640,5120]{1,0:T(8,128)(2,1)S(1)}, bf16[640,5120]{1,0:T(8,128)(2,1)}, u32[]{:S(2)}) copy-start(bf16[640,5120]{1,0:T(8,128)(2,1)} %weight_ref.1) | copy-start | bytes 19660804
  16.2 67.7 %copy-start.6 = (bf16[384,640]{1,0:T(8,128)(2,1)S(1)}, bf16[384,640]{1,0:T(8,128)(2,1)}, u32[]{:S(2)}) copy-start(bf16[384,640]{1,0:T(8,128)(2,1)} %q_ref.6) | copy-start | bytes 1474564
  22.1 27.4 %collective-permute-start.2 = (bf16[2304,128]{1,0:T(8,128)(2,1)S(1)}, bf16[2304,128]{1,0:T(8,128)(2,1)S(1)}, u32[]{:S(2)}, u32[]{:S(2)}) collective-permute-start(bf16[2304,128]{1,0:T(8,128)(2,1)S(1)} %collective-permute-done.refs_1_), channel_id=1, source_target_pairs={{0,32},{16,48},{32,64},{48,80},{64,96},{80,112},{96,128},{112,144}... | collective-permute-start | bytes 1769480 | tf_op jit(solution)/shard_map/ppermute | solution.py:412
  22.1 24.1 %collective-permute-start.3 = (bf16[1536,128]{1,0:T(8,128)(2,1)S(1)}, bf16[1536,128]{1,0:T(8,128)(2,1)S(1)}, u32[]{:S(2)}, u32[]{:S(2)}) collective-permute-start(bf16[1536,128]{1,0:T(8,128)(2,1)S(1)} %get-tuple-element.65.refs_0_), channel_id=1, source_target_pairs={{0,32},{16,48},{32,64},{48,80},{64,96},{80,112},{96,128},{112,144}... | collective-permute-start | bytes 1179656 | tf_op jit(solution)/shard_map/ppermute | solution.py:412
  22.1 31.3 %collective-permute-start.6 = (bf16[640,640]{1,0:T(8,128)(2,1)S(1)}, bf16[640,640]{1,0:T(8,128)(2,1)S(1)}, u32[]{:S(2)}, u32[]{:S(2)}) collective-permute-start(bf16[640,640]{1,0:T(8,128)(2,1)S(1)} %get-tuple-element.71), channel_id=1, source_target_pairs={{0,12},{2,14},{4,0},{6,2},{8,4},{10,6},{12,8},{14,10},{1,13},{3,15... | collective-permute-start | bytes 2457608 | tf_op jit(solution)/shard_map/ppermute | solution.py:435
  25.2 26.0 %collective-permute-start.11 = (bf16[2304,128]{1,0:T(8,128)(2,1)S(1)}, bf16[2304,128]{1,0:T(8,128)(2,1)S(1)}, u32[]{:S(2)}, u32[]{:S(2)}) collective-permute-start(bf16[2304,128]{1,0:T(8,128)(2,1)S(1)} %collective-permute-done.10.refs_7_), channel_id=1, source_target_pairs={{0,224},{16,240},{32,0},{48,16},{64,32},{80,48},{96,64},{112,80},{... | collective-permute-start | bytes 1769480 | tf_op jit(solution)/shard_map/ppermute | solution.py:412
  28.4 21.7 %collective-permute-start.12 = (bf16[1536,128]{1,0:T(8,128)(2,1)S(1)}, bf16[1536,128]{1,0:T(8,128)(2,1)S(1)}, u32[]{:S(2)}, u32[]{:S(2)}) collective-permute-start(bf16[1536,128]{1,0:T(8,128)(2,1)S(1)} %get-tuple-element.65.refs_0_), channel_id=1, source_target_pairs={{0,224},{16,240},{32,0},{48,16},{64,32},{80,48},{96,64},{112,80},{... | collective-permute-start | bytes 1179656 | tf_op jit(solution)/shard_map/ppermute | solution.py:412
  46.3 22.7 %collective-permute-start.7 = (bf16[640,640]{1,0:T(8,128)(2,1)S(1)}, bf16[640,640]{1,0:T(8,128)(2,1)S(1)}, u32[]{:S(2)}, u32[]{:S(2)}) collective-permute-start(bf16[640,640]{1,0:T(8,128)(2,1)S(1)} %get-tuple-element.72), channel_id=1, source_target_pairs={{0,8},{2,10},{4,12},{6,14},{8,0},{10,2},{12,4},{14,6},{1,9},{3,11}... | collective-permute-start | bytes 2457608 | tf_op jit(solution)/shard_map/ppermute | solution.py:435
  49.5 34.4 %collective-permute-start.8 = (bf16[640,640]{1,0:T(8,128)(2,1)S(1)}, bf16[640,640]{1,0:T(8,128)(2,1)S(1)}, u32[]{:S(2)}, u32[]{:S(2)}) collective-permute-start(bf16[640,640]{1,0:T(8,128)(2,1)S(1)} %get-tuple-element.73), channel_id=1, source_target_pairs={{0,4},{2,6},{4,8},{6,10},{8,12},{10,14},{12,0},{14,2},{1,5},{3,7},... | collective-permute-start | bytes 2457608 | tf_op jit(solution)/shard_map/ppermute | solution.py:435
  50.2 33.7 %collective-permute-start.4 = (bf16[2304,128]{1,0:T(8,128)(2,1)S(1)}, bf16[2304,128]{1,0:T(8,128)(2,1)S(1)}, u32[]{:S(2)}, u32[]{:S(2)}) collective-permute-start(bf16[2304,128]{1,0:T(8,128)(2,1)S(1)} %collective-permute-done.2.refs_2_), channel_id=1, source_target_pairs={{0,32},{16,48},{32,64},{48,80},{64,96},{80,112},{96,128},{112,144}... | collective-permute-start | bytes 1769480 | tf_op jit(solution)/shard_map/ppermute | solution.py:412
  51.2 34.0 %collective-permute-start.14 = (bf16[2304,128]{1,0:T(8,128)(2,1)S(1)}, bf16[2304,128]{1,0:T(8,128)(2,1)S(1)}, u32[]{:S(2)}, u32[]{:S(2)}) collective-permute-start(bf16[2304,128]{1,0:T(8,128)(2,1)S(1)} %collective-permute-done.11.refs_6_), channel_id=1, source_target_pairs={{0,224},{16,240},{32,0},{48,16},{64,32},{80,48},{96,64},{112,80},{... | collective-permute-start | bytes 1769480 | tf_op jit(solution)/shard_map/ppermute | solution.py:412
  53.4 31.7 %collective-permute-start.13 = (bf16[1536,128]{1,0:T(8,128)(2,1)S(1)}, bf16[1536,128]{1,0:T(8,128)(2,1)S(1)}, u32[]{:S(2)}, u32[]{:S(2)}) collective-permute-start(bf16[1536,128]{1,0:T(8,128)(2,1)S(1)} %collective-permute-done.12.refs_7_), channel_id=1, source_target_pairs={{0,224},{16,240},{32,0},{48,16},{64,32},{80,48},{96,64},{112,80},{... | collective-permute-start | bytes 1179656 | tf_op jit(solution)/shard_map/ppermute | solution.py:412
  83.8 24.9 %collective-permute-start.9 = (bf16[2304,128]{1,0:T(8,128)(2,1)S(1)}, bf16[2304,128]{1,0:T(8,128)(2,1)S(1)}, u32[]{:S(2)}, u32[]{:S(2)}) collective-permute-start(bf16[2304,128]{1,0:T(8,128)(2,1)S(1)} %collective-permute-done.4.refs_3_), channel_id=1, source_target_pairs={{0,32},{16,48},{32,64},{48,80},{64,96},{80,112},{96,128},{112,144}... | collective-permute-start | bytes 1769480 | tf_op jit(solution)/shard_map/ppermute | solution.py:412
  83.9 24.9 %collective-permute-start.1 = (bf16[384,640]{1,0:T(8,128)(2,1)S(1)}, bf16[384,640]{1,0:T(8,128)(2,1)S(1)}, u32[]{:S(2)}, u32[]{:S(2)}) collective-permute-start(bf16[384,640]{1,0:T(8,128)(2,1)S(1)} %copy-done.6), channel_id=1, source_target_pairs={{0,16},{16,0},{32,48},{48,32},{64,80},{80,64},{96,112},{112,96},{1... | collective-permute-start | bytes 1474568 | tf_op jit(solution)/shard_map/ppermute | solution.py:392
  85.1 11.1 %collective-permute-start.16 = (bf16[1536,128]{1,0:T(8,128)(2,1)S(1)}, bf16[1536,128]{1,0:T(8,128)(2,1)S(1)}, u32[]{:S(2)}, u32[]{:S(2)}) collective-permute-start(bf16[1536,128]{1,0:T(8,128)(2,1)S(1)} %collective-permute-done.13.refs_6_), channel_id=1, source_target_pairs={{0,224},{16,240},{32,0},{48,16},{64,32},{80,48},{96,64},{112,80},{... | collective-permute-start | bytes 1179656 | tf_op jit(solution)/shard_map/ppermute | solution.py:412
  88.3 20.4 %collective-permute-start.5 = (bf16[1536,128]{1,0:T(8,128)(2,1)S(1)}, bf16[1536,128]{1,0:T(8,128)(2,1)S(1)}, u32[]{:S(2)}, u32[]{:S(2)}) collective-permute-start(bf16[1536,128]{1,0:T(8,128)(2,1)S(1)} %collective-permute-done.3.refs_1_), channel_id=1, source_target_pairs={{0,32},{16,48},{32,64},{48,80},{64,96},{80,112},{96,128},{112,144}... | collective-permute-start | bytes 1179656 | tf_op jit(solution)/shard_map/ppermute | solution.py:412
  118.1 11.5 %collective-permute-start.15 = (bf16[1536,128]{1,0:T(8,128)(2,1)S(1)}, bf16[1536,128]{1,0:T(8,128)(2,1)S(1)}, u32[]{:S(2)}, u32[]{:S(2)}) collective-permute-start(bf16[1536,128]{1,0:T(8,128)(2,1)S(1)} %collective-permute-done.5.refs_2_), channel_id=1, source_target_pairs={{0,32},{16,48},{32,64},{48,80},{64,96},{80,112},{96,128},{112,144}... | collective-permute-start | bytes 1179656 | tf_op jit(solution)/shard_map/ppermute | solution.py:412
  119.0 12.8 %collective-permute-start.17 = (bf16[1536,128]{1,0:T(8,128)(2,1)S(1)}, bf16[1536,128]{1,0:T(8,128)(2,1)S(1)}, u32[]{:S(2)}, u32[]{:S(2)}) collective-permute-start(bf16[1536,128]{1,0:T(8,128)(2,1)S(1)} %collective-permute-done.16.refs_5_), channel_id=1, source_target_pairs={{0,224},{16,240},{32,0},{48,16},{64,32},{80,48},{96,64},{112,80},{... | collective-permute-start | bytes 1179656 | tf_op jit(solution)/shard_map/ppermute | solution.py:412
  121.4 27.1 %collective-permute-start.22 = (bf16[640,640]{1,0:T(8,128)(2,1)S(1)}, bf16[640,640]{1,0:T(8,128)(2,1)S(1)}, u32[]{:S(2)}, u32[]{:S(2)}) collective-permute-start(bf16[640,640]{1,0:T(8,128)(2,1)S(1)} %collective-permute-done.6.refs_6_.refs_7_), channel_id=1, source_target_pairs={{0,1},{1,0},{2,3},{3,2},{4,5},{5,4},{6,7},{7,6},{8,9},{9,8},{10,11... | collective-permute-start | bytes 2457608 | tf_op jit(solution)/shard_map/ppermute | solution.py:443
  121.4 27.2 %collective-permute-start.23 = (bf16[640,640]{1,0:T(8,128)(2,1)S(1)}, bf16[640,640]{1,0:T(8,128)(2,1)S(1)}, u32[]{:S(2)}, u32[]{:S(2)}) collective-permute-start(bf16[640,640]{1,0:T(8,128)(2,1)S(1)} %collective-permute-done.7.refs_8_.refs_9_), channel_id=1, source_target_pairs={{0,1},{1,0},{2,3},{3,2},{4,5},{5,4},{6,7},{7,6},{8,9},{9,8},{10,11... | collective-permute-start | bytes 2457608 | tf_op jit(solution)/shard_map/ppermute | solution.py:443
  121.9 31.8 %collective-permute-start.24 = (bf16[640,640]{1,0:T(8,128)(2,1)S(1)}, bf16[640,640]{1,0:T(8,128)(2,1)S(1)}, u32[]{:S(2)}, u32[]{:S(2)}) collective-permute-start(bf16[640,640]{1,0:T(8,128)(2,1)S(1)} %collective-permute-done.8.refs_10_.refs_11_), channel_id=1, source_target_pairs={{0,1},{1,0},{2,3},{3,2},{4,5},{5,4},{6,7},{7,6},{8,9},{9,8},{10,11... | collective-permute-start | bytes 2457608 | tf_op jit(solution)/shard_map/ppermute | solution.py:443
  129.5 16.6 %collective-permute-start.29 = (bf16[2304,128]{1,0:T(8,128)(2,1)S(1)}, bf16[2304,128]{1,0:T(8,128)(2,1)S(1)}, u32[]{:S(2)}, u32[]{:S(2)}) collective-permute-start(bf16[2304,128]{1,0:T(8,128)(2,1)S(1)} %get-tuple-element.109), channel_id=1, source_target_pairs={{0,16},{16,0},{32,48},{48,32},{64,80},{80,64},{96,112},{112,96},{1... | collective-permute-start | bytes 1769480 | tf_op jit(solution)/shard_map/ppermute | solution.py:392
  136.1 13.8 %collective-permute-start.25 = (bf16[768,128]{1,0:T(8,128)(2,1)S(1)}, bf16[768,128]{1,0:T(8,128)(2,1)S(1)}, u32[]{:S(2)}, u32[]{:S(2)}) collective-permute-start(bf16[768,128]{1,0:T(8,128)(2,1)S(1)} %get-tuple-element.106), channel_id=1, source_target_pairs={{0,16},{16,0},{32,48},{48,32},{64,80},{80,64},{96,112},{112,96},{1... | collective-permute-start | bytes 589832 | tf_op jit(solution)/shard_map/ppermute | solution.py:392
  146.1 5.9 %collective-permute-start.18 = (bf16[768,128]{1,0:T(8,128)(2,1)S(1)}, bf16[768,128]{1,0:T(8,128)(2,1)S(1)}, u32[]{:S(2)}, u32[]{:S(2)}) collective-permute-start(bf16[768,128]{1,0:T(8,128)(2,1)S(1)} %get-tuple-element.98), channel_id=1, source_target_pairs={{0,16},{16,0},{32,48},{48,32},{64,80},{80,64},{96,112},{112,96},{1... | collective-permute-start | bytes 589832 | tf_op jit(solution)/shard_map/ppermute | solution.py:392
  148.5 15.5 %collective-permute-start.30 = (bf16[384,384]{1,0:T(8,128)(2,1)S(1)}, bf16[384,384]{1,0:T(8,128)(2,1)S(1)}, u32[]{:S(2)}, u32[]{:S(2)}) collective-permute-start(bf16[384,384]{1,0:T(8,128)(2,1)S(1)} %merge.5.refs_0_), channel_id=1, source_target_pairs={{0,12},{2,14},{4,0},{6,2},{8,4},{10,6},{12,8},{14,10},{1,13},{3,15... | collective-permute-start | bytes 884744 | tf_op jit(solution)/shard_map/ppermute | solution.py:423
  148.6 18.3 %collective-permute-start.31 = (bf16[384,384]{1,0:T(8,128)(2,1)S(1)}, bf16[384,384]{1,0:T(8,128)(2,1)S(1)}, u32[]{:S(2)}, u32[]{:S(2)}) collective-permute-start(bf16[384,384]{1,0:T(8,128)(2,1)S(1)} %merge.5.refs_0_), channel_id=1, source_target_pairs={{0,8},{2,10},{4,12},{6,14},{8,0},{10,2},{12,4},{14,6},{1,9},{3,11}... | collective-permute-start | bytes 884744 | tf_op jit(solution)/shard_map/ppermute | solution.py:423
  149.9 17.6 %collective-permute-start.32 = (bf16[384,384]{1,0:T(8,128)(2,1)S(1)}, bf16[384,384]{1,0:T(8,128)(2,1)S(1)}, u32[]{:S(2)}, u32[]{:S(2)}) collective-permute-start(bf16[384,384]{1,0:T(8,128)(2,1)S(1)} %merge.5.refs_0_), channel_id=1, source_target_pairs={{0,4},{2,6},{4,8},{6,10},{8,12},{10,14},{12,0},{14,2},{1,5},{3,7},... | collective-permute-start | bytes 884744 | tf_op jit(solution)/shard_map/ppermute | solution.py:423
  152.0 11.7 %collective-permute-start.26 = (bf16[384,128]{1,0:T(8,128)(2,1)S(1)}, bf16[384,128]{1,0:T(8,128)(2,1)S(1)}, u32[]{:S(2)}, u32[]{:S(2)}) collective-permute-start(bf16[384,128]{1,0:T(8,128)(2,1)S(1)} %merge.4.refs_0_), channel_id=1, source_target_pairs={{0,12},{2,14},{4,0},{6,2},{8,4},{10,6},{12,8},{14,10},{1,13},{3,15... | collective-permute-start | bytes 294920 | tf_op jit(solution)/shard_map/ppermute | solution.py:423
  153.7 21.5 %collective-permute-start.19 = (bf16[384,128]{1,0:T(8,128)(2,1)S(1)}, bf16[384,128]{1,0:T(8,128)(2,1)S(1)}, u32[]{:S(2)}, u32[]{:S(2)}) collective-permute-start(bf16[384,128]{1,0:T(8,128)(2,1)S(1)} %merge.3.refs_1_), channel_id=1, source_target_pairs={{0,12},{2,14},{4,0},{6,2},{8,4},{10,6},{12,8},{14,10},{1,13},{3,15... | collective-permute-start | bytes 294920 | tf_op jit(solution)/shard_map/ppermute | solution.py:423
  163.7 11.5 %collective-permute-start.20 = (bf16[384,128]{1,0:T(8,128)(2,1)S(1)}, bf16[384,128]{1,0:T(8,128)(2,1)S(1)}, u32[]{:S(2)}, u32[]{:S(2)}) collective-permute-start(bf16[384,128]{1,0:T(8,128)(2,1)S(1)} %merge.3.refs_1_), channel_id=1, source_target_pairs={{0,8},{2,10},{4,12},{6,14},{8,0},{10,2},{12,4},{14,6},{1,9},{3,11}... | collective-permute-start | bytes 294920 | tf_op jit(solution)/shard_map/ppermute | solution.py:423
  164.0 11.3 %collective-permute-start.21 = (bf16[384,128]{1,0:T(8,128)(2,1)S(1)}, bf16[384,128]{1,0:T(8,128)(2,1)S(1)}, u32[]{:S(2)}, u32[]{:S(2)}) collective-permute-start(bf16[384,128]{1,0:T(8,128)(2,1)S(1)} %merge.3.refs_1_), channel_id=1, source_target_pairs={{0,4},{2,6},{4,8},{6,10},{8,12},{10,14},{12,0},{14,2},{1,5},{3,7},... | collective-permute-start | bytes 294920 | tf_op jit(solution)/shard_map/ppermute | solution.py:423
  166.9 6.2 %collective-permute-start.27 = (bf16[384,128]{1,0:T(8,128)(2,1)S(1)}, bf16[384,128]{1,0:T(8,128)(2,1)S(1)}, u32[]{:S(2)}, u32[]{:S(2)}) collective-permute-start(bf16[384,128]{1,0:T(8,128)(2,1)S(1)} %merge.4.refs_0_), channel_id=1, source_target_pairs={{0,8},{2,10},{4,12},{6,14},{8,0},{10,2},{12,4},{14,6},{1,9},{3,11}... | collective-permute-start | bytes 294920 | tf_op jit(solution)/shard_map/ppermute | solution.py:423
  167.5 6.6 %collective-permute-start.28 = (bf16[384,128]{1,0:T(8,128)(2,1)S(1)}, bf16[384,128]{1,0:T(8,128)(2,1)S(1)}, u32[]{:S(2)}, u32[]{:S(2)}) collective-permute-start(bf16[384,128]{1,0:T(8,128)(2,1)S(1)} %merge.4.refs_0_), channel_id=1, source_target_pairs={{0,4},{2,6},{4,8},{6,10},{8,12},{10,14},{12,0},{14,2},{1,5},{3,7},... | collective-permute-start | bytes 294920 | tf_op jit(solution)/shard_map/ppermute | solution.py:423
  175.2 2.2 %copy-start.4 = (bf16[512,640]{1,0:T(8,128)(2,1)S(1)}, bf16[512,640]{1,0:T(8,128)(2,1)}, u32[]{:S(2)}) copy-start(bf16[512,640]{1,0:T(8,128)(2,1)} %k_ref.3) | copy-start | bytes 1966084
  175.2 2.2 %copy-start.5 = (bf16[512,640]{1,0:T(8,128)(2,1)S(1)}, bf16[512,640]{1,0:T(8,128)(2,1)}, u32[]{:S(2)}) copy-start(bf16[512,640]{1,0:T(8,128)(2,1)} %v_ref.3) | copy-start | bytes 1966084
  175.2 2.2 %copy-start.7 = (bf16[384,640]{1,0:T(8,128)(2,1)S(1)}, bf16[384,640]{1,0:T(8,128)(2,1)}, u32[]{:S(2)}) copy-start(bf16[384,640]{1,0:T(8,128)(2,1)} %q_ref.7) | copy-start | bytes 1474564
  176.6 10.4 %collective-permute-start.33 = (bf16[384,640]{1,0:T(8,128)(2,1)S(1)}, bf16[384,640]{1,0:T(8,128)(2,1)S(1)}, u32[]{:S(2)}, u32[]{:S(2)}) collective-permute-start(bf16[384,640]{1,0:T(8,128)(2,1)S(1)} %get-tuple-element.111), channel_id=1, source_target_pairs={{0,2},{2,0},{4,6},{6,4},{8,10},{10,8},{12,14},{14,12},{1,3},{3,1},... | collective-permute-start | bytes 1474568 | tf_op jit(solution)/shard_map/ppermute | solution.py:454
where the time goes:
time: 187 us; the launch traced here: 188 us
  waiting for transfers between devices  103 us (55%)
  starting transfers between devices  45.1 us (24%)
  Pallas kernels  31.2 us (17%)
  local copies, waits for them, and re-layouts  6.37 us (3%)
    ppermute x14, waiting for transfers between devices, hop(): held[group][place] = lax.ppermute(array, 'seq', z_shift(way))  49.3 us
    ppermute x3, waiting for transfers between devices, body(): lax.ppermute(tiles[dy], 'head', y_shift(dy))  29.8 us
    ppermute x14, starting transfers between devices, hop(): held[group][place] = lax.ppermute(array, 'seq', z_shift(way))  21.6 us
    pallas_call x3, Pallas kernels, attend(): pl.pallas_call(functools.partial(attend_kernel, heads, first, planes), ou...  17.8 us
    ppermute x9, waiting for transfers between devices, along_y(): lax.ppermute(array, 'head', y_shift(-dy))  11.5 us
    ppermute x9, starting transfers between devices, along_y(): lax.ppermute(array, 'head', y_shift(-dy))  9.46 us
    ppermute x4, waiting for transfers between devices, to_other(): return lax.ppermute(array, 'seq', swap)  7.38 us
    ppermute x3, starting transfers between devices, body(): lax.ppermute(tiles[dy], 'head', y_shift(dy))  6.89 us
  transfers between devices with their start and end apart: 34, of which 14 were waited for; matrix products, arithmetic and copies ran while one was open for 0% of the time, Pallas kernels for 11%

commit v1 on v0

--- a/solution.py
+++ b/solution.py
@@ -433,24 +433,28 @@
     hop(-1, 0, 2)
     blocks, counts, near = early
     tiles[1:n_y] = [lax.ppermute(tiles[dy], "head", y_shift(dy)) for dy in range(1, n_y)][::-1]
-    hop(1, 0, 3)
+    one_away = [(tiles[1], tiles[n_y - 1])]
+    hop(1, 0, 3, one_away)
+    tiles[1], tiles[n_y - 1] = one_away[0]
     hop(-1, 0, 3)
-    far_tiles = [lax.optimization_barrier(tuple(tiles[1:n_y]))]
-    hop(1, 0, 4, far_tiles)
+    hop(1, 0, 4)
     hop(-1, 1, 2)
-    weights = [tiles[0], tiles[n_y]]
-    for mine in far_tiles[0]:
-        weights += [mine, lax.ppermute(mine, "pair", [(0, 1), (1, 0)])]
     hop(1, 1, 2)
     hop(-1, 1, 3)
+    near, tiles[2] = lax.optimization_barrier((near, tiles[2]))
+    weights = [tiles[0], tiles[n_y]]
+    for mine in tiles[1:n_y]:
+        weights += [mine, lax.ppermute(mine, "pair", [(0, 1), (1, 0)])]
     most = partial(0, 0, 3)
     hop(1, 1, 3, most)
     hop(-1, 1, 4, most)
     before = project(GROUPS[0][0], along_y(join(most)), weights)
     one, two = partial(1, 0, 1), partial(1, 1, 2)
+    two = join(two)
+    before, two = lax.optimization_barrier((before, two))
     before = project(GROUPS[1][0], along_y(join(one)), weights, before)
     keep_block = (lax.rem(head, 2) != pair).astype(jnp.int32)
-    keep, send = project(GROUPS[1][1], along_y(join(two)), weights, before, keep_block)
+    keep, send = project(GROUPS[1][1], along_y(two), weights, before, keep_block)
     got = lax.ppermute(send, "head", [(g, g ^ 1) for g in range(n_head)])
     return (keep + got.astype(jnp.float32)).astype(jnp.bfloat16), cross_heads
 

time: 187 us -> 161 us (0.86); the launches traced: 188 us -> 160 us
  waiting for transfers between devices: 103 us -> 70.8 us
  Pallas kernels: 31.2 us -> 36.6 us
    ppermute x3, waiting for transfers between devices: 29.8 us -> 0.01 us  [body(): lax.ppermute(tiles[dy], 'head', y_shift(dy))]
    ppermute x4, waiting for transfers between devices: 7.38 us -> 2.46 us  [to_other(): return lax.ppermute(array, 'seq', swap)]
    pallas_call x3, Pallas kernels: 17.8 us -> 21.2 us  [attend(): pl.pallas_call(functools.partial(attend_kernel, heads, first, planes), ou...]
    ppermute x9, starting transfers between devices: 9.46 us -> 11.5 us  [along_y(): lax.ppermute(array, 'head', y_shift(-dy))]
    unnamed x17 -> x23, local copies, waits for them, and re-layouts: 6.37 us -> 6.06 us
  transfers between devices with their start and end apart: 34 -> 34, of which waited for: 14 -> 17; matrix products, arithmetic and copies ran while one was open for 0% -> 0% of each run, Pallas kernels for 11% -> 15%
where the time goes in v1:
time: 161 us; the launch traced here: 160 us
  waiting for transfers between devices  70.8 us (44%)
  starting transfers between devices  44.8 us (28%)
  Pallas kernels  36.6 us (23%)
  local copies, waits for them, and re-layouts  6.06 us (4%)
    ppermute x14, waiting for transfers between devices, hop(): held[group][place] = lax.ppermute(array, 'seq', z_shift(way))  50.9 us
    pallas_call x3, Pallas kernels, attend(): pl.pallas_call(functools.partial(attend_kernel, heads, first, planes), ou...  21.2 us
    ppermute x14, starting transfers between devices, hop(): held[group][place] = lax.ppermute(array, 'seq', z_shift(way))  20.6 us
    ppermute x9, waiting for transfers between devices, along_y(): lax.ppermute(array, 'head', y_shift(-dy))  11.9 us
    ppermute x9, starting transfers between devices, along_y(): lax.ppermute(array, 'head', y_shift(-dy))  11.5 us
    ppermute x3, starting transfers between devices, body(): lax.ppermute(tiles[dy], 'head', y_shift(dy))  7.09 us
    unnamed x23, local copies, waits for them, and re-layouts  6.06 us
    ppermute x1, waiting for transfers between devices, body(): got = lax.ppermute(send, 'head', [(g, g ^ 1) for g in range(n_head)])  5.56 us
  transfers between devices with their start and end apart: 34, of which 17 were waited for; matrix products, arithmetic and copies ran while one was open for 0% of the time, Pallas kernels for 15%

profile of v1, /device:TPU:4, one launch (start us, length us, event | category | flops | bytes accessed | tf_op | source)
XLA Modules:
  0.0 160.0 jit_solution(4777435657078884829)
XLA Ops:
  0.6 1.0 copy-done.1
  1.7 1.0 copy-done.2
  2.7 1.1 pack.1
  3.8 1.9 %collective-permute-start.6 = (bf16[2304,128]{1,0:T(8,128)(2,1)}, bf16[2304,128]{1,0:T(8,128)(2,1)}, u32[]{:S(2)}, u32[]{:S(2)}) collective-permute-start(bf16[2304,128]{1,0:T(8,128)(2,1)} %get-tuple-element.57.refs_0_), channel_id=1, source_target_pairs={{0,32},{16,48},{32,64},{48,80},{64,96},{80,112},{96,128},{112,144}... | collective-permute-start | bytes 1769480 | tf_op jit(solution)/shard_map/ppermute | solution.py:412
  5.7 3.9 %collective-permute-start = (bf16[2304,128]{1,0:T(8,128)(2,1)}, bf16[2304,128]{1,0:T(8,128)(2,1)}, u32[]{:S(2)}, u32[]{:S(2)}) collective-permute-start(bf16[2304,128]{1,0:T(8,128)(2,1)} %get-tuple-element.57.refs_0_), channel_id=1, source_target_pairs={{0,224},{16,240},{32,0},{48,16},{64,32},{80,48},{96,64},{112,80},{... | collective-permute-start | bytes 1769480 | tf_op jit(solution)/shard_map/ppermute | solution.py:412
  9.7 2.9 %copy-done = bf16[640,5120]{1,0:T(8,128)(2,1)S(1)} copy-done((bf16[640,5120]{1,0:T(8,128)(2,1)S(1)}, bf16[640,5120]{1,0:T(8,128)(2,1)}, u32[]{:S(2)}) %copy-start) | copy-done | bytes 6553624
  12.5 1.3 tile.1
  13.9 1.7 %collective-permute-start.10 = (bf16[640,640]{1,0:T(8,128)(2,1)}, bf16[640,640]{1,0:T(8,128)(2,1)S(1)}, u32[]{:S(2)}, u32[]{:S(2)}) collective-permute-start(bf16[640,640]{1,0:T(8,128)(2,1)} %get-tuple-element.73), channel_id=1, source_target_pairs={{0,4},{2,6},{4,8},{6,10},{8,12},{10,14},{12,0},{14,2},{1,5},{3,7},... | collective-permute-start | bytes 2457608 | tf_op jit(solution)/shard_map/ppermute | solution.py:435
  15.5 2.2 %collective-permute-start.9 = (bf16[640,640]{1,0:T(8,128)(2,1)}, bf16[640,640]{1,0:T(8,128)(2,1)S(1)}, u32[]{:S(2)}, u32[]{:S(2)}) collective-permute-start(bf16[640,640]{1,0:T(8,128)(2,1)} %get-tuple-element.72), channel_id=1, source_target_pairs={{0,12},{2,14},{4,0},{6,2},{8,4},{10,6},{12,8},{14,10},{1,13},{3,15... | collective-permute-start | bytes 2457608 | tf_op jit(solution)/shard_map/ppermute | solution.py:435
  17.9 3.3 %plan.1 = (s32[6,13]{1,0:T(8,128)S(1)}, s32[6]{0:T(128)S(1)}, s32[8]{0:T(128)S(1)}) custom-call(s32[1]{0:T(128)} %bitcast.2.seq_ref, s32[48,18]{1,0:T(8,128)S(1)} %copy.11.list_ref, s32[48]{0:T(128)S(1)} %copy-done.3), custom_call_target="tpu_custom_call" | custom-call | flops 1000 | bytes 8000 | tf_op jit(solution)/shard_map/plan/pallas_call | solution.py:60
  21.2 3.0 %collective-permute-done.6.refs_1_ = bf16[2304,128]{1,0:T(8,128)(2,1)} collective-permute-done((bf16[2304,128]{1,0:T(8,128)(2,1)}, bf16[2304,128]{1,0:T(8,128)(2,1)}, u32[]{:S(2)}, u32[]{:S(2)}) %collective-permute-start.6) | collective-permute-done | bytes 589856 | tf_op jit(solution)/shard_map/ppermute | solution.py:412
  24.1 3.2 %collective-permute-start.1 = (bf16[2304,128]{1,0:T(8,128)(2,1)}, bf16[2304,128]{1,0:T(8,128)(2,1)S(1)}, u32[]{:S(2)}, u32[]{:S(2)}) collective-permute-start(bf16[2304,128]{1,0:T(8,128)(2,1)} %collective-permute-done.refs_7_), channel_id=1, source_target_pairs={{0,224},{16,240},{32,0},{48,16},{64,32},{80,48},{96,64},{112,80},{... | collective-permute-start | bytes 1769480 | tf_op jit(solution)/shard_map/ppermute | solution.py:412
  27.4 5.2 %collective-permute-done.8.refs_1_ = bf16[1536,128]{1,0:T(8,128)(2,1)} collective-permute-done((bf16[1536,128]{1,0:T(8,128)(2,1)}, bf16[1536,128]{1,0:T(8,128)(2,1)}, u32[]{:S(2)}, u32[]{:S(2)}) %collective-permute-start.8) | collective-permute-done | bytes 393248 | tf_op jit(solution)/shard_map/ppermute | solution.py:412
  32.6 2.1 %collective-permute-start.2 = (bf16[1536,128]{1,0:T(8,128)(2,1)}, bf16[1536,128]{1,0:T(8,128)(2,1)S(1)}, u32[]{:S(2)}, u32[]{:S(2)}) collective-permute-start(bf16[1536,128]{1,0:T(8,128)(2,1)} %get-tuple-element.59.refs_0_), channel_id=1, source_target_pairs={{0,224},{16,240},{32,0},{48,16},{64,32},{80,48},{96,64},{112,80},{... | collective-permute-start | bytes 1179656 | tf_op jit(solution)/shard_map/ppermute | solution.py:412
  34.6 9.6 %collective-permute-done.7.refs_2_ = bf16[2304,128]{1,0:T(8,128)(2,1)S(1)} collective-permute-done((bf16[2304,128]{1,0:T(8,128)(2,1)}, bf16[2304,128]{1,0:T(8,128)(2,1)S(1)}, u32[]{:S(2)}, u32[]{:S(2)}) %collective-permute-start.7) | collective-permute-done | bytes 589856 | tf_op jit(solution)/shard_map/ppermute | solution.py:412
  44.3 2.8 %collective-permute-done.2.refs_7_ = bf16[1536,128]{1,0:T(8,128)(2,1)S(1)} collective-permute-done((bf16[1536,128]{1,0:T(8,128)(2,1)}, bf16[1536,128]{1,0:T(8,128)(2,1)S(1)}, u32[]{:S(2)}, u32[]{:S(2)}) %collective-permute-start.2) | collective-permute-done | bytes 393248 | tf_op jit(solution)/shard_map/ppermute | solution.py:412
  47.0 3.6 %collective-permute-start.4 = (bf16[2304,128]{1,0:T(8,128)(2,1)S(1)}, bf16[2304,128]{1,0:T(8,128)(2,1)S(1)}, u32[]{:S(2)}, u32[]{:S(2)}) collective-permute-start(bf16[2304,128]{1,0:T(8,128)(2,1)S(1)} %collective-permute-done.1.refs_6_), channel_id=1, source_target_pairs={{0,224},{16,240},{32,0},{48,16},{64,32},{80,48},{96,64},{112,80},{... | collective-permute-start | bytes 1769480 | tf_op jit(solution)/shard_map/ppermute | solution.py:412
  50.6 3.2 %collective-permute-start.14 = (bf16[640,640]{1,0:T(8,128)(2,1)}, bf16[640,640]{1,0:T(8,128)(2,1)S(1)}, u32[]{:S(2)}, u32[]{:S(2)}) collective-permute-start(bf16[640,640]{1,0:T(8,128)(2,1)} %copy-done.4), channel_id=1, source_target_pairs={{0,8},{2,10},{4,12},{6,14},{8,0},{10,2},{12,4},{14,6},{1,9},{3,11}... | collective-permute-start | bytes 2457608 | tf_op jit(solution)/shard_map/ppermute | solution.py:435
  53.8 6.2 %collective-permute-done.11.refs_3_ = bf16[2304,128]{1,0:T(8,128)(2,1)S(1)} collective-permute-done((bf16[2304,128]{1,0:T(8,128)(2,1)S(1)}, bf16[2304,128]{1,0:T(8,128)(2,1)S(1)}, u32[]{:S(2)}, u32[]{:S(2)}) %collective-permute-start.11) | collective-permute-done | bytes 589856 | tf_op jit(solution)/shard_map/ppermute | solution.py:412
  60.0 1.2 collective-permute-start.15
  61.2 7.9 %collective-permute-done.3.refs_6_ = bf16[1536,128]{1,0:T(8,128)(2,1)S(1)} collective-permute-done((bf16[1536,128]{1,0:T(8,128)(2,1)S(1)}, bf16[1536,128]{1,0:T(8,128)(2,1)S(1)}, u32[]{:S(2)}, u32[]{:S(2)}) %collective-permute-start.3) | collective-permute-done | bytes 393248 | tf_op jit(solution)/shard_map/ppermute | solution.py:412
  69.1 3.7 %collective-permute-start.5 = (bf16[1536,128]{1,0:T(8,128)(2,1)S(1)}, bf16[1536,128]{1,0:T(8,128)(2,1)S(1)}, u32[]{:S(2)}, u32[]{:S(2)}) collective-permute-start(bf16[1536,128]{1,0:T(8,128)(2,1)S(1)} %collective-permute-done.3.refs_6_), channel_id=1, source_target_pairs={{0,224},{16,240},{32,0},{48,16},{64,32},{80,48},{96,64},{112,80},{... | collective-permute-start | bytes 1179656 | tf_op jit(solution)/shard_map/ppermute | solution.py:412
  72.8 5.3 %collective-permute-done.5.refs_5_ = bf16[1536,128]{1,0:T(8,128)(2,1)S(1)} collective-permute-done((bf16[1536,128]{1,0:T(8,128)(2,1)S(1)}, bf16[1536,128]{1,0:T(8,128)(2,1)S(1)}, u32[]{:S(2)}, u32[]{:S(2)}) %collective-permute-start.5) | collective-permute-done | bytes 393248 | tf_op jit(solution)/shard_map/ppermute | solution.py:412
  78.0 5.2 %collective-permute-done.12.refs_2_ = bf16[1536,128]{1,0:T(8,128)(2,1)S(1)} collective-permute-done((bf16[1536,128]{1,0:T(8,128)(2,1)}, bf16[1536,128]{1,0:T(8,128)(2,1)S(1)}, u32[]{:S(2)}, u32[]{:S(2)}) %collective-permute-start.12) | collective-permute-done | bytes 393248 | tf_op jit(solution)/shard_map/ppermute | solution.py:412
  83.2 1.0 copy-done.7
  84.3 10.2 %attend.3 = (f32[1152,128]{1,0:T(8,128)S(1)}, f32[1152,128]{1,0:T(8,128)S(1)}, bf16[2304,128]{1,0:T(8,128)(2,1)S(1)}) custom-call(s32[1]{0:T(128)} %bitcast.2.seq_ref, s32[8]{0:T(128)S(1)} %get-tuple-element.80.near_ref, s32[6,13]{1,0:T(8,128)S(1)} %get-tuple-element.81.blocks_ref, s32[6]{0:T(128)S(1)} %get-tuple-element.82.count_ref, ...), custom_call_target="tpu_custom_call" | custom-call | flops 13589544960 | bytes 4718592 | tf_op jit(solution)/shard_map/attend/pallas_call | solution.py:226
  95.1 1.5 collective-permute-start.23
  97.1 5.6 %collective-permute-done.24.refs_4_ = bf16[1536,128]{1,0:T(8,128)(2,1)S(1)} collective-permute-done((bf16[1536,128]{1,0:T(8,128)(2,1)S(1)}, bf16[1536,128]{1,0:T(8,128)(2,1)S(1)}, u32[]{:S(2)}, u32[]{:S(2)}) %collective-permute-start.24) | collective-permute-done | bytes 393248 | tf_op jit(solution)/shard_map/ppermute | solution.py:412
  102.7 1.3 collective-permute-start.16
  104.2 5.5 %attend.5 = (f32[384,128]{1,0:T(8,128)S(1)}, f32[384,128]{1,0:T(8,128)S(1)}, bf16[768,128]{1,0:T(8,128)(2,1)S(1)}) custom-call(s32[1]{0:T(128)} %bitcast.2.seq_ref, s32[8]{0:T(128)S(1)} %get-tuple-element.80.near_ref, s32[6,13]{1,0:T(8,128)S(1)} %get-tuple-element.81.blocks_ref, s32[6]{0:T(128)S(1)} %get-tuple-element.82.count_ref, ...), custom_call_target="tpu_custom_call" | custom-call | flops 4529848320 | bytes 1572864 | tf_op jit(solution)/shard_map/attend/pallas_call | solution.py:226
  110.3 5.5 %attend.4 = (f32[384,128]{1,0:T(8,128)S(1)}, f32[384,128]{1,0:T(8,128)S(1)}, bf16[768,128]{1,0:T(8,128)(2,1)S(1)}) custom-call(s32[1]{0:T(128)} %bitcast.2.seq_ref, s32[8]{0:T(128)S(1)} %get-tuple-element.80.near_ref, s32[6,13]{1,0:T(8,128)S(1)} %get-tuple-element.81.blocks_ref, s32[6]{0:T(128)S(1)} %get-tuple-element.82.count_ref, ...), custom_call_target="tpu_custom_call" | custom-call | flops 4529848320 | bytes 1572864 | tf_op jit(solution)/shard_map/attend/pallas_call | solution.py:226
  115.9 2.4 %collective-permute-done.16.refs_2_ = bf16[2304,128]{1,0:T(8,128)(2,1)S(1)} collective-permute-done((bf16[2304,128]{1,0:T(8,128)(2,1)S(1)}, bf16[2304,128]{1,0:T(8,128)(2,1)S(1)}, u32[]{:S(2)}, u32[]{:S(2)}) %collective-permute-start.16) | collective-permute-done | bytes 589856 | tf_op jit(solution)/shard_map/ppermute | solution.py:392
  118.3 1.3 collective-permute-start.25
  119.9 3.4 %collective-permute-start.17 = (bf16[384,384]{1,0:T(8,128)(2,1)S(1)}, bf16[384,384]{1,0:T(8,128)(2,1)S(1)}, u32[]{:S(2)}, u32[]{:S(2)}) collective-permute-start(bf16[384,384]{1,0:T(8,128)(2,1)S(1)} %merge.3.refs_0_), channel_id=1, source_target_pairs={{0,12},{2,14},{4,0},{6,2},{8,4},{10,6},{12,8},{14,10},{1,13},{3,15... | collective-permute-start | bytes 884744 | tf_op jit(solution)/shard_map/ppermute | solution.py:423
  124.0 1.6 collective-permute-start.19
  125.9 1.8 %collective-permute-start.30 = (bf16[384,128]{1,0:T(8,128)(2,1)S(1)}, bf16[384,128]{1,0:T(8,128)(2,1)S(1)}, u32[]{:S(2)}, u32[]{:S(2)}) collective-permute-start(bf16[384,128]{1,0:T(8,128)(2,1)S(1)} %merge.5.refs_0_), channel_id=1, source_target_pairs={{0,12},{2,14},{4,0},{6,2},{8,4},{10,6},{12,8},{14,10},{1,13},{3,15... | collective-permute-start | bytes 294920 | tf_op jit(solution)/shard_map/ppermute | solution.py:423
  127.6 2.0 %collective-permute-start.31 = (bf16[384,128]{1,0:T(8,128)(2,1)S(1)}, bf16[384,128]{1,0:T(8,128)(2,1)S(1)}, u32[]{:S(2)}, u32[]{:S(2)}) collective-permute-start(bf16[384,128]{1,0:T(8,128)(2,1)S(1)} %merge.5.refs_0_), channel_id=1, source_target_pairs={{0,8},{2,10},{4,12},{6,14},{8,0},{10,2},{12,4},{14,6},{1,9},{3,11}... | collective-permute-start | bytes 294920 | tf_op jit(solution)/shard_map/ppermute | solution.py:423
  129.6 2.8 %collective-permute-done.17.refs_1_ = bf16[384,384]{1,0:T(8,128)(2,1)S(1)} collective-permute-done((bf16[384,384]{1,0:T(8,128)(2,1)S(1)}, bf16[384,384]{1,0:T(8,128)(2,1)S(1)}, u32[]{:S(2)}, u32[]{:S(2)}) %collective-permute-start.17) | collective-permute-done | bytes 294944 | tf_op jit(solution)/shard_map/ppermute | solution.py:423
  132.4 5.1 %collective-permute-done.19.refs_3_ = bf16[384,384]{1,0:T(8,128)(2,1)S(1)} collective-permute-done((bf16[384,384]{1,0:T(8,128)(2,1)S(1)}, bf16[384,384]{1,0:T(8,128)(2,1)S(1)}, u32[]{:S(2)}, u32[]{:S(2)}) %collective-permute-start.19) | collective-permute-done | bytes 294944 | tf_op jit(solution)/shard_map/ppermute | solution.py:423
  137.6 2.4 %project.3.refs_12_ = f32[2,384,640]{2,1,0:T(8,128)S(1)} custom-call(bf16[384,384]{1,0:T(8,128)(2,1)S(1)} %merge.3.refs_0_, bf16[384,384]{1,0:T(8,128)(2,1)S(1)} %collective-permute-done.17.refs_1_, bf16[384,384]{1,0:T(8,128)(2,1)S(1)} %collective-permute-done.18.refs_2_, bf16[384,384]{1,0:T(8,128)(2,1)S(1)} %collective-permute-done.19.refs_3_, ...), custom_call_target="tpu_custom_call" | custom-call | flops 1509949440 | bytes 5111808 | tf_op jit(solution)/shard_map/project/pallas_call | solution.py:367
  140.9 1.3 collective-permute-start.28
  142.2 1.2 project.4.refs_13_
  143.5 1.2 collective-permute-done.26.refs_2_
  144.7 1.6 %collective-permute-done.27.refs_3_ = bf16[384,128]{1,0:T(8,128)(2,1)S(1)} collective-permute-done((bf16[384,128]{1,0:T(8,128)(2,1)S(1)}, bf16[384,128]{1,0:T(8,128)(2,1)S(1)}, u32[]{:S(2)}, u32[]{:S(2)}) %collective-permute-start.27) | collective-permute-done | bytes 98336 | tf_op jit(solution)/shard_map/ppermute | solution.py:423
  146.3 1.1 collective-permute-done.28.refs_4_
  147.4 1.3 project.5
  149.4 4.1 %cross.1 = bf16[384,640]{1,0:T(8,128)(2,1)} custom-call(bf16[384,640]{1,0:T(8,128)(2,1)S(1)} %copy-done.9, bf16[512,640]{1,0:T(8,128)(2,1)S(1)} %copy-done.5, bf16[512,640]{1,0:T(8,128)(2,1)S(1)} %copy-done.6), custom_call_target="tpu_custom_call" | custom-call | flops 5033164800 | bytes 983040 | tf_op jit(solution)/shard_map/cross/pallas_call | solution.py:329
  153.5 5.6 %collective-permute-done.33 = bf16[384,640]{1,0:T(8,128)(2,1)S(1)} collective-permute-done((bf16[384,640]{1,0:T(8,128)(2,1)S(1)}, bf16[384,640]{1,0:T(8,128)(2,1)S(1)}, u32[]{:S(2)}, u32[]{:S(2)}) %collective-permute-start.33) | collective-permute-done | bytes 491552 | tf_op jit(solution)/shard_map/ppermute | solution.py:458
  (57 shorter events, 6.0 us)
Async XLA Ops:
  0.6 1.0 copy-start.1
  1.7 1.0 copy-start.2
  3.8 20.3 %collective-permute-start.6 = (bf16[2304,128]{1,0:T(8,128)(2,1)}, bf16[2304,128]{1,0:T(8,128)(2,1)}, u32[]{:S(2)}, u32[]{:S(2)}) collective-permute-start(bf16[2304,128]{1,0:T(8,128)(2,1)} %get-tuple-element.57.refs_0_), channel_id=1, source_target_pairs={{0,32},{16,48},{32,64},{48,80},{64,96},{80,112},{96,128},{112,144}... | collective-permute-start | bytes 1769480 | tf_op jit(solution)/shard_map/ppermute | solution.py:412
  5.7 18.4 %collective-permute-start = (bf16[2304,128]{1,0:T(8,128)(2,1)}, bf16[2304,128]{1,0:T(8,128)(2,1)}, u32[]{:S(2)}, u32[]{:S(2)}) collective-permute-start(bf16[2304,128]{1,0:T(8,128)(2,1)} %get-tuple-element.57.refs_0_), channel_id=1, source_target_pairs={{0,224},{16,240},{32,0},{48,16},{64,32},{80,48},{96,64},{112,80},{... | collective-permute-start | bytes 1769480 | tf_op jit(solution)/shard_map/ppermute | solution.py:412
  9.7 2.9 %copy-start = (bf16[640,5120]{1,0:T(8,128)(2,1)S(1)}, bf16[640,5120]{1,0:T(8,128)(2,1)}, u32[]{:S(2)}) copy-start(bf16[640,5120]{1,0:T(8,128)(2,1)} %weight_ref.1) | copy-start | bytes 19660804
  12.5 5.3 %copy-start.10 = (s32[48,18]{0,1:T(8,128)S(1)}, s32[48,18]{0,1:T(8,128)}, u32[]{:S(2)}) copy-start(s32[48,18]{0,1:T(8,128)} %param.16) | copy-start | bytes 10372
  12.5 5.3 %copy-start.3 = (s32[48]{0:T(128)S(1)}, s32[48]{0:T(128)}, u32[]{:S(2)}) copy-start(s32[48]{0:T(128)} %count_ref.1) | copy-start | bytes 580
  13.9 1.7 %copy-start.4 = (bf16[640,640]{1,0:T(8,128)(2,1)}, bf16[640,640]{1,0:T(8,128)(2,1)S(1)}, u32[]{:S(2)}) copy-start(bf16[640,640]{1,0:T(8,128)(2,1)S(1)} %get-tuple-element.79) | copy-start | bytes 2457604
  13.9 30.4 %collective-permute-start.10 = (bf16[640,640]{1,0:T(8,128)(2,1)}, bf16[640,640]{1,0:T(8,128)(2,1)S(1)}, u32[]{:S(2)}, u32[]{:S(2)}) collective-permute-start(bf16[640,640]{1,0:T(8,128)(2,1)} %get-tuple-element.73), channel_id=1, source_target_pairs={{0,4},{2,6},{4,8},{6,10},{8,12},{10,14},{12,0},{14,2},{1,5},{3,7},... | collective-permute-start | bytes 2457608 | tf_op jit(solution)/shard_map/ppermute | solution.py:435
  15.5 28.7 %collective-permute-start.9 = (bf16[640,640]{1,0:T(8,128)(2,1)}, bf16[640,640]{1,0:T(8,128)(2,1)S(1)}, u32[]{:S(2)}, u32[]{:S(2)}) collective-permute-start(bf16[640,640]{1,0:T(8,128)(2,1)} %get-tuple-element.72), channel_id=1, source_target_pairs={{0,12},{2,14},{4,0},{6,2},{8,4},{10,6},{12,8},{14,10},{1,13},{3,15... | collective-permute-start | bytes 2457608 | tf_op jit(solution)/shard_map/ppermute | solution.py:435
  17.8 14.8 %collective-permute-start.8 = (bf16[1536,128]{1,0:T(8,128)(2,1)}, bf16[1536,128]{1,0:T(8,128)(2,1)}, u32[]{:S(2)}, u32[]{:S(2)}) collective-permute-start(bf16[1536,128]{1,0:T(8,128)(2,1)} %get-tuple-element.59.refs_0_), channel_id=1, source_target_pairs={{0,32},{16,48},{32,64},{48,80},{64,96},{80,112},{96,128},{112,144}... | collective-permute-start | bytes 1179656 | tf_op jit(solution)/shard_map/ppermute | solution.py:412
  24.1 20.1 %collective-permute-start.7 = (bf16[2304,128]{1,0:T(8,128)(2,1)}, bf16[2304,128]{1,0:T(8,128)(2,1)S(1)}, u32[]{:S(2)}, u32[]{:S(2)}) collective-permute-start(bf16[2304,128]{1,0:T(8,128)(2,1)} %collective-permute-done.6.refs_1_), channel_id=1, source_target_pairs={{0,32},{16,48},{32,64},{48,80},{64,96},{80,112},{96,128},{112,144}... | collective-permute-start | bytes 1769480 | tf_op jit(solution)/shard_map/ppermute | solution.py:412
  24.1 22.9 %collective-permute-start.1 = (bf16[2304,128]{1,0:T(8,128)(2,1)}, bf16[2304,128]{1,0:T(8,128)(2,1)S(1)}, u32[]{:S(2)}, u32[]{:S(2)}) collective-permute-start(bf16[2304,128]{1,0:T(8,128)(2,1)} %collective-permute-done.refs_7_), channel_id=1, source_target_pairs={{0,224},{16,240},{32,0},{48,16},{64,32},{80,48},{96,64},{112,80},{... | collective-permute-start | bytes 1769480 | tf_op jit(solution)/shard_map/ppermute | solution.py:412
  32.6 14.5 %collective-permute-start.2 = (bf16[1536,128]{1,0:T(8,128)(2,1)}, bf16[1536,128]{1,0:T(8,128)(2,1)S(1)}, u32[]{:S(2)}, u32[]{:S(2)}) collective-permute-start(bf16[1536,128]{1,0:T(8,128)(2,1)} %get-tuple-element.59.refs_0_), channel_id=1, source_target_pairs={{0,224},{16,240},{32,0},{48,16},{64,32},{80,48},{96,64},{112,80},{... | collective-permute-start | bytes 1179656 | tf_op jit(solution)/shard_map/ppermute | solution.py:412
  44.3 15.7 %collective-permute-start.11 = (bf16[2304,128]{1,0:T(8,128)(2,1)S(1)}, bf16[2304,128]{1,0:T(8,128)(2,1)S(1)}, u32[]{:S(2)}, u32[]{:S(2)}) collective-permute-start(bf16[2304,128]{1,0:T(8,128)(2,1)S(1)} %collective-permute-done.7.refs_2_), channel_id=1, source_target_pairs={{0,32},{16,48},{32,64},{48,80},{64,96},{80,112},{96,128},{112,144}... | collective-permute-start | bytes 1769480 | tf_op jit(solution)/shard_map/ppermute | solution.py:412
  47.0 22.0 %collective-permute-start.4 = (bf16[2304,128]{1,0:T(8,128)(2,1)S(1)}, bf16[2304,128]{1,0:T(8,128)(2,1)S(1)}, u32[]{:S(2)}, u32[]{:S(2)}) collective-permute-start(bf16[2304,128]{1,0:T(8,128)(2,1)S(1)} %collective-permute-done.1.refs_6_), channel_id=1, source_target_pairs={{0,224},{16,240},{32,0},{48,16},{64,32},{80,48},{96,64},{112,80},{... | collective-permute-start | bytes 1769480 | tf_op jit(solution)/shard_map/ppermute | solution.py:412
  50.6 22.1 %collective-permute-start.14 = (bf16[640,640]{1,0:T(8,128)(2,1)}, bf16[640,640]{1,0:T(8,128)(2,1)S(1)}, u32[]{:S(2)}, u32[]{:S(2)}) collective-permute-start(bf16[640,640]{1,0:T(8,128)(2,1)} %copy-done.4), channel_id=1, source_target_pairs={{0,8},{2,10},{4,12},{6,14},{8,0},{10,2},{12,4},{14,6},{1,9},{3,11}... | collective-permute-start | bytes 2457608 | tf_op jit(solution)/shard_map/ppermute | solution.py:435
  53.8 15.2 %collective-permute-start.3 = (bf16[1536,128]{1,0:T(8,128)(2,1)S(1)}, bf16[1536,128]{1,0:T(8,128)(2,1)S(1)}, u32[]{:S(2)}, u32[]{:S(2)}) collective-permute-start(bf16[1536,128]{1,0:T(8,128)(2,1)S(1)} %collective-permute-done.2.refs_7_), channel_id=1, source_target_pairs={{0,224},{16,240},{32,0},{48,16},{64,32},{80,48},{96,64},{112,80},{... | collective-permute-start | bytes 1179656 | tf_op jit(solution)/shard_map/ppermute | solution.py:412
  60.0 23.2 %collective-permute-start.13 = (bf16[2304,128]{1,0:T(8,128)(2,1)S(1)}, bf16[2304,128]{1,0:T(8,128)(2,1)S(1)}, u32[]{:S(2)}, u32[]{:S(2)}) collective-permute-start(bf16[2304,128]{1,0:T(8,128)(2,1)S(1)} %collective-permute-done.11.refs_3_), channel_id=1, source_target_pairs={{0,32},{16,48},{32,64},{48,80},{64,96},{80,112},{96,128},{112,144}... | collective-permute-start | bytes 1769480 | tf_op jit(solution)/shard_map/ppermute | solution.py:412
  60.0 23.2 %collective-permute-start.15 = (bf16[384,640]{1,0:T(8,128)(2,1)}, bf16[384,640]{1,0:T(8,128)(2,1)S(1)}, u32[]{:S(2)}, u32[]{:S(2)}) collective-permute-start(bf16[384,640]{1,0:T(8,128)(2,1)} %q_ref.6), channel_id=1, source_target_pairs={{0,16},{16,0},{32,48},{48,32},{64,80},{80,64},{96,112},{112,96},{1... | collective-permute-start | bytes 1474568 | tf_op jit(solution)/shard_map/ppermute | solution.py:392
  69.1 9.0 %collective-permute-start.5 = (bf16[1536,128]{1,0:T(8,128)(2,1)S(1)}, bf16[1536,128]{1,0:T(8,128)(2,1)S(1)}, u32[]{:S(2)}, u32[]{:S(2)}) collective-permute-start(bf16[1536,128]{1,0:T(8,128)(2,1)S(1)} %collective-permute-done.3.refs_6_), channel_id=1, source_target_pairs={{0,224},{16,240},{32,0},{48,16},{64,32},{80,48},{96,64},{112,80},{... | collective-permute-start | bytes 1179656 | tf_op jit(solution)/shard_map/ppermute | solution.py:412
  72.8 10.5 %collective-permute-start.12 = (bf16[1536,128]{1,0:T(8,128)(2,1)}, bf16[1536,128]{1,0:T(8,128)(2,1)S(1)}, u32[]{:S(2)}, u32[]{:S(2)}) collective-permute-start(bf16[1536,128]{1,0:T(8,128)(2,1)} %collective-permute-done.8.refs_1_), channel_id=1, source_target_pairs={{0,32},{16,48},{32,64},{48,80},{64,96},{80,112},{96,128},{112,144}... | collective-permute-start | bytes 1179656 | tf_op jit(solution)/shard_map/ppermute | solution.py:412
  83.2 1.0 copy-start.7
  84.3 19.9 %copy-start.8 = (bf16[384,640]{1,0:T(8,128)(2,1)S(1)}, bf16[384,640]{1,0:T(8,128)(2,1)}, u32[]{:S(2)}) copy-start(bf16[384,640]{1,0:T(8,128)(2,1)} %q_ref.6) | copy-start | bytes 1474564
  94.5 8.2 %collective-permute-start.24 = (bf16[1536,128]{1,0:T(8,128)(2,1)S(1)}, bf16[1536,128]{1,0:T(8,128)(2,1)S(1)}, u32[]{:S(2)}, u32[]{:S(2)}) collective-permute-start(bf16[1536,128]{1,0:T(8,128)(2,1)S(1)} %collective-permute-done.5.refs_5_), channel_id=1, source_target_pairs={{0,224},{16,240},{32,0},{48,16},{64,32},{80,48},{96,64},{112,80},{... | collective-permute-start | bytes 1179656 | tf_op jit(solution)/shard_map/ppermute | solution.py:412
  95.1 9.1 %collective-permute-start.23 = (bf16[1536,128]{1,0:T(8,128)(2,1)S(1)}, bf16[1536,128]{1,0:T(8,128)(2,1)S(1)}, u32[]{:S(2)}, u32[]{:S(2)}) collective-permute-start(bf16[1536,128]{1,0:T(8,128)(2,1)S(1)} %collective-permute-done.12.refs_2_), channel_id=1, source_target_pairs={{0,32},{16,48},{32,64},{48,80},{64,96},{80,112},{96,128},{112,144}... | collective-permute-start | bytes 1179656 | tf_op jit(solution)/shard_map/ppermute | solution.py:412
  96.6 23.4 %collective-permute-start.21 = (bf16[640,640]{1,0:T(8,128)(2,1)S(1)}, bf16[640,640]{1,0:T(8,128)(2,1)S(1)}, u32[]{:S(2)}, u32[]{:S(2)}) collective-permute-start(bf16[640,640]{1,0:T(8,128)(2,1)S(1)} %collective-permute-done.14.refs_8_.refs_9_), channel_id=1, source_target_pairs={{0,1},{1,0},{2,3},{3,2},{4,5},{5,4},{6,7},{7,6},{8,9},{9,8},{10,11... | collective-permute-start | bytes 2457608 | tf_op jit(solution)/shard_map/ppermute | solution.py:447
  96.6 29.3 %collective-permute-start.20 = (bf16[640,640]{1,0:T(8,128)(2,1)S(1)}, bf16[640,640]{1,0:T(8,128)(2,1)S(1)}, u32[]{:S(2)}, u32[]{:S(2)}) collective-permute-start(bf16[640,640]{1,0:T(8,128)(2,1)S(1)} %collective-permute-done.9.refs_6_.refs_7_), channel_id=1, source_target_pairs={{0,1},{1,0},{2,3},{3,2},{4,5},{5,4},{6,7},{7,6},{8,9},{9,8},{10,11... | collective-permute-start | bytes 2457608 | tf_op jit(solution)/shard_map/ppermute | solution.py:447
  97.1 30.5 %collective-permute-start.22 = (bf16[640,640]{1,0:T(8,128)(2,1)S(1)}, bf16[640,640]{1,0:T(8,128)(2,1)S(1)}, u32[]{:S(2)}, u32[]{:S(2)}) collective-permute-start(bf16[640,640]{1,0:T(8,128)(2,1)S(1)} %collective-permute-done.10.refs_10_.refs_11_), channel_id=1, source_target_pairs={{0,1},{1,0},{2,3},{3,2},{4,5},{5,4},{6,7},{7,6},{8,9},{9,8},{10,11... | collective-permute-start | bytes 2457608 | tf_op jit(solution)/shard_map/ppermute | solution.py:447
  102.7 15.6 %collective-permute-start.16 = (bf16[2304,128]{1,0:T(8,128)(2,1)S(1)}, bf16[2304,128]{1,0:T(8,128)(2,1)S(1)}, u32[]{:S(2)}, u32[]{:S(2)}) collective-permute-start(bf16[2304,128]{1,0:T(8,128)(2,1)S(1)} %get-tuple-element.93), channel_id=1, source_target_pairs={{0,16},{16,0},{32,48},{48,32},{64,80},{80,64},{96,112},{112,96},{1... | collective-permute-start | bytes 1769480 | tf_op jit(solution)/shard_map/ppermute | solution.py:392
  109.7 13.6 %collective-permute-start.29 = (bf16[768,128]{1,0:T(8,128)(2,1)S(1)}, bf16[768,128]{1,0:T(8,128)(2,1)S(1)}, u32[]{:S(2)}, u32[]{:S(2)}) collective-permute-start(bf16[768,128]{1,0:T(8,128)(2,1)S(1)} %get-tuple-element.108), channel_id=1, source_target_pairs={{0,16},{16,0},{32,48},{48,32},{64,80},{80,64},{96,112},{112,96},{1... | collective-permute-start | bytes 589832 | tf_op jit(solution)/shard_map/ppermute | solution.py:392
  118.3 5.7 %collective-permute-start.25 = (bf16[768,128]{1,0:T(8,128)(2,1)S(1)}, bf16[768,128]{1,0:T(8,128)(2,1)S(1)}, u32[]{:S(2)}, u32[]{:S(2)}) collective-permute-start(bf16[768,128]{1,0:T(8,128)(2,1)S(1)} %get-tuple-element.104), channel_id=1, source_target_pairs={{0,16},{16,0},{32,48},{48,32},{64,80},{80,64},{96,112},{112,96},{1... | collective-permute-start | bytes 589832 | tf_op jit(solution)/shard_map/ppermute | solution.py:392
  119.9 12.5 %collective-permute-start.17 = (bf16[384,384]{1,0:T(8,128)(2,1)S(1)}, bf16[384,384]{1,0:T(8,128)(2,1)S(1)}, u32[]{:S(2)}, u32[]{:S(2)}) collective-permute-start(bf16[384,384]{1,0:T(8,128)(2,1)S(1)} %merge.3.refs_0_), channel_id=1, source_target_pairs={{0,12},{2,14},{4,0},{6,2},{8,4},{10,6},{12,8},{14,10},{1,13},{3,15... | collective-permute-start | bytes 884744 | tf_op jit(solution)/shard_map/ppermute | solution.py:423
  123.3 9.2 %collective-permute-start.18 = (bf16[384,384]{1,0:T(8,128)(2,1)S(1)}, bf16[384,384]{1,0:T(8,128)(2,1)S(1)}, u32[]{:S(2)}, u32[]{:S(2)}) collective-permute-start(bf16[384,384]{1,0:T(8,128)(2,1)S(1)} %merge.3.refs_0_), channel_id=1, source_target_pairs={{0,8},{2,10},{4,12},{6,14},{8,0},{10,2},{12,4},{14,6},{1,9},{3,11}... | collective-permute-start | bytes 884744 | tf_op jit(solution)/shard_map/ppermute | solution.py:423
  124.0 13.6 %collective-permute-start.19 = (bf16[384,384]{1,0:T(8,128)(2,1)S(1)}, bf16[384,384]{1,0:T(8,128)(2,1)S(1)}, u32[]{:S(2)}, u32[]{:S(2)}) collective-permute-start(bf16[384,384]{1,0:T(8,128)(2,1)S(1)} %merge.3.refs_0_), channel_id=1, source_target_pairs={{0,4},{2,6},{4,8},{6,10},{8,12},{10,14},{12,0},{14,2},{1,5},{3,7},... | collective-permute-start | bytes 884744 | tf_op jit(solution)/shard_map/ppermute | solution.py:423
  125.9 15.1 %collective-permute-start.30 = (bf16[384,128]{1,0:T(8,128)(2,1)S(1)}, bf16[384,128]{1,0:T(8,128)(2,1)S(1)}, u32[]{:S(2)}, u32[]{:S(2)}) collective-permute-start(bf16[384,128]{1,0:T(8,128)(2,1)S(1)} %merge.5.refs_0_), channel_id=1, source_target_pairs={{0,12},{2,14},{4,0},{6,2},{8,4},{10,6},{12,8},{14,10},{1,13},{3,15... | collective-permute-start | bytes 294920 | tf_op jit(solution)/shard_map/ppermute | solution.py:423
  127.6 14.6 %collective-permute-start.31 = (bf16[384,128]{1,0:T(8,128)(2,1)S(1)}, bf16[384,128]{1,0:T(8,128)(2,1)S(1)}, u32[]{:S(2)}, u32[]{:S(2)}) collective-permute-start(bf16[384,128]{1,0:T(8,128)(2,1)S(1)} %merge.5.refs_0_), channel_id=1, source_target_pairs={{0,8},{2,10},{4,12},{6,14},{8,0},{10,2},{12,4},{14,6},{1,9},{3,11}... | collective-permute-start | bytes 294920 | tf_op jit(solution)/shard_map/ppermute | solution.py:423
  132.4 9.8 %collective-permute-start.32 = (bf16[384,128]{1,0:T(8,128)(2,1)S(1)}, bf16[384,128]{1,0:T(8,128)(2,1)S(1)}, u32[]{:S(2)}, u32[]{:S(2)}) collective-permute-start(bf16[384,128]{1,0:T(8,128)(2,1)S(1)} %merge.5.refs_0_), channel_id=1, source_target_pairs={{0,4},{2,6},{4,8},{6,10},{8,12},{10,14},{12,0},{14,2},{1,5},{3,7},... | collective-permute-start | bytes 294920 | tf_op jit(solution)/shard_map/ppermute | solution.py:423
  140.0 4.7 %collective-permute-start.26 = (bf16[384,128]{1,0:T(8,128)(2,1)S(1)}, bf16[384,128]{1,0:T(8,128)(2,1)S(1)}, u32[]{:S(2)}, u32[]{:S(2)}) collective-permute-start(bf16[384,128]{1,0:T(8,128)(2,1)S(1)} %merge.4.refs_1_), channel_id=1, source_target_pairs={{0,12},{2,14},{4,0},{6,2},{8,4},{10,6},{12,8},{14,10},{1,13},{3,15... | collective-permute-start | bytes 294920 | tf_op jit(solution)/shard_map/ppermute | solution.py:423
  140.1 6.2 %collective-permute-start.27 = (bf16[384,128]{1,0:T(8,128)(2,1)S(1)}, bf16[384,128]{1,0:T(8,128)(2,1)S(1)}, u32[]{:S(2)}, u32[]{:S(2)}) collective-permute-start(bf16[384,128]{1,0:T(8,128)(2,1)S(1)} %merge.4.refs_1_), channel_id=1, source_target_pairs={{0,8},{2,10},{4,12},{6,14},{8,0},{10,2},{12,4},{14,6},{1,9},{3,11}... | collective-permute-start | bytes 294920 | tf_op jit(solution)/shard_map/ppermute | solution.py:423
  140.9 6.5 %collective-permute-start.28 = (bf16[384,128]{1,0:T(8,128)(2,1)S(1)}, bf16[384,128]{1,0:T(8,128)(2,1)S(1)}, u32[]{:S(2)}, u32[]{:S(2)}) collective-permute-start(bf16[384,128]{1,0:T(8,128)(2,1)S(1)} %merge.4.refs_1_), channel_id=1, source_target_pairs={{0,4},{2,6},{4,8},{6,10},{8,12},{10,14},{12,0},{14,2},{1,5},{3,7},... | collective-permute-start | bytes 294920 | tf_op jit(solution)/shard_map/ppermute | solution.py:423
  143.4 6.0 %copy-start.5 = (bf16[512,640]{1,0:T(8,128)(2,1)S(1)}, bf16[512,640]{1,0:T(8,128)(2,1)}, u32[]{:S(2)}) copy-start(bf16[512,640]{1,0:T(8,128)(2,1)} %k_ref.3) | copy-start | bytes 1966084
  143.4 6.0 %copy-start.6 = (bf16[512,640]{1,0:T(8,128)(2,1)S(1)}, bf16[512,640]{1,0:T(8,128)(2,1)}, u32[]{:S(2)}) copy-start(bf16[512,640]{1,0:T(8,128)(2,1)} %v_ref.3) | copy-start | bytes 1966084
  143.4 6.0 %copy-start.9 = (bf16[384,640]{1,0:T(8,128)(2,1)S(1)}, bf16[384,640]{1,0:T(8,128)(2,1)}, u32[]{:S(2)}) copy-start(bf16[384,640]{1,0:T(8,128)(2,1)} %q_ref.7) | copy-start | bytes 1474564
  148.7 10.4 %collective-permute-start.33 = (bf16[384,640]{1,0:T(8,128)(2,1)S(1)}, bf16[384,640]{1,0:T(8,128)(2,1)S(1)}, u32[]{:S(2)}, u32[]{:S(2)}) collective-permute-start(bf16[384,640]{1,0:T(8,128)(2,1)S(1)} %get-tuple-element.111), channel_id=1, source_target_pairs={{0,2},{2,0},{4,6},{6,4},{8,10},{10,8},{12,14},{14,12},{1,3},{3,1},... | collective-permute-start | bytes 1474568 | tf_op jit(solution)/shard_map/ppermute | solution.py:458

commit v2 on v1

--- a/solution.py
+++ b/solution.py
@@ -382,6 +382,7 @@
 
 def body(n_seq, n_head, queries, keys, values, cross_query, text_keys, text_values, out_weight, block_list, block_count):
     n_z, n_y = n_seq // 2, n_head // 2
+    half = n_z // 2
     seq = lax.axis_index("seq").reshape(1)
     head = lax.axis_index("head").reshape(1)
     pair = lax.axis_index("pair").reshape(1)
@@ -439,15 +440,17 @@
     hop(-1, 0, 3)
     hop(1, 0, 4)
     hop(-1, 1, 2)
-    hop(1, 1, 2)
+    whole = [held[0][half]]
+    hop(1, 1, 2, whole)
+    held[0][half] = whole[0]
     hop(-1, 1, 3)
+    hop(1, 1, 3)
+    hop(-1, 1, 4)
     near, tiles[2] = lax.optimization_barrier((near, tiles[2]))
     weights = [tiles[0], tiles[n_y]]
     for mine in tiles[1:n_y]:
         weights += [mine, lax.ppermute(mine, "pair", [(0, 1), (1, 0)])]
     most = partial(0, 0, 3)
-    hop(1, 1, 3, most)
-    hop(-1, 1, 4, most)
     before = project(GROUPS[0][0], along_y(join(most)), weights)
     one, two = partial(1, 0, 1), partial(1, 1, 2)
     two = join(two)

time: 161 us -> 169 us (1.050)
  the two profiles are of different devices: /device:TPU:4 before, /device:TPU:100 now
where the time goes in v2:
time: 169 us; the launch traced here: 168 us
  waiting for transfers between devices  74.2 us (44%)
  starting transfers between devices  48.4 us (29%)
  Pallas kernels  36.4 us (22%)
  local copies, waits for them, and re-layouts  6.81 us (4%)
    ppermute x14, waiting for transfers between devices, hop(): held[group][place] = lax.ppermute(array, 'seq', z_shift(way))  51.5 us
    pallas_call x3, Pallas kernels, attend(): pl.pallas_call(functools.partial(attend_kernel, heads, first, planes), ou...  20.9 us
    ppermute x14, starting transfers between devices, hop(): held[group][place] = lax.ppermute(array, 'seq', z_shift(way))  20.7 us
    ppermute x9, starting transfers between devices, along_y(): lax.ppermute(array, 'head', y_shift(-dy))  15.5 us
    ppermute x9, waiting for transfers between devices, along_y(): lax.ppermute(array, 'head', y_shift(-dy))  12 us
    unnamed x25, local copies, waits for them, and re-layouts  6.81 us
    ppermute x1, waiting for transfers between devices, body(): got = lax.ppermute(send, 'head', [(g, g ^ 1) for g in range(n_head)])  6.49 us
    ppermute x3, starting transfers between devices, body(): lax.ppermute(tiles[dy], 'head', y_shift(dy))  6.29 us
  transfers between devices with their start and end apart: 34, of which 13 were waited for; matrix products, arithmetic and copies ran while one was open for 0% of the time, Pallas kernels for 20%

profile of v2, /device:TPU:100, one launch (start us, length us, event | category | flops | bytes accessed | tf_op | source)
XLA Modules:
  0.0 167.6 jit_solution(14616318611934489551)
XLA Ops:
  0.6 1.0 copy-done.1
  1.7 1.0 copy-done.2
  2.7 1.0 pack.1
  3.7 0.7 copy-done.9
  4.4 3.1 %collective-permute-start.1 = (bf16[2304,128]{1,0:T(8,128)(2,1)}, bf16[2304,128]{1,0:T(8,128)(2,1)}, u32[]{:S(2)}, u32[]{:S(2)}) collective-permute-start(bf16[2304,128]{1,0:T(8,128)(2,1)} %get-tuple-element.59.refs_0_), channel_id=1, source_target_pairs={{0,32},{16,48},{32,64},{48,80},{64,96},{80,112},{96,128},{112,144}... | collective-permute-start | bytes 1769480 | tf_op jit(solution)/shard_map/ppermute | solution.py:413
  7.6 2.9 %copy-done = bf16[640,5120]{1,0:T(8,128)(2,1)S(1)} copy-done((bf16[640,5120]{1,0:T(8,128)(2,1)S(1)}, bf16[640,5120]{1,0:T(8,128)(2,1)}, u32[]{:S(2)}) %copy-start) | copy-done | bytes 6553624
  10.4 1.4 tile.1
  11.8 3.1 %collective-permute-start.5 = (bf16[640,640]{1,0:T(8,128)(2,1)}, bf16[640,640]{1,0:T(8,128)(2,1)S(1)}, u32[]{:S(2)}, u32[]{:S(2)}) collective-permute-start(bf16[640,640]{1,0:T(8,128)(2,1)} %get-tuple-element.70), channel_id=1, source_target_pairs={{0,12},{2,14},{4,0},{6,2},{8,4},{10,6},{12,8},{14,10},{1,13},{3,15... | collective-permute-start | bytes 2457608 | tf_op jit(solution)/shard_map/ppermute | solution.py:436
  15.0 3.6 %plan.1 = (s32[6,13]{1,0:T(8,128)S(1)}, s32[6]{0:T(128)S(1)}, s32[8]{0:T(128)S(1)}) custom-call(s32[1]{0:T(128)} %bitcast.2.seq_ref, s32[48,18]{1,0:T(8,128)S(1)} %copy.11.list_ref, s32[48]{0:T(128)S(1)} %copy-done.3), custom_call_target="tpu_custom_call" | custom-call | flops 1000 | bytes 8000 | tf_op jit(solution)/shard_map/plan/pallas_call | solution.py:60
  18.6 1.9 %collective-permute-done.1.refs_1_ = bf16[2304,128]{1,0:T(8,128)(2,1)} collective-permute-done((bf16[2304,128]{1,0:T(8,128)(2,1)}, bf16[2304,128]{1,0:T(8,128)(2,1)}, u32[]{:S(2)}, u32[]{:S(2)}) %collective-permute-start.1) | collective-permute-done | bytes 589856 | tf_op jit(solution)/shard_map/ppermute | solution.py:413
  20.5 3.7 %collective-permute-start.3 = (bf16[2304,128]{1,0:T(8,128)(2,1)}, bf16[2304,128]{1,0:T(8,128)(2,1)S(1)}, u32[]{:S(2)}, u32[]{:S(2)}) collective-permute-start(bf16[2304,128]{1,0:T(8,128)(2,1)} %collective-permute-done.1.refs_1_), channel_id=1, source_target_pairs={{0,32},{16,48},{32,64},{48,80},{64,96},{80,112},{96,128},{112,144}... | collective-permute-start | bytes 1769480 | tf_op jit(solution)/shard_map/ppermute | solution.py:413
  24.2 6.7 %collective-permute-done.10.refs_7_ = bf16[2304,128]{1,0:T(8,128)(2,1)} collective-permute-done((bf16[2304,128]{1,0:T(8,128)(2,1)}, bf16[2304,128]{1,0:T(8,128)(2,1)}, u32[]{:S(2)}, u32[]{:S(2)}) %collective-permute-start.10) | collective-permute-done | bytes 589856 | tf_op jit(solution)/shard_map/ppermute | solution.py:413
  30.9 13.7 %collective-permute-done.4.refs_1_ = bf16[1536,128]{1,0:T(8,128)(2,1)S(1)} collective-permute-done((bf16[1536,128]{1,0:T(8,128)(2,1)}, bf16[1536,128]{1,0:T(8,128)(2,1)S(1)}, u32[]{:S(2)}, u32[]{:S(2)}) %collective-permute-start.4) | collective-permute-done | bytes 393248 | tf_op jit(solution)/shard_map/ppermute | solution.py:413
  44.6 3.7 %collective-permute-start.7 = (bf16[2304,128]{1,0:T(8,128)(2,1)S(1)}, bf16[2304,128]{1,0:T(8,128)(2,1)S(1)}, u32[]{:S(2)}, u32[]{:S(2)}) collective-permute-start(bf16[2304,128]{1,0:T(8,128)(2,1)S(1)} %collective-permute-done.3.refs_2_), channel_id=1, source_target_pairs={{0,32},{16,48},{32,64},{48,80},{64,96},{80,112},{96,128},{112,144}... | collective-permute-start | bytes 1769480 | tf_op jit(solution)/shard_map/ppermute | solution.py:413
  48.3 10.2 %collective-permute-done.12.refs_7_ = bf16[1536,128]{1,0:T(8,128)(2,1)S(1)} collective-permute-done((bf16[1536,128]{1,0:T(8,128)(2,1)}, bf16[1536,128]{1,0:T(8,128)(2,1)S(1)}, u32[]{:S(2)}, u32[]{:S(2)}) %collective-permute-start.12) | collective-permute-done | bytes 393248 | tf_op jit(solution)/shard_map/ppermute | solution.py:413
  58.5 0.6 collective-permute-done.7.refs_3_
  59.1 3.7 %collective-permute-start.8 = (bf16[2304,128]{1,0:T(8,128)(2,1)S(1)}, bf16[2304,128]{1,0:T(8,128)(2,1)S(1)}, u32[]{:S(2)}, u32[]{:S(2)}) collective-permute-start(bf16[2304,128]{1,0:T(8,128)(2,1)S(1)} %collective-permute-done.7.refs_3_), channel_id=1, source_target_pairs={{0,32},{16,48},{32,64},{48,80},{64,96},{80,112},{96,128},{112,144}... | collective-permute-start | bytes 1769480 | tf_op jit(solution)/shard_map/ppermute | solution.py:413
  62.8 3.2 %collective-permute-start = (bf16[640,640]{1,0:T(8,128)(2,1)}, bf16[640,640]{1,0:T(8,128)(2,1)S(1)}, u32[]{:S(2)}, u32[]{:S(2)}) collective-permute-start(bf16[640,640]{1,0:T(8,128)(2,1)} %copy-done.4), channel_id=1, source_target_pairs={{0,8},{2,10},{4,12},{6,14},{8,0},{10,2},{12,4},{14,6},{1,9},{3,11}... | collective-permute-start | bytes 2457608 | tf_op jit(solution)/shard_map/ppermute | solution.py:436
  66.0 1.2 collective-permute-start.2
  67.2 13.2 %collective-permute-done.13.refs_6_ = bf16[1536,128]{1,0:T(8,128)(2,1)S(1)} collective-permute-done((bf16[1536,128]{1,0:T(8,128)(2,1)S(1)}, bf16[1536,128]{1,0:T(8,128)(2,1)S(1)}, u32[]{:S(2)}, u32[]{:S(2)}) %collective-permute-start.13) | collective-permute-done | bytes 393248 | tf_op jit(solution)/shard_map/ppermute | solution.py:413
  80.4 3.2 %collective-permute-start.9 = (bf16[1536,128]{1,0:T(8,128)(2,1)S(1)}, bf16[1536,128]{1,0:T(8,128)(2,1)S(1)}, u32[]{:S(2)}, u32[]{:S(2)}) collective-permute-start(bf16[1536,128]{1,0:T(8,128)(2,1)S(1)} %collective-permute-done.4.refs_1_), channel_id=1, source_target_pairs={{0,32},{16,48},{32,64},{48,80},{64,96},{80,112},{96,128},{112,144}... | collective-permute-start | bytes 1179656 | tf_op jit(solution)/shard_map/ppermute | solution.py:413
  84.2 5.2 %collective-permute-done.23.refs_5_ = bf16[1536,128]{1,0:T(8,128)(2,1)S(1)} collective-permute-done((bf16[1536,128]{1,0:T(8,128)(2,1)S(1)}, bf16[1536,128]{1,0:T(8,128)(2,1)S(1)}, u32[]{:S(2)}, u32[]{:S(2)}) %collective-permute-start.23) | collective-permute-done | bytes 393248 | tf_op jit(solution)/shard_map/ppermute | solution.py:413
  89.4 3.2 %collective-permute-start.22 = (bf16[1536,128]{1,0:T(8,128)(2,1)S(1)}, bf16[1536,128]{1,0:T(8,128)(2,1)S(1)}, u32[]{:S(2)}, u32[]{:S(2)}) collective-permute-start(bf16[1536,128]{1,0:T(8,128)(2,1)S(1)} %collective-permute-done.9.refs_2_), channel_id=1, source_target_pairs={{0,32},{16,48},{32,64},{48,80},{64,96},{80,112},{96,128},{112,144}... | collective-permute-start | bytes 1179656 | tf_op jit(solution)/shard_map/ppermute | solution.py:413
  92.7 1.0 copy-done.7
  93.7 11.0 %attend.3 = (f32[1152,128]{1,0:T(8,128)S(1)}, f32[1152,128]{1,0:T(8,128)S(1)}, bf16[2304,128]{1,0:T(8,128)(2,1)S(1)}) custom-call(s32[1]{0:T(128)} %bitcast.2.seq_ref, s32[8]{0:T(128)S(1)} %get-tuple-element.58.near_ref, s32[6,13]{1,0:T(8,128)S(1)} %get-tuple-element.64.blocks_ref, s32[6]{0:T(128)S(1)} %get-tuple-element.65.count_ref, ...), custom_call_target="tpu_custom_call" | custom-call | flops 13589544960 | bytes 4718592 | tf_op jit(solution)/shard_map/attend/pallas_call | solution.py:226
  104.7 1.4 collective-permute-start.15
  106.1 4.9 %attend.4 = (f32[384,128]{1,0:T(8,128)S(1)}, f32[384,128]{1,0:T(8,128)S(1)}, bf16[768,128]{1,0:T(8,128)(2,1)S(1)}) custom-call(s32[1]{0:T(128)} %bitcast.2.seq_ref, s32[8]{0:T(128)S(1)} %get-tuple-element.58.near_ref, s32[6,13]{1,0:T(8,128)S(1)} %get-tuple-element.64.blocks_ref, s32[6]{0:T(128)S(1)} %get-tuple-element.65.count_ref, ...), custom_call_target="tpu_custom_call" | custom-call | flops 4529848320 | bytes 1572864 | tf_op jit(solution)/shard_map/attend/pallas_call | solution.py:226
  111.1 0.8 collective-permute-start.25
  111.9 5.0 %attend.5 = (f32[384,128]{1,0:T(8,128)S(1)}, f32[384,128]{1,0:T(8,128)S(1)}, bf16[768,128]{1,0:T(8,128)(2,1)S(1)}) custom-call(s32[1]{0:T(128)} %bitcast.2.seq_ref, s32[8]{0:T(128)S(1)} %get-tuple-element.58.near_ref, s32[6,13]{1,0:T(8,128)S(1)} %get-tuple-element.64.blocks_ref, s32[6]{0:T(128)S(1)} %get-tuple-element.65.count_ref, ...), custom_call_target="tpu_custom_call" | custom-call | flops 4529848320 | bytes 1572864 | tf_op jit(solution)/shard_map/attend/pallas_call | solution.py:226
  116.9 4.1 %collective-permute-done.15.refs_2_ = bf16[2304,128]{1,0:T(8,128)(2,1)S(1)} collective-permute-done((bf16[2304,128]{1,0:T(8,128)(2,1)S(1)}, bf16[2304,128]{1,0:T(8,128)(2,1)S(1)}, u32[]{:S(2)}, u32[]{:S(2)}) %collective-permute-start.15) | collective-permute-done | bytes 589856 | tf_op jit(solution)/shard_map/ppermute | solution.py:393
  121.0 1.4 collective-permute-start.29
  122.7 3.3 %collective-permute-start.16 = (bf16[384,384]{1,0:T(8,128)(2,1)S(1)}, bf16[384,384]{1,0:T(8,128)(2,1)S(1)}, u32[]{:S(2)}, u32[]{:S(2)}) collective-permute-start(bf16[384,384]{1,0:T(8,128)(2,1)S(1)} %merge.3.refs_0_), channel_id=1, source_target_pairs={{0,12},{2,14},{4,0},{6,2},{8,4},{10,6},{12,8},{14,10},{1,13},{3,15... | collective-permute-start | bytes 884744 | tf_op jit(solution)/shard_map/ppermute | solution.py:424
  126.0 2.4 %collective-permute-start.17 = (bf16[384,384]{1,0:T(8,128)(2,1)S(1)}, bf16[384,384]{1,0:T(8,128)(2,1)S(1)}, u32[]{:S(2)}, u32[]{:S(2)}) collective-permute-start(bf16[384,384]{1,0:T(8,128)(2,1)S(1)} %merge.3.refs_0_), channel_id=1, source_target_pairs={{0,8},{2,10},{4,12},{6,14},{8,0},{10,2},{12,4},{14,6},{1,9},{3,11}... | collective-permute-start | bytes 884744 | tf_op jit(solution)/shard_map/ppermute | solution.py:424
  128.4 1.6 collective-permute-start.18
  130.3 1.7 %collective-permute-start.30 = (bf16[384,128]{1,0:T(8,128)(2,1)S(1)}, bf16[384,128]{1,0:T(8,128)(2,1)S(1)}, u32[]{:S(2)}, u32[]{:S(2)}) collective-permute-start(bf16[384,128]{1,0:T(8,128)(2,1)S(1)} %merge.5.refs_0_), channel_id=1, source_target_pairs={{0,12},{2,14},{4,0},{6,2},{8,4},{10,6},{12,8},{14,10},{1,13},{3,15... | collective-permute-start | bytes 294920 | tf_op jit(solution)/shard_map/ppermute | solution.py:424
  132.1 2.0 %collective-permute-start.31 = (bf16[384,128]{1,0:T(8,128)(2,1)S(1)}, bf16[384,128]{1,0:T(8,128)(2,1)S(1)}, u32[]{:S(2)}, u32[]{:S(2)}) collective-permute-start(bf16[384,128]{1,0:T(8,128)(2,1)S(1)} %merge.5.refs_0_), channel_id=1, source_target_pairs={{0,8},{2,10},{4,12},{6,14},{8,0},{10,2},{12,4},{14,6},{1,9},{3,11}... | collective-permute-start | bytes 294920 | tf_op jit(solution)/shard_map/ppermute | solution.py:424
  134.0 5.7 %collective-permute-done.16.refs_1_ = bf16[384,384]{1,0:T(8,128)(2,1)S(1)} collective-permute-done((bf16[384,384]{1,0:T(8,128)(2,1)S(1)}, bf16[384,384]{1,0:T(8,128)(2,1)S(1)}, u32[]{:S(2)}, u32[]{:S(2)}) %collective-permute-start.16) | collective-permute-done | bytes 294944 | tf_op jit(solution)/shard_map/ppermute | solution.py:424
  139.8 2.2 %collective-permute-done.18.refs_3_ = bf16[384,384]{1,0:T(8,128)(2,1)S(1)} collective-permute-done((bf16[384,384]{1,0:T(8,128)(2,1)S(1)}, bf16[384,384]{1,0:T(8,128)(2,1)S(1)}, u32[]{:S(2)}, u32[]{:S(2)}) %collective-permute-start.18) | collective-permute-done | bytes 294944 | tf_op jit(solution)/shard_map/ppermute | solution.py:424
  141.9 2.4 %project.3.refs_12_ = f32[2,384,640]{2,1,0:T(8,128)S(1)} custom-call(bf16[384,384]{1,0:T(8,128)(2,1)S(1)} %merge.3.refs_0_, bf16[384,384]{1,0:T(8,128)(2,1)S(1)} %collective-permute-done.16.refs_1_, bf16[384,384]{1,0:T(8,128)(2,1)S(1)} %collective-permute-done.17.refs_2_, bf16[384,384]{1,0:T(8,128)(2,1)S(1)} %collective-permute-done.18.refs_3_, ...), custom_call_target="tpu_custom_call" | custom-call | flops 1509949440 | bytes 5111808 | tf_op jit(solution)/shard_map/project/pallas_call | solution.py:367
  144.3 1.6 collective-permute-start.26
  145.9 2.4 %collective-permute-start.27 = (bf16[384,128]{1,0:T(8,128)(2,1)S(1)}, bf16[384,128]{1,0:T(8,128)(2,1)S(1)}, u32[]{:S(2)}, u32[]{:S(2)}) collective-permute-start(bf16[384,128]{1,0:T(8,128)(2,1)S(1)} %merge.4.refs_1_), channel_id=1, source_target_pairs={{0,8},{2,10},{4,12},{6,14},{8,0},{10,2},{12,4},{14,6},{1,9},{3,11}... | collective-permute-start | bytes 294920 | tf_op jit(solution)/shard_map/ppermute | solution.py:424
  148.8 1.2 project.4.refs_13_
  150.1 2.2 %collective-permute-done.27.refs_3_ = bf16[384,128]{1,0:T(8,128)(2,1)S(1)} collective-permute-done((bf16[384,128]{1,0:T(8,128)(2,1)S(1)}, bf16[384,128]{1,0:T(8,128)(2,1)S(1)}, u32[]{:S(2)}, u32[]{:S(2)}) %collective-permute-start.27) | collective-permute-done | bytes 98336 | tf_op jit(solution)/shard_map/ppermute | solution.py:424
  152.2 2.0 %collective-permute-done.28.refs_4_ = bf16[384,128]{1,0:T(8,128)(2,1)S(1)} collective-permute-done((bf16[384,128]{1,0:T(8,128)(2,1)S(1)}, bf16[384,128]{1,0:T(8,128)(2,1)S(1)}, u32[]{:S(2)}, u32[]{:S(2)}) %collective-permute-start.28) | collective-permute-done | bytes 98336 | tf_op jit(solution)/shard_map/ppermute | solution.py:424
  154.2 1.3 project.5
  156.1 4.1 %cross.1 = bf16[384,640]{1,0:T(8,128)(2,1)} custom-call(bf16[384,640]{1,0:T(8,128)(2,1)S(1)} %copy-done.8, bf16[512,640]{1,0:T(8,128)(2,1)S(1)} %copy-done.5, bf16[512,640]{1,0:T(8,128)(2,1)S(1)} %copy-done.6), custom_call_target="tpu_custom_call" | custom-call | flops 5033164800 | bytes 983040 | tf_op jit(solution)/shard_map/cross/pallas_call | solution.py:329
  160.2 6.5 %collective-permute-done.33 = bf16[384,640]{1,0:T(8,128)(2,1)S(1)} collective-permute-done((bf16[384,640]{1,0:T(8,128)(2,1)S(1)}, bf16[384,640]{1,0:T(8,128)(2,1)S(1)}, u32[]{:S(2)}, u32[]{:S(2)}) %collective-permute-start.33) | collective-permute-done | bytes 491552 | tf_op jit(solution)/shard_map/ppermute | solution.py:461
  166.7 0.9 add_convert_fusion
  (59 shorter events, 2.5 us)
Async XLA Ops:
  0.6 1.0 copy-start.1
  1.7 1.0 copy-start.2
  3.7 0.7 copy-start.9
  4.4 16.0 %collective-permute-start.1 = (bf16[2304,128]{1,0:T(8,128)(2,1)}, bf16[2304,128]{1,0:T(8,128)(2,1)}, u32[]{:S(2)}, u32[]{:S(2)}) collective-permute-start(bf16[2304,128]{1,0:T(8,128)(2,1)} %get-tuple-element.59.refs_0_), channel_id=1, source_target_pairs={{0,32},{16,48},{32,64},{48,80},{64,96},{80,112},{96,128},{112,144}... | collective-permute-start | bytes 1769480 | tf_op jit(solution)/shard_map/ppermute | solution.py:413
  7.6 2.9 %copy-start = (bf16[640,5120]{1,0:T(8,128)(2,1)S(1)}, bf16[640,5120]{1,0:T(8,128)(2,1)}, u32[]{:S(2)}) copy-start(bf16[640,5120]{1,0:T(8,128)(2,1)} %weight_ref.1) | copy-start | bytes 19660804
  10.4 4.5 %copy-start.11 = (s32[48,18]{0,1:T(8,128)S(1)}, s32[48,18]{0,1:T(8,128)}, u32[]{:S(2)}) copy-start(s32[48,18]{0,1:T(8,128)} %param.16) | copy-start | bytes 10372
  10.4 4.6 %copy-start.3 = (s32[48]{0:T(128)S(1)}, s32[48]{0:T(128)}, u32[]{:S(2)}) copy-start(s32[48]{0:T(128)} %count_ref.1) | copy-start | bytes 580
  11.8 3.1 %copy-start.4 = (bf16[640,640]{1,0:T(8,128)(2,1)}, bf16[640,640]{1,0:T(8,128)(2,1)S(1)}, u32[]{:S(2)}) copy-start(bf16[640,640]{1,0:T(8,128)(2,1)S(1)} %get-tuple-element.57) | copy-start | bytes 2457604
  11.8 32.8 %collective-permute-start.5 = (bf16[640,640]{1,0:T(8,128)(2,1)}, bf16[640,640]{1,0:T(8,128)(2,1)S(1)}, u32[]{:S(2)}, u32[]{:S(2)}) collective-permute-start(bf16[640,640]{1,0:T(8,128)(2,1)} %get-tuple-element.70), channel_id=1, source_target_pairs={{0,12},{2,14},{4,0},{6,2},{8,4},{10,6},{12,8},{14,10},{1,13},{3,15... | collective-permute-start | bytes 2457608 | tf_op jit(solution)/shard_map/ppermute | solution.py:436
  14.9 29.7 %collective-permute-start.6 = (bf16[640,640]{1,0:T(8,128)(2,1)}, bf16[640,640]{1,0:T(8,128)(2,1)S(1)}, u32[]{:S(2)}, u32[]{:S(2)}) collective-permute-start(bf16[640,640]{1,0:T(8,128)(2,1)} %get-tuple-element.71), channel_id=1, source_target_pairs={{0,4},{2,6},{4,8},{6,10},{8,12},{10,14},{12,0},{14,2},{1,5},{3,7},... | collective-permute-start | bytes 2457608 | tf_op jit(solution)/shard_map/ppermute | solution.py:436
  14.9 16.0 %collective-permute-start.10 = (bf16[2304,128]{1,0:T(8,128)(2,1)}, bf16[2304,128]{1,0:T(8,128)(2,1)}, u32[]{:S(2)}, u32[]{:S(2)}) collective-permute-start(bf16[2304,128]{1,0:T(8,128)(2,1)} %get-tuple-element.59.refs_0_), channel_id=1, source_target_pairs={{0,224},{16,240},{32,0},{48,16},{64,32},{80,48},{96,64},{112,80},{... | collective-permute-start | bytes 1769480 | tf_op jit(solution)/shard_map/ppermute | solution.py:413
  20.5 24.2 %collective-permute-start.3 = (bf16[2304,128]{1,0:T(8,128)(2,1)}, bf16[2304,128]{1,0:T(8,128)(2,1)S(1)}, u32[]{:S(2)}, u32[]{:S(2)}) collective-permute-start(bf16[2304,128]{1,0:T(8,128)(2,1)} %collective-permute-done.1.refs_1_), channel_id=1, source_target_pairs={{0,32},{16,48},{32,64},{48,80},{64,96},{80,112},{96,128},{112,144}... | collective-permute-start | bytes 1769480 | tf_op jit(solution)/shard_map/ppermute | solution.py:413
  24.2 20.5 %collective-permute-start.4 = (bf16[1536,128]{1,0:T(8,128)(2,1)}, bf16[1536,128]{1,0:T(8,128)(2,1)S(1)}, u32[]{:S(2)}, u32[]{:S(2)}) collective-permute-start(bf16[1536,128]{1,0:T(8,128)(2,1)} %copy-done.9), channel_id=1, source_target_pairs={{0,32},{16,48},{32,64},{48,80},{64,96},{80,112},{96,128},{112,144}... | collective-permute-start | bytes 1179656 | tf_op jit(solution)/shard_map/ppermute | solution.py:413
  30.9 27.6 %collective-permute-start.11 = (bf16[2304,128]{1,0:T(8,128)(2,1)}, bf16[2304,128]{1,0:T(8,128)(2,1)S(1)}, u32[]{:S(2)}, u32[]{:S(2)}) collective-permute-start(bf16[2304,128]{1,0:T(8,128)(2,1)} %collective-permute-done.10.refs_7_), channel_id=1, source_target_pairs={{0,224},{16,240},{32,0},{48,16},{64,32},{80,48},{96,64},{112,80},{... | collective-permute-start | bytes 1769480 | tf_op jit(solution)/shard_map/ppermute | solution.py:413
  44.6 14.5 %collective-permute-start.7 = (bf16[2304,128]{1,0:T(8,128)(2,1)S(1)}, bf16[2304,128]{1,0:T(8,128)(2,1)S(1)}, u32[]{:S(2)}, u32[]{:S(2)}) collective-permute-start(bf16[2304,128]{1,0:T(8,128)(2,1)S(1)} %collective-permute-done.3.refs_2_), channel_id=1, source_target_pairs={{0,32},{16,48},{32,64},{48,80},{64,96},{80,112},{96,128},{112,144}... | collective-permute-start | bytes 1769480 | tf_op jit(solution)/shard_map/ppermute | solution.py:413
  48.3 10.2 %collective-permute-start.12 = (bf16[1536,128]{1,0:T(8,128)(2,1)}, bf16[1536,128]{1,0:T(8,128)(2,1)S(1)}, u32[]{:S(2)}, u32[]{:S(2)}) collective-permute-start(bf16[1536,128]{1,0:T(8,128)(2,1)} %copy-done.9), channel_id=1, source_target_pairs={{0,224},{16,240},{32,0},{48,16},{64,32},{80,48},{96,64},{112,80},{... | collective-permute-start | bytes 1179656 | tf_op jit(solution)/shard_map/ppermute | solution.py:413
  58.5 21.9 %collective-permute-start.14 = (bf16[2304,128]{1,0:T(8,128)(2,1)S(1)}, bf16[2304,128]{1,0:T(8,128)(2,1)S(1)}, u32[]{:S(2)}, u32[]{:S(2)}) collective-permute-start(bf16[2304,128]{1,0:T(8,128)(2,1)S(1)} %collective-permute-done.11.refs_6_), channel_id=1, source_target_pairs={{0,224},{16,240},{32,0},{48,16},{64,32},{80,48},{96,64},{112,80},{... | collective-permute-start | bytes 1769480 | tf_op jit(solution)/shard_map/ppermute | solution.py:413
  59.1 21.3 %collective-permute-start.8 = (bf16[2304,128]{1,0:T(8,128)(2,1)S(1)}, bf16[2304,128]{1,0:T(8,128)(2,1)S(1)}, u32[]{:S(2)}, u32[]{:S(2)}) collective-permute-start(bf16[2304,128]{1,0:T(8,128)(2,1)S(1)} %collective-permute-done.7.refs_3_), channel_id=1, source_target_pairs={{0,32},{16,48},{32,64},{48,80},{64,96},{80,112},{96,128},{112,144}... | collective-permute-start | bytes 1769480 | tf_op jit(solution)/shard_map/ppermute | solution.py:413
  62.8 20.9 %collective-permute-start = (bf16[640,640]{1,0:T(8,128)(2,1)}, bf16[640,640]{1,0:T(8,128)(2,1)S(1)}, u32[]{:S(2)}, u32[]{:S(2)}) collective-permute-start(bf16[640,640]{1,0:T(8,128)(2,1)} %copy-done.4), channel_id=1, source_target_pairs={{0,8},{2,10},{4,12},{6,14},{8,0},{10,2},{12,4},{14,6},{1,9},{3,11}... | collective-permute-start | bytes 2457608 | tf_op jit(solution)/shard_map/ppermute | solution.py:436
  66.0 14.4 %collective-permute-start.13 = (bf16[1536,128]{1,0:T(8,128)(2,1)S(1)}, bf16[1536,128]{1,0:T(8,128)(2,1)S(1)}, u32[]{:S(2)}, u32[]{:S(2)}) collective-permute-start(bf16[1536,128]{1,0:T(8,128)(2,1)S(1)} %collective-permute-done.12.refs_7_), channel_id=1, source_target_pairs={{0,224},{16,240},{32,0},{48,16},{64,32},{80,48},{96,64},{112,80},{... | collective-permute-start | bytes 1179656 | tf_op jit(solution)/shard_map/ppermute | solution.py:413
  66.0 23.4 %collective-permute-start.2 = (bf16[384,640]{1,0:T(8,128)(2,1)}, bf16[384,640]{1,0:T(8,128)(2,1)S(1)}, u32[]{:S(2)}, u32[]{:S(2)}) collective-permute-start(bf16[384,640]{1,0:T(8,128)(2,1)} %q_ref.6), channel_id=1, source_target_pairs={{0,16},{16,0},{32,48},{48,32},{64,80},{80,64},{96,112},{112,96},{1... | collective-permute-start | bytes 1474568 | tf_op jit(solution)/shard_map/ppermute | solution.py:393
  80.4 9.0 %collective-permute-start.23 = (bf16[1536,128]{1,0:T(8,128)(2,1)S(1)}, bf16[1536,128]{1,0:T(8,128)(2,1)S(1)}, u32[]{:S(2)}, u32[]{:S(2)}) collective-permute-start(bf16[1536,128]{1,0:T(8,128)(2,1)S(1)} %collective-permute-done.13.refs_6_), channel_id=1, source_target_pairs={{0,224},{16,240},{32,0},{48,16},{64,32},{80,48},{96,64},{112,80},{... | collective-permute-start | bytes 1179656 | tf_op jit(solution)/shard_map/ppermute | solution.py:413
  80.4 9.0 %collective-permute-start.9 = (bf16[1536,128]{1,0:T(8,128)(2,1)S(1)}, bf16[1536,128]{1,0:T(8,128)(2,1)S(1)}, u32[]{:S(2)}, u32[]{:S(2)}) collective-permute-start(bf16[1536,128]{1,0:T(8,128)(2,1)S(1)} %collective-permute-done.4.refs_1_), channel_id=1, source_target_pairs={{0,32},{16,48},{32,64},{48,80},{64,96},{80,112},{96,128},{112,144}... | collective-permute-start | bytes 1179656 | tf_op jit(solution)/shard_map/ppermute | solution.py:413
  83.7 39.0 %collective-permute-start.20 = (bf16[640,640]{1,0:T(8,128)(2,1)S(1)}, bf16[640,640]{1,0:T(8,128)(2,1)S(1)}, u32[]{:S(2)}, u32[]{:S(2)}) collective-permute-start(bf16[640,640]{1,0:T(8,128)(2,1)S(1)} %collective-permute-done.refs_8_.refs_9_), channel_id=1, source_target_pairs={{0,1},{1,0},{2,3},{3,2},{4,5},{5,4},{6,7},{7,6},{8,9},{9,8},{10,11... | collective-permute-start | bytes 2457608 | tf_op jit(solution)/shard_map/ppermute | solution.py:452
  83.7 46.6 %collective-permute-start.19 = (bf16[640,640]{1,0:T(8,128)(2,1)S(1)}, bf16[640,640]{1,0:T(8,128)(2,1)S(1)}, u32[]{:S(2)}, u32[]{:S(2)}) collective-permute-start(bf16[640,640]{1,0:T(8,128)(2,1)S(1)} %collective-permute-done.5.refs_6_.refs_7_), channel_id=1, source_target_pairs={{0,1},{1,0},{2,3},{3,2},{4,5},{5,4},{6,7},{7,6},{8,9},{9,8},{10,11... | collective-permute-start | bytes 2457608 | tf_op jit(solution)/shard_map/ppermute | solution.py:452
  89.4 42.7 %collective-permute-start.21 = (bf16[640,640]{1,0:T(8,128)(2,1)S(1)}, bf16[640,640]{1,0:T(8,128)(2,1)S(1)}, u32[]{:S(2)}, u32[]{:S(2)}) collective-permute-start(bf16[640,640]{1,0:T(8,128)(2,1)S(1)} %collective-permute-done.6.refs_10_.refs_11_), channel_id=1, source_target_pairs={{0,1},{1,0},{2,3},{3,2},{4,5},{5,4},{6,7},{7,6},{8,9},{9,8},{10,11... | collective-permute-start | bytes 2457608 | tf_op jit(solution)/shard_map/ppermute | solution.py:452
  89.4 15.3 %collective-permute-start.24 = (bf16[1536,128]{1,0:T(8,128)(2,1)S(1)}, bf16[1536,128]{1,0:T(8,128)(2,1)S(1)}, u32[]{:S(2)}, u32[]{:S(2)}) collective-permute-start(bf16[1536,128]{1,0:T(8,128)(2,1)S(1)} %collective-permute-done.23.refs_5_), channel_id=1, source_target_pairs={{0,224},{16,240},{32,0},{48,16},{64,32},{80,48},{96,64},{112,80},{... | collective-permute-start | bytes 1179656 | tf_op jit(solution)/shard_map/ppermute | solution.py:413
  89.4 16.7 %collective-permute-start.22 = (bf16[1536,128]{1,0:T(8,128)(2,1)S(1)}, bf16[1536,128]{1,0:T(8,128)(2,1)S(1)}, u32[]{:S(2)}, u32[]{:S(2)}) collective-permute-start(bf16[1536,128]{1,0:T(8,128)(2,1)S(1)} %collective-permute-done.9.refs_2_), channel_id=1, source_target_pairs={{0,32},{16,48},{32,64},{48,80},{64,96},{80,112},{96,128},{112,144}... | collective-permute-start | bytes 1179656 | tf_op jit(solution)/shard_map/ppermute | solution.py:413
  92.7 1.0 copy-start.7
  93.7 12.5 %copy-start.10 = (bf16[1536,128]{1,0:T(8,128)(2,1)S(1)}, bf16[1536,128]{1,0:T(8,128)(2,1)}, u32[]{:S(2)}) copy-start(bf16[1536,128]{1,0:T(8,128)(2,1)} %copy-done.9) | copy-start | bytes 1179652
  104.7 16.3 %collective-permute-start.15 = (bf16[2304,128]{1,0:T(8,128)(2,1)S(1)}, bf16[2304,128]{1,0:T(8,128)(2,1)S(1)}, u32[]{:S(2)}, u32[]{:S(2)}) collective-permute-start(bf16[2304,128]{1,0:T(8,128)(2,1)S(1)} %get-tuple-element.90), channel_id=1, source_target_pairs={{0,16},{16,0},{32,48},{48,32},{64,80},{80,64},{96,112},{112,96},{1... | collective-permute-start | bytes 1769480 | tf_op jit(solution)/shard_map/ppermute | solution.py:393
  111.1 15.0 %collective-permute-start.25 = (bf16[768,128]{1,0:T(8,128)(2,1)S(1)}, bf16[768,128]{1,0:T(8,128)(2,1)S(1)}, u32[]{:S(2)}, u32[]{:S(2)}) collective-permute-start(bf16[768,128]{1,0:T(8,128)(2,1)S(1)} %get-tuple-element.102), channel_id=1, source_target_pairs={{0,16},{16,0},{32,48},{48,32},{64,80},{80,64},{96,112},{112,96},{1... | collective-permute-start | bytes 589832 | tf_op jit(solution)/shard_map/ppermute | solution.py:393
  121.0 7.4 %collective-permute-start.29 = (bf16[768,128]{1,0:T(8,128)(2,1)S(1)}, bf16[768,128]{1,0:T(8,128)(2,1)S(1)}, u32[]{:S(2)}, u32[]{:S(2)}) collective-permute-start(bf16[768,128]{1,0:T(8,128)(2,1)S(1)} %get-tuple-element.106), channel_id=1, source_target_pairs={{0,16},{16,0},{32,48},{48,32},{64,80},{80,64},{96,112},{112,96},{1... | collective-permute-start | bytes 589832 | tf_op jit(solution)/shard_map/ppermute | solution.py:393
  122.7 17.1 %collective-permute-start.16 = (bf16[384,384]{1,0:T(8,128)(2,1)S(1)}, bf16[384,384]{1,0:T(8,128)(2,1)S(1)}, u32[]{:S(2)}, u32[]{:S(2)}) collective-permute-start(bf16[384,384]{1,0:T(8,128)(2,1)S(1)} %merge.3.refs_0_), channel_id=1, source_target_pairs={{0,12},{2,14},{4,0},{6,2},{8,4},{10,6},{12,8},{14,10},{1,13},{3,15... | collective-permute-start | bytes 884744 | tf_op jit(solution)/shard_map/ppermute | solution.py:424
  126.0 13.7 %collective-permute-start.17 = (bf16[384,384]{1,0:T(8,128)(2,1)S(1)}, bf16[384,384]{1,0:T(8,128)(2,1)S(1)}, u32[]{:S(2)}, u32[]{:S(2)}) collective-permute-start(bf16[384,384]{1,0:T(8,128)(2,1)S(1)} %merge.3.refs_0_), channel_id=1, source_target_pairs={{0,8},{2,10},{4,12},{6,14},{8,0},{10,2},{12,4},{14,6},{1,9},{3,11}... | collective-permute-start | bytes 884744 | tf_op jit(solution)/shard_map/ppermute | solution.py:424
  128.4 13.5 %collective-permute-start.18 = (bf16[384,384]{1,0:T(8,128)(2,1)S(1)}, bf16[384,384]{1,0:T(8,128)(2,1)S(1)}, u32[]{:S(2)}, u32[]{:S(2)}) collective-permute-start(bf16[384,384]{1,0:T(8,128)(2,1)S(1)} %merge.3.refs_0_), channel_id=1, source_target_pairs={{0,4},{2,6},{4,8},{6,10},{8,12},{10,14},{12,0},{14,2},{1,5},{3,7},... | collective-permute-start | bytes 884744 | tf_op jit(solution)/shard_map/ppermute | solution.py:424
  130.3 18.0 %collective-permute-start.30 = (bf16[384,128]{1,0:T(8,128)(2,1)S(1)}, bf16[384,128]{1,0:T(8,128)(2,1)S(1)}, u32[]{:S(2)}, u32[]{:S(2)}) collective-permute-start(bf16[384,128]{1,0:T(8,128)(2,1)S(1)} %merge.5.refs_0_), channel_id=1, source_target_pairs={{0,12},{2,14},{4,0},{6,2},{8,4},{10,6},{12,8},{14,10},{1,13},{3,15... | collective-permute-start | bytes 294920 | tf_op jit(solution)/shard_map/ppermute | solution.py:424
  132.1 16.8 %collective-permute-start.31 = (bf16[384,128]{1,0:T(8,128)(2,1)S(1)}, bf16[384,128]{1,0:T(8,128)(2,1)S(1)}, u32[]{:S(2)}, u32[]{:S(2)}) collective-permute-start(bf16[384,128]{1,0:T(8,128)(2,1)S(1)} %merge.5.refs_0_), channel_id=1, source_target_pairs={{0,8},{2,10},{4,12},{6,14},{8,0},{10,2},{12,4},{14,6},{1,9},{3,11}... | collective-permute-start | bytes 294920 | tf_op jit(solution)/shard_map/ppermute | solution.py:424
  139.8 9.1 %collective-permute-start.32 = (bf16[384,128]{1,0:T(8,128)(2,1)S(1)}, bf16[384,128]{1,0:T(8,128)(2,1)S(1)}, u32[]{:S(2)}, u32[]{:S(2)}) collective-permute-start(bf16[384,128]{1,0:T(8,128)(2,1)S(1)} %merge.5.refs_0_), channel_id=1, source_target_pairs={{0,4},{2,6},{4,8},{6,10},{8,12},{10,14},{12,0},{14,2},{1,5},{3,7},... | collective-permute-start | bytes 294920 | tf_op jit(solution)/shard_map/ppermute | solution.py:424
  144.3 5.7 %collective-permute-start.26 = (bf16[384,128]{1,0:T(8,128)(2,1)S(1)}, bf16[384,128]{1,0:T(8,128)(2,1)S(1)}, u32[]{:S(2)}, u32[]{:S(2)}) collective-permute-start(bf16[384,128]{1,0:T(8,128)(2,1)S(1)} %merge.4.refs_1_), channel_id=1, source_target_pairs={{0,12},{2,14},{4,0},{6,2},{8,4},{10,6},{12,8},{14,10},{1,13},{3,15... | collective-permute-start | bytes 294920 | tf_op jit(solution)/shard_map/ppermute | solution.py:424
  145.9 6.3 %collective-permute-start.27 = (bf16[384,128]{1,0:T(8,128)(2,1)S(1)}, bf16[384,128]{1,0:T(8,128)(2,1)S(1)}, u32[]{:S(2)}, u32[]{:S(2)}) collective-permute-start(bf16[384,128]{1,0:T(8,128)(2,1)S(1)} %merge.4.refs_1_), channel_id=1, source_target_pairs={{0,8},{2,10},{4,12},{6,14},{8,0},{10,2},{12,4},{14,6},{1,9},{3,11}... | collective-permute-start | bytes 294920 | tf_op jit(solution)/shard_map/ppermute | solution.py:424
  148.3 5.8 %collective-permute-start.28 = (bf16[384,128]{1,0:T(8,128)(2,1)S(1)}, bf16[384,128]{1,0:T(8,128)(2,1)S(1)}, u32[]{:S(2)}, u32[]{:S(2)}) collective-permute-start(bf16[384,128]{1,0:T(8,128)(2,1)S(1)} %merge.4.refs_1_), channel_id=1, source_target_pairs={{0,4},{2,6},{4,8},{6,10},{8,12},{10,14},{12,0},{14,2},{1,5},{3,7},... | collective-permute-start | bytes 294920 | tf_op jit(solution)/shard_map/ppermute | solution.py:424
  150.0 6.1 %copy-start.5 = (bf16[512,640]{1,0:T(8,128)(2,1)S(1)}, bf16[512,640]{1,0:T(8,128)(2,1)}, u32[]{:S(2)}) copy-start(bf16[512,640]{1,0:T(8,128)(2,1)} %k_ref.3) | copy-start | bytes 1966084
  150.0 6.0 %copy-start.6 = (bf16[512,640]{1,0:T(8,128)(2,1)S(1)}, bf16[512,640]{1,0:T(8,128)(2,1)}, u32[]{:S(2)}) copy-start(bf16[512,640]{1,0:T(8,128)(2,1)} %v_ref.3) | copy-start | bytes 1966084
  150.0 6.0 %copy-start.8 = (bf16[384,640]{1,0:T(8,128)(2,1)S(1)}, bf16[384,640]{1,0:T(8,128)(2,1)}, u32[]{:S(2)}) copy-start(bf16[384,640]{1,0:T(8,128)(2,1)} %q_ref.7) | copy-start | bytes 1474564
  155.5 11.2 %collective-permute-start.33 = (bf16[384,640]{1,0:T(8,128)(2,1)S(1)}, bf16[384,640]{1,0:T(8,128)(2,1)S(1)}, u32[]{:S(2)}, u32[]{:S(2)}) collective-permute-start(bf16[384,640]{1,0:T(8,128)(2,1)S(1)} %get-tuple-element.109), channel_id=1, source_target_pairs={{0,2},{2,0},{4,6},{6,4},{8,10},{10,8},{12,14},{14,12},{1,3},{3,1},... | collective-permute-start | bytes 1474568 | tf_op jit(solution)/shard_map/ppermute | solution.py:461

commit v3 on v1

--- a/solution.py
+++ b/solution.py
@@ -416,8 +416,8 @@
         pieces = [held[group][d] for d in range(n_z)]
         return list(attend(GROUPS[group][start:stop], start, queries, queries_other, pieces, seq, near, blocks, counts))
 
-    def join(part):
-        return merge(*part[:2], to_other(part[2]))
+    def join(*parts):
+        return merge(*(array for part in parts for array in (*part[:2], to_other(part[2]))))
 
     def along_y(array):
         return [array] + [lax.ppermute(array, "head", y_shift(-dy)) for dy in range(1, n_y)]
@@ -428,7 +428,7 @@
     queries_other = to_other(queries)
     early = list(plan(n_seq, seq, block_list, block_count))
     tiles = list(tile(lax.div(head, 2), pair, out_weight, n_y))
-    early[0], tiles[0] = lax.optimization_barrier((early[0], tiles[0]))
+    early[0], tiles[0], queries_other = lax.optimization_barrier((early[0], tiles[0], queries_other))
     hop(1, 0, 2, early)
     hop(-1, 0, 2)
     blocks, counts, near = early
@@ -441,20 +441,20 @@
     hop(-1, 1, 2)
     hop(1, 1, 2)
     hop(-1, 1, 3)
+    hop(1, 1, 3)
+    hop(-1, 1, 4)
     near, tiles[2] = lax.optimization_barrier((near, tiles[2]))
     weights = [tiles[0], tiles[n_y]]
     for mine in tiles[1:n_y]:
         weights += [mine, lax.ppermute(mine, "pair", [(0, 1), (1, 0)])]
     most = partial(0, 0, 3)
-    hop(1, 1, 3, most)
-    hop(-1, 1, 4, most)
+    near, *weights = lax.optimization_barrier((near, *weights))
+    one, two = partial(1, 0, 1), partial(1, 1, 2)
+    most[0], two[2] = lax.optimization_barrier((most[0], two[2]))
     before = project(GROUPS[0][0], along_y(join(most)), weights)
-    one, two = partial(1, 0, 1), partial(1, 1, 2)
-    two = join(two)
-    before, two = lax.optimization_barrier((before, two))
-    before = project(GROUPS[1][0], along_y(join(one)), weights, before)
+    rest = join(one, two)
     keep_block = (lax.rem(head, 2) != pair).astype(jnp.int32)
-    keep, send = project(GROUPS[1][1], along_y(two), weights, before, keep_block)
+    keep, send = project(GROUPS[1][0], along_y(rest), weights, before, keep_block)
     got = lax.ppermute(send, "head", [(g, g ^ 1) for g in range(n_head)])
     return (keep + got.astype(jnp.float32)).astype(jnp.bfloat16), cross_heads
 

time: 161 us -> 155 us (0.963)
  starting transfers between devices: 44.8 us -> 39.9 us
  waiting for transfers between devices: 70.8 us -> 68 us
  local copies, waits for them, and re-layouts: 6.06 us -> 7.69 us
    ppermute x4, waiting for transfers between devices: 2.46 us -> 12.4 us  [to_other(): return lax.ppermute(array, 'seq', swap)]
    ppermute x9 -> x6, waiting for transfers between devices: 11.9 us -> 5.14 us  [along_y(): lax.ppermute(array, 'head', y_shift(-dy))]
    ppermute x14, waiting for transfers between devices: 50.9 us -> 45.1 us  [hop(): held[group][place] = lax.ppermute(array, 'seq', z_shift(way))]
    ppermute x9 -> x6, starting transfers between devices: 11.5 us -> 8.72 us  [along_y(): lax.ppermute(array, 'head', y_shift(-dy))]
    pallas_call x3, Pallas kernels: 21.2 us -> 23.4 us  [attend(): pl.pallas_call(functools.partial(attend_kernel, heads, first, planes), ou...]
    unnamed x23 -> x25, local copies, waits for them, and re-layouts: 6.06 us -> 7.69 us
    pallas_call x3 -> x2, Pallas kernels: 4.85 us -> 3.9 us  [project(): pl.pallas_call(functools.partial(project_kernel, first, len(heads), last)...]
  transfers between devices with their start and end apart: 34 -> 31, of which waited for: 17 -> 15; matrix products, arithmetic and copies ran while one was open for 0% -> 0% of each run, Pallas kernels for 15% -> 23%
where the time goes in v3:
time: 155 us
  waiting for transfers between devices  68 us (44%)
  starting transfers between devices  39.9 us (26%)
  Pallas kernels  37.9 us (24%)
  local copies, waits for them, and re-layouts  7.69 us (5%)
    ppermute x14, waiting for transfers between devices, hop(): held[group][place] = lax.ppermute(array, 'seq', z_shift(way))  45.1 us
    pallas_call x3, Pallas kernels, attend(): pl.pallas_call(functools.partial(attend_kernel, heads, first, planes), ou...  23.4 us
    ppermute x14, starting transfers between devices, hop(): held[group][place] = lax.ppermute(array, 'seq', z_shift(way))  19.7 us
    ppermute x4, waiting for transfers between devices, to_other(): return lax.ppermute(array, 'seq', swap)  12.4 us
    ppermute x6, starting transfers between devices, along_y(): lax.ppermute(array, 'head', y_shift(-dy))  8.72 us
    unnamed x25, local copies, waits for them, and re-layouts  7.69 us
    ppermute x3, starting transfers between devices, body(): lax.ppermute(tiles[dy], 'head', y_shift(dy))  6.21 us
    ppermute x1, waiting for transfers between devices, body(): got = lax.ppermute(send, 'head', [(g, g ^ 1) for g in range(n_head)])  5.38 us
  transfers between devices with their start and end apart: 31, of which 15 were waited for; matrix products, arithmetic and copies ran while one was open for 0% of the time, Pallas kernels for 23%

profile of v3, /device:TPU:4, one launch (start us, length us, event | category | flops | bytes accessed | tf_op | source)
XLA Modules:
  0.0 155.4 jit_solution(12415536506172869620)
XLA Ops:
  0.6 1.0 copy-done.1
  1.7 1.0 copy-done.2
  2.7 1.0 pack.1
  3.7 0.7 copy-done.9
  4.5 1.9 %collective-permute-start.2 = (bf16[2304,128]{1,0:T(8,128)(2,1)}, bf16[2304,128]{1,0:T(8,128)(2,1)}, u32[]{:S(2)}, u32[]{:S(2)}) collective-permute-start(bf16[2304,128]{1,0:T(8,128)(2,1)} %get-tuple-element.71.refs_0_), channel_id=1, source_target_pairs={{0,32},{16,48},{32,64},{48,80},{64,96},{80,112},{96,128},{112,144}... | collective-permute-start | bytes 1769480 | tf_op jit(solution)/shard_map/ppermute | solution.py:412
  6.4 1.2 collective-permute-start.1
  7.6 3.9 %collective-permute-start.14 = (bf16[2304,128]{1,0:T(8,128)(2,1)}, bf16[2304,128]{1,0:T(8,128)(2,1)}, u32[]{:S(2)}, u32[]{:S(2)}) collective-permute-start(bf16[2304,128]{1,0:T(8,128)(2,1)} %get-tuple-element.71.refs_0_), channel_id=1, source_target_pairs={{0,224},{16,240},{32,0},{48,16},{64,32},{80,48},{96,64},{112,80},{... | collective-permute-start | bytes 1769480 | tf_op jit(solution)/shard_map/ppermute | solution.py:412
  11.5 2.9 %copy-done = bf16[640,5120]{1,0:T(8,128)(2,1)S(1)} copy-done((bf16[640,5120]{1,0:T(8,128)(2,1)S(1)}, bf16[640,5120]{1,0:T(8,128)(2,1)}, u32[]{:S(2)}) %copy-start) | copy-done | bytes 6553624
  14.4 1.3 tile.1
  15.7 0.9 copy-done.4
  16.6 3.0 %collective-permute-start.5 = (bf16[640,640]{1,0:T(8,128)(2,1)}, bf16[640,640]{1,0:T(8,128)(2,1)S(1)}, u32[]{:S(2)}, u32[]{:S(2)}) collective-permute-start(bf16[640,640]{1,0:T(8,128)(2,1)} %get-tuple-element.77), channel_id=1, source_target_pairs={{0,12},{2,14},{4,0},{6,2},{8,4},{10,6},{12,8},{14,10},{1,13},{3,15... | collective-permute-start | bytes 2457608 | tf_op jit(solution)/shard_map/ppermute | solution.py:435
  19.7 3.6 %plan.1 = (s32[6,13]{1,0:T(8,128)S(1)}, s32[6]{0:T(128)S(1)}, s32[8]{0:T(128)S(1)}) custom-call(s32[1]{0:T(128)} %bitcast.2.seq_ref, s32[48,18]{1,0:T(8,128)S(1)} %copy.11.list_ref, s32[48]{0:T(128)S(1)} %copy-done.3), custom_call_target="tpu_custom_call" | custom-call | flops 1000 | bytes 8000 | tf_op jit(solution)/shard_map/plan/pallas_call | solution.py:60
  23.4 0.6 collective-permute-done.2.refs_1_
  24.1 3.7 %collective-permute-start.15 = (bf16[2304,128]{1,0:T(8,128)(2,1)}, bf16[2304,128]{1,0:T(8,128)(2,1)S(1)}, u32[]{:S(2)}, u32[]{:S(2)}) collective-permute-start(bf16[2304,128]{1,0:T(8,128)(2,1)} %collective-permute-done.14.refs_7_), channel_id=1, source_target_pairs={{0,224},{16,240},{32,0},{48,16},{64,32},{80,48},{96,64},{112,80},{... | collective-permute-start | bytes 1769480 | tf_op jit(solution)/shard_map/ppermute | solution.py:412
  27.8 9.0 %collective-permute-done.4.refs_1_ = bf16[1536,128]{1,0:T(8,128)(2,1)S(1)} collective-permute-done((bf16[1536,128]{1,0:T(8,128)(2,1)}, bf16[1536,128]{1,0:T(8,128)(2,1)S(1)}, u32[]{:S(2)}, u32[]{:S(2)}) %collective-permute-start.4) | collective-permute-done | bytes 393248 | tf_op jit(solution)/shard_map/ppermute | solution.py:412
  36.8 0.8 collective-permute-start.16
  37.6 9.8 %collective-permute-done.3.refs_2_ = bf16[2304,128]{1,0:T(8,128)(2,1)S(1)} collective-permute-done((bf16[2304,128]{1,0:T(8,128)(2,1)}, bf16[2304,128]{1,0:T(8,128)(2,1)S(1)}, u32[]{:S(2)}, u32[]{:S(2)}) %collective-permute-start.3) | collective-permute-done | bytes 589856 | tf_op jit(solution)/shard_map/ppermute | solution.py:412
  47.5 0.5 collective-permute-done.16.refs_7_
  48.0 3.6 %collective-permute-start.18 = (bf16[2304,128]{1,0:T(8,128)(2,1)S(1)}, bf16[2304,128]{1,0:T(8,128)(2,1)S(1)}, u32[]{:S(2)}, u32[]{:S(2)}) collective-permute-start(bf16[2304,128]{1,0:T(8,128)(2,1)S(1)} %collective-permute-done.15.refs_6_), channel_id=1, source_target_pairs={{0,224},{16,240},{32,0},{48,16},{64,32},{80,48},{96,64},{112,80},{... | collective-permute-start | bytes 1769480 | tf_op jit(solution)/shard_map/ppermute | solution.py:412
  51.6 3.2 %collective-permute-start = (bf16[640,640]{1,0:T(8,128)(2,1)}, bf16[640,640]{1,0:T(8,128)(2,1)S(1)}, u32[]{:S(2)}, u32[]{:S(2)}) collective-permute-start(bf16[640,640]{1,0:T(8,128)(2,1)} %copy-done.4), channel_id=1, source_target_pairs={{0,8},{2,10},{4,12},{6,14},{8,0},{10,2},{12,4},{14,6},{1,9},{3,11}... | collective-permute-start | bytes 2457608 | tf_op jit(solution)/shard_map/ppermute | solution.py:435
  54.8 7.2 %collective-permute-done.10.refs_3_ = bf16[2304,128]{1,0:T(8,128)(2,1)S(1)} collective-permute-done((bf16[2304,128]{1,0:T(8,128)(2,1)S(1)}, bf16[2304,128]{1,0:T(8,128)(2,1)S(1)}, u32[]{:S(2)}, u32[]{:S(2)}) %collective-permute-start.10) | collective-permute-done | bytes 589856 | tf_op jit(solution)/shard_map/ppermute | solution.py:412
  62.0 8.5 %collective-permute-done.17.refs_6_ = bf16[1536,128]{1,0:T(8,128)(2,1)S(1)} collective-permute-done((bf16[1536,128]{1,0:T(8,128)(2,1)S(1)}, bf16[1536,128]{1,0:T(8,128)(2,1)S(1)}, u32[]{:S(2)}, u32[]{:S(2)}) %collective-permute-start.17) | collective-permute-done | bytes 393248 | tf_op jit(solution)/shard_map/ppermute | solution.py:412
  70.5 3.7 %collective-permute-start.19 = (bf16[1536,128]{1,0:T(8,128)(2,1)S(1)}, bf16[1536,128]{1,0:T(8,128)(2,1)S(1)}, u32[]{:S(2)}, u32[]{:S(2)}) collective-permute-start(bf16[1536,128]{1,0:T(8,128)(2,1)S(1)} %collective-permute-done.17.refs_6_), channel_id=1, source_target_pairs={{0,224},{16,240},{32,0},{48,16},{64,32},{80,48},{96,64},{112,80},{... | collective-permute-start | bytes 1179656 | tf_op jit(solution)/shard_map/ppermute | solution.py:412
  74.2 0.5 collective-permute-start.7
  74.7 4.8 %collective-permute-done.19.refs_5_ = bf16[1536,128]{1,0:T(8,128)(2,1)S(1)} collective-permute-done((bf16[1536,128]{1,0:T(8,128)(2,1)S(1)}, bf16[1536,128]{1,0:T(8,128)(2,1)S(1)}, u32[]{:S(2)}, u32[]{:S(2)}) %collective-permute-start.19) | collective-permute-done | bytes 393248 | tf_op jit(solution)/shard_map/ppermute | solution.py:412
  79.5 4.5 %collective-permute-done.11.refs_2_ = bf16[1536,128]{1,0:T(8,128)(2,1)S(1)} collective-permute-done((bf16[1536,128]{1,0:T(8,128)(2,1)S(1)}, bf16[1536,128]{1,0:T(8,128)(2,1)S(1)}, u32[]{:S(2)}, u32[]{:S(2)}) %collective-permute-start.11) | collective-permute-done | bytes 393248 | tf_op jit(solution)/shard_map/ppermute | solution.py:412
  84.0 2.0 %collective-permute-start.13 = (bf16[1536,128]{1,0:T(8,128)(2,1)S(1)}, bf16[1536,128]{1,0:T(8,128)(2,1)S(1)}, u32[]{:S(2)}, u32[]{:S(2)}) collective-permute-start(bf16[1536,128]{1,0:T(8,128)(2,1)S(1)} %collective-permute-done.11.refs_2_), channel_id=1, source_target_pairs={{0,32},{16,48},{32,64},{48,80},{64,96},{80,112},{96,128},{112,144}... | collective-permute-start | bytes 1179656 | tf_op jit(solution)/shard_map/ppermute | solution.py:412
  86.0 1.0 copy-done.7
  87.1 12.3 %attend.5 = (f32[1152,128]{1,0:T(8,128)S(1)}, f32[1152,128]{1,0:T(8,128)S(1)}, bf16[2304,128]{1,0:T(8,128)(2,1)S(1)}) custom-call(s32[1]{0:T(128)} %bitcast.2.seq_ref, s32[8]{0:T(128)S(1)} %get-tuple-element.82.near_ref, s32[6,13]{1,0:T(8,128)S(1)} %get-tuple-element.83.blocks_ref, s32[6]{0:T(128)S(1)} %get-tuple-element.84.count_ref, ...), custom_call_target="tpu_custom_call" | custom-call | flops 13589544960 | bytes 4718592 | tf_op jit(solution)/shard_map/attend/pallas_call | solution.py:226
  99.5 5.5 %attend.4 = (f32[384,128]{1,0:T(8,128)S(1)}, f32[384,128]{1,0:T(8,128)S(1)}, bf16[768,128]{1,0:T(8,128)(2,1)S(1)}) custom-call(s32[1]{0:T(128)} %bitcast.2.seq_ref, s32[8]{0:T(128)S(1)} %get-tuple-element.82.near_ref, s32[6,13]{1,0:T(8,128)S(1)} %get-tuple-element.83.blocks_ref, s32[6]{0:T(128)S(1)} %get-tuple-element.84.count_ref, ...), custom_call_target="tpu_custom_call" | custom-call | flops 4529848320 | bytes 1572864 | tf_op jit(solution)/shard_map/attend/pallas_call | solution.py:226
  105.0 2.1 %collective-permute-start.22 = (bf16[768,128]{1,0:T(8,128)(2,1)S(1)}, bf16[768,128]{1,0:T(8,128)(2,1)S(1)}, u32[]{:S(2)}, u32[]{:S(2)}) collective-permute-start(bf16[768,128]{1,0:T(8,128)(2,1)S(1)} %get-tuple-element.112), channel_id=1, source_target_pairs={{0,16},{16,0},{32,48},{48,32},{64,80},{80,64},{96,112},{112,96},{1... | collective-permute-start | bytes 589832 | tf_op jit(solution)/shard_map/ppermute | solution.py:392
  107.1 7.1 %collective-permute-done.26.refs_2_ = bf16[2304,128]{1,0:T(8,128)(2,1)S(1)} collective-permute-done((bf16[2304,128]{1,0:T(8,128)(2,1)S(1)}, bf16[2304,128]{1,0:T(8,128)(2,1)S(1)}, u32[]{:S(2)}, u32[]{:S(2)}) %collective-permute-start.26) | collective-permute-done | bytes 589856 | tf_op jit(solution)/shard_map/ppermute | solution.py:392
  114.6 3.1 %collective-permute-start.27 = (bf16[384,384]{1,0:T(8,128)(2,1)S(1)}, bf16[384,384]{1,0:T(8,128)(2,1)S(1)}, u32[]{:S(2)}, u32[]{:S(2)}) collective-permute-start(bf16[384,384]{1,0:T(8,128)(2,1)S(1)} %merge.3.refs_0_), channel_id=1, source_target_pairs={{0,12},{2,14},{4,0},{6,2},{8,4},{10,6},{12,8},{14,10},{1,13},{3,15... | collective-permute-start | bytes 884744 | tf_op jit(solution)/shard_map/ppermute | solution.py:423
  117.7 0.6 collective-permute-start.28
  118.3 1.0 collective-permute-start.29
  119.3 5.6 %attend.3 = (f32[384,128]{1,0:T(8,128)S(1)}, f32[384,128]{1,0:T(8,128)S(1)}, bf16[768,128]{1,0:T(8,128)(2,1)S(1)}) custom-call(s32[1]{0:T(128)} %bitcast.2.seq_ref, s32[8]{0:T(128)S(1)} %get-tuple-element.82.near_ref, s32[6,13]{1,0:T(8,128)S(1)} %get-tuple-element.83.blocks_ref, s32[6]{0:T(128)S(1)} %get-tuple-element.84.count_ref, ...), custom_call_target="tpu_custom_call" | custom-call | flops 4529848320 | bytes 1572864 | tf_op jit(solution)/shard_map/attend/pallas_call | solution.py:226
  125.4 5.3 %collective-permute-done.21.refs_2_ = bf16[768,128]{1,0:T(8,128)(2,1)S(1)} collective-permute-done((bf16[768,128]{1,0:T(8,128)(2,1)S(1)}, bf16[768,128]{1,0:T(8,128)(2,1)S(1)}, u32[]{:S(2)}, u32[]{:S(2)}) %collective-permute-start.21) | collective-permute-done | bytes 196640 | tf_op jit(solution)/shard_map/ppermute | solution.py:392
  130.9 2.4 %collective-permute-start.23 = (bf16[384,256]{1,0:T(8,128)(2,1)S(1)}, bf16[384,256]{1,0:T(8,128)(2,1)S(1)}, u32[]{:S(2)}, u32[]{:S(2)}) collective-permute-start(bf16[384,256]{1,0:T(8,128)(2,1)S(1)} %merge.2.refs_1_), channel_id=1, source_target_pairs={{0,12},{2,14},{4,0},{6,2},{8,4},{10,6},{12,8},{14,10},{1,13},{3,15... | collective-permute-start | bytes 589832 | tf_op jit(solution)/shard_map/ppermute | solution.py:423
  133.3 1.7 %collective-permute-start.24 = (bf16[384,256]{1,0:T(8,128)(2,1)S(1)}, bf16[384,256]{1,0:T(8,128)(2,1)S(1)}, u32[]{:S(2)}, u32[]{:S(2)}) collective-permute-start(bf16[384,256]{1,0:T(8,128)(2,1)S(1)} %merge.2.refs_1_), channel_id=1, source_target_pairs={{0,8},{2,10},{4,12},{6,14},{8,0},{10,2},{12,4},{14,6},{1,9},{3,11}... | collective-permute-start | bytes 589832 | tf_op jit(solution)/shard_map/ppermute | solution.py:423
  135.0 2.4 %project.2.refs_13_ = f32[2,384,640]{2,1,0:T(8,128)S(1)} custom-call(bf16[384,384]{1,0:T(8,128)(2,1)S(1)} %merge.3.refs_0_, bf16[384,384]{1,0:T(8,128)(2,1)S(1)} %collective-permute-done.27.refs_1_, bf16[384,384]{1,0:T(8,128)(2,1)S(1)} %collective-permute-done.28.refs_2_, bf16[384,384]{1,0:T(8,128)(2,1)S(1)} %collective-permute-done.29.refs_3_, ...), custom_call_target="tpu_custom_call" | custom-call | flops 1509949440 | bytes 5111808 | tf_op jit(solution)/shard_map/project/pallas_call | solution.py:367
  137.4 1.2 collective-permute-done.23.refs_2_
  138.6 1.9 %collective-permute-done.24.refs_3_ = bf16[384,256]{1,0:T(8,128)(2,1)S(1)} collective-permute-done((bf16[384,256]{1,0:T(8,128)(2,1)S(1)}, bf16[384,256]{1,0:T(8,128)(2,1)S(1)}, u32[]{:S(2)}, u32[]{:S(2)}) %collective-permute-start.24) | collective-permute-done | bytes 196640 | tf_op jit(solution)/shard_map/ppermute | solution.py:423
  140.5 2.0 %collective-permute-done.25.refs_4_ = bf16[384,256]{1,0:T(8,128)(2,1)S(1)} collective-permute-done((bf16[384,256]{1,0:T(8,128)(2,1)S(1)}, bf16[384,256]{1,0:T(8,128)(2,1)S(1)}, u32[]{:S(2)}, u32[]{:S(2)}) %collective-permute-start.25) | collective-permute-done | bytes 196640 | tf_op jit(solution)/shard_map/ppermute | solution.py:423
  142.6 1.5 project.3
  144.1 0.9 collective-permute-start.30
  145.0 4.1 %cross.1 = bf16[384,640]{1,0:T(8,128)(2,1)} custom-call(bf16[384,640]{1,0:T(8,128)(2,1)S(1)} %copy-done.8, bf16[512,640]{1,0:T(8,128)(2,1)S(1)} %copy-done.5, bf16[512,640]{1,0:T(8,128)(2,1)S(1)} %copy-done.6), custom_call_target="tpu_custom_call" | custom-call | flops 5033164800 | bytes 983040 | tf_op jit(solution)/shard_map/cross/pallas_call | solution.py:329
  149.1 5.4 %collective-permute-done.30 = bf16[384,640]{1,0:T(8,128)(2,1)S(1)} collective-permute-done((bf16[384,640]{1,0:T(8,128)(2,1)S(1)}, bf16[384,640]{1,0:T(8,128)(2,1)S(1)}, u32[]{:S(2)}, u32[]{:S(2)}) %collective-permute-start.30) | collective-permute-done | bytes 491552 | tf_op jit(solution)/shard_map/ppermute | solution.py:458
  154.5 0.9 add_convert_fusion
  (51 shorter events, 1.6 us)
Async XLA Ops:
  0.6 1.0 copy-start.1
  1.7 1.0 copy-start.2
  2.7 16.9 %copy-start.11 = (s32[48,18]{0,1:T(8,128)S(1)}, s32[48,18]{0,1:T(8,128)}, u32[]{:S(2)}) copy-start(s32[48,18]{0,1:T(8,128)} %param.16) | copy-start | bytes 10372
  2.7 17.0 %copy-start.3 = (s32[48]{0:T(128)S(1)}, s32[48]{0:T(128)}, u32[]{:S(2)}) copy-start(s32[48]{0:T(128)} %count_ref.1) | copy-start | bytes 580
  3.7 0.7 copy-start.9
  4.5 19.5 %collective-permute-start.2 = (bf16[2304,128]{1,0:T(8,128)(2,1)}, bf16[2304,128]{1,0:T(8,128)(2,1)}, u32[]{:S(2)}, u32[]{:S(2)}) collective-permute-start(bf16[2304,128]{1,0:T(8,128)(2,1)} %get-tuple-element.71.refs_0_), channel_id=1, source_target_pairs={{0,32},{16,48},{32,64},{48,80},{64,96},{80,112},{96,128},{112,144}... | collective-permute-start | bytes 1769480 | tf_op jit(solution)/shard_map/ppermute | solution.py:412
  6.4 16.9 %collective-permute-start.1 = (bf16[384,640]{1,0:T(8,128)(2,1)}, bf16[384,640]{1,0:T(8,128)(2,1)}, u32[]{:S(2)}, u32[]{:S(2)}) collective-permute-start(bf16[384,640]{1,0:T(8,128)(2,1)} %q_ref.6), channel_id=1, source_target_pairs={{0,16},{16,0},{32,48},{48,32},{64,80},{80,64},{96,112},{112,96},{1... | collective-permute-start | bytes 1474568 | tf_op jit(solution)/shard_map/ppermute | solution.py:392
  7.6 16.6 %collective-permute-start.14 = (bf16[2304,128]{1,0:T(8,128)(2,1)}, bf16[2304,128]{1,0:T(8,128)(2,1)}, u32[]{:S(2)}, u32[]{:S(2)}) collective-permute-start(bf16[2304,128]{1,0:T(8,128)(2,1)} %get-tuple-element.71.refs_0_), channel_id=1, source_target_pairs={{0,224},{16,240},{32,0},{48,16},{64,32},{80,48},{96,64},{112,80},{... | collective-permute-start | bytes 1769480 | tf_op jit(solution)/shard_map/ppermute | solution.py:412
  11.5 2.9 %copy-start = (bf16[640,5120]{1,0:T(8,128)(2,1)S(1)}, bf16[640,5120]{1,0:T(8,128)(2,1)}, u32[]{:S(2)}) copy-start(bf16[640,5120]{1,0:T(8,128)(2,1)} %weight_ref.1) | copy-start | bytes 19660804
  15.7 0.9 copy-start.4
  16.6 30.8 %collective-permute-start.5 = (bf16[640,640]{1,0:T(8,128)(2,1)}, bf16[640,640]{1,0:T(8,128)(2,1)S(1)}, u32[]{:S(2)}, u32[]{:S(2)}) collective-permute-start(bf16[640,640]{1,0:T(8,128)(2,1)} %get-tuple-element.77), channel_id=1, source_target_pairs={{0,12},{2,14},{4,0},{6,2},{8,4},{10,6},{12,8},{14,10},{1,13},{3,15... | collective-permute-start | bytes 2457608 | tf_op jit(solution)/shard_map/ppermute | solution.py:435
  19.6 27.8 %collective-permute-start.6 = (bf16[640,640]{1,0:T(8,128)(2,1)}, bf16[640,640]{1,0:T(8,128)(2,1)S(1)}, u32[]{:S(2)}, u32[]{:S(2)}) collective-permute-start(bf16[640,640]{1,0:T(8,128)(2,1)} %get-tuple-element.78), channel_id=1, source_target_pairs={{0,4},{2,6},{4,8},{6,10},{8,12},{10,14},{12,0},{14,2},{1,5},{3,7},... | collective-permute-start | bytes 2457608 | tf_op jit(solution)/shard_map/ppermute | solution.py:435
  23.3 13.6 %collective-permute-start.4 = (bf16[1536,128]{1,0:T(8,128)(2,1)}, bf16[1536,128]{1,0:T(8,128)(2,1)S(1)}, u32[]{:S(2)}, u32[]{:S(2)}) collective-permute-start(bf16[1536,128]{1,0:T(8,128)(2,1)} %copy-done.9), channel_id=1, source_target_pairs={{0,32},{16,48},{32,64},{48,80},{64,96},{80,112},{96,128},{112,144}... | collective-permute-start | bytes 1179656 | tf_op jit(solution)/shard_map/ppermute | solution.py:412
  23.9 23.5 %collective-permute-start.3 = (bf16[2304,128]{1,0:T(8,128)(2,1)}, bf16[2304,128]{1,0:T(8,128)(2,1)S(1)}, u32[]{:S(2)}, u32[]{:S(2)}) collective-permute-start(bf16[2304,128]{1,0:T(8,128)(2,1)} %collective-permute-done.2.refs_1_), channel_id=1, source_target_pairs={{0,32},{16,48},{32,64},{48,80},{64,96},{80,112},{96,128},{112,144}... | collective-permute-start | bytes 1769480 | tf_op jit(solution)/shard_map/ppermute | solution.py:412
  24.1 23.8 %collective-permute-start.15 = (bf16[2304,128]{1,0:T(8,128)(2,1)}, bf16[2304,128]{1,0:T(8,128)(2,1)S(1)}, u32[]{:S(2)}, u32[]{:S(2)}) collective-permute-start(bf16[2304,128]{1,0:T(8,128)(2,1)} %collective-permute-done.14.refs_7_), channel_id=1, source_target_pairs={{0,224},{16,240},{32,0},{48,16},{64,32},{80,48},{96,64},{112,80},{... | collective-permute-start | bytes 1769480 | tf_op jit(solution)/shard_map/ppermute | solution.py:412
  36.8 11.1 %collective-permute-start.16 = (bf16[1536,128]{1,0:T(8,128)(2,1)}, bf16[1536,128]{1,0:T(8,128)(2,1)S(1)}, u32[]{:S(2)}, u32[]{:S(2)}) collective-permute-start(bf16[1536,128]{1,0:T(8,128)(2,1)} %copy-done.9), channel_id=1, source_target_pairs={{0,224},{16,240},{32,0},{48,16},{64,32},{80,48},{96,64},{112,80},{... | collective-permute-start | bytes 1179656 | tf_op jit(solution)/shard_map/ppermute | solution.py:412
  47.5 14.5 %collective-permute-start.10 = (bf16[2304,128]{1,0:T(8,128)(2,1)S(1)}, bf16[2304,128]{1,0:T(8,128)(2,1)S(1)}, u32[]{:S(2)}, u32[]{:S(2)}) collective-permute-start(bf16[2304,128]{1,0:T(8,128)(2,1)S(1)} %collective-permute-done.3.refs_2_), channel_id=1, source_target_pairs={{0,32},{16,48},{32,64},{48,80},{64,96},{80,112},{96,128},{112,144}... | collective-permute-start | bytes 1769480 | tf_op jit(solution)/shard_map/ppermute | solution.py:412
  48.0 22.5 %collective-permute-start.18 = (bf16[2304,128]{1,0:T(8,128)(2,1)S(1)}, bf16[2304,128]{1,0:T(8,128)(2,1)S(1)}, u32[]{:S(2)}, u32[]{:S(2)}) collective-permute-start(bf16[2304,128]{1,0:T(8,128)(2,1)S(1)} %collective-permute-done.15.refs_6_), channel_id=1, source_target_pairs={{0,224},{16,240},{32,0},{48,16},{64,32},{80,48},{96,64},{112,80},{... | collective-permute-start | bytes 1769480 | tf_op jit(solution)/shard_map/ppermute | solution.py:412
  51.6 22.6 %collective-permute-start = (bf16[640,640]{1,0:T(8,128)(2,1)}, bf16[640,640]{1,0:T(8,128)(2,1)S(1)}, u32[]{:S(2)}, u32[]{:S(2)}) collective-permute-start(bf16[640,640]{1,0:T(8,128)(2,1)} %copy-done.4), channel_id=1, source_target_pairs={{0,8},{2,10},{4,12},{6,14},{8,0},{10,2},{12,4},{14,6},{1,9},{3,11}... | collective-permute-start | bytes 2457608 | tf_op jit(solution)/shard_map/ppermute | solution.py:435
  54.8 15.7 %collective-permute-start.17 = (bf16[1536,128]{1,0:T(8,128)(2,1)S(1)}, bf16[1536,128]{1,0:T(8,128)(2,1)S(1)}, u32[]{:S(2)}, u32[]{:S(2)}) collective-permute-start(bf16[1536,128]{1,0:T(8,128)(2,1)S(1)} %collective-permute-done.16.refs_7_), channel_id=1, source_target_pairs={{0,224},{16,240},{32,0},{48,16},{64,32},{80,48},{96,64},{112,80},{... | collective-permute-start | bytes 1179656 | tf_op jit(solution)/shard_map/ppermute | solution.py:412
  62.0 22.0 %collective-permute-start.12 = (bf16[2304,128]{1,0:T(8,128)(2,1)S(1)}, bf16[2304,128]{1,0:T(8,128)(2,1)S(1)}, u32[]{:S(2)}, u32[]{:S(2)}) collective-permute-start(bf16[2304,128]{1,0:T(8,128)(2,1)S(1)} %collective-permute-done.10.refs_3_), channel_id=1, source_target_pairs={{0,32},{16,48},{32,64},{48,80},{64,96},{80,112},{96,128},{112,144}... | collective-permute-start | bytes 1769480 | tf_op jit(solution)/shard_map/ppermute | solution.py:412
  70.5 9.0 %collective-permute-start.19 = (bf16[1536,128]{1,0:T(8,128)(2,1)S(1)}, bf16[1536,128]{1,0:T(8,128)(2,1)S(1)}, u32[]{:S(2)}, u32[]{:S(2)}) collective-permute-start(bf16[1536,128]{1,0:T(8,128)(2,1)S(1)} %collective-permute-done.17.refs_6_), channel_id=1, source_target_pairs={{0,224},{16,240},{32,0},{48,16},{64,32},{80,48},{96,64},{112,80},{... | collective-permute-start | bytes 1179656 | tf_op jit(solution)/shard_map/ppermute | solution.py:412
  74.2 9.8 %collective-permute-start.11 = (bf16[1536,128]{1,0:T(8,128)(2,1)S(1)}, bf16[1536,128]{1,0:T(8,128)(2,1)S(1)}, u32[]{:S(2)}, u32[]{:S(2)}) collective-permute-start(bf16[1536,128]{1,0:T(8,128)(2,1)S(1)} %collective-permute-done.4.refs_1_), channel_id=1, source_target_pairs={{0,32},{16,48},{32,64},{48,80},{64,96},{80,112},{96,128},{112,144}... | collective-permute-start | bytes 1179656 | tf_op jit(solution)/shard_map/ppermute | solution.py:412
  74.2 25.2 %collective-permute-start.8 = (bf16[640,640]{1,0:T(8,128)(2,1)S(1)}, bf16[640,640]{1,0:T(8,128)(2,1)S(1)}, u32[]{:S(2)}, u32[]{:S(2)}) collective-permute-start(bf16[640,640]{1,0:T(8,128)(2,1)S(1)} %collective-permute-done.refs_8_.refs_9_), channel_id=1, source_target_pairs={{0,1},{1,0},{2,3},{3,2},{4,5},{5,4},{6,7},{7,6},{8,9},{9,8},{10,11... | collective-permute-start | bytes 2457608 | tf_op jit(solution)/shard_map/ppermute | solution.py:449
  74.2 25.3 %collective-permute-start.7 = (bf16[640,640]{1,0:T(8,128)(2,1)S(1)}, bf16[640,640]{1,0:T(8,128)(2,1)S(1)}, u32[]{:S(2)}, u32[]{:S(2)}) collective-permute-start(bf16[640,640]{1,0:T(8,128)(2,1)S(1)} %collective-permute-done.5.refs_6_.refs_7_), channel_id=1, source_target_pairs={{0,1},{1,0},{2,3},{3,2},{4,5},{5,4},{6,7},{7,6},{8,9},{9,8},{10,11... | collective-permute-start | bytes 2457608 | tf_op jit(solution)/shard_map/ppermute | solution.py:449
  79.5 20.0 %collective-permute-start.9 = (bf16[640,640]{1,0:T(8,128)(2,1)S(1)}, bf16[640,640]{1,0:T(8,128)(2,1)S(1)}, u32[]{:S(2)}, u32[]{:S(2)}) collective-permute-start(bf16[640,640]{1,0:T(8,128)(2,1)S(1)} %collective-permute-done.6.refs_10_.refs_11_), channel_id=1, source_target_pairs={{0,1},{1,0},{2,3},{3,2},{4,5},{5,4},{6,7},{7,6},{8,9},{9,8},{10,11... | collective-permute-start | bytes 2457608 | tf_op jit(solution)/shard_map/ppermute | solution.py:449
  84.0 15.5 %collective-permute-start.20 = (bf16[1536,128]{1,0:T(8,128)(2,1)S(1)}, bf16[1536,128]{1,0:T(8,128)(2,1)S(1)}, u32[]{:S(2)}, u32[]{:S(2)}) collective-permute-start(bf16[1536,128]{1,0:T(8,128)(2,1)S(1)} %collective-permute-done.19.refs_5_), channel_id=1, source_target_pairs={{0,224},{16,240},{32,0},{48,16},{64,32},{80,48},{96,64},{112,80},{... | collective-permute-start | bytes 1179656 | tf_op jit(solution)/shard_map/ppermute | solution.py:412
  84.0 15.5 %collective-permute-start.13 = (bf16[1536,128]{1,0:T(8,128)(2,1)S(1)}, bf16[1536,128]{1,0:T(8,128)(2,1)S(1)}, u32[]{:S(2)}, u32[]{:S(2)}) collective-permute-start(bf16[1536,128]{1,0:T(8,128)(2,1)S(1)} %collective-permute-done.11.refs_2_), channel_id=1, source_target_pairs={{0,32},{16,48},{32,64},{48,80},{64,96},{80,112},{96,128},{112,144}... | collective-permute-start | bytes 1179656 | tf_op jit(solution)/shard_map/ppermute | solution.py:412
  86.0 1.0 copy-start.7
  87.0 12.5 %copy-start.10 = (bf16[1536,128]{1,0:T(8,128)(2,1)S(1)}, bf16[1536,128]{1,0:T(8,128)(2,1)}, u32[]{:S(2)}) copy-start(bf16[1536,128]{1,0:T(8,128)(2,1)} %copy-done.9) | copy-start | bytes 1179652
  99.4 14.8 %collective-permute-start.26 = (bf16[2304,128]{1,0:T(8,128)(2,1)S(1)}, bf16[2304,128]{1,0:T(8,128)(2,1)S(1)}, u32[]{:S(2)}, u32[]{:S(2)}) collective-permute-start(bf16[2304,128]{1,0:T(8,128)(2,1)S(1)} %get-tuple-element.123), channel_id=1, source_target_pairs={{0,16},{16,0},{32,48},{48,32},{64,80},{80,64},{96,112},{112,96},{1... | collective-permute-start | bytes 1769480 | tf_op jit(solution)/shard_map/ppermute | solution.py:392
  105.0 20.4 %collective-permute-start.22 = (bf16[768,128]{1,0:T(8,128)(2,1)S(1)}, bf16[768,128]{1,0:T(8,128)(2,1)S(1)}, u32[]{:S(2)}, u32[]{:S(2)}) collective-permute-start(bf16[768,128]{1,0:T(8,128)(2,1)S(1)} %get-tuple-element.112), channel_id=1, source_target_pairs={{0,16},{16,0},{32,48},{48,32},{64,80},{80,64},{96,112},{112,96},{1... | collective-permute-start | bytes 589832 | tf_op jit(solution)/shard_map/ppermute | solution.py:392
  114.6 20.4 %collective-permute-start.27 = (bf16[384,384]{1,0:T(8,128)(2,1)S(1)}, bf16[384,384]{1,0:T(8,128)(2,1)S(1)}, u32[]{:S(2)}, u32[]{:S(2)}) collective-permute-start(bf16[384,384]{1,0:T(8,128)(2,1)S(1)} %merge.3.refs_0_), channel_id=1, source_target_pairs={{0,12},{2,14},{4,0},{6,2},{8,4},{10,6},{12,8},{14,10},{1,13},{3,15... | collective-permute-start | bytes 884744 | tf_op jit(solution)/shard_map/ppermute | solution.py:423
  117.7 17.3 %collective-permute-start.28 = (bf16[384,384]{1,0:T(8,128)(2,1)S(1)}, bf16[384,384]{1,0:T(8,128)(2,1)S(1)}, u32[]{:S(2)}, u32[]{:S(2)}) collective-permute-start(bf16[384,384]{1,0:T(8,128)(2,1)S(1)} %merge.3.refs_0_), channel_id=1, source_target_pairs={{0,8},{2,10},{4,12},{6,14},{8,0},{10,2},{12,4},{14,6},{1,9},{3,11}... | collective-permute-start | bytes 884744 | tf_op jit(solution)/shard_map/ppermute | solution.py:423
  118.3 16.7 %collective-permute-start.29 = (bf16[384,384]{1,0:T(8,128)(2,1)S(1)}, bf16[384,384]{1,0:T(8,128)(2,1)S(1)}, u32[]{:S(2)}, u32[]{:S(2)}) collective-permute-start(bf16[384,384]{1,0:T(8,128)(2,1)S(1)} %merge.3.refs_0_), channel_id=1, source_target_pairs={{0,4},{2,6},{4,8},{6,10},{8,12},{10,14},{12,0},{14,2},{1,5},{3,7},... | collective-permute-start | bytes 884744 | tf_op jit(solution)/shard_map/ppermute | solution.py:423
  124.9 5.8 %collective-permute-start.21 = (bf16[768,128]{1,0:T(8,128)(2,1)S(1)}, bf16[768,128]{1,0:T(8,128)(2,1)S(1)}, u32[]{:S(2)}, u32[]{:S(2)}) collective-permute-start(bf16[768,128]{1,0:T(8,128)(2,1)S(1)} %get-tuple-element.100), channel_id=1, source_target_pairs={{0,16},{16,0},{32,48},{48,32},{64,80},{80,64},{96,112},{112,96},{1... | collective-permute-start | bytes 589832 | tf_op jit(solution)/shard_map/ppermute | solution.py:392
  130.9 7.7 %collective-permute-start.23 = (bf16[384,256]{1,0:T(8,128)(2,1)S(1)}, bf16[384,256]{1,0:T(8,128)(2,1)S(1)}, u32[]{:S(2)}, u32[]{:S(2)}) collective-permute-start(bf16[384,256]{1,0:T(8,128)(2,1)S(1)} %merge.2.refs_1_), channel_id=1, source_target_pairs={{0,12},{2,14},{4,0},{6,2},{8,4},{10,6},{12,8},{14,10},{1,13},{3,15... | collective-permute-start | bytes 589832 | tf_op jit(solution)/shard_map/ppermute | solution.py:423
  133.3 7.3 %collective-permute-start.24 = (bf16[384,256]{1,0:T(8,128)(2,1)S(1)}, bf16[384,256]{1,0:T(8,128)(2,1)S(1)}, u32[]{:S(2)}, u32[]{:S(2)}) collective-permute-start(bf16[384,256]{1,0:T(8,128)(2,1)S(1)} %merge.2.refs_1_), channel_id=1, source_target_pairs={{0,8},{2,10},{4,12},{6,14},{8,0},{10,2},{12,4},{14,6},{1,9},{3,11}... | collective-permute-start | bytes 589832 | tf_op jit(solution)/shard_map/ppermute | solution.py:423
  135.0 7.6 %collective-permute-start.25 = (bf16[384,256]{1,0:T(8,128)(2,1)S(1)}, bf16[384,256]{1,0:T(8,128)(2,1)S(1)}, u32[]{:S(2)}, u32[]{:S(2)}) collective-permute-start(bf16[384,256]{1,0:T(8,128)(2,1)S(1)} %merge.2.refs_1_), channel_id=1, source_target_pairs={{0,4},{2,6},{4,8},{6,10},{8,12},{10,14},{12,0},{14,2},{1,5},{3,7},... | collective-permute-start | bytes 589832 | tf_op jit(solution)/shard_map/ppermute | solution.py:423
  137.4 7.6 %copy-start.5 = (bf16[512,640]{1,0:T(8,128)(2,1)S(1)}, bf16[512,640]{1,0:T(8,128)(2,1)}, u32[]{:S(2)}) copy-start(bf16[512,640]{1,0:T(8,128)(2,1)} %k_ref.3) | copy-start | bytes 1966084
  137.4 7.6 %copy-start.6 = (bf16[512,640]{1,0:T(8,128)(2,1)S(1)}, bf16[512,640]{1,0:T(8,128)(2,1)}, u32[]{:S(2)}) copy-start(bf16[512,640]{1,0:T(8,128)(2,1)} %v_ref.3) | copy-start | bytes 1966084
  137.4 7.6 %copy-start.8 = (bf16[384,640]{1,0:T(8,128)(2,1)S(1)}, bf16[384,640]{1,0:T(8,128)(2,1)}, u32[]{:S(2)}) copy-start(bf16[384,640]{1,0:T(8,128)(2,1)} %q_ref.7) | copy-start | bytes 1474564
  144.1 10.4 %collective-permute-start.30 = (bf16[384,640]{1,0:T(8,128)(2,1)S(1)}, bf16[384,640]{1,0:T(8,128)(2,1)S(1)}, u32[]{:S(2)}, u32[]{:S(2)}) collective-permute-start(bf16[384,640]{1,0:T(8,128)(2,1)S(1)} %get-tuple-element.125), channel_id=1, source_target_pairs={{0,2},{2,0},{4,6},{6,4},{8,10},{10,8},{12,14},{14,12},{1,3},{3,1},... | collective-permute-start | bytes 1474568 | tf_op jit(solution)/shard_map/ppermute | solution.py:458

commit v4 on v3

--- a/solution.py
+++ b/solution.py
@@ -72,21 +72,30 @@
     )(seq, block_list, block_count)
 
 
-def pack_kernel(k_ref, v_ref, *outs):
+def pack_kernel(k_ref, v_ref, *refs):
+    outs, sems = refs[:-1], refs[-1]
+    copies = []
     for heads, out in zip(GROUPS, outs):
         for n, head in enumerate(heads):
-            columns = slice(head * DH, (head + 1) * DH)
-            out[2 * n * ROWS : (2 * n + 1) * ROWS, :] = k_ref[:, columns]
-            out[(2 * n + 1) * ROWS : (2 * n + 2) * ROWS, :] = v_ref[:, columns]
+            for m, ref in enumerate((k_ref, v_ref)):
+                source = ref.at[:, head * DH : (head + 1) * DH]
+                target = out.at[(2 * n + m) * ROWS : (2 * n + m + 1) * ROWS, :]
+                copies.append(pltpu.make_async_copy(source, target, sems.at[len(copies)]))
+    for copy in copies:
+        copy.start()
+    for copy in copies:
+        copy.wait()
 
 
 def pack(keys, values):
+    stay = pl.BlockSpec(memory_space=pltpu.HBM)
     return pl.pallas_call(
         pack_kernel,
         out_shape=[jax.ShapeDtypeStruct((2 * ROWS * len(heads), DH), jnp.bfloat16) for heads in GROUPS],
-        in_specs=[VMEM, VMEM],
-        out_specs=[VMEM] * len(GROUPS),
-        compiler_params=pltpu.CompilerParams(vmem_limit_bytes=6 << 20),
+        in_specs=[stay] * 2,
+        out_specs=[stay] * len(GROUPS),
+        scratch_shapes=[pltpu.SemaphoreType.DMA((2 * sum(len(heads) for heads in GROUPS),))],
+        compiler_params=pltpu.CompilerParams(vmem_limit_bytes=1 << 20),
         cost_estimate=pl.CostEstimate(flops=0, bytes_accessed=4 * keys.size * 2, transcendentals=0),
         name="pack",
     )(keys, values)
@@ -427,30 +436,31 @@
         hop(-1, group, 1)
     queries_other = to_other(queries)
     early = list(plan(n_seq, seq, block_list, block_count))
+    early[0], queries_other = lax.optimization_barrier((early[0], queries_other))
+    hop(1, 0, 2, early)
+    out_weight, held[0][1] = lax.optimization_barrier((out_weight, held[0][1]))
     tiles = list(tile(lax.div(head, 2), pair, out_weight, n_y))
-    early[0], tiles[0], queries_other = lax.optimization_barrier((early[0], tiles[0], queries_other))
-    hop(1, 0, 2, early)
     hop(-1, 0, 2)
     blocks, counts, near = early
     tiles[1:n_y] = [lax.ppermute(tiles[dy], "head", y_shift(dy)) for dy in range(1, n_y)][::-1]
+    hop(1, 0, 3)
+    hop(-1, 0, 3)
     one_away = [(tiles[1], tiles[n_y - 1])]
-    hop(1, 0, 3, one_away)
+    hop(1, 0, 4, one_away)
     tiles[1], tiles[n_y - 1] = one_away[0]
-    hop(-1, 0, 3)
-    hop(1, 0, 4)
     hop(-1, 1, 2)
     hop(1, 1, 2)
     hop(-1, 1, 3)
     hop(1, 1, 3)
     hop(-1, 1, 4)
     near, tiles[2] = lax.optimization_barrier((near, tiles[2]))
+    most = partial(0, 0, 3)
+    most[1], *tiles[1:n_y] = lax.optimization_barrier((most[1], *tiles[1:n_y]))
     weights = [tiles[0], tiles[n_y]]
     for mine in tiles[1:n_y]:
         weights += [mine, lax.ppermute(mine, "pair", [(0, 1), (1, 0)])]
-    most = partial(0, 0, 3)
-    near, *weights = lax.optimization_barrier((near, *weights))
     one, two = partial(1, 0, 1), partial(1, 1, 2)
-    most[0], two[2] = lax.optimization_barrier((most[0], two[2]))
+    most[0], one[2], two[2] = lax.optimization_barrier((most[0], one[2], two[2]))
     before = project(GROUPS[0][0], along_y(join(most)), weights)
     rest = join(one, two)
     keep_block = (lax.rem(head, 2) != pair).astype(jnp.int32)

time: 155 us -> 169 us (1.090); the launches traced: 155 us -> 167 us
  waiting for transfers between devices: 68 us -> 82.4 us
  Pallas kernels: 37.9 us -> 32.3 us
  starting transfers between devices: 39.9 us -> 43.6 us
    ppermute x6, waiting for transfers between devices: 5.14 us -> 15.7 us  [along_y(): lax.ppermute(array, 'head', y_shift(-dy))]
    pallas_call x3, Pallas kernels: 23.4 us -> 18.8 us  [attend(): pl.pallas_call(functools.partial(attend_kernel, heads, first, planes), ou...]
    ppermute x1, waiting for transfers between devices: 5.38 us -> 9.62 us  [body(): got = lax.ppermute(send, 'head', [(g, g ^ 1) for g in range(n_head)])]
    ppermute x4, waiting for transfers between devices: 12.4 us -> 8.81 us  [to_other(): return lax.ppermute(array, 'seq', swap)]
    ppermute x14, waiting for transfers between devices: 45.1 us -> 48.3 us  [hop(): held[group][place] = lax.ppermute(array, 'seq', z_shift(way))]
    ppermute x4, starting transfers between devices: 3.89 us -> 6.94 us  [to_other(): return lax.ppermute(array, 'seq', swap)]
    unnamed x25 -> x21, local copies, waits for them, and re-layouts: 7.69 us -> 7.16 us
  transfers between devices with their start and end apart: 31 -> 31, of which waited for: 15 -> 15; matrix products, arithmetic and copies ran while one was open for 0% -> 0% of each run, Pallas kernels for 23% -> 18%
where the time goes in v4:
time: 169 us; the launch traced here: 167 us
  waiting for transfers between devices  82.4 us (49%)
  starting transfers between devices  43.6 us (26%)
  Pallas kernels  32.3 us (19%)
  local copies, waits for them, and re-layouts  7.16 us (4%)
    ppermute x14, waiting for transfers between devices, hop(): held[group][place] = lax.ppermute(array, 'seq', z_shift(way))  48.3 us
    ppermute x14, starting transfers between devices, hop(): held[group][place] = lax.ppermute(array, 'seq', z_shift(way))  19.5 us
    pallas_call x3, Pallas kernels, attend(): pl.pallas_call(functools.partial(attend_kernel, heads, first, planes), ou...  18.8 us
    ppermute x6, waiting for transfers between devices, along_y(): lax.ppermute(array, 'head', y_shift(-dy))  15.7 us
    ppermute x1, waiting for transfers between devices, body(): got = lax.ppermute(send, 'head', [(g, g ^ 1) for g in range(n_head)])  9.62 us
    ppermute x6, starting transfers between devices, along_y(): lax.ppermute(array, 'head', y_shift(-dy))  9.52 us
    ppermute x4, waiting for transfers between devices, to_other(): return lax.ppermute(array, 'seq', swap)  8.81 us
    unnamed x21, local copies, waits for them, and re-layouts  7.16 us
  transfers between devices with their start and end apart: 31, of which 15 were waited for; matrix products, arithmetic and copies ran while one was open for 0% of the time, Pallas kernels for 18%

profile of v4, /device:TPU:4, one launch (start us, length us, event | category | flops | bytes accessed | tf_op | source)
XLA Modules:
  0.0 167.2 jit_solution(10761452441401954980)
XLA Ops:
  0.6 1.0 copy-done.1
  1.7 1.0 copy-done.2
  2.7 0.9 pack.1
  3.6 2.0 %collective-permute-start = (bf16[2304,128]{1,0:T(8,128)(2,1)S(1)}, bf16[2304,128]{1,0:T(8,128)(2,1)S(1)}, u32[]{:S(2)}, u32[]{:S(2)}) collective-permute-start(bf16[2304,128]{1,0:T(8,128)(2,1)S(1)} %get-tuple-element.62.refs_0_), channel_id=1, source_target_pairs={{0,32},{16,48},{32,64},{48,80},{64,96},{80,112},{96,128},{112,144}... | collective-permute-start | bytes 1769480 | tf_op jit(solution)/shard_map/ppermute | solution.py:421
  5.6 1.2 collective-permute-start.2
  6.8 4.0 %collective-permute-start.11 = (bf16[2304,128]{1,0:T(8,128)(2,1)S(1)}, bf16[2304,128]{1,0:T(8,128)(2,1)S(1)}, u32[]{:S(2)}, u32[]{:S(2)}) collective-permute-start(bf16[2304,128]{1,0:T(8,128)(2,1)S(1)} %get-tuple-element.62.refs_0_), channel_id=1, source_target_pairs={{0,224},{16,240},{32,0},{48,16},{64,32},{80,48},{96,64},{112,80},{... | collective-permute-start | bytes 1769480 | tf_op jit(solution)/shard_map/ppermute | solution.py:421
  10.9 0.8 copy.11.list_ref
  11.7 0.7 copy-done.3
  12.3 3.4 %plan.1 = (s32[6,13]{1,0:T(8,128)S(1)}, s32[6]{0:T(128)S(1)}, s32[8]{0:T(128)S(1)}) custom-call(s32[1]{0:T(128)} %bitcast.2.seq_ref, s32[48,18]{1,0:T(8,128)S(1)} %copy.11.list_ref, s32[48]{0:T(128)S(1)} %copy-done.3), custom_call_target="tpu_custom_call" | custom-call | flops 1000 | bytes 8000 | tf_op jit(solution)/shard_map/plan/pallas_call | solution.py:60
  15.7 2.9 %collective-permute-done.2.q_other_ref = bf16[384,640]{1,0:T(8,128)(2,1)S(1)} collective-permute-done((bf16[384,640]{1,0:T(8,128)(2,1)}, bf16[384,640]{1,0:T(8,128)(2,1)S(1)}, u32[]{:S(2)}, u32[]{:S(2)}) %collective-permute-start.2) | collective-permute-done | bytes 491552 | tf_op jit(solution)/shard_map/ppermute | solution.py:401
  18.5 0.8 copy-done.8
  19.3 3.6 %collective-permute-done.refs_1_ = bf16[2304,128]{1,0:T(8,128)(2,1)S(1)} collective-permute-done((bf16[2304,128]{1,0:T(8,128)(2,1)S(1)}, bf16[2304,128]{1,0:T(8,128)(2,1)S(1)}, u32[]{:S(2)}, u32[]{:S(2)}) %collective-permute-start) | collective-permute-done | bytes 589856 | tf_op jit(solution)/shard_map/ppermute | solution.py:421
  23.2 3.7 %collective-permute-start.12 = (bf16[2304,128]{1,0:T(8,128)(2,1)S(1)}, bf16[2304,128]{1,0:T(8,128)(2,1)S(1)}, u32[]{:S(2)}, u32[]{:S(2)}) collective-permute-start(bf16[2304,128]{1,0:T(8,128)(2,1)S(1)} %collective-permute-done.11.refs_7_), channel_id=1, source_target_pairs={{0,224},{16,240},{32,0},{48,16},{64,32},{80,48},{96,64},{112,80},{... | collective-permute-start | bytes 1769480 | tf_op jit(solution)/shard_map/ppermute | solution.py:421
  26.9 2.9 %copy-done = bf16[640,5120]{1,0:T(8,128)(2,1)S(1)} copy-done((bf16[640,5120]{1,0:T(8,128)(2,1)S(1)}, bf16[640,5120]{1,0:T(8,128)(2,1)}, u32[]{:S(2)}) %copy-start) | copy-done | bytes 6553624
  29.7 0.6 tile.1
  30.3 3.1 %collective-permute-start.7 = (bf16[640,640]{1,0:T(8,128)(2,1)S(1)}, bf16[640,640]{1,0:T(8,128)(2,1)S(1)}, u32[]{:S(2)}, u32[]{:S(2)}) collective-permute-start(bf16[640,640]{1,0:T(8,128)(2,1)S(1)} %get-tuple-element.79), channel_id=1, source_target_pairs={{0,12},{2,14},{4,0},{6,2},{8,4},{10,6},{12,8},{14,10},{1,13},{3,15... | collective-permute-start | bytes 2457608 | tf_op jit(solution)/shard_map/ppermute | solution.py:445
  33.4 13.7 %collective-permute-done.4.refs_1_ = bf16[1536,128]{1,0:T(8,128)(2,1)} collective-permute-done((bf16[1536,128]{1,0:T(8,128)(2,1)}, bf16[1536,128]{1,0:T(8,128)(2,1)}, u32[]{:S(2)}, u32[]{:S(2)}) %collective-permute-start.4) | collective-permute-done | bytes 393248 | tf_op jit(solution)/shard_map/ppermute | solution.py:421
  47.4 1.8 %collective-permute-start.5 = (bf16[2304,128]{1,0:T(8,128)(2,1)S(1)}, bf16[2304,128]{1,0:T(8,128)(2,1)S(1)}, u32[]{:S(2)}, u32[]{:S(2)}) collective-permute-start(bf16[2304,128]{1,0:T(8,128)(2,1)S(1)} %collective-permute-done.3.refs_2_), channel_id=1, source_target_pairs={{0,32},{16,48},{32,64},{48,80},{64,96},{80,112},{96,128},{112,144}... | collective-permute-start | bytes 1769480 | tf_op jit(solution)/shard_map/ppermute | solution.py:421
  49.2 7.6 %collective-permute-done.13.refs_7_ = bf16[1536,128]{1,0:T(8,128)(2,1)S(1)} collective-permute-done((bf16[1536,128]{1,0:T(8,128)(2,1)}, bf16[1536,128]{1,0:T(8,128)(2,1)S(1)}, u32[]{:S(2)}, u32[]{:S(2)}) %collective-permute-start.13) | collective-permute-done | bytes 393248 | tf_op jit(solution)/shard_map/ppermute | solution.py:421
  56.7 1.5 collective-permute-start.15
  58.2 3.2 %collective-permute-start.1 = (bf16[640,640]{1,0:T(8,128)(2,1)S(1)}, bf16[640,640]{1,0:T(8,128)(2,1)S(1)}, u32[]{:S(2)}, u32[]{:S(2)}) collective-permute-start(bf16[640,640]{1,0:T(8,128)(2,1)S(1)} %get-tuple-element.65), channel_id=1, source_target_pairs={{0,8},{2,10},{4,12},{6,14},{8,0},{10,2},{12,4},{14,6},{1,9},{3,11}... | collective-permute-start | bytes 2457608 | tf_op jit(solution)/shard_map/ppermute | solution.py:445
  61.4 0.5 collective-permute-done.5.refs_3_
  62.0 2.0 %collective-permute-start.9 = (bf16[2304,128]{1,0:T(8,128)(2,1)S(1)}, bf16[2304,128]{1,0:T(8,128)(2,1)S(1)}, u32[]{:S(2)}, u32[]{:S(2)}) collective-permute-start(bf16[2304,128]{1,0:T(8,128)(2,1)S(1)} %collective-permute-done.5.refs_3_), channel_id=1, source_target_pairs={{0,32},{16,48},{32,64},{48,80},{64,96},{80,112},{96,128},{112,144}... | collective-permute-start | bytes 1769480 | tf_op jit(solution)/shard_map/ppermute | solution.py:421
  64.0 14.7 %collective-permute-done.14.refs_6_ = bf16[1536,128]{1,0:T(8,128)(2,1)S(1)} collective-permute-done((bf16[1536,128]{1,0:T(8,128)(2,1)S(1)}, bf16[1536,128]{1,0:T(8,128)(2,1)S(1)}, u32[]{:S(2)}, u32[]{:S(2)}) %collective-permute-start.14) | collective-permute-done | bytes 393248 | tf_op jit(solution)/shard_map/ppermute | solution.py:421
  78.7 2.0 %collective-permute-start.16 = (bf16[1536,128]{1,0:T(8,128)(2,1)S(1)}, bf16[1536,128]{1,0:T(8,128)(2,1)S(1)}, u32[]{:S(2)}, u32[]{:S(2)}) collective-permute-start(bf16[1536,128]{1,0:T(8,128)(2,1)S(1)} %collective-permute-done.14.refs_6_), channel_id=1, source_target_pairs={{0,224},{16,240},{32,0},{48,16},{64,32},{80,48},{96,64},{112,80},{... | collective-permute-start | bytes 1179656 | tf_op jit(solution)/shard_map/ppermute | solution.py:421
  80.7 7.7 %collective-permute-done.16.refs_5_ = bf16[1536,128]{1,0:T(8,128)(2,1)S(1)} collective-permute-done((bf16[1536,128]{1,0:T(8,128)(2,1)S(1)}, bf16[1536,128]{1,0:T(8,128)(2,1)S(1)}, u32[]{:S(2)}, u32[]{:S(2)}) %collective-permute-start.16) | collective-permute-done | bytes 393248 | tf_op jit(solution)/shard_map/ppermute | solution.py:421
  88.3 2.0 %collective-permute-start.17 = (bf16[1536,128]{1,0:T(8,128)(2,1)S(1)}, bf16[1536,128]{1,0:T(8,128)(2,1)S(1)}, u32[]{:S(2)}, u32[]{:S(2)}) collective-permute-start(bf16[1536,128]{1,0:T(8,128)(2,1)S(1)} %collective-permute-done.16.refs_5_), channel_id=1, source_target_pairs={{0,224},{16,240},{32,0},{48,16},{64,32},{80,48},{96,64},{112,80},{... | collective-permute-start | bytes 1179656 | tf_op jit(solution)/shard_map/ppermute | solution.py:421
  90.8 9.3 %attend.4 = (f32[1152,128]{1,0:T(8,128)S(1)}, f32[1152,128]{1,0:T(8,128)S(1)}, bf16[2304,128]{1,0:T(8,128)(2,1)S(1)}) custom-call(s32[1]{0:T(128)} %bitcast.2.seq_ref, s32[8]{0:T(128)S(1)} %get-tuple-element.66.near_ref, s32[6,13]{1,0:T(8,128)S(1)} %get-tuple-element.70.blocks_ref, s32[6]{0:T(128)S(1)} %get-tuple-element.71.count_ref, ...), custom_call_target="tpu_custom_call" | custom-call | flops 13589544960 | bytes 4718592 | tf_op jit(solution)/shard_map/attend/pallas_call | solution.py:235
  100.1 3.4 %collective-permute-start.26 = (bf16[2304,128]{1,0:T(8,128)(2,1)S(1)}, bf16[2304,128]{1,0:T(8,128)(2,1)S(1)}, u32[]{:S(2)}, u32[]{:S(2)}) collective-permute-start(bf16[2304,128]{1,0:T(8,128)(2,1)S(1)} %get-tuple-element.117), channel_id=1, source_target_pairs={{0,16},{16,0},{32,48},{48,32},{64,80},{80,64},{96,112},{112,96},{1... | collective-permute-start | bytes 1769480 | tf_op jit(solution)/shard_map/ppermute | solution.py:401
  104.0 4.8 %attend.5 = (f32[384,128]{1,0:T(8,128)S(1)}, f32[384,128]{1,0:T(8,128)S(1)}, bf16[768,128]{1,0:T(8,128)(2,1)S(1)}) custom-call(s32[1]{0:T(128)} %bitcast.2.seq_ref, s32[8]{0:T(128)S(1)} %get-tuple-element.66.near_ref, s32[6,13]{1,0:T(8,128)S(1)} %get-tuple-element.70.blocks_ref, s32[6]{0:T(128)S(1)} %get-tuple-element.71.count_ref, ...), custom_call_target="tpu_custom_call" | custom-call | flops 4529848320 | bytes 1572864 | tf_op jit(solution)/shard_map/attend/pallas_call | solution.py:235
  108.8 4.8 %attend.3 = (f32[384,128]{1,0:T(8,128)S(1)}, f32[384,128]{1,0:T(8,128)S(1)}, bf16[768,128]{1,0:T(8,128)(2,1)S(1)}) custom-call(s32[1]{0:T(128)} %bitcast.2.seq_ref, s32[8]{0:T(128)S(1)} %get-tuple-element.66.near_ref, s32[6,13]{1,0:T(8,128)S(1)} %get-tuple-element.70.blocks_ref, s32[6]{0:T(128)S(1)} %get-tuple-element.71.count_ref, ...), custom_call_target="tpu_custom_call" | custom-call | flops 4529848320 | bytes 1572864 | tf_op jit(solution)/shard_map/attend/pallas_call | solution.py:235
  113.6 2.0 %collective-permute-start.18 = (bf16[768,128]{1,0:T(8,128)(2,1)S(1)}, bf16[768,128]{1,0:T(8,128)(2,1)S(1)}, u32[]{:S(2)}, u32[]{:S(2)}) collective-permute-start(bf16[768,128]{1,0:T(8,128)(2,1)S(1)} %get-tuple-element.102), channel_id=1, source_target_pairs={{0,16},{16,0},{32,48},{48,32},{64,80},{80,64},{96,112},{112,96},{1... | collective-permute-start | bytes 589832 | tf_op jit(solution)/shard_map/ppermute | solution.py:401
  116.2 5.1 %collective-permute-done.18.refs_2_ = bf16[768,128]{1,0:T(8,128)(2,1)S(1)} collective-permute-done((bf16[768,128]{1,0:T(8,128)(2,1)S(1)}, bf16[768,128]{1,0:T(8,128)(2,1)S(1)}, u32[]{:S(2)}, u32[]{:S(2)}) %collective-permute-start.18) | collective-permute-done | bytes 196640 | tf_op jit(solution)/shard_map/ppermute | solution.py:401
  121.3 3.0 %collective-permute-start.27 = (bf16[384,384]{1,0:T(8,128)(2,1)S(1)}, bf16[384,384]{1,0:T(8,128)(2,1)S(1)}, u32[]{:S(2)}, u32[]{:S(2)}) collective-permute-start(bf16[384,384]{1,0:T(8,128)(2,1)S(1)} %merge.3.refs_0_), channel_id=1, source_target_pairs={{0,12},{2,14},{4,0},{6,2},{8,4},{10,6},{12,8},{14,10},{1,13},{3,15... | collective-permute-start | bytes 884744 | tf_op jit(solution)/shard_map/ppermute | solution.py:432
  124.4 0.9 collective-permute-done.19.refs_5_
  125.2 3.2 %collective-permute-start.28 = (bf16[384,384]{1,0:T(8,128)(2,1)S(1)}, bf16[384,384]{1,0:T(8,128)(2,1)S(1)}, u32[]{:S(2)}, u32[]{:S(2)}) collective-permute-start(bf16[384,384]{1,0:T(8,128)(2,1)S(1)} %merge.3.refs_0_), channel_id=1, source_target_pairs={{0,8},{2,10},{4,12},{6,14},{8,0},{10,2},{12,4},{14,6},{1,9},{3,11}... | collective-permute-start | bytes 884744 | tf_op jit(solution)/shard_map/ppermute | solution.py:432
  128.4 0.7 collective-permute-start.29
  129.3 2.6 %collective-permute-start.20 = (bf16[384,256]{1,0:T(8,128)(2,1)S(1)}, bf16[384,256]{1,0:T(8,128)(2,1)S(1)}, u32[]{:S(2)}, u32[]{:S(2)}) collective-permute-start(bf16[384,256]{1,0:T(8,128)(2,1)S(1)} %merge.2.refs_1_), channel_id=1, source_target_pairs={{0,12},{2,14},{4,0},{6,2},{8,4},{10,6},{12,8},{14,10},{1,13},{3,15... | collective-permute-start | bytes 589832 | tf_op jit(solution)/shard_map/ppermute | solution.py:432
  132.0 5.9 %collective-permute-done.27.refs_1_ = bf16[384,384]{1,0:T(8,128)(2,1)S(1)} collective-permute-done((bf16[384,384]{1,0:T(8,128)(2,1)S(1)}, bf16[384,384]{1,0:T(8,128)(2,1)S(1)}, u32[]{:S(2)}, u32[]{:S(2)}) %collective-permute-start.27) | collective-permute-done | bytes 294944 | tf_op jit(solution)/shard_map/ppermute | solution.py:432
  137.9 5.1 %collective-permute-done.29.refs_3_ = bf16[384,384]{1,0:T(8,128)(2,1)S(1)} collective-permute-done((bf16[384,384]{1,0:T(8,128)(2,1)S(1)}, bf16[384,384]{1,0:T(8,128)(2,1)S(1)}, u32[]{:S(2)}, u32[]{:S(2)}) %collective-permute-start.29) | collective-permute-done | bytes 294944 | tf_op jit(solution)/shard_map/ppermute | solution.py:432
  143.0 2.4 %project.2.refs_13_ = f32[2,384,640]{2,1,0:T(8,128)S(1)} custom-call(bf16[384,384]{1,0:T(8,128)(2,1)S(1)} %merge.3.refs_0_, bf16[384,384]{1,0:T(8,128)(2,1)S(1)} %collective-permute-done.27.refs_1_, bf16[384,384]{1,0:T(8,128)(2,1)S(1)} %collective-permute-done.28.refs_2_, bf16[384,384]{1,0:T(8,128)(2,1)S(1)} %collective-permute-done.29.refs_3_, ...), custom_call_target="tpu_custom_call" | custom-call | flops 1509949440 | bytes 5111808 | tf_op jit(solution)/shard_map/project/pallas_call | solution.py:376
  145.5 1.7 %collective-permute-done.21.refs_3_ = bf16[384,256]{1,0:T(8,128)(2,1)S(1)} collective-permute-done((bf16[384,256]{1,0:T(8,128)(2,1)S(1)}, bf16[384,256]{1,0:T(8,128)(2,1)S(1)}, u32[]{:S(2)}, u32[]{:S(2)}) %collective-permute-start.21) | collective-permute-done | bytes 196640 | tf_op jit(solution)/shard_map/ppermute | solution.py:432
  147.2 2.9 %collective-permute-done.22.refs_4_ = bf16[384,256]{1,0:T(8,128)(2,1)S(1)} collective-permute-done((bf16[384,256]{1,0:T(8,128)(2,1)S(1)}, bf16[384,256]{1,0:T(8,128)(2,1)S(1)}, u32[]{:S(2)}, u32[]{:S(2)}) %collective-permute-start.22) | collective-permute-done | bytes 196640 | tf_op jit(solution)/shard_map/ppermute | solution.py:432
  150.1 1.5 project.3
  151.7 0.9 collective-permute-start.30
  152.6 4.1 %cross.1 = bf16[384,640]{1,0:T(8,128)(2,1)} custom-call(bf16[384,640]{1,0:T(8,128)(2,1)S(1)} %copy-done.7, bf16[512,640]{1,0:T(8,128)(2,1)S(1)} %copy-done.4, bf16[512,640]{1,0:T(8,128)(2,1)S(1)} %copy-done.5), custom_call_target="tpu_custom_call" | custom-call | flops 5033164800 | bytes 983040 | tf_op jit(solution)/shard_map/cross/pallas_call | solution.py:338
  156.7 9.6 %collective-permute-done.30 = bf16[384,640]{1,0:T(8,128)(2,1)S(1)} collective-permute-done((bf16[384,640]{1,0:T(8,128)(2,1)S(1)}, bf16[384,640]{1,0:T(8,128)(2,1)S(1)}, u32[]{:S(2)}, u32[]{:S(2)}) %collective-permute-start.30) | collective-permute-done | bytes 491552 | tf_op jit(solution)/shard_map/ppermute | solution.py:468
  166.3 0.9 add_convert_fusion
  (47 shorter events, 2.6 us)
Async XLA Ops:
  0.6 1.0 copy-start.1
  1.7 1.0 copy-start.2
  2.7 88.1 %copy-start.6 = (bf16[384,640]{1,0:T(8,128)(2,1)S(1)}, bf16[384,640]{1,0:T(8,128)(2,1)}, u32[]{:S(2)}) copy-start(bf16[384,640]{1,0:T(8,128)(2,1)} %q_ref.6) | copy-start | bytes 1474564
  3.6 19.3 %collective-permute-start = (bf16[2304,128]{1,0:T(8,128)(2,1)S(1)}, bf16[2304,128]{1,0:T(8,128)(2,1)S(1)}, u32[]{:S(2)}, u32[]{:S(2)}) collective-permute-start(bf16[2304,128]{1,0:T(8,128)(2,1)S(1)} %get-tuple-element.62.refs_0_), channel_id=1, source_target_pairs={{0,32},{16,48},{32,64},{48,80},{64,96},{80,112},{96,128},{112,144}... | collective-permute-start | bytes 1769480 | tf_op jit(solution)/shard_map/ppermute | solution.py:421
  5.6 12.9 %collective-permute-start.2 = (bf16[384,640]{1,0:T(8,128)(2,1)}, bf16[384,640]{1,0:T(8,128)(2,1)S(1)}, u32[]{:S(2)}, u32[]{:S(2)}) collective-permute-start(bf16[384,640]{1,0:T(8,128)(2,1)} %q_ref.6), channel_id=1, source_target_pairs={{0,16},{16,0},{32,48},{48,32},{64,80},{80,64},{96,112},{112,96},{1... | collective-permute-start | bytes 1474568 | tf_op jit(solution)/shard_map/ppermute | solution.py:401
  6.8 16.3 %collective-permute-start.11 = (bf16[2304,128]{1,0:T(8,128)(2,1)S(1)}, bf16[2304,128]{1,0:T(8,128)(2,1)S(1)}, u32[]{:S(2)}, u32[]{:S(2)}) collective-permute-start(bf16[2304,128]{1,0:T(8,128)(2,1)S(1)} %get-tuple-element.62.refs_0_), channel_id=1, source_target_pairs={{0,224},{16,240},{32,0},{48,16},{64,32},{80,48},{96,64},{112,80},{... | collective-permute-start | bytes 1769480 | tf_op jit(solution)/shard_map/ppermute | solution.py:421
  11.6 0.7 copy-start.3
  18.5 0.8 copy-start.8
  22.9 24.5 %collective-permute-start.3 = (bf16[2304,128]{1,0:T(8,128)(2,1)S(1)}, bf16[2304,128]{1,0:T(8,128)(2,1)S(1)}, u32[]{:S(2)}, u32[]{:S(2)}) collective-permute-start(bf16[2304,128]{1,0:T(8,128)(2,1)S(1)} %collective-permute-done.refs_1_), channel_id=1, source_target_pairs={{0,32},{16,48},{32,64},{48,80},{64,96},{80,112},{96,128},{112,144}... | collective-permute-start | bytes 1769480 | tf_op jit(solution)/shard_map/ppermute | solution.py:421
  22.9 24.3 %collective-permute-start.4 = (bf16[1536,128]{1,0:T(8,128)(2,1)}, bf16[1536,128]{1,0:T(8,128)(2,1)}, u32[]{:S(2)}, u32[]{:S(2)}) collective-permute-start(bf16[1536,128]{1,0:T(8,128)(2,1)} %get-tuple-element.73.refs_0_), channel_id=1, source_target_pairs={{0,32},{16,48},{32,64},{48,80},{64,96},{80,112},{96,128},{112,144}... | collective-permute-start | bytes 1179656 | tf_op jit(solution)/shard_map/ppermute | solution.py:421
  23.2 33.6 %collective-permute-start.12 = (bf16[2304,128]{1,0:T(8,128)(2,1)S(1)}, bf16[2304,128]{1,0:T(8,128)(2,1)S(1)}, u32[]{:S(2)}, u32[]{:S(2)}) collective-permute-start(bf16[2304,128]{1,0:T(8,128)(2,1)S(1)} %collective-permute-done.11.refs_7_), channel_id=1, source_target_pairs={{0,224},{16,240},{32,0},{48,16},{64,32},{80,48},{96,64},{112,80},{... | collective-permute-start | bytes 1769480 | tf_op jit(solution)/shard_map/ppermute | solution.py:421
  26.9 2.9 %copy-start = (bf16[640,5120]{1,0:T(8,128)(2,1)S(1)}, bf16[640,5120]{1,0:T(8,128)(2,1)}, u32[]{:S(2)}) copy-start(bf16[640,5120]{1,0:T(8,128)(2,1)} %weight_ref) | copy-start | bytes 19660804
  29.7 61.1 %copy-start.9 = (bf16[384,640]{1,0:T(8,128)(2,1)S(1)}, bf16[384,640]{1,0:T(8,128)(2,1)}, u32[]{:S(2)}) copy-start(bf16[384,640]{1,0:T(8,128)(2,1)} %copy-done.8) | copy-start | bytes 1474564
  30.3 31.6 %collective-permute-start.7 = (bf16[640,640]{1,0:T(8,128)(2,1)S(1)}, bf16[640,640]{1,0:T(8,128)(2,1)S(1)}, u32[]{:S(2)}, u32[]{:S(2)}) collective-permute-start(bf16[640,640]{1,0:T(8,128)(2,1)S(1)} %get-tuple-element.79), channel_id=1, source_target_pairs={{0,12},{2,14},{4,0},{6,2},{8,4},{10,6},{12,8},{14,10},{1,13},{3,15... | collective-permute-start | bytes 2457608 | tf_op jit(solution)/shard_map/ppermute | solution.py:445
  33.4 28.6 %collective-permute-start.8 = (bf16[640,640]{1,0:T(8,128)(2,1)S(1)}, bf16[640,640]{1,0:T(8,128)(2,1)S(1)}, u32[]{:S(2)}, u32[]{:S(2)}) collective-permute-start(bf16[640,640]{1,0:T(8,128)(2,1)S(1)} %get-tuple-element.80), channel_id=1, source_target_pairs={{0,4},{2,6},{4,8},{6,10},{8,12},{10,14},{12,0},{14,2},{1,5},{3,7},... | collective-permute-start | bytes 2457608 | tf_op jit(solution)/shard_map/ppermute | solution.py:445
  47.1 9.6 %collective-permute-start.13 = (bf16[1536,128]{1,0:T(8,128)(2,1)}, bf16[1536,128]{1,0:T(8,128)(2,1)S(1)}, u32[]{:S(2)}, u32[]{:S(2)}) collective-permute-start(bf16[1536,128]{1,0:T(8,128)(2,1)} %get-tuple-element.73.refs_0_), channel_id=1, source_target_pairs={{0,224},{16,240},{32,0},{48,16},{64,32},{80,48},{96,64},{112,80},{... | collective-permute-start | bytes 1179656 | tf_op jit(solution)/shard_map/ppermute | solution.py:421
  47.4 14.6 %collective-permute-start.5 = (bf16[2304,128]{1,0:T(8,128)(2,1)S(1)}, bf16[2304,128]{1,0:T(8,128)(2,1)S(1)}, u32[]{:S(2)}, u32[]{:S(2)}) collective-permute-start(bf16[2304,128]{1,0:T(8,128)(2,1)S(1)} %collective-permute-done.3.refs_2_), channel_id=1, source_target_pairs={{0,32},{16,48},{32,64},{48,80},{64,96},{80,112},{96,128},{112,144}... | collective-permute-start | bytes 1769480 | tf_op jit(solution)/shard_map/ppermute | solution.py:421
  56.7 21.9 %collective-permute-start.15 = (bf16[2304,128]{1,0:T(8,128)(2,1)S(1)}, bf16[2304,128]{1,0:T(8,128)(2,1)S(1)}, u32[]{:S(2)}, u32[]{:S(2)}) collective-permute-start(bf16[2304,128]{1,0:T(8,128)(2,1)S(1)} %collective-permute-done.12.refs_6_), channel_id=1, source_target_pairs={{0,224},{16,240},{32,0},{48,16},{64,32},{80,48},{96,64},{112,80},{... | collective-permute-start | bytes 1769480 | tf_op jit(solution)/shard_map/ppermute | solution.py:421
  58.2 22.5 %collective-permute-start.1 = (bf16[640,640]{1,0:T(8,128)(2,1)S(1)}, bf16[640,640]{1,0:T(8,128)(2,1)S(1)}, u32[]{:S(2)}, u32[]{:S(2)}) collective-permute-start(bf16[640,640]{1,0:T(8,128)(2,1)S(1)} %get-tuple-element.65), channel_id=1, source_target_pairs={{0,8},{2,10},{4,12},{6,14},{8,0},{10,2},{12,4},{14,6},{1,9},{3,11}... | collective-permute-start | bytes 2457608 | tf_op jit(solution)/shard_map/ppermute | solution.py:445
  62.0 16.7 %collective-permute-start.14 = (bf16[1536,128]{1,0:T(8,128)(2,1)S(1)}, bf16[1536,128]{1,0:T(8,128)(2,1)S(1)}, u32[]{:S(2)}, u32[]{:S(2)}) collective-permute-start(bf16[1536,128]{1,0:T(8,128)(2,1)S(1)} %collective-permute-done.13.refs_7_), channel_id=1, source_target_pairs={{0,224},{16,240},{32,0},{48,16},{64,32},{80,48},{96,64},{112,80},{... | collective-permute-start | bytes 1179656 | tf_op jit(solution)/shard_map/ppermute | solution.py:421
  62.0 28.8 %collective-permute-start.9 = (bf16[2304,128]{1,0:T(8,128)(2,1)S(1)}, bf16[2304,128]{1,0:T(8,128)(2,1)S(1)}, u32[]{:S(2)}, u32[]{:S(2)}) collective-permute-start(bf16[2304,128]{1,0:T(8,128)(2,1)S(1)} %collective-permute-done.5.refs_3_), channel_id=1, source_target_pairs={{0,32},{16,48},{32,64},{48,80},{64,96},{80,112},{96,128},{112,144}... | collective-permute-start | bytes 1769480 | tf_op jit(solution)/shard_map/ppermute | solution.py:421
  78.7 9.7 %collective-permute-start.16 = (bf16[1536,128]{1,0:T(8,128)(2,1)S(1)}, bf16[1536,128]{1,0:T(8,128)(2,1)S(1)}, u32[]{:S(2)}, u32[]{:S(2)}) collective-permute-start(bf16[1536,128]{1,0:T(8,128)(2,1)S(1)} %collective-permute-done.14.refs_6_), channel_id=1, source_target_pairs={{0,224},{16,240},{32,0},{48,16},{64,32},{80,48},{96,64},{112,80},{... | collective-permute-start | bytes 1179656 | tf_op jit(solution)/shard_map/ppermute | solution.py:421
  80.6 10.2 %collective-permute-start.6 = (bf16[1536,128]{1,0:T(8,128)(2,1)}, bf16[1536,128]{1,0:T(8,128)(2,1)S(1)}, u32[]{:S(2)}, u32[]{:S(2)}) collective-permute-start(bf16[1536,128]{1,0:T(8,128)(2,1)} %collective-permute-done.4.refs_1_), channel_id=1, source_target_pairs={{0,32},{16,48},{32,64},{48,80},{64,96},{80,112},{96,128},{112,144}... | collective-permute-start | bytes 1179656 | tf_op jit(solution)/shard_map/ppermute | solution.py:421
  88.3 15.7 %collective-permute-start.17 = (bf16[1536,128]{1,0:T(8,128)(2,1)S(1)}, bf16[1536,128]{1,0:T(8,128)(2,1)S(1)}, u32[]{:S(2)}, u32[]{:S(2)}) collective-permute-start(bf16[1536,128]{1,0:T(8,128)(2,1)S(1)} %collective-permute-done.16.refs_5_), channel_id=1, source_target_pairs={{0,224},{16,240},{32,0},{48,16},{64,32},{80,48},{96,64},{112,80},{... | collective-permute-start | bytes 1179656 | tf_op jit(solution)/shard_map/ppermute | solution.py:421
  90.8 13.3 %collective-permute-start.10 = (bf16[1536,128]{1,0:T(8,128)(2,1)S(1)}, bf16[1536,128]{1,0:T(8,128)(2,1)S(1)}, u32[]{:S(2)}, u32[]{:S(2)}) collective-permute-start(bf16[1536,128]{1,0:T(8,128)(2,1)S(1)} %collective-permute-done.6.refs_2_), channel_id=1, source_target_pairs={{0,32},{16,48},{32,64},{48,80},{64,96},{80,112},{96,128},{112,144}... | collective-permute-start | bytes 1179656 | tf_op jit(solution)/shard_map/ppermute | solution.py:421
  100.1 15.5 %collective-permute-start.26 = (bf16[2304,128]{1,0:T(8,128)(2,1)S(1)}, bf16[2304,128]{1,0:T(8,128)(2,1)S(1)}, u32[]{:S(2)}, u32[]{:S(2)}) collective-permute-start(bf16[2304,128]{1,0:T(8,128)(2,1)S(1)} %get-tuple-element.117), channel_id=1, source_target_pairs={{0,16},{16,0},{32,48},{48,32},{64,80},{80,64},{96,112},{112,96},{1... | collective-permute-start | bytes 1769480 | tf_op jit(solution)/shard_map/ppermute | solution.py:401
  103.5 24.9 %collective-permute-start.23 = (bf16[640,640]{1,0:T(8,128)(2,1)S(1)}, bf16[640,640]{1,0:T(8,128)(2,1)S(1)}, u32[]{:S(2)}, u32[]{:S(2)}) collective-permute-start(bf16[640,640]{1,0:T(8,128)(2,1)S(1)} %collective-permute-done.7.refs_6_.refs_7_), channel_id=1, source_target_pairs={{0,1},{1,0},{2,3},{3,2},{4,5},{5,4},{6,7},{7,6},{8,9},{9,8},{10,11... | collective-permute-start | bytes 2457608 | tf_op jit(solution)/shard_map/ppermute | solution.py:461
  103.5 25.8 %collective-permute-start.24 = (bf16[640,640]{1,0:T(8,128)(2,1)S(1)}, bf16[640,640]{1,0:T(8,128)(2,1)S(1)}, u32[]{:S(2)}, u32[]{:S(2)}) collective-permute-start(bf16[640,640]{1,0:T(8,128)(2,1)S(1)} %collective-permute-done.1.refs_8_.refs_9_), channel_id=1, source_target_pairs={{0,1},{1,0},{2,3},{3,2},{4,5},{5,4},{6,7},{7,6},{8,9},{9,8},{10,11... | collective-permute-start | bytes 2457608 | tf_op jit(solution)/shard_map/ppermute | solution.py:461
  104.0 27.9 %collective-permute-start.25 = (bf16[640,640]{1,0:T(8,128)(2,1)S(1)}, bf16[640,640]{1,0:T(8,128)(2,1)S(1)}, u32[]{:S(2)}, u32[]{:S(2)}) collective-permute-start(bf16[640,640]{1,0:T(8,128)(2,1)S(1)} %collective-permute-done.8.refs_10_.refs_11_), channel_id=1, source_target_pairs={{0,1},{1,0},{2,3},{3,2},{4,5},{5,4},{6,7},{7,6},{8,9},{9,8},{10,11... | collective-permute-start | bytes 2457608 | tf_op jit(solution)/shard_map/ppermute | solution.py:461
  113.6 7.8 %collective-permute-start.18 = (bf16[768,128]{1,0:T(8,128)(2,1)S(1)}, bf16[768,128]{1,0:T(8,128)(2,1)S(1)}, u32[]{:S(2)}, u32[]{:S(2)}) collective-permute-start(bf16[768,128]{1,0:T(8,128)(2,1)S(1)} %get-tuple-element.102), channel_id=1, source_target_pairs={{0,16},{16,0},{32,48},{48,32},{64,80},{80,64},{96,112},{112,96},{1... | collective-permute-start | bytes 589832 | tf_op jit(solution)/shard_map/ppermute | solution.py:401
  115.6 9.6 %collective-permute-start.19 = (bf16[768,128]{1,0:T(8,128)(2,1)S(1)}, bf16[768,128]{1,0:T(8,128)(2,1)S(1)}, u32[]{:S(2)}, u32[]{:S(2)}) collective-permute-start(bf16[768,128]{1,0:T(8,128)(2,1)S(1)} %get-tuple-element.105), channel_id=1, source_target_pairs={{0,16},{16,0},{32,48},{48,32},{64,80},{80,64},{96,112},{112,96},{1... | collective-permute-start | bytes 589832 | tf_op jit(solution)/shard_map/ppermute | solution.py:401
  121.3 16.5 %collective-permute-start.27 = (bf16[384,384]{1,0:T(8,128)(2,1)S(1)}, bf16[384,384]{1,0:T(8,128)(2,1)S(1)}, u32[]{:S(2)}, u32[]{:S(2)}) collective-permute-start(bf16[384,384]{1,0:T(8,128)(2,1)S(1)} %merge.3.refs_0_), channel_id=1, source_target_pairs={{0,12},{2,14},{4,0},{6,2},{8,4},{10,6},{12,8},{14,10},{1,13},{3,15... | collective-permute-start | bytes 884744 | tf_op jit(solution)/shard_map/ppermute | solution.py:432
  125.2 12.7 %collective-permute-start.28 = (bf16[384,384]{1,0:T(8,128)(2,1)S(1)}, bf16[384,384]{1,0:T(8,128)(2,1)S(1)}, u32[]{:S(2)}, u32[]{:S(2)}) collective-permute-start(bf16[384,384]{1,0:T(8,128)(2,1)S(1)} %merge.3.refs_0_), channel_id=1, source_target_pairs={{0,8},{2,10},{4,12},{6,14},{8,0},{10,2},{12,4},{14,6},{1,9},{3,11}... | collective-permute-start | bytes 884744 | tf_op jit(solution)/shard_map/ppermute | solution.py:432
  128.4 14.6 %collective-permute-start.29 = (bf16[384,384]{1,0:T(8,128)(2,1)S(1)}, bf16[384,384]{1,0:T(8,128)(2,1)S(1)}, u32[]{:S(2)}, u32[]{:S(2)}) collective-permute-start(bf16[384,384]{1,0:T(8,128)(2,1)S(1)} %merge.3.refs_0_), channel_id=1, source_target_pairs={{0,4},{2,6},{4,8},{6,10},{8,12},{10,14},{12,0},{14,2},{1,5},{3,7},... | collective-permute-start | bytes 884744 | tf_op jit(solution)/shard_map/ppermute | solution.py:432
  129.3 16.1 %collective-permute-start.20 = (bf16[384,256]{1,0:T(8,128)(2,1)S(1)}, bf16[384,256]{1,0:T(8,128)(2,1)S(1)}, u32[]{:S(2)}, u32[]{:S(2)}) collective-permute-start(bf16[384,256]{1,0:T(8,128)(2,1)S(1)} %merge.2.refs_1_), channel_id=1, source_target_pairs={{0,12},{2,14},{4,0},{6,2},{8,4},{10,6},{12,8},{14,10},{1,13},{3,15... | collective-permute-start | bytes 589832 | tf_op jit(solution)/shard_map/ppermute | solution.py:432
  132.0 15.3 %collective-permute-start.21 = (bf16[384,256]{1,0:T(8,128)(2,1)S(1)}, bf16[384,256]{1,0:T(8,128)(2,1)S(1)}, u32[]{:S(2)}, u32[]{:S(2)}) collective-permute-start(bf16[384,256]{1,0:T(8,128)(2,1)S(1)} %merge.2.refs_1_), channel_id=1, source_target_pairs={{0,8},{2,10},{4,12},{6,14},{8,0},{10,2},{12,4},{14,6},{1,9},{3,11}... | collective-permute-start | bytes 589832 | tf_op jit(solution)/shard_map/ppermute | solution.py:432
  137.9 12.2 %collective-permute-start.22 = (bf16[384,256]{1,0:T(8,128)(2,1)S(1)}, bf16[384,256]{1,0:T(8,128)(2,1)S(1)}, u32[]{:S(2)}, u32[]{:S(2)}) collective-permute-start(bf16[384,256]{1,0:T(8,128)(2,1)S(1)} %merge.2.refs_1_), channel_id=1, source_target_pairs={{0,4},{2,6},{4,8},{6,10},{8,12},{10,14},{12,0},{14,2},{1,5},{3,7},... | collective-permute-start | bytes 589832 | tf_op jit(solution)/shard_map/ppermute | solution.py:432
  145.5 7.1 %copy-start.4 = (bf16[512,640]{1,0:T(8,128)(2,1)S(1)}, bf16[512,640]{1,0:T(8,128)(2,1)}, u32[]{:S(2)}) copy-start(bf16[512,640]{1,0:T(8,128)(2,1)} %k_ref.3) | copy-start | bytes 1966084
  145.5 7.1 %copy-start.5 = (bf16[512,640]{1,0:T(8,128)(2,1)S(1)}, bf16[512,640]{1,0:T(8,128)(2,1)}, u32[]{:S(2)}) copy-start(bf16[512,640]{1,0:T(8,128)(2,1)} %v_ref.3) | copy-start | bytes 1966084
  145.5 7.1 %copy-start.7 = (bf16[384,640]{1,0:T(8,128)(2,1)S(1)}, bf16[384,640]{1,0:T(8,128)(2,1)}, u32[]{:S(2)}) copy-start(bf16[384,640]{1,0:T(8,128)(2,1)} %q_ref.7) | copy-start | bytes 1474564
  151.7 14.6 %collective-permute-start.30 = (bf16[384,640]{1,0:T(8,128)(2,1)S(1)}, bf16[384,640]{1,0:T(8,128)(2,1)S(1)}, u32[]{:S(2)}, u32[]{:S(2)}) collective-permute-start(bf16[384,640]{1,0:T(8,128)(2,1)S(1)} %get-tuple-element.119), channel_id=1, source_target_pairs={{0,2},{2,0},{4,6},{6,4},{8,10},{10,8},{12,14},{14,12},{1,3},{3,1},... | collective-permute-start | bytes 1474568 | tf_op jit(solution)/shard_map/ppermute | solution.py:468

commit v5 on v3

--- a/solution.py
+++ b/solution.py
@@ -14,6 +14,7 @@
 ROWS = FB * BLK
 MAX_EXTRA = 12
 MAX_NEAR = 3
+TERMS = 3
 GROUPS = ((0, 1, 2), (3, 4))
 IN_FLIGHT = 2
 NEG = -1e30
@@ -203,18 +204,18 @@
 
         lax.fori_loop(0, 2, one, 0)
     lane = lax.broadcasted_iota(jnp.int32, (ROWS, DH), 1)
+    packed = jnp.zeros((ROWS, DH), jnp.float32)
     for n in range(len(heads)):
         rows = slice(n * ROWS, (n + 1) * ROWS)
         keep_o[rows, :] = o_s[2 * n]
         keep_lse[rows, :] = lse_s[2 * n]
-        send[2 * n * ROWS : (2 * n + 1) * ROWS, :] = o_s[2 * n + 1].astype(jnp.bfloat16)
+        send[rows, :] = o_s[2 * n + 1].astype(jnp.bfloat16)
         left = lse_s[2 * n + 1]
-        packed = jnp.zeros((ROWS, DH), jnp.float32)
-        for term in range(3):
+        for term in range(TERMS):
             piece = left.astype(jnp.bfloat16).astype(jnp.float32)
-            packed = jnp.where(lane == term, piece, packed)
+            packed = jnp.where(lane == n * TERMS + term, piece, packed)
             left = left - piece
-        send[(2 * n + 1) * ROWS : (2 * n + 2) * ROWS, :] = packed.astype(jnp.bfloat16)
+    send[len(heads) * ROWS :, :] = packed.astype(jnp.bfloat16)
 
 
 def attend(heads, first, queries, queries_other, pieces, seq, near, blocks, counts):
@@ -228,7 +229,7 @@
         out_shape=[
             jax.ShapeDtypeStruct((held * ROWS, DH), jnp.float32),
             jax.ShapeDtypeStruct((held * ROWS, DH), jnp.float32),
-            jax.ShapeDtypeStruct((2 * held * ROWS, DH), jnp.bfloat16),
+            jax.ShapeDtypeStruct(((held + 1) * ROWS, DH), jnp.bfloat16),
         ],
         in_specs=[SMEM] * 4 + [VMEM] * (2 + planes),
         out_specs=[VMEM] * 3,
@@ -255,11 +256,14 @@
     out_ref, parts = refs[-1], refs[:-1]
     column = 0
     for o_ref, lse_ref, got_ref in zip(parts[0::3], parts[1::3], parts[2::3]):
-        for n in range(o_ref.shape[0] // ROWS):
+        held = o_ref.shape[0] // ROWS
+        packed = got_ref[held * ROWS :, :].astype(jnp.float32)
+        lane = lax.broadcasted_iota(jnp.int32, packed.shape, 1)
+        for n in range(held):
             rows = slice(n * ROWS, (n + 1) * ROWS)
-            other_o = got_ref[2 * n * ROWS : (2 * n + 1) * ROWS, :].astype(jnp.float32)
-            packed = got_ref[(2 * n + 1) * ROWS : (2 * n + 2) * ROWS, :].astype(jnp.float32)
-            other_lse = jnp.sum(packed, axis=1, keepdims=True)
+            other_o = got_ref[rows, :].astype(jnp.float32)
+            terms = (lane >= n * TERMS) & (lane < (n + 1) * TERMS)
+            other_lse = jnp.sum(jnp.where(terms, packed, 0.0), axis=1, keepdims=True)
             lse = lse_ref[rows, :]
             top = jnp.maximum(lse, other_lse)
             mine, other = jnp.exp2(lse - top), jnp.exp2(other_lse - top)
@@ -429,14 +433,16 @@
     early = list(plan(n_seq, seq, block_list, block_count))
     tiles = list(tile(lax.div(head, 2), pair, out_weight, n_y))
     early[0], tiles[0], queries_other = lax.optimization_barrier((early[0], tiles[0], queries_other))
-    hop(1, 0, 2, early)
+    hop(1, 0, 2)
     hop(-1, 0, 2)
-    blocks, counts, near = early
-    tiles[1:n_y] = [lax.ppermute(tiles[dy], "head", y_shift(dy)) for dy in range(1, n_y)][::-1]
+    arrived = [lax.ppermute(tiles[dy], "head", y_shift(dy)) for dy in (1, n_y - 1)]
+    arrived[1], tiles[2] = lax.optimization_barrier((arrived[1], tiles[2]))
+    tiles[1:n_y] = [arrived[1], lax.ppermute(tiles[2], "head", y_shift(2)), arrived[0]]
     one_away = [(tiles[1], tiles[n_y - 1])]
     hop(1, 0, 3, one_away)
     tiles[1], tiles[n_y - 1] = one_away[0]
-    hop(-1, 0, 3)
+    hop(-1, 0, 3, early)
+    blocks, counts, near = early
     hop(1, 0, 4)
     hop(-1, 1, 2)
     hop(1, 1, 2)
@@ -450,7 +456,7 @@
     most = partial(0, 0, 3)
     near, *weights = lax.optimization_barrier((near, *weights))
     one, two = partial(1, 0, 1), partial(1, 1, 2)
-    most[0], two[2] = lax.optimization_barrier((most[0], two[2]))
+    most[0], one[0], two[0] = lax.optimization_barrier((most[0], one[0], two[0]))
     before = project(GROUPS[0][0], along_y(join(most)), weights)
     rest = join(one, two)
     keep_block = (lax.rem(head, 2) != pair).astype(jnp.int32)

time: 155 us -> 157 us (1.013); the launches traced: 155 us -> 155 us
  waiting for transfers between devices: 68 us -> 73.4 us
  starting transfers between devices: 39.9 us -> 36.2 us
  local copies, waits for them, and re-layouts: 7.69 us -> 5.93 us
    ppermute x14, waiting for transfers between devices: 45.1 us -> 54.2 us  [hop(): held[group][place] = lax.ppermute(array, 'seq', z_shift(way))]
    ppermute x4, waiting for transfers between devices: 12.4 us -> 6.18 us  [to_other(): return lax.ppermute(array, 'seq', swap)]
    ppermute x3 -> x2, starting transfers between devices: 6.21 us -> 3.02 us  [body(): lax.ppermute(tiles[dy], 'head', y_shift(dy))]
    ppermute x1, waiting for transfers between devices: 5.38 us -> 7.95 us  [body(): got = lax.ppermute(send, 'head', [(g, g ^ 1) for g in range(n_head)])]
    unnamed x25 -> x23, local copies, waits for them, and re-layouts: 7.69 us -> 5.93 us
  transfers between devices with their start and end apart: 31 -> 31, of which waited for: 15 -> 15; matrix products, arithmetic and copies ran while one was open for 0% -> 0% of each run, Pallas kernels for 23% -> 22%
where the time goes in v5:
time: 157 us; the launch traced here: 155 us
  waiting for transfers between devices  73.4 us (47%)
  Pallas kernels  37.4 us (24%)
  starting transfers between devices  36.2 us (23%)
  local copies, waits for them, and re-layouts  5.93 us (4%)
    ppermute x14, waiting for transfers between devices, hop(): held[group][place] = lax.ppermute(array, 'seq', z_shift(way))  54.2 us
    pallas_call x3, Pallas kernels, attend(): pl.pallas_call(functools.partial(attend_kernel, heads, first, planes), ou...  23.7 us
    ppermute x14, starting transfers between devices, hop(): held[group][place] = lax.ppermute(array, 'seq', z_shift(way))  20 us
    ppermute x1, waiting for transfers between devices, body(): got = lax.ppermute(send, 'head', [(g, g ^ 1) for g in range(n_head)])  7.95 us
    ppermute x6, starting transfers between devices, along_y(): lax.ppermute(array, 'head', y_shift(-dy))  7.49 us
    ppermute x4, waiting for transfers between devices, to_other(): return lax.ppermute(array, 'seq', swap)  6.18 us
    unnamed x23, local copies, waits for them, and re-layouts  5.93 us
    ppermute x6, waiting for transfers between devices, along_y(): lax.ppermute(array, 'head', y_shift(-dy))  5.08 us
  transfers between devices with their start and end apart: 31, of which 15 were waited for; matrix products, arithmetic and copies ran while one was open for 0% of the time, Pallas kernels for 22%

profile of v5, /device:TPU:4, one launch (start us, length us, event | category | flops | bytes accessed | tf_op | source)
XLA Modules:
  0.0 154.6 jit_solution(9596482024233310548)
XLA Ops:
  0.6 1.0 copy-done.1
  1.7 1.0 copy-done.2
  2.7 1.1 pack.1
  3.8 1.9 %collective-permute-start.6 = (bf16[2304,128]{1,0:T(8,128)(2,1)}, bf16[2304,128]{1,0:T(8,128)(2,1)}, u32[]{:S(2)}, u32[]{:S(2)}) collective-permute-start(bf16[2304,128]{1,0:T(8,128)(2,1)} %get-tuple-element.72.refs_0_), channel_id=1, source_target_pairs={{0,32},{16,48},{32,64},{48,80},{64,96},{80,112},{96,128},{112,144}... | collective-permute-start | bytes 1769480 | tf_op jit(solution)/shard_map/ppermute | solution.py:416
  5.7 2.9 %copy-done = bf16[640,5120]{1,0:T(8,128)(2,1)S(1)} copy-done((bf16[640,5120]{1,0:T(8,128)(2,1)S(1)}, bf16[640,5120]{1,0:T(8,128)(2,1)}, u32[]{:S(2)}) %copy-start) | copy-done | bytes 6553624
  8.6 0.6 tile.1
  9.2 0.9 copy-done.4
  10.1 3.0 %collective-permute-start = (bf16[640,640]{1,0:T(8,128)(2,1)S(1)}, bf16[640,640]{1,0:T(8,128)(2,1)S(1)}, u32[]{:S(2)}, u32[]{:S(2)}) collective-permute-start(bf16[640,640]{1,0:T(8,128)(2,1)S(1)} %get-tuple-element.68), channel_id=1, source_target_pairs={{0,12},{2,14},{4,0},{6,2},{8,4},{10,6},{12,8},{14,10},{1,13},{3,15... | collective-permute-start | bytes 2457608 | tf_op jit(solution)/shard_map/ppermute | solution.py:438
  13.1 3.9 %collective-permute-start.2 = (bf16[2304,128]{1,0:T(8,128)(2,1)}, bf16[2304,128]{1,0:T(8,128)(2,1)}, u32[]{:S(2)}, u32[]{:S(2)}) collective-permute-start(bf16[2304,128]{1,0:T(8,128)(2,1)} %get-tuple-element.72.refs_0_), channel_id=1, source_target_pairs={{0,224},{16,240},{32,0},{48,16},{64,32},{80,48},{96,64},{112,80},{... | collective-permute-start | bytes 1769480 | tf_op jit(solution)/shard_map/ppermute | solution.py:416
  17.1 7.1 %collective-permute-done.6.refs_1_ = bf16[2304,128]{1,0:T(8,128)(2,1)} collective-permute-done((bf16[2304,128]{1,0:T(8,128)(2,1)}, bf16[2304,128]{1,0:T(8,128)(2,1)}, u32[]{:S(2)}, u32[]{:S(2)}) %collective-permute-start.6) | collective-permute-done | bytes 589856 | tf_op jit(solution)/shard_map/ppermute | solution.py:416
  24.1 5.5 %collective-permute-done.2.refs_7_ = bf16[2304,128]{1,0:T(8,128)(2,1)} collective-permute-done((bf16[2304,128]{1,0:T(8,128)(2,1)}, bf16[2304,128]{1,0:T(8,128)(2,1)}, u32[]{:S(2)}, u32[]{:S(2)}) %collective-permute-start.2) | collective-permute-done | bytes 589856 | tf_op jit(solution)/shard_map/ppermute | solution.py:416
  29.7 3.7 %collective-permute-start.3 = (bf16[2304,128]{1,0:T(8,128)(2,1)}, bf16[2304,128]{1,0:T(8,128)(2,1)}, u32[]{:S(2)}, u32[]{:S(2)}) collective-permute-start(bf16[2304,128]{1,0:T(8,128)(2,1)} %collective-permute-done.2.refs_7_), channel_id=1, source_target_pairs={{0,224},{16,240},{32,0},{48,16},{64,32},{80,48},{96,64},{112,80},{... | collective-permute-start | bytes 1769480 | tf_op jit(solution)/shard_map/ppermute | solution.py:416
  33.4 1.2 collective-permute-start.5
  34.6 1.2 collective-permute-start.4
  35.7 8.7 %collective-permute-done.7.refs_2_ = bf16[2304,128]{1,0:T(8,128)(2,1)} collective-permute-done((bf16[2304,128]{1,0:T(8,128)(2,1)}, bf16[2304,128]{1,0:T(8,128)(2,1)}, u32[]{:S(2)}, u32[]{:S(2)}) %collective-permute-start.7) | collective-permute-done | bytes 589856 | tf_op jit(solution)/shard_map/ppermute | solution.py:416
  44.5 3.4 %plan.1 = (s32[6,13]{1,0:T(8,128)S(1)}, s32[6]{0:T(128)S(1)}, s32[8]{0:T(128)S(1)}) custom-call(s32[1]{0:T(128)} %bitcast.2.seq_ref, s32[48,18]{1,0:T(8,128)S(1)} %copy.11.list_ref, s32[48]{0:T(128)S(1)} %copy-done.3), custom_call_target="tpu_custom_call" | custom-call | flops 1000 | bytes 8000 | tf_op jit(solution)/shard_map/plan/pallas_call | solution.py:61
  47.9 5.6 %collective-permute-done.4.refs_7_ = bf16[1536,128]{1,0:T(8,128)(2,1)} collective-permute-done((bf16[1536,128]{1,0:T(8,128)(2,1)}, bf16[1536,128]{1,0:T(8,128)(2,1)}, u32[]{:S(2)}, u32[]{:S(2)}) %collective-permute-start.4) | collective-permute-done | bytes 393248 | tf_op jit(solution)/shard_map/ppermute | solution.py:416
  53.5 3.7 %collective-permute-start.14 = (bf16[2304,128]{1,0:T(8,128)(2,1)}, bf16[2304,128]{1,0:T(8,128)(2,1)S(1)}, u32[]{:S(2)}, u32[]{:S(2)}) collective-permute-start(bf16[2304,128]{1,0:T(8,128)(2,1)} %collective-permute-done.3.refs_6_), channel_id=1, source_target_pairs={{0,224},{16,240},{32,0},{48,16},{64,32},{80,48},{96,64},{112,80},{... | collective-permute-start | bytes 1769480 | tf_op jit(solution)/shard_map/ppermute | solution.py:416
  57.2 0.6 collective-permute-start.1
  57.8 2.6 %collective-permute-done.10.refs_3_ = bf16[2304,128]{1,0:T(8,128)(2,1)} collective-permute-done((bf16[2304,128]{1,0:T(8,128)(2,1)}, bf16[2304,128]{1,0:T(8,128)(2,1)}, u32[]{:S(2)}, u32[]{:S(2)}) %collective-permute-start.10) | collective-permute-done | bytes 589856 | tf_op jit(solution)/shard_map/ppermute | solution.py:416
  60.4 16.0 %collective-permute-done.13.refs_6_ = bf16[1536,128]{1,0:T(8,128)(2,1)S(1)} collective-permute-done((bf16[1536,128]{1,0:T(8,128)(2,1)}, bf16[1536,128]{1,0:T(8,128)(2,1)S(1)}, u32[]{:S(2)}, u32[]{:S(2)}) %collective-permute-start.13) | collective-permute-done | bytes 393248 | tf_op jit(solution)/shard_map/ppermute | solution.py:416
  76.4 3.6 %collective-permute-start.19 = (bf16[1536,128]{1,0:T(8,128)(2,1)S(1)}, bf16[1536,128]{1,0:T(8,128)(2,1)S(1)}, u32[]{:S(2)}, u32[]{:S(2)}) collective-permute-start(bf16[1536,128]{1,0:T(8,128)(2,1)S(1)} %collective-permute-done.13.refs_6_), channel_id=1, source_target_pairs={{0,224},{16,240},{32,0},{48,16},{64,32},{80,48},{96,64},{112,80},{... | collective-permute-start | bytes 1179656 | tf_op jit(solution)/shard_map/ppermute | solution.py:416
  80.0 0.5 collective-permute-start.17
  80.5 4.8 %collective-permute-done.19.refs_5_ = bf16[1536,128]{1,0:T(8,128)(2,1)S(1)} collective-permute-done((bf16[1536,128]{1,0:T(8,128)(2,1)S(1)}, bf16[1536,128]{1,0:T(8,128)(2,1)S(1)}, u32[]{:S(2)}, u32[]{:S(2)}) %collective-permute-start.19) | collective-permute-done | bytes 393248 | tf_op jit(solution)/shard_map/ppermute | solution.py:416
  85.3 3.9 %collective-permute-done.11.refs_2_ = bf16[1536,128]{1,0:T(8,128)(2,1)S(1)} collective-permute-done((bf16[1536,128]{1,0:T(8,128)(2,1)}, bf16[1536,128]{1,0:T(8,128)(2,1)S(1)}, u32[]{:S(2)}, u32[]{:S(2)}) %collective-permute-start.11) | collective-permute-done | bytes 393248 | tf_op jit(solution)/shard_map/ppermute | solution.py:416
  89.2 2.0 %collective-permute-start.18 = (bf16[1536,128]{1,0:T(8,128)(2,1)S(1)}, bf16[1536,128]{1,0:T(8,128)(2,1)S(1)}, u32[]{:S(2)}, u32[]{:S(2)}) collective-permute-start(bf16[1536,128]{1,0:T(8,128)(2,1)S(1)} %collective-permute-done.11.refs_2_), channel_id=1, source_target_pairs={{0,32},{16,48},{32,64},{48,80},{64,96},{80,112},{96,128},{112,144}... | collective-permute-start | bytes 1179656 | tf_op jit(solution)/shard_map/ppermute | solution.py:416
  91.2 12.1 %attend.3 = (f32[1152,128]{1,0:T(8,128)S(1)}, f32[1152,128]{1,0:T(8,128)S(1)}, bf16[1536,128]{1,0:T(8,128)(2,1)S(1)}) custom-call(s32[1]{0:T(128)} %bitcast.2.seq_ref, s32[8]{0:T(128)S(1)} %get-tuple-element.106.near_ref, s32[6,13]{1,0:T(8,128)S(1)} %get-tuple-element.79.blocks_ref, s32[6]{0:T(128)S(1)} %get-tuple-element.80.count_ref, ...), custom_call_target="tpu_custom_call" | custom-call | flops 13589544960 | bytes 4718592 | tf_op jit(solution)/shard_map/attend/pallas_call | solution.py:227
  103.3 0.4 collective-permute-start.26
  103.7 5.8 %attend.4 = (f32[384,128]{1,0:T(8,128)S(1)}, f32[384,128]{1,0:T(8,128)S(1)}, bf16[768,128]{1,0:T(8,128)(2,1)S(1)}) custom-call(s32[1]{0:T(128)} %bitcast.2.seq_ref, s32[8]{0:T(128)S(1)} %get-tuple-element.106.near_ref, s32[6,13]{1,0:T(8,128)S(1)} %get-tuple-element.79.blocks_ref, s32[6]{0:T(128)S(1)} %get-tuple-element.80.count_ref, bf16[384,640]{1,0:T(8,128)(2,1)} %q_ref.6, ...), custom_call_target="tpu_custom_call" | custom-call | flops 4529848320 | bytes 1572864 | tf_op jit(solution)/shard_map/attend/pallas_call | solution.py:227
  109.6 5.8 %attend.5 = (f32[384,128]{1,0:T(8,128)S(1)}, f32[384,128]{1,0:T(8,128)S(1)}, bf16[768,128]{1,0:T(8,128)(2,1)S(1)}) custom-call(s32[1]{0:T(128)} %bitcast.2.seq_ref, s32[8]{0:T(128)S(1)} %get-tuple-element.106.near_ref, s32[6,13]{1,0:T(8,128)S(1)} %get-tuple-element.79.blocks_ref, s32[6]{0:T(128)S(1)} %get-tuple-element.80.count_ref, bf16[384,640]{1,0:T(8,128)(2,1)} %q_ref.6, ...), custom_call_target="tpu_custom_call" | custom-call | flops 4529848320 | bytes 1572864 | tf_op jit(solution)/shard_map/attend/pallas_call | solution.py:227
  115.8 0.8 collective-permute-start.27
  116.9 1.0 collective-permute-start.29
  118.2 1.8 %collective-permute-start.22 = (bf16[768,128]{1,0:T(8,128)(2,1)S(1)}, bf16[768,128]{1,0:T(8,128)(2,1)S(1)}, u32[]{:S(2)}, u32[]{:S(2)}) collective-permute-start(bf16[768,128]{1,0:T(8,128)(2,1)S(1)} %get-tuple-element.118), channel_id=1, source_target_pairs={{0,16},{16,0},{32,48},{48,32},{64,80},{80,64},{96,112},{112,96},{1... | collective-permute-start | bytes 589832 | tf_op jit(solution)/shard_map/ppermute | solution.py:396
  119.9 4.1 %collective-permute-done.21.refs_2_ = bf16[768,128]{1,0:T(8,128)(2,1)S(1)} collective-permute-done((bf16[768,128]{1,0:T(8,128)(2,1)S(1)}, bf16[768,128]{1,0:T(8,128)(2,1)S(1)}, u32[]{:S(2)}, u32[]{:S(2)}) %collective-permute-start.21) | collective-permute-done | bytes 196640 | tf_op jit(solution)/shard_map/ppermute | solution.py:396
  124.0 2.1 %collective-permute-done.22.refs_5_ = bf16[768,128]{1,0:T(8,128)(2,1)S(1)} collective-permute-done((bf16[768,128]{1,0:T(8,128)(2,1)S(1)}, bf16[768,128]{1,0:T(8,128)(2,1)S(1)}, u32[]{:S(2)}, u32[]{:S(2)}) %collective-permute-start.22) | collective-permute-done | bytes 196640 | tf_op jit(solution)/shard_map/ppermute | solution.py:396
  126.4 2.8 %collective-permute-start.23 = (bf16[384,256]{1,0:T(8,128)(2,1)S(1)}, bf16[384,256]{1,0:T(8,128)(2,1)S(1)}, u32[]{:S(2)}, u32[]{:S(2)}) collective-permute-start(bf16[384,256]{1,0:T(8,128)(2,1)S(1)} %merge.2.refs_1_), channel_id=1, source_target_pairs={{0,12},{2,14},{4,0},{6,2},{8,4},{10,6},{12,8},{14,10},{1,13},{3,15... | collective-permute-start | bytes 589832 | tf_op jit(solution)/shard_map/ppermute | solution.py:427
  129.1 1.3 collective-permute-start.24
  130.4 1.3 collective-permute-start.25
  131.7 1.8 %collective-permute-done.29.refs_3_ = bf16[384,384]{1,0:T(8,128)(2,1)S(1)} collective-permute-done((bf16[384,384]{1,0:T(8,128)(2,1)S(1)}, bf16[384,384]{1,0:T(8,128)(2,1)S(1)}, u32[]{:S(2)}, u32[]{:S(2)}) %collective-permute-start.29) | collective-permute-done | bytes 294944 | tf_op jit(solution)/shard_map/ppermute | solution.py:427
  133.6 2.4 %project.2.refs_13_ = f32[2,384,640]{2,1,0:T(8,128)S(1)} custom-call(bf16[384,384]{1,0:T(8,128)(2,1)S(1)} %merge.3.refs_0_, bf16[384,384]{1,0:T(8,128)(2,1)S(1)} %collective-permute-done.27.refs_1_, bf16[384,384]{1,0:T(8,128)(2,1)S(1)} %collective-permute-done.28.refs_2_, bf16[384,384]{1,0:T(8,128)(2,1)S(1)} %collective-permute-done.29.refs_3_, ...), custom_call_target="tpu_custom_call" | custom-call | flops 1509949440 | bytes 5111808 | tf_op jit(solution)/shard_map/project/pallas_call | solution.py:371
  136.0 0.8 collective-permute-done.23.refs_2_
  136.8 0.5 collective-permute-done.24.refs_3_
  137.3 2.0 %collective-permute-done.25.refs_4_ = bf16[384,256]{1,0:T(8,128)(2,1)S(1)} collective-permute-done((bf16[384,256]{1,0:T(8,128)(2,1)S(1)}, bf16[384,256]{1,0:T(8,128)(2,1)S(1)}, u32[]{:S(2)}, u32[]{:S(2)}) %collective-permute-start.25) | collective-permute-done | bytes 196640 | tf_op jit(solution)/shard_map/ppermute | solution.py:427
  139.3 1.5 project.3
  140.8 0.9 collective-permute-start.30
  141.6 4.1 %cross.1 = bf16[384,640]{1,0:T(8,128)(2,1)} custom-call(bf16[384,640]{1,0:T(8,128)(2,1)S(1)} %copy-done.7, bf16[512,640]{1,0:T(8,128)(2,1)S(1)} %copy-done.5, bf16[512,640]{1,0:T(8,128)(2,1)S(1)} %copy-done.6), custom_call_target="tpu_custom_call" | custom-call | flops 5033164800 | bytes 983040 | tf_op jit(solution)/shard_map/cross/pallas_call | solution.py:333
  145.8 8.0 %collective-permute-done.30 = bf16[384,640]{1,0:T(8,128)(2,1)S(1)} collective-permute-done((bf16[384,640]{1,0:T(8,128)(2,1)S(1)}, bf16[384,640]{1,0:T(8,128)(2,1)S(1)}, u32[]{:S(2)}, u32[]{:S(2)}) %collective-permute-start.30) | collective-permute-done | bytes 491552 | tf_op jit(solution)/shard_map/ppermute | solution.py:464
  153.7 0.9 add_convert_fusion
  (49 shorter events, 1.4 us)
Async XLA Ops:
  0.6 1.0 copy-start.1
  1.7 1.0 copy-start.2
  2.7 41.7 %copy-start.10 = (s32[48,18]{0,1:T(8,128)S(1)}, s32[48,18]{0,1:T(8,128)}, u32[]{:S(2)}) copy-start(s32[48,18]{0,1:T(8,128)} %param.16) | copy-start | bytes 10372
  2.7 41.8 %copy-start.3 = (s32[48]{0:T(128)S(1)}, s32[48]{0:T(128)}, u32[]{:S(2)}) copy-start(s32[48]{0:T(128)} %count_ref.1) | copy-start | bytes 580
  3.8 20.3 %collective-permute-start.6 = (bf16[2304,128]{1,0:T(8,128)(2,1)}, bf16[2304,128]{1,0:T(8,128)(2,1)}, u32[]{:S(2)}, u32[]{:S(2)}) collective-permute-start(bf16[2304,128]{1,0:T(8,128)(2,1)} %get-tuple-element.72.refs_0_), channel_id=1, source_target_pairs={{0,32},{16,48},{32,64},{48,80},{64,96},{80,112},{96,128},{112,144}... | collective-permute-start | bytes 1769480 | tf_op jit(solution)/shard_map/ppermute | solution.py:416
  5.7 2.9 %copy-start = (bf16[640,5120]{1,0:T(8,128)(2,1)S(1)}, bf16[640,5120]{1,0:T(8,128)(2,1)}, u32[]{:S(2)}) copy-start(bf16[640,5120]{1,0:T(8,128)(2,1)} %weight_ref.1) | copy-start | bytes 19660804
  9.2 0.9 copy-start.4
  10.1 24.5 %collective-permute-start = (bf16[640,640]{1,0:T(8,128)(2,1)S(1)}, bf16[640,640]{1,0:T(8,128)(2,1)S(1)}, u32[]{:S(2)}, u32[]{:S(2)}) collective-permute-start(bf16[640,640]{1,0:T(8,128)(2,1)S(1)} %get-tuple-element.68), channel_id=1, source_target_pairs={{0,12},{2,14},{4,0},{6,2},{8,4},{10,6},{12,8},{14,10},{1,13},{3,15... | collective-permute-start | bytes 2457608 | tf_op jit(solution)/shard_map/ppermute | solution.py:438
  13.1 16.6 %collective-permute-start.2 = (bf16[2304,128]{1,0:T(8,128)(2,1)}, bf16[2304,128]{1,0:T(8,128)(2,1)}, u32[]{:S(2)}, u32[]{:S(2)}) collective-permute-start(bf16[2304,128]{1,0:T(8,128)(2,1)} %get-tuple-element.72.refs_0_), channel_id=1, source_target_pairs={{0,224},{16,240},{32,0},{48,16},{64,32},{80,48},{96,64},{112,80},{... | collective-permute-start | bytes 1769480 | tf_op jit(solution)/shard_map/ppermute | solution.py:416
  17.0 27.3 %collective-permute-start.9 = (bf16[640,640]{1,0:T(8,128)(2,1)S(1)}, bf16[640,640]{1,0:T(8,128)(2,1)S(1)}, u32[]{:S(2)}, u32[]{:S(2)}) collective-permute-start(bf16[640,640]{1,0:T(8,128)(2,1)S(1)} %get-tuple-element.86), channel_id=1, source_target_pairs={{0,4},{2,6},{4,8},{6,10},{8,12},{10,14},{12,0},{14,2},{1,5},{3,7},... | collective-permute-start | bytes 2457608 | tf_op jit(solution)/shard_map/ppermute | solution.py:438
  17.0 16.3 %collective-permute-start.8 = (bf16[1536,128]{1,0:T(8,128)(2,1)}, bf16[1536,128]{1,0:T(8,128)(2,1)S(1)}, u32[]{:S(2)}, u32[]{:S(2)}) collective-permute-start(bf16[1536,128]{1,0:T(8,128)(2,1)} %get-tuple-element.74.refs_0_), channel_id=1, source_target_pairs={{0,32},{16,48},{32,64},{48,80},{64,96},{80,112},{96,128},{112,144}... | collective-permute-start | bytes 1179656 | tf_op jit(solution)/shard_map/ppermute | solution.py:416
  24.1 20.2 %collective-permute-start.7 = (bf16[2304,128]{1,0:T(8,128)(2,1)}, bf16[2304,128]{1,0:T(8,128)(2,1)}, u32[]{:S(2)}, u32[]{:S(2)}) collective-permute-start(bf16[2304,128]{1,0:T(8,128)(2,1)} %collective-permute-done.6.refs_1_), channel_id=1, source_target_pairs={{0,32},{16,48},{32,64},{48,80},{64,96},{80,112},{96,128},{112,144}... | collective-permute-start | bytes 1769480 | tf_op jit(solution)/shard_map/ppermute | solution.py:416
  29.7 23.8 %collective-permute-start.3 = (bf16[2304,128]{1,0:T(8,128)(2,1)}, bf16[2304,128]{1,0:T(8,128)(2,1)}, u32[]{:S(2)}, u32[]{:S(2)}) collective-permute-start(bf16[2304,128]{1,0:T(8,128)(2,1)} %collective-permute-done.2.refs_7_), channel_id=1, source_target_pairs={{0,224},{16,240},{32,0},{48,16},{64,32},{80,48},{96,64},{112,80},{... | collective-permute-start | bytes 1769480 | tf_op jit(solution)/shard_map/ppermute | solution.py:416
  33.4 11.0 %copy-start.8 = (bf16[1536,128]{1,0:T(8,128)(2,1)}, bf16[1536,128]{1,0:T(8,128)(2,1)S(1)}, u32[]{:S(2)}) copy-start(bf16[1536,128]{1,0:T(8,128)(2,1)S(1)} %collective-permute-done.8.refs_1_) | copy-start | bytes 1179652
  33.4 14.5 %collective-permute-start.5 = (bf16[384,640]{1,0:T(8,128)(2,1)}, bf16[384,640]{1,0:T(8,128)(2,1)}, u32[]{:S(2)}, u32[]{:S(2)}) collective-permute-start(bf16[384,640]{1,0:T(8,128)(2,1)} %q_ref.6), channel_id=1, source_target_pairs={{0,16},{16,0},{32,48},{48,32},{64,80},{80,64},{96,112},{112,96},{1... | collective-permute-start | bytes 1474568 | tf_op jit(solution)/shard_map/ppermute | solution.py:396
  34.6 18.9 %collective-permute-start.4 = (bf16[1536,128]{1,0:T(8,128)(2,1)}, bf16[1536,128]{1,0:T(8,128)(2,1)}, u32[]{:S(2)}, u32[]{:S(2)}) collective-permute-start(bf16[1536,128]{1,0:T(8,128)(2,1)} %get-tuple-element.74.refs_0_), channel_id=1, source_target_pairs={{0,224},{16,240},{32,0},{48,16},{64,32},{80,48},{96,64},{112,80},{... | collective-permute-start | bytes 1179656 | tf_op jit(solution)/shard_map/ppermute | solution.py:416
  44.4 16.0 %collective-permute-start.10 = (bf16[2304,128]{1,0:T(8,128)(2,1)}, bf16[2304,128]{1,0:T(8,128)(2,1)}, u32[]{:S(2)}, u32[]{:S(2)}) collective-permute-start(bf16[2304,128]{1,0:T(8,128)(2,1)} %collective-permute-done.7.refs_2_), channel_id=1, source_target_pairs={{0,32},{16,48},{32,64},{48,80},{64,96},{80,112},{96,128},{112,144}... | collective-permute-start | bytes 1769480 | tf_op jit(solution)/shard_map/ppermute | solution.py:416
  53.5 22.9 %collective-permute-start.14 = (bf16[2304,128]{1,0:T(8,128)(2,1)}, bf16[2304,128]{1,0:T(8,128)(2,1)S(1)}, u32[]{:S(2)}, u32[]{:S(2)}) collective-permute-start(bf16[2304,128]{1,0:T(8,128)(2,1)} %collective-permute-done.3.refs_6_), channel_id=1, source_target_pairs={{0,224},{16,240},{32,0},{48,16},{64,32},{80,48},{96,64},{112,80},{... | collective-permute-start | bytes 1769480 | tf_op jit(solution)/shard_map/ppermute | solution.py:416
  57.2 22.8 %collective-permute-start.1 = (bf16[640,640]{1,0:T(8,128)(2,1)}, bf16[640,640]{1,0:T(8,128)(2,1)S(1)}, u32[]{:S(2)}, u32[]{:S(2)}) collective-permute-start(bf16[640,640]{1,0:T(8,128)(2,1)} %copy-done.4), channel_id=1, source_target_pairs={{0,8},{2,10},{4,12},{6,14},{8,0},{10,2},{12,4},{14,6},{1,9},{3,11}... | collective-permute-start | bytes 2457608 | tf_op jit(solution)/shard_map/ppermute | solution.py:440
  57.8 18.6 %collective-permute-start.13 = (bf16[1536,128]{1,0:T(8,128)(2,1)}, bf16[1536,128]{1,0:T(8,128)(2,1)S(1)}, u32[]{:S(2)}, u32[]{:S(2)}) collective-permute-start(bf16[1536,128]{1,0:T(8,128)(2,1)} %collective-permute-done.4.refs_7_), channel_id=1, source_target_pairs={{0,224},{16,240},{32,0},{48,16},{64,32},{80,48},{96,64},{112,80},{... | collective-permute-start | bytes 1179656 | tf_op jit(solution)/shard_map/ppermute | solution.py:416
  60.4 28.8 %collective-permute-start.12 = (bf16[2304,128]{1,0:T(8,128)(2,1)}, bf16[2304,128]{1,0:T(8,128)(2,1)S(1)}, u32[]{:S(2)}, u32[]{:S(2)}) collective-permute-start(bf16[2304,128]{1,0:T(8,128)(2,1)} %collective-permute-done.10.refs_3_), channel_id=1, source_target_pairs={{0,32},{16,48},{32,64},{48,80},{64,96},{80,112},{96,128},{112,144}... | collective-permute-start | bytes 1769480 | tf_op jit(solution)/shard_map/ppermute | solution.py:416
  76.4 8.9 %collective-permute-start.19 = (bf16[1536,128]{1,0:T(8,128)(2,1)S(1)}, bf16[1536,128]{1,0:T(8,128)(2,1)S(1)}, u32[]{:S(2)}, u32[]{:S(2)}) collective-permute-start(bf16[1536,128]{1,0:T(8,128)(2,1)S(1)} %collective-permute-done.13.refs_6_), channel_id=1, source_target_pairs={{0,224},{16,240},{32,0},{48,16},{64,32},{80,48},{96,64},{112,80},{... | collective-permute-start | bytes 1179656 | tf_op jit(solution)/shard_map/ppermute | solution.py:416
  80.0 9.2 %collective-permute-start.11 = (bf16[1536,128]{1,0:T(8,128)(2,1)}, bf16[1536,128]{1,0:T(8,128)(2,1)S(1)}, u32[]{:S(2)}, u32[]{:S(2)}) collective-permute-start(bf16[1536,128]{1,0:T(8,128)(2,1)} %copy-done.8), channel_id=1, source_target_pairs={{0,32},{16,48},{32,64},{48,80},{64,96},{80,112},{96,128},{112,144}... | collective-permute-start | bytes 1179656 | tf_op jit(solution)/shard_map/ppermute | solution.py:416
  80.0 23.3 %collective-permute-start.15 = (bf16[640,640]{1,0:T(8,128)(2,1)S(1)}, bf16[640,640]{1,0:T(8,128)(2,1)S(1)}, u32[]{:S(2)}, u32[]{:S(2)}) collective-permute-start(bf16[640,640]{1,0:T(8,128)(2,1)S(1)} %collective-permute-done.refs_6_.refs_7_), channel_id=1, source_target_pairs={{0,1},{1,0},{2,3},{3,2},{4,5},{5,4},{6,7},{7,6},{8,9},{9,8},{10,11... | collective-permute-start | bytes 2457608 | tf_op jit(solution)/shard_map/ppermute | solution.py:455
  80.0 23.7 %collective-permute-start.17 = (bf16[640,640]{1,0:T(8,128)(2,1)S(1)}, bf16[640,640]{1,0:T(8,128)(2,1)S(1)}, u32[]{:S(2)}, u32[]{:S(2)}) collective-permute-start(bf16[640,640]{1,0:T(8,128)(2,1)S(1)} %collective-permute-done.9.refs_10_.refs_11_), channel_id=1, source_target_pairs={{0,1},{1,0},{2,3},{3,2},{4,5},{5,4},{6,7},{7,6},{8,9},{9,8},{10,11... | collective-permute-start | bytes 2457608 | tf_op jit(solution)/shard_map/ppermute | solution.py:455
  85.3 18.4 %collective-permute-start.16 = (bf16[640,640]{1,0:T(8,128)(2,1)S(1)}, bf16[640,640]{1,0:T(8,128)(2,1)S(1)}, u32[]{:S(2)}, u32[]{:S(2)}) collective-permute-start(bf16[640,640]{1,0:T(8,128)(2,1)S(1)} %collective-permute-done.1.refs_8_.refs_9_), channel_id=1, source_target_pairs={{0,1},{1,0},{2,3},{3,2},{4,5},{5,4},{6,7},{7,6},{8,9},{9,8},{10,11... | collective-permute-start | bytes 2457608 | tf_op jit(solution)/shard_map/ppermute | solution.py:455
  89.2 14.5 %collective-permute-start.20 = (bf16[1536,128]{1,0:T(8,128)(2,1)S(1)}, bf16[1536,128]{1,0:T(8,128)(2,1)S(1)}, u32[]{:S(2)}, u32[]{:S(2)}) collective-permute-start(bf16[1536,128]{1,0:T(8,128)(2,1)S(1)} %collective-permute-done.19.refs_5_), channel_id=1, source_target_pairs={{0,224},{16,240},{32,0},{48,16},{64,32},{80,48},{96,64},{112,80},{... | collective-permute-start | bytes 1179656 | tf_op jit(solution)/shard_map/ppermute | solution.py:416
  89.2 14.5 %collective-permute-start.18 = (bf16[1536,128]{1,0:T(8,128)(2,1)S(1)}, bf16[1536,128]{1,0:T(8,128)(2,1)S(1)}, u32[]{:S(2)}, u32[]{:S(2)}) collective-permute-start(bf16[1536,128]{1,0:T(8,128)(2,1)S(1)} %collective-permute-done.11.refs_2_), channel_id=1, source_target_pairs={{0,32},{16,48},{32,64},{48,80},{64,96},{80,112},{96,128},{112,144}... | collective-permute-start | bytes 1179656 | tf_op jit(solution)/shard_map/ppermute | solution.py:416
  91.2 12.5 %copy-start.9 = (bf16[1536,128]{1,0:T(8,128)(2,1)S(1)}, bf16[1536,128]{1,0:T(8,128)(2,1)}, u32[]{:S(2)}) copy-start(bf16[1536,128]{1,0:T(8,128)(2,1)} %copy-done.8) | copy-start | bytes 1179652
  103.3 12.1 %collective-permute-start.26 = (bf16[1536,128]{1,0:T(8,128)(2,1)S(1)}, bf16[1536,128]{1,0:T(8,128)(2,1)S(1)}, u32[]{:S(2)}, u32[]{:S(2)}) collective-permute-start(bf16[1536,128]{1,0:T(8,128)(2,1)S(1)} %get-tuple-element.129), channel_id=1, source_target_pairs={{0,16},{16,0},{32,48},{48,32},{64,80},{80,64},{96,112},{112,96},{1... | collective-permute-start | bytes 1179656 | tf_op jit(solution)/shard_map/ppermute | solution.py:396
  115.8 14.7 %collective-permute-start.27 = (bf16[384,384]{1,0:T(8,128)(2,1)S(1)}, bf16[384,384]{1,0:T(8,128)(2,1)S(1)}, u32[]{:S(2)}, u32[]{:S(2)}) collective-permute-start(bf16[384,384]{1,0:T(8,128)(2,1)S(1)} %merge.3.refs_0_), channel_id=1, source_target_pairs={{0,12},{2,14},{4,0},{6,2},{8,4},{10,6},{12,8},{14,10},{1,13},{3,15... | collective-permute-start | bytes 884744 | tf_op jit(solution)/shard_map/ppermute | solution.py:427
  116.6 15.1 %collective-permute-start.28 = (bf16[384,384]{1,0:T(8,128)(2,1)S(1)}, bf16[384,384]{1,0:T(8,128)(2,1)S(1)}, u32[]{:S(2)}, u32[]{:S(2)}) collective-permute-start(bf16[384,384]{1,0:T(8,128)(2,1)S(1)} %merge.3.refs_0_), channel_id=1, source_target_pairs={{0,8},{2,10},{4,12},{6,14},{8,0},{10,2},{12,4},{14,6},{1,9},{3,11}... | collective-permute-start | bytes 884744 | tf_op jit(solution)/shard_map/ppermute | solution.py:427
  116.9 16.6 %collective-permute-start.29 = (bf16[384,384]{1,0:T(8,128)(2,1)S(1)}, bf16[384,384]{1,0:T(8,128)(2,1)S(1)}, u32[]{:S(2)}, u32[]{:S(2)}) collective-permute-start(bf16[384,384]{1,0:T(8,128)(2,1)S(1)} %merge.3.refs_0_), channel_id=1, source_target_pairs={{0,4},{2,6},{4,8},{6,10},{8,12},{10,14},{12,0},{14,2},{1,5},{3,7},... | collective-permute-start | bytes 884744 | tf_op jit(solution)/shard_map/ppermute | solution.py:427
  117.9 6.1 %collective-permute-start.21 = (bf16[768,128]{1,0:T(8,128)(2,1)S(1)}, bf16[768,128]{1,0:T(8,128)(2,1)S(1)}, u32[]{:S(2)}, u32[]{:S(2)}) collective-permute-start(bf16[768,128]{1,0:T(8,128)(2,1)S(1)} %get-tuple-element.115), channel_id=1, source_target_pairs={{0,16},{16,0},{32,48},{48,32},{64,80},{80,64},{96,112},{112,96},{1... | collective-permute-start | bytes 589832 | tf_op jit(solution)/shard_map/ppermute | solution.py:396
  118.2 7.9 %collective-permute-start.22 = (bf16[768,128]{1,0:T(8,128)(2,1)S(1)}, bf16[768,128]{1,0:T(8,128)(2,1)S(1)}, u32[]{:S(2)}, u32[]{:S(2)}) collective-permute-start(bf16[768,128]{1,0:T(8,128)(2,1)S(1)} %get-tuple-element.118), channel_id=1, source_target_pairs={{0,16},{16,0},{32,48},{48,32},{64,80},{80,64},{96,112},{112,96},{1... | collective-permute-start | bytes 589832 | tf_op jit(solution)/shard_map/ppermute | solution.py:396
  126.4 10.4 %collective-permute-start.23 = (bf16[384,256]{1,0:T(8,128)(2,1)S(1)}, bf16[384,256]{1,0:T(8,128)(2,1)S(1)}, u32[]{:S(2)}, u32[]{:S(2)}) collective-permute-start(bf16[384,256]{1,0:T(8,128)(2,1)S(1)} %merge.2.refs_1_), channel_id=1, source_target_pairs={{0,12},{2,14},{4,0},{6,2},{8,4},{10,6},{12,8},{14,10},{1,13},{3,15... | collective-permute-start | bytes 589832 | tf_op jit(solution)/shard_map/ppermute | solution.py:427
  129.1 8.2 %collective-permute-start.24 = (bf16[384,256]{1,0:T(8,128)(2,1)S(1)}, bf16[384,256]{1,0:T(8,128)(2,1)S(1)}, u32[]{:S(2)}, u32[]{:S(2)}) collective-permute-start(bf16[384,256]{1,0:T(8,128)(2,1)S(1)} %merge.2.refs_1_), channel_id=1, source_target_pairs={{0,8},{2,10},{4,12},{6,14},{8,0},{10,2},{12,4},{14,6},{1,9},{3,11}... | collective-permute-start | bytes 589832 | tf_op jit(solution)/shard_map/ppermute | solution.py:427
  130.4 8.8 %collective-permute-start.25 = (bf16[384,256]{1,0:T(8,128)(2,1)S(1)}, bf16[384,256]{1,0:T(8,128)(2,1)S(1)}, u32[]{:S(2)}, u32[]{:S(2)}) collective-permute-start(bf16[384,256]{1,0:T(8,128)(2,1)S(1)} %merge.2.refs_1_), channel_id=1, source_target_pairs={{0,4},{2,6},{4,8},{6,10},{8,12},{10,14},{12,0},{14,2},{1,5},{3,7},... | collective-permute-start | bytes 589832 | tf_op jit(solution)/shard_map/ppermute | solution.py:427
  136.0 5.7 %copy-start.5 = (bf16[512,640]{1,0:T(8,128)(2,1)S(1)}, bf16[512,640]{1,0:T(8,128)(2,1)}, u32[]{:S(2)}) copy-start(bf16[512,640]{1,0:T(8,128)(2,1)} %k_ref.3) | copy-start | bytes 1966084
  136.0 5.7 %copy-start.6 = (bf16[512,640]{1,0:T(8,128)(2,1)S(1)}, bf16[512,640]{1,0:T(8,128)(2,1)}, u32[]{:S(2)}) copy-start(bf16[512,640]{1,0:T(8,128)(2,1)} %v_ref.3) | copy-start | bytes 1966084
  136.0 5.7 %copy-start.7 = (bf16[384,640]{1,0:T(8,128)(2,1)S(1)}, bf16[384,640]{1,0:T(8,128)(2,1)}, u32[]{:S(2)}) copy-start(bf16[384,640]{1,0:T(8,128)(2,1)} %q_ref.7) | copy-start | bytes 1474564
  140.8 13.0 %collective-permute-start.30 = (bf16[384,640]{1,0:T(8,128)(2,1)S(1)}, bf16[384,640]{1,0:T(8,128)(2,1)S(1)}, u32[]{:S(2)}, u32[]{:S(2)}) collective-permute-start(bf16[384,640]{1,0:T(8,128)(2,1)S(1)} %get-tuple-element.131), channel_id=1, source_target_pairs={{0,2},{2,0},{4,6},{6,4},{8,10},{10,8},{12,14},{14,12},{1,3},{3,1},... | collective-permute-start | bytes 1474568 | tf_op jit(solution)/shard_map/ppermute | solution.py:464

commit v6 on v5

--- a/solution.py
+++ b/solution.py
@@ -431,6 +431,7 @@
         hop(-1, group, 1)
     queries_other = to_other(queries)
     early = list(plan(n_seq, seq, block_list, block_count))
+    out_weight, queries_other = lax.optimization_barrier((out_weight, queries_other))
     tiles = list(tile(lax.div(head, 2), pair, out_weight, n_y))
     early[0], tiles[0], queries_other = lax.optimization_barrier((early[0], tiles[0], queries_other))
     hop(1, 0, 2)
@@ -438,6 +439,7 @@
     arrived = [lax.ppermute(tiles[dy], "head", y_shift(dy)) for dy in (1, n_y - 1)]
     arrived[1], tiles[2] = lax.optimization_barrier((arrived[1], tiles[2]))
     tiles[1:n_y] = [arrived[1], lax.ppermute(tiles[2], "head", y_shift(2)), arrived[0]]
+    hop(1, 1, 2)
     one_away = [(tiles[1], tiles[n_y - 1])]
     hop(1, 0, 3, one_away)
     tiles[1], tiles[n_y - 1] = one_away[0]
@@ -445,7 +447,6 @@
     blocks, counts, near = early
     hop(1, 0, 4)
     hop(-1, 1, 2)
-    hop(1, 1, 2)
     hop(-1, 1, 3)
     hop(1, 1, 3)
     hop(-1, 1, 4)
@@ -455,10 +456,10 @@
         weights += [mine, lax.ppermute(mine, "pair", [(0, 1), (1, 0)])]
     most = partial(0, 0, 3)
     near, *weights = lax.optimization_barrier((near, *weights))
-    one, two = partial(1, 0, 1), partial(1, 1, 2)
-    most[0], one[0], two[0] = lax.optimization_barrier((most[0], one[0], two[0]))
+    rest = partial(1, 0, 2)
+    most[0], rest[0] = lax.optimization_barrier((most[0], rest[0]))
     before = project(GROUPS[0][0], along_y(join(most)), weights)
-    rest = join(one, two)
+    rest = join(rest)
     keep_block = (lax.rem(head, 2) != pair).astype(jnp.int32)
     keep, send = project(GROUPS[1][0], along_y(rest), weights, before, keep_block)
     got = lax.ppermute(send, "head", [(g, g ^ 1) for g in range(n_head)])

time: 157 us -> 154 us (0.981)
  waiting for transfers between devices: 73.4 us -> 68.5 us
  Pallas kernels: 37.4 us -> 33.8 us
  starting transfers between devices: 36.2 us -> 39.2 us
  local copies, waits for them, and re-layouts: 5.93 us -> 8.76 us
    ppermute x14, waiting for transfers between devices: 54.2 us -> 39.5 us  [hop(): held[group][place] = lax.ppermute(array, 'seq', z_shift(way))]
    ppermute x6, waiting for transfers between devices: 5.08 us -> 10.8 us  [along_y(): lax.ppermute(array, 'head', y_shift(-dy))]
    ppermute x14, starting transfers between devices: 20 us -> 23.7 us  [hop(): held[group][place] = lax.ppermute(array, 'seq', z_shift(way))]
    pallas_call x3 -> x2, Pallas kernels: 23.7 us -> 20.3 us  [attend(): pl.pallas_call(functools.partial(attend_kernel, heads, first, planes), ou...]
    ppermute x4 -> x3, waiting for transfers between devices: 6.18 us -> 9.41 us  [to_other(): return lax.ppermute(array, 'seq', swap)]
    ppermute x2, waiting for transfers between devices: 0.01 us -> 3 us  [body(): lax.ppermute(tiles[dy], 'head', y_shift(dy))]
    unnamed x23 -> x25, local copies, waits for them, and re-layouts: 5.93 us -> 8.76 us
    ppermute x1, waiting for transfers between devices: 7.95 us -> 5.7 us  [body(): got = lax.ppermute(send, 'head', [(g, g ^ 1) for g in range(n_head)])]
  transfers between devices with their start and end apart: 31 -> 30, of which waited for: 15 -> 13; matrix products, arithmetic and copies ran while one was open for 0% -> 0% of each run, Pallas kernels for 22% -> 21%
where the time goes in v6:
time: 154 us; the launch traced here: 152 us
  waiting for transfers between devices  68.5 us (44%)
  starting transfers between devices  39.2 us (25%)
  Pallas kernels  33.8 us (22%)
  local copies, waits for them, and re-layouts  8.76 us (6%)
    ppermute x14, waiting for transfers between devices, hop(): held[group][place] = lax.ppermute(array, 'seq', z_shift(way))  39.5 us
    ppermute x14, starting transfers between devices, hop(): held[group][place] = lax.ppermute(array, 'seq', z_shift(way))  23.7 us
    pallas_call x2, Pallas kernels, attend(): pl.pallas_call(functools.partial(attend_kernel, heads, first, planes), ou...  20.3 us
    ppermute x6, waiting for transfers between devices, along_y(): lax.ppermute(array, 'head', y_shift(-dy))  10.8 us
    ppermute x3, waiting for transfers between devices, to_other(): return lax.ppermute(array, 'seq', swap)  9.41 us
    unnamed x25, local copies, waits for them, and re-layouts  8.76 us
    ppermute x6, starting transfers between devices, along_y(): lax.ppermute(array, 'head', y_shift(-dy))  6.75 us
    ppermute x1, waiting for transfers between devices, body(): got = lax.ppermute(send, 'head', [(g, g ^ 1) for g in range(n_head)])  5.7 us
  transfers between devices with their start and end apart: 30, of which 13 were waited for; matrix products, arithmetic and copies ran while one was open for 0% of the time, Pallas kernels for 21%

profile of v6, /device:TPU:4, one launch (start us, length us, event | category | flops | bytes accessed | tf_op | source)
XLA Modules:
  0.0 152.0 jit_solution(174175297785984716)
XLA Ops:
  0.6 1.0 copy-done.1
  1.7 1.0 copy-done.2
  2.7 1.1 pack.1
  3.8 1.9 %collective-permute-start.6 = (bf16[2304,128]{1,0:T(8,128)(2,1)}, bf16[2304,128]{1,0:T(8,128)(2,1)}, u32[]{:S(2)}, u32[]{:S(2)}) collective-permute-start(bf16[2304,128]{1,0:T(8,128)(2,1)} %get-tuple-element.71.refs_0_), channel_id=1, source_target_pairs={{0,32},{16,48},{32,64},{48,80},{64,96},{80,112},{96,128},{112,144}... | collective-permute-start | bytes 1769480 | tf_op jit(solution)/shard_map/ppermute | solution.py:416
  5.7 1.2 collective-permute-start
  6.9 3.9 %collective-permute-start.3 = (bf16[2304,128]{1,0:T(8,128)(2,1)}, bf16[2304,128]{1,0:T(8,128)(2,1)}, u32[]{:S(2)}, u32[]{:S(2)}) collective-permute-start(bf16[2304,128]{1,0:T(8,128)(2,1)} %get-tuple-element.71.refs_0_), channel_id=1, source_target_pairs={{0,224},{16,240},{32,0},{48,16},{64,32},{80,48},{96,64},{112,80},{... | collective-permute-start | bytes 1769480 | tf_op jit(solution)/shard_map/ppermute | solution.py:416
  10.9 7.8 %collective-permute-done.q_other_ref = bf16[384,640]{1,0:T(8,128)(2,1)S(1)} collective-permute-done((bf16[384,640]{1,0:T(8,128)(2,1)}, bf16[384,640]{1,0:T(8,128)(2,1)S(1)}, u32[]{:S(2)}, u32[]{:S(2)}) %collective-permute-start) | collective-permute-done | bytes 491552 | tf_op jit(solution)/shard_map/ppermute | solution.py:396
  18.6 0.8 copy-done.9
  19.4 2.9 %copy-done = bf16[640,5120]{1,0:T(8,128)(2,1)S(1)} copy-done((bf16[640,5120]{1,0:T(8,128)(2,1)S(1)}, bf16[640,5120]{1,0:T(8,128)(2,1)}, u32[]{:S(2)}) %copy-start) | copy-done | bytes 6553624
  22.3 0.6 tile.1
  22.9 0.9 copy-done.4
  23.8 3.0 %collective-permute-start.1 = (bf16[640,640]{1,0:T(8,128)(2,1)S(1)}, bf16[640,640]{1,0:T(8,128)(2,1)S(1)}, u32[]{:S(2)}, u32[]{:S(2)}) collective-permute-start(bf16[640,640]{1,0:T(8,128)(2,1)S(1)} %get-tuple-element.67), channel_id=1, source_target_pairs={{0,12},{2,14},{4,0},{6,2},{8,4},{10,6},{12,8},{14,10},{1,13},{3,15... | collective-permute-start | bytes 2457608 | tf_op jit(solution)/shard_map/ppermute | solution.py:439
  26.8 1.9 %collective-permute-start.7 = (bf16[2304,128]{1,0:T(8,128)(2,1)}, bf16[2304,128]{1,0:T(8,128)(2,1)}, u32[]{:S(2)}, u32[]{:S(2)}) collective-permute-start(bf16[2304,128]{1,0:T(8,128)(2,1)} %collective-permute-done.6.refs_1_), channel_id=1, source_target_pairs={{0,32},{16,48},{32,64},{48,80},{64,96},{80,112},{96,128},{112,144}... | collective-permute-start | bytes 1769480 | tf_op jit(solution)/shard_map/ppermute | solution.py:416
  28.7 2.4 %collective-permute-start.4 = (bf16[2304,128]{1,0:T(8,128)(2,1)}, bf16[2304,128]{1,0:T(8,128)(2,1)}, u32[]{:S(2)}, u32[]{:S(2)}) collective-permute-start(bf16[2304,128]{1,0:T(8,128)(2,1)} %collective-permute-done.3.refs_7_), channel_id=1, source_target_pairs={{0,224},{16,240},{32,0},{48,16},{64,32},{80,48},{96,64},{112,80},{... | collective-permute-start | bytes 1769480 | tf_op jit(solution)/shard_map/ppermute | solution.py:416
  31.1 1.9 %collective-permute-start.5 = (bf16[1536,128]{1,0:T(8,128)(2,1)}, bf16[1536,128]{1,0:T(8,128)(2,1)}, u32[]{:S(2)}, u32[]{:S(2)}) collective-permute-start(bf16[1536,128]{1,0:T(8,128)(2,1)} %get-tuple-element.73.refs_0_), channel_id=1, source_target_pairs={{0,224},{16,240},{32,0},{48,16},{64,32},{80,48},{96,64},{112,80},{... | collective-permute-start | bytes 1179656 | tf_op jit(solution)/shard_map/ppermute | solution.py:416
  33.0 10.6 %collective-permute-done.7.refs_2_ = bf16[2304,128]{1,0:T(8,128)(2,1)} collective-permute-done((bf16[2304,128]{1,0:T(8,128)(2,1)}, bf16[2304,128]{1,0:T(8,128)(2,1)}, u32[]{:S(2)}, u32[]{:S(2)}) %collective-permute-start.7) | collective-permute-done | bytes 589856 | tf_op jit(solution)/shard_map/ppermute | solution.py:416
  43.6 3.0 %collective-permute-done.8.refs_10_.refs_11_ = bf16[640,640]{1,0:T(8,128)(2,1)S(1)} collective-permute-done((bf16[640,640]{1,0:T(8,128)(2,1)S(1)}, bf16[640,640]{1,0:T(8,128)(2,1)S(1)}, u32[]{:S(2)}, u32[]{:S(2)}) %collective-permute-start.8) | collective-permute-done | bytes 819232 | tf_op jit(solution)/shard_map/ppermute | solution.py:439
  46.6 1.9 %collective-permute-start.9 = (bf16[2304,128]{1,0:T(8,128)(2,1)}, bf16[2304,128]{1,0:T(8,128)(2,1)}, u32[]{:S(2)}, u32[]{:S(2)}) collective-permute-start(bf16[2304,128]{1,0:T(8,128)(2,1)} %collective-permute-done.7.refs_2_), channel_id=1, source_target_pairs={{0,32},{16,48},{32,64},{48,80},{64,96},{80,112},{96,128},{112,144}... | collective-permute-start | bytes 1769480 | tf_op jit(solution)/shard_map/ppermute | solution.py:416
  48.6 3.2 %plan.1 = (s32[6,13]{1,0:T(8,128)S(1)}, s32[6]{0:T(128)S(1)}, s32[8]{0:T(128)S(1)}) custom-call(s32[1]{0:T(128)} %bitcast.2.seq_ref, s32[48,18]{1,0:T(8,128)S(1)} %copy.11.list_ref, s32[48]{0:T(128)S(1)} %copy-done.3), custom_call_target="tpu_custom_call" | custom-call | flops 1000 | bytes 8000 | tf_op jit(solution)/shard_map/plan/pallas_call | solution.py:61
  51.8 3.2 %collective-permute-start.14 = (bf16[2304,128]{1,0:T(8,128)(2,1)}, bf16[2304,128]{1,0:T(8,128)(2,1)S(1)}, u32[]{:S(2)}, u32[]{:S(2)}) collective-permute-start(bf16[2304,128]{1,0:T(8,128)(2,1)} %collective-permute-done.4.refs_6_), channel_id=1, source_target_pairs={{0,224},{16,240},{32,0},{48,16},{64,32},{80,48},{96,64},{112,80},{... | collective-permute-start | bytes 1769480 | tf_op jit(solution)/shard_map/ppermute | solution.py:416
  55.1 2.1 %collective-permute-done.10.refs_1_ = bf16[1536,128]{1,0:T(8,128)(2,1)} collective-permute-done((bf16[1536,128]{1,0:T(8,128)(2,1)}, bf16[1536,128]{1,0:T(8,128)(2,1)}, u32[]{:S(2)}, u32[]{:S(2)}) %collective-permute-start.10) | collective-permute-done | bytes 393248 | tf_op jit(solution)/shard_map/ppermute | solution.py:416
  57.2 1.9 %collective-permute-start.2 = (bf16[640,640]{1,0:T(8,128)(2,1)}, bf16[640,640]{1,0:T(8,128)(2,1)S(1)}, u32[]{:S(2)}, u32[]{:S(2)}) collective-permute-start(bf16[640,640]{1,0:T(8,128)(2,1)} %copy-done.4), channel_id=1, source_target_pairs={{0,8},{2,10},{4,12},{6,14},{8,0},{10,2},{12,4},{14,6},{1,9},{3,11}... | collective-permute-start | bytes 2457608 | tf_op jit(solution)/shard_map/ppermute | solution.py:441
  59.1 3.2 %collective-permute-start.13 = (bf16[1536,128]{1,0:T(8,128)(2,1)}, bf16[1536,128]{1,0:T(8,128)(2,1)S(1)}, u32[]{:S(2)}, u32[]{:S(2)}) collective-permute-start(bf16[1536,128]{1,0:T(8,128)(2,1)} %collective-permute-done.5.refs_7_), channel_id=1, source_target_pairs={{0,224},{16,240},{32,0},{48,16},{64,32},{80,48},{96,64},{112,80},{... | collective-permute-start | bytes 1179656 | tf_op jit(solution)/shard_map/ppermute | solution.py:416
  62.3 12.9 %collective-permute-done.11.refs_2_ = bf16[1536,128]{1,0:T(8,128)(2,1)S(1)} collective-permute-done((bf16[1536,128]{1,0:T(8,128)(2,1)}, bf16[1536,128]{1,0:T(8,128)(2,1)S(1)}, u32[]{:S(2)}, u32[]{:S(2)}) %collective-permute-start.11) | collective-permute-done | bytes 393248 | tf_op jit(solution)/shard_map/ppermute | solution.py:416
  75.3 3.2 %collective-permute-start.19 = (bf16[1536,128]{1,0:T(8,128)(2,1)S(1)}, bf16[1536,128]{1,0:T(8,128)(2,1)S(1)}, u32[]{:S(2)}, u32[]{:S(2)}) collective-permute-start(bf16[1536,128]{1,0:T(8,128)(2,1)S(1)} %collective-permute-done.13.refs_6_), channel_id=1, source_target_pairs={{0,224},{16,240},{32,0},{48,16},{64,32},{80,48},{96,64},{112,80},{... | collective-permute-start | bytes 1179656 | tf_op jit(solution)/shard_map/ppermute | solution.py:416
  78.5 0.5 collective-permute-start.17
  79.0 5.0 %collective-permute-done.19.refs_5_ = bf16[1536,128]{1,0:T(8,128)(2,1)S(1)} collective-permute-done((bf16[1536,128]{1,0:T(8,128)(2,1)S(1)}, bf16[1536,128]{1,0:T(8,128)(2,1)S(1)}, u32[]{:S(2)}, u32[]{:S(2)}) %collective-permute-start.19) | collective-permute-done | bytes 393248 | tf_op jit(solution)/shard_map/ppermute | solution.py:416
  84.0 9.0 %collective-permute-done.12.refs_4_ = bf16[2304,128]{1,0:T(8,128)(2,1)S(1)} collective-permute-done((bf16[2304,128]{1,0:T(8,128)(2,1)}, bf16[2304,128]{1,0:T(8,128)(2,1)S(1)}, u32[]{:S(2)}, u32[]{:S(2)}) %collective-permute-start.12) | collective-permute-done | bytes 589856 | tf_op jit(solution)/shard_map/ppermute | solution.py:416
  92.9 1.0 copy-done.7
  94.0 1.0 copy-done.10
  95.0 11.7 %attend.2 = (f32[1152,128]{1,0:T(8,128)S(1)}, f32[1152,128]{1,0:T(8,128)S(1)}, bf16[1536,128]{1,0:T(8,128)(2,1)S(1)}) custom-call(s32[1]{0:T(128)} %bitcast.2.seq_ref, s32[8]{0:T(128)S(1)} %get-tuple-element.105.near_ref, s32[6,13]{1,0:T(8,128)S(1)} %get-tuple-element.79.blocks_ref, s32[6]{0:T(128)S(1)} %get-tuple-element.80.count_ref, ...), custom_call_target="tpu_custom_call" | custom-call | flops 13589544960 | bytes 4718592 | tf_op jit(solution)/shard_map/attend/pallas_call | solution.py:227
  106.7 0.4 collective-permute-start.25
  107.2 8.6 %attend.3 = (f32[768,128]{1,0:T(8,128)S(1)}, f32[768,128]{1,0:T(8,128)S(1)}, bf16[1152,128]{1,0:T(8,128)(2,1)S(1)}) custom-call(s32[1]{0:T(128)} %bitcast.2.seq_ref, s32[8]{0:T(128)S(1)} %get-tuple-element.105.near_ref, s32[6,13]{1,0:T(8,128)S(1)} %get-tuple-element.79.blocks_ref, s32[6]{0:T(128)S(1)} %get-tuple-element.80.count_ref, ...), custom_call_target="tpu_custom_call" | custom-call | flops 9059696640 | bytes 3145728 | tf_op jit(solution)/shard_map/attend/pallas_call | solution.py:227
  115.8 1.1 collective-permute-start.21
  116.9 0.3 merge.3.refs_0_
  117.2 2.8 %collective-permute-start.26 = (bf16[384,384]{1,0:T(8,128)(2,1)S(1)}, bf16[384,384]{1,0:T(8,128)(2,1)S(1)}, u32[]{:S(2)}, u32[]{:S(2)}) collective-permute-start(bf16[384,384]{1,0:T(8,128)(2,1)S(1)} %merge.3.refs_0_), channel_id=1, source_target_pairs={{0,12},{2,14},{4,0},{6,2},{8,4},{10,6},{12,8},{14,10},{1,13},{3,15... | collective-permute-start | bytes 884744 | tf_op jit(solution)/shard_map/ppermute | solution.py:427
  120.0 1.0 collective-permute-start.28
  121.0 1.7 %collective-permute-done.21.refs_2_ = bf16[1152,128]{1,0:T(8,128)(2,1)S(1)} collective-permute-done((bf16[1152,128]{1,0:T(8,128)(2,1)S(1)}, bf16[1152,128]{1,0:T(8,128)(2,1)S(1)}, u32[]{:S(2)}, u32[]{:S(2)}) %collective-permute-start.21) | collective-permute-done | bytes 294944 | tf_op jit(solution)/shard_map/ppermute | solution.py:396
  122.9 2.7 %collective-permute-start.22 = (bf16[384,256]{1,0:T(8,128)(2,1)S(1)}, bf16[384,256]{1,0:T(8,128)(2,1)S(1)}, u32[]{:S(2)}, u32[]{:S(2)}) collective-permute-start(bf16[384,256]{1,0:T(8,128)(2,1)S(1)} %merge.2.refs_1_), channel_id=1, source_target_pairs={{0,12},{2,14},{4,0},{6,2},{8,4},{10,6},{12,8},{14,10},{1,13},{3,15... | collective-permute-start | bytes 589832 | tf_op jit(solution)/shard_map/ppermute | solution.py:427
  125.9 5.4 %collective-permute-done.26.refs_1_ = bf16[384,384]{1,0:T(8,128)(2,1)S(1)} collective-permute-done((bf16[384,384]{1,0:T(8,128)(2,1)S(1)}, bf16[384,384]{1,0:T(8,128)(2,1)S(1)}, u32[]{:S(2)}, u32[]{:S(2)}) %collective-permute-start.26) | collective-permute-done | bytes 294944 | tf_op jit(solution)/shard_map/ppermute | solution.py:427
  131.4 3.6 %collective-permute-done.28.refs_3_ = bf16[384,384]{1,0:T(8,128)(2,1)S(1)} collective-permute-done((bf16[384,384]{1,0:T(8,128)(2,1)S(1)}, bf16[384,384]{1,0:T(8,128)(2,1)S(1)}, u32[]{:S(2)}, u32[]{:S(2)}) %collective-permute-start.28) | collective-permute-done | bytes 294944 | tf_op jit(solution)/shard_map/ppermute | solution.py:427
  135.0 2.4 %project.2.refs_13_ = f32[2,384,640]{2,1,0:T(8,128)S(1)} custom-call(bf16[384,384]{1,0:T(8,128)(2,1)S(1)} %merge.3.refs_0_, bf16[384,384]{1,0:T(8,128)(2,1)S(1)} %collective-permute-done.26.refs_1_, bf16[384,384]{1,0:T(8,128)(2,1)S(1)} %collective-permute-done.27.refs_2_, bf16[384,384]{1,0:T(8,128)(2,1)S(1)} %collective-permute-done.28.refs_3_, ...), custom_call_target="tpu_custom_call" | custom-call | flops 1509949440 | bytes 5111808 | tf_op jit(solution)/shard_map/project/pallas_call | solution.py:371
  137.4 1.8 %collective-permute-done.24.refs_4_ = bf16[384,256]{1,0:T(8,128)(2,1)S(1)} collective-permute-done((bf16[384,256]{1,0:T(8,128)(2,1)S(1)}, bf16[384,256]{1,0:T(8,128)(2,1)S(1)}, u32[]{:S(2)}, u32[]{:S(2)}) %collective-permute-start.24) | collective-permute-done | bytes 196640 | tf_op jit(solution)/shard_map/ppermute | solution.py:427
  139.2 1.5 project.3
  140.7 0.6 collective-permute-start.29
  141.3 4.1 %cross.1 = bf16[384,640]{1,0:T(8,128)(2,1)} custom-call(bf16[384,640]{1,0:T(8,128)(2,1)S(1)} %copy-done.8, bf16[512,640]{1,0:T(8,128)(2,1)S(1)} %copy-done.5, bf16[512,640]{1,0:T(8,128)(2,1)S(1)} %copy-done.6), custom_call_target="tpu_custom_call" | custom-call | flops 5033164800 | bytes 983040 | tf_op jit(solution)/shard_map/cross/pallas_call | solution.py:333
  145.4 5.7 %collective-permute-done.29 = bf16[384,640]{1,0:T(8,128)(2,1)S(1)} collective-permute-done((bf16[384,640]{1,0:T(8,128)(2,1)S(1)}, bf16[384,640]{1,0:T(8,128)(2,1)S(1)}, u32[]{:S(2)}, u32[]{:S(2)}) %collective-permute-start.29) | collective-permute-done | bytes 491552 | tf_op jit(solution)/shard_map/ppermute | solution.py:465
  151.1 0.9 add_convert_fusion
  (48 shorter events, 0.8 us)
Async XLA Ops:
  0.6 1.0 copy-start.1
  1.7 1.0 copy-start.2
  2.7 45.8 %copy-start.11 = (s32[48,18]{0,1:T(8,128)S(1)}, s32[48,18]{0,1:T(8,128)}, u32[]{:S(2)}) copy-start(s32[48,18]{0,1:T(8,128)} %param.16) | copy-start | bytes 10372
  2.7 45.9 %copy-start.3 = (s32[48]{0:T(128)S(1)}, s32[48]{0:T(128)}, u32[]{:S(2)}) copy-start(s32[48]{0:T(128)} %count_ref.1) | copy-start | bytes 580
  3.8 23.0 %collective-permute-start.6 = (bf16[2304,128]{1,0:T(8,128)(2,1)}, bf16[2304,128]{1,0:T(8,128)(2,1)}, u32[]{:S(2)}, u32[]{:S(2)}) collective-permute-start(bf16[2304,128]{1,0:T(8,128)(2,1)} %get-tuple-element.71.refs_0_), channel_id=1, source_target_pairs={{0,32},{16,48},{32,64},{48,80},{64,96},{80,112},{96,128},{112,144}... | collective-permute-start | bytes 1769480 | tf_op jit(solution)/shard_map/ppermute | solution.py:416
  5.7 12.9 %collective-permute-start = (bf16[384,640]{1,0:T(8,128)(2,1)}, bf16[384,640]{1,0:T(8,128)(2,1)S(1)}, u32[]{:S(2)}, u32[]{:S(2)}) collective-permute-start(bf16[384,640]{1,0:T(8,128)(2,1)} %q_ref.4), channel_id=1, source_target_pairs={{0,16},{16,0},{32,48},{48,32},{64,80},{80,64},{96,112},{112,96},{1... | collective-permute-start | bytes 1474568 | tf_op jit(solution)/shard_map/ppermute | solution.py:396
  6.9 21.8 %collective-permute-start.3 = (bf16[2304,128]{1,0:T(8,128)(2,1)}, bf16[2304,128]{1,0:T(8,128)(2,1)}, u32[]{:S(2)}, u32[]{:S(2)}) collective-permute-start(bf16[2304,128]{1,0:T(8,128)(2,1)} %get-tuple-element.71.refs_0_), channel_id=1, source_target_pairs={{0,224},{16,240},{32,0},{48,16},{64,32},{80,48},{96,64},{112,80},{... | collective-permute-start | bytes 1769480 | tf_op jit(solution)/shard_map/ppermute | solution.py:416
  18.6 0.8 copy-start.9
  19.4 2.9 %copy-start = (bf16[640,5120]{1,0:T(8,128)(2,1)S(1)}, bf16[640,5120]{1,0:T(8,128)(2,1)}, u32[]{:S(2)}) copy-start(bf16[640,5120]{1,0:T(8,128)(2,1)} %weight_ref) | copy-start | bytes 19660804
  22.9 0.9 copy-start.4
  23.8 19.8 %collective-permute-start.1 = (bf16[640,640]{1,0:T(8,128)(2,1)S(1)}, bf16[640,640]{1,0:T(8,128)(2,1)S(1)}, u32[]{:S(2)}, u32[]{:S(2)}) collective-permute-start(bf16[640,640]{1,0:T(8,128)(2,1)S(1)} %get-tuple-element.67), channel_id=1, source_target_pairs={{0,12},{2,14},{4,0},{6,2},{8,4},{10,6},{12,8},{14,10},{1,13},{3,15... | collective-permute-start | bytes 2457608 | tf_op jit(solution)/shard_map/ppermute | solution.py:439
  26.8 19.8 %collective-permute-start.8 = (bf16[640,640]{1,0:T(8,128)(2,1)S(1)}, bf16[640,640]{1,0:T(8,128)(2,1)S(1)}, u32[]{:S(2)}, u32[]{:S(2)}) collective-permute-start(bf16[640,640]{1,0:T(8,128)(2,1)S(1)} %get-tuple-element.87), channel_id=1, source_target_pairs={{0,4},{2,6},{4,8},{6,10},{8,12},{10,14},{12,0},{14,2},{1,5},{3,7},... | collective-permute-start | bytes 2457608 | tf_op jit(solution)/shard_map/ppermute | solution.py:439
  26.8 16.8 %collective-permute-start.7 = (bf16[2304,128]{1,0:T(8,128)(2,1)}, bf16[2304,128]{1,0:T(8,128)(2,1)}, u32[]{:S(2)}, u32[]{:S(2)}) collective-permute-start(bf16[2304,128]{1,0:T(8,128)(2,1)} %collective-permute-done.6.refs_1_), channel_id=1, source_target_pairs={{0,32},{16,48},{32,64},{48,80},{64,96},{80,112},{96,128},{112,144}... | collective-permute-start | bytes 1769480 | tf_op jit(solution)/shard_map/ppermute | solution.py:416
  28.7 23.1 %collective-permute-start.4 = (bf16[2304,128]{1,0:T(8,128)(2,1)}, bf16[2304,128]{1,0:T(8,128)(2,1)}, u32[]{:S(2)}, u32[]{:S(2)}) collective-permute-start(bf16[2304,128]{1,0:T(8,128)(2,1)} %collective-permute-done.3.refs_7_), channel_id=1, source_target_pairs={{0,224},{16,240},{32,0},{48,16},{64,32},{80,48},{96,64},{112,80},{... | collective-permute-start | bytes 1769480 | tf_op jit(solution)/shard_map/ppermute | solution.py:416
  31.1 20.7 %collective-permute-start.5 = (bf16[1536,128]{1,0:T(8,128)(2,1)}, bf16[1536,128]{1,0:T(8,128)(2,1)}, u32[]{:S(2)}, u32[]{:S(2)}) collective-permute-start(bf16[1536,128]{1,0:T(8,128)(2,1)} %get-tuple-element.73.refs_0_), channel_id=1, source_target_pairs={{0,224},{16,240},{32,0},{48,16},{64,32},{80,48},{96,64},{112,80},{... | collective-permute-start | bytes 1179656 | tf_op jit(solution)/shard_map/ppermute | solution.py:416
  43.6 13.6 %collective-permute-start.10 = (bf16[1536,128]{1,0:T(8,128)(2,1)}, bf16[1536,128]{1,0:T(8,128)(2,1)}, u32[]{:S(2)}, u32[]{:S(2)}) collective-permute-start(bf16[1536,128]{1,0:T(8,128)(2,1)} %get-tuple-element.73.refs_0_), channel_id=1, source_target_pairs={{0,32},{16,48},{32,64},{48,80},{64,96},{80,112},{96,128},{112,144}... | collective-permute-start | bytes 1179656 | tf_op jit(solution)/shard_map/ppermute | solution.py:416
  46.6 28.7 %collective-permute-start.9 = (bf16[2304,128]{1,0:T(8,128)(2,1)}, bf16[2304,128]{1,0:T(8,128)(2,1)}, u32[]{:S(2)}, u32[]{:S(2)}) collective-permute-start(bf16[2304,128]{1,0:T(8,128)(2,1)} %collective-permute-done.7.refs_2_), channel_id=1, source_target_pairs={{0,32},{16,48},{32,64},{48,80},{64,96},{80,112},{96,128},{112,144}... | collective-permute-start | bytes 1769480 | tf_op jit(solution)/shard_map/ppermute | solution.py:416
  51.8 23.4 %collective-permute-start.14 = (bf16[2304,128]{1,0:T(8,128)(2,1)}, bf16[2304,128]{1,0:T(8,128)(2,1)S(1)}, u32[]{:S(2)}, u32[]{:S(2)}) collective-permute-start(bf16[2304,128]{1,0:T(8,128)(2,1)} %collective-permute-done.4.refs_6_), channel_id=1, source_target_pairs={{0,224},{16,240},{32,0},{48,16},{64,32},{80,48},{96,64},{112,80},{... | collective-permute-start | bytes 1769480 | tf_op jit(solution)/shard_map/ppermute | solution.py:416
  57.2 18.1 %collective-permute-start.11 = (bf16[1536,128]{1,0:T(8,128)(2,1)}, bf16[1536,128]{1,0:T(8,128)(2,1)S(1)}, u32[]{:S(2)}, u32[]{:S(2)}) collective-permute-start(bf16[1536,128]{1,0:T(8,128)(2,1)} %collective-permute-done.10.refs_1_), channel_id=1, source_target_pairs={{0,32},{16,48},{32,64},{48,80},{64,96},{80,112},{96,128},{112,144}... | collective-permute-start | bytes 1179656 | tf_op jit(solution)/shard_map/ppermute | solution.py:416
  57.2 21.8 %collective-permute-start.2 = (bf16[640,640]{1,0:T(8,128)(2,1)}, bf16[640,640]{1,0:T(8,128)(2,1)S(1)}, u32[]{:S(2)}, u32[]{:S(2)}) collective-permute-start(bf16[640,640]{1,0:T(8,128)(2,1)} %copy-done.4), channel_id=1, source_target_pairs={{0,8},{2,10},{4,12},{6,14},{8,0},{10,2},{12,4},{14,6},{1,9},{3,11}... | collective-permute-start | bytes 2457608 | tf_op jit(solution)/shard_map/ppermute | solution.py:441
  59.1 16.2 %collective-permute-start.13 = (bf16[1536,128]{1,0:T(8,128)(2,1)}, bf16[1536,128]{1,0:T(8,128)(2,1)S(1)}, u32[]{:S(2)}, u32[]{:S(2)}) collective-permute-start(bf16[1536,128]{1,0:T(8,128)(2,1)} %collective-permute-done.5.refs_7_), channel_id=1, source_target_pairs={{0,224},{16,240},{32,0},{48,16},{64,32},{80,48},{96,64},{112,80},{... | collective-permute-start | bytes 1179656 | tf_op jit(solution)/shard_map/ppermute | solution.py:416
  75.3 17.7 %collective-permute-start.12 = (bf16[2304,128]{1,0:T(8,128)(2,1)}, bf16[2304,128]{1,0:T(8,128)(2,1)S(1)}, u32[]{:S(2)}, u32[]{:S(2)}) collective-permute-start(bf16[2304,128]{1,0:T(8,128)(2,1)} %collective-permute-done.9.refs_3_), channel_id=1, source_target_pairs={{0,32},{16,48},{32,64},{48,80},{64,96},{80,112},{96,128},{112,144}... | collective-permute-start | bytes 1769480 | tf_op jit(solution)/shard_map/ppermute | solution.py:416
  75.3 8.7 %collective-permute-start.19 = (bf16[1536,128]{1,0:T(8,128)(2,1)S(1)}, bf16[1536,128]{1,0:T(8,128)(2,1)S(1)}, u32[]{:S(2)}, u32[]{:S(2)}) collective-permute-start(bf16[1536,128]{1,0:T(8,128)(2,1)S(1)} %collective-permute-done.13.refs_6_), channel_id=1, source_target_pairs={{0,224},{16,240},{32,0},{48,16},{64,32},{80,48},{96,64},{112,80},{... | collective-permute-start | bytes 1179656 | tf_op jit(solution)/shard_map/ppermute | solution.py:416
  78.5 28.2 %collective-permute-start.15 = (bf16[640,640]{1,0:T(8,128)(2,1)S(1)}, bf16[640,640]{1,0:T(8,128)(2,1)S(1)}, u32[]{:S(2)}, u32[]{:S(2)}) collective-permute-start(bf16[640,640]{1,0:T(8,128)(2,1)S(1)} %collective-permute-done.1.refs_6_.refs_7_), channel_id=1, source_target_pairs={{0,1},{1,0},{2,3},{3,2},{4,5},{5,4},{6,7},{7,6},{8,9},{9,8},{10,11... | collective-permute-start | bytes 2457608 | tf_op jit(solution)/shard_map/ppermute | solution.py:456
  78.5 28.7 %collective-permute-start.17 = (bf16[640,640]{1,0:T(8,128)(2,1)S(1)}, bf16[640,640]{1,0:T(8,128)(2,1)S(1)}, u32[]{:S(2)}, u32[]{:S(2)}) collective-permute-start(bf16[640,640]{1,0:T(8,128)(2,1)S(1)} %collective-permute-done.8.refs_10_.refs_11_), channel_id=1, source_target_pairs={{0,1},{1,0},{2,3},{3,2},{4,5},{5,4},{6,7},{7,6},{8,9},{9,8},{10,11... | collective-permute-start | bytes 2457608 | tf_op jit(solution)/shard_map/ppermute | solution.py:456
  79.0 28.1 %collective-permute-start.18 = (bf16[1536,128]{1,0:T(8,128)(2,1)S(1)}, bf16[1536,128]{1,0:T(8,128)(2,1)S(1)}, u32[]{:S(2)}, u32[]{:S(2)}) collective-permute-start(bf16[1536,128]{1,0:T(8,128)(2,1)S(1)} %collective-permute-done.11.refs_2_), channel_id=1, source_target_pairs={{0,32},{16,48},{32,64},{48,80},{64,96},{80,112},{96,128},{112,144}... | collective-permute-start | bytes 1179656 | tf_op jit(solution)/shard_map/ppermute | solution.py:416
  84.0 23.2 %collective-permute-start.16 = (bf16[640,640]{1,0:T(8,128)(2,1)S(1)}, bf16[640,640]{1,0:T(8,128)(2,1)S(1)}, u32[]{:S(2)}, u32[]{:S(2)}) collective-permute-start(bf16[640,640]{1,0:T(8,128)(2,1)S(1)} %collective-permute-done.2.refs_8_.refs_9_), channel_id=1, source_target_pairs={{0,1},{1,0},{2,3},{3,2},{4,5},{5,4},{6,7},{7,6},{8,9},{9,8},{10,11... | collective-permute-start | bytes 2457608 | tf_op jit(solution)/shard_map/ppermute | solution.py:456
  92.9 14.2 %collective-permute-start.20 = (bf16[1536,128]{1,0:T(8,128)(2,1)S(1)}, bf16[1536,128]{1,0:T(8,128)(2,1)S(1)}, u32[]{:S(2)}, u32[]{:S(2)}) collective-permute-start(bf16[1536,128]{1,0:T(8,128)(2,1)S(1)} %collective-permute-done.19.refs_5_), channel_id=1, source_target_pairs={{0,224},{16,240},{32,0},{48,16},{64,32},{80,48},{96,64},{112,80},{... | collective-permute-start | bytes 1179656 | tf_op jit(solution)/shard_map/ppermute | solution.py:416
  92.9 1.0 copy-start.7
  94.0 1.0 copy-start.10
  106.7 10.2 %collective-permute-start.25 = (bf16[1536,128]{1,0:T(8,128)(2,1)S(1)}, bf16[1536,128]{1,0:T(8,128)(2,1)S(1)}, u32[]{:S(2)}, u32[]{:S(2)}) collective-permute-start(bf16[1536,128]{1,0:T(8,128)(2,1)S(1)} %get-tuple-element.125), channel_id=1, source_target_pairs={{0,16},{16,0},{32,48},{48,32},{64,80},{80,64},{96,112},{112,96},{1... | collective-permute-start | bytes 1179656 | tf_op jit(solution)/shard_map/ppermute | solution.py:396
  115.8 6.8 %collective-permute-start.21 = (bf16[1152,128]{1,0:T(8,128)(2,1)S(1)}, bf16[1152,128]{1,0:T(8,128)(2,1)S(1)}, u32[]{:S(2)}, u32[]{:S(2)}) collective-permute-start(bf16[1152,128]{1,0:T(8,128)(2,1)S(1)} %get-tuple-element.114), channel_id=1, source_target_pairs={{0,16},{16,0},{32,48},{48,32},{64,80},{80,64},{96,112},{112,96},{1... | collective-permute-start | bytes 884744 | tf_op jit(solution)/shard_map/ppermute | solution.py:396
  117.2 14.0 %collective-permute-start.26 = (bf16[384,384]{1,0:T(8,128)(2,1)S(1)}, bf16[384,384]{1,0:T(8,128)(2,1)S(1)}, u32[]{:S(2)}, u32[]{:S(2)}) collective-permute-start(bf16[384,384]{1,0:T(8,128)(2,1)S(1)} %merge.3.refs_0_), channel_id=1, source_target_pairs={{0,12},{2,14},{4,0},{6,2},{8,4},{10,6},{12,8},{14,10},{1,13},{3,15... | collective-permute-start | bytes 884744 | tf_op jit(solution)/shard_map/ppermute | solution.py:427
  120.0 11.4 %collective-permute-start.27 = (bf16[384,384]{1,0:T(8,128)(2,1)S(1)}, bf16[384,384]{1,0:T(8,128)(2,1)S(1)}, u32[]{:S(2)}, u32[]{:S(2)}) collective-permute-start(bf16[384,384]{1,0:T(8,128)(2,1)S(1)} %merge.3.refs_0_), channel_id=1, source_target_pairs={{0,8},{2,10},{4,12},{6,14},{8,0},{10,2},{12,4},{14,6},{1,9},{3,11}... | collective-permute-start | bytes 884744 | tf_op jit(solution)/shard_map/ppermute | solution.py:427
  120.0 14.9 %collective-permute-start.28 = (bf16[384,384]{1,0:T(8,128)(2,1)S(1)}, bf16[384,384]{1,0:T(8,128)(2,1)S(1)}, u32[]{:S(2)}, u32[]{:S(2)}) collective-permute-start(bf16[384,384]{1,0:T(8,128)(2,1)S(1)} %merge.3.refs_0_), channel_id=1, source_target_pairs={{0,4},{2,6},{4,8},{6,10},{8,12},{10,14},{12,0},{14,2},{1,5},{3,7},... | collective-permute-start | bytes 884744 | tf_op jit(solution)/shard_map/ppermute | solution.py:427
  122.9 14.5 %collective-permute-start.22 = (bf16[384,256]{1,0:T(8,128)(2,1)S(1)}, bf16[384,256]{1,0:T(8,128)(2,1)S(1)}, u32[]{:S(2)}, u32[]{:S(2)}) collective-permute-start(bf16[384,256]{1,0:T(8,128)(2,1)S(1)} %merge.2.refs_1_), channel_id=1, source_target_pairs={{0,12},{2,14},{4,0},{6,2},{8,4},{10,6},{12,8},{14,10},{1,13},{3,15... | collective-permute-start | bytes 589832 | tf_op jit(solution)/shard_map/ppermute | solution.py:427
  125.6 11.8 %collective-permute-start.23 = (bf16[384,256]{1,0:T(8,128)(2,1)S(1)}, bf16[384,256]{1,0:T(8,128)(2,1)S(1)}, u32[]{:S(2)}, u32[]{:S(2)}) collective-permute-start(bf16[384,256]{1,0:T(8,128)(2,1)S(1)} %merge.2.refs_1_), channel_id=1, source_target_pairs={{0,8},{2,10},{4,12},{6,14},{8,0},{10,2},{12,4},{14,6},{1,9},{3,11}... | collective-permute-start | bytes 589832 | tf_op jit(solution)/shard_map/ppermute | solution.py:427
  131.3 7.9 %collective-permute-start.24 = (bf16[384,256]{1,0:T(8,128)(2,1)S(1)}, bf16[384,256]{1,0:T(8,128)(2,1)S(1)}, u32[]{:S(2)}, u32[]{:S(2)}) collective-permute-start(bf16[384,256]{1,0:T(8,128)(2,1)S(1)} %merge.2.refs_1_), channel_id=1, source_target_pairs={{0,4},{2,6},{4,8},{6,10},{8,12},{10,14},{12,0},{14,2},{1,5},{3,7},... | collective-permute-start | bytes 589832 | tf_op jit(solution)/shard_map/ppermute | solution.py:427
  137.4 4.0 %copy-start.5 = (bf16[512,640]{1,0:T(8,128)(2,1)S(1)}, bf16[512,640]{1,0:T(8,128)(2,1)}, u32[]{:S(2)}) copy-start(bf16[512,640]{1,0:T(8,128)(2,1)} %k_ref.3) | copy-start | bytes 1966084
  137.4 3.9 %copy-start.6 = (bf16[512,640]{1,0:T(8,128)(2,1)S(1)}, bf16[512,640]{1,0:T(8,128)(2,1)}, u32[]{:S(2)}) copy-start(bf16[512,640]{1,0:T(8,128)(2,1)} %v_ref.3) | copy-start | bytes 1966084
  137.4 3.9 %copy-start.8 = (bf16[384,640]{1,0:T(8,128)(2,1)S(1)}, bf16[384,640]{1,0:T(8,128)(2,1)}, u32[]{:S(2)}) copy-start(bf16[384,640]{1,0:T(8,128)(2,1)} %q_ref.5) | copy-start | bytes 1474564
  140.7 10.4 %collective-permute-start.29 = (bf16[384,640]{1,0:T(8,128)(2,1)S(1)}, bf16[384,640]{1,0:T(8,128)(2,1)S(1)}, u32[]{:S(2)}, u32[]{:S(2)}) collective-permute-start(bf16[384,640]{1,0:T(8,128)(2,1)S(1)} %get-tuple-element.127), channel_id=1, source_target_pairs={{0,2},{2,0},{4,6},{6,4},{8,10},{10,8},{12,14},{14,12},{1,3},{3,1},... | collective-permute-start | bytes 1474568 | tf_op jit(solution)/shard_map/ppermute | solution.py:465

commit v7 on v6

--- a/solution.py
+++ b/solution.py
@@ -431,7 +431,7 @@
         hop(-1, group, 1)
     queries_other = to_other(queries)
     early = list(plan(n_seq, seq, block_list, block_count))
-    out_weight, queries_other = lax.optimization_barrier((out_weight, queries_other))
+    out_weight, held[0][1] = lax.optimization_barrier((out_weight, held[0][1]))
     tiles = list(tile(lax.div(head, 2), pair, out_weight, n_y))
     early[0], tiles[0], queries_other = lax.optimization_barrier((early[0], tiles[0], queries_other))
     hop(1, 0, 2)
@@ -440,12 +440,12 @@
     arrived[1], tiles[2] = lax.optimization_barrier((arrived[1], tiles[2]))
     tiles[1:n_y] = [arrived[1], lax.ppermute(tiles[2], "head", y_shift(2)), arrived[0]]
     hop(1, 1, 2)
-    one_away = [(tiles[1], tiles[n_y - 1])]
-    hop(1, 0, 3, one_away)
-    tiles[1], tiles[n_y - 1] = one_away[0]
+    hop(1, 0, 3)
     hop(-1, 0, 3, early)
     blocks, counts, near = early
-    hop(1, 0, 4)
+    one_away = [(tiles[1], tiles[n_y - 1])]
+    hop(1, 0, 4, one_away)
+    tiles[1], tiles[n_y - 1] = one_away[0]
     hop(-1, 1, 2)
     hop(-1, 1, 3)
     hop(1, 1, 3)

time: 154 us -> 156 us (1.013); the launches traced: 152 us -> 157 us
  Pallas kernels: 33.8 us -> 38.8 us
  starting transfers between devices: 39.2 us -> 42.3 us
  local copies, waits for them, and re-layouts: 8.76 us -> 6.95 us
    ppermute x3, waiting for transfers between devices: 9.41 us -> 4.41 us  [to_other(): return lax.ppermute(array, 'seq', swap)]
    ppermute x1, waiting for transfers between devices: 5.7 us -> 9.87 us  [body(): got = lax.ppermute(send, 'head', [(g, g ^ 1) for g in range(n_head)])]
    pallas_call x2, Pallas kernels: 20.3 us -> 24.3 us  [attend(): pl.pallas_call(functools.partial(attend_kernel, heads, first, planes), ou...]
    ppermute x2, waiting for transfers between devices: 3 us -> 0.01 us  [body(): lax.ppermute(tiles[dy], 'head', y_shift(dy))]
    ppermute x6, waiting for transfers between devices: 10.8 us -> 13 us  [along_y(): lax.ppermute(array, 'head', y_shift(-dy))]
    unnamed x25 -> x21, local copies, waits for them, and re-layouts: 8.76 us -> 6.95 us
    ppermute x6, starting transfers between devices: 6.75 us -> 8.39 us  [along_y(): lax.ppermute(array, 'head', y_shift(-dy))]
  transfers between devices with their start and end apart: 30 -> 30, of which waited for: 13 -> 13; matrix products, arithmetic and copies ran while one was open for 0% -> 0% of each run, Pallas kernels for 21% -> 23%
where the time goes in v7:
time: 156 us; the launch traced here: 157 us
  waiting for transfers between devices  67.5 us (43%)
  starting transfers between devices  42.3 us (27%)
  Pallas kernels  38.8 us (25%)
  local copies, waits for them, and re-layouts  6.95 us (4%)
    ppermute x14, waiting for transfers between devices, hop(): held[group][place] = lax.ppermute(array, 'seq', z_shift(way))  40.1 us
    ppermute x14, starting transfers between devices, hop(): held[group][place] = lax.ppermute(array, 'seq', z_shift(way))  25.2 us
    pallas_call x2, Pallas kernels, attend(): pl.pallas_call(functools.partial(attend_kernel, heads, first, planes), ou...  24.3 us
    ppermute x6, waiting for transfers between devices, along_y(): lax.ppermute(array, 'head', y_shift(-dy))  13 us
    ppermute x1, waiting for transfers between devices, body(): got = lax.ppermute(send, 'head', [(g, g ^ 1) for g in range(n_head)])  9.87 us
    ppermute x6, starting transfers between devices, along_y(): lax.ppermute(array, 'head', y_shift(-dy))  8.39 us
    unnamed x21, local copies, waits for them, and re-layouts  6.95 us
    ppermute x3, waiting for transfers between devices, to_other(): return lax.ppermute(array, 'seq', swap)  4.41 us
  transfers between devices with their start and end apart: 30, of which 13 were waited for; matrix products, arithmetic and copies ran while one was open for 0% of the time, Pallas kernels for 23%

profile of v7, /device:TPU:4, one launch (start us, length us, event | category | flops | bytes accessed | tf_op | source)
XLA Modules:
  0.0 157.1 jit_solution(11554969273620541893)
XLA Ops:
  0.6 1.0 copy-done.1
  1.7 1.0 copy-done.2
  2.7 1.1 pack.1
  3.8 1.9 %collective-permute-start = (bf16[2304,128]{1,0:T(8,128)(2,1)}, bf16[2304,128]{1,0:T(8,128)(2,1)}, u32[]{:S(2)}, u32[]{:S(2)}) collective-permute-start(bf16[2304,128]{1,0:T(8,128)(2,1)} %get-tuple-element.66.refs_0_), channel_id=1, source_target_pairs={{0,32},{16,48},{32,64},{48,80},{64,96},{80,112},{96,128},{112,144}... | collective-permute-start | bytes 1769480 | tf_op jit(solution)/shard_map/ppermute | solution.py:416
  5.7 3.9 %collective-permute-start.3 = (bf16[2304,128]{1,0:T(8,128)(2,1)}, bf16[2304,128]{1,0:T(8,128)(2,1)}, u32[]{:S(2)}, u32[]{:S(2)}) collective-permute-start(bf16[2304,128]{1,0:T(8,128)(2,1)} %get-tuple-element.66.refs_0_), channel_id=1, source_target_pairs={{0,224},{16,240},{32,0},{48,16},{64,32},{80,48},{96,64},{112,80},{... | collective-permute-start | bytes 1769480 | tf_op jit(solution)/shard_map/ppermute | solution.py:416
  9.7 2.0 %collective-permute-start.5 = (bf16[1536,128]{1,0:T(8,128)(2,1)}, bf16[1536,128]{1,0:T(8,128)(2,1)}, u32[]{:S(2)}, u32[]{:S(2)}) collective-permute-start(bf16[1536,128]{1,0:T(8,128)(2,1)} %get-tuple-element.73.refs_0_), channel_id=1, source_target_pairs={{0,224},{16,240},{32,0},{48,16},{64,32},{80,48},{96,64},{112,80},{... | collective-permute-start | bytes 1179656 | tf_op jit(solution)/shard_map/ppermute | solution.py:416
  11.7 12.4 %collective-permute-done.refs_1_ = bf16[2304,128]{1,0:T(8,128)(2,1)} collective-permute-done((bf16[2304,128]{1,0:T(8,128)(2,1)}, bf16[2304,128]{1,0:T(8,128)(2,1)}, u32[]{:S(2)}, u32[]{:S(2)}) %collective-permute-start) | collective-permute-done | bytes 589856 | tf_op jit(solution)/shard_map/ppermute | solution.py:416
  24.1 1.2 collective-permute-start.6
  25.3 2.9 %copy-done = bf16[640,5120]{1,0:T(8,128)(2,1)S(1)} copy-done((bf16[640,5120]{1,0:T(8,128)(2,1)S(1)}, bf16[640,5120]{1,0:T(8,128)(2,1)}, u32[]{:S(2)}) %copy-start) | copy-done | bytes 6553624
  28.2 1.4 tile.1
  29.6 0.9 copy-done.4
  30.5 3.0 %collective-permute-start.1 = (bf16[640,640]{1,0:T(8,128)(2,1)}, bf16[640,640]{1,0:T(8,128)(2,1)S(1)}, u32[]{:S(2)}, u32[]{:S(2)}) collective-permute-start(bf16[640,640]{1,0:T(8,128)(2,1)} %get-tuple-element.68), channel_id=1, source_target_pairs={{0,12},{2,14},{4,0},{6,2},{8,4},{10,6},{12,8},{14,10},{1,13},{3,15... | collective-permute-start | bytes 2457608 | tf_op jit(solution)/shard_map/ppermute | solution.py:439
  33.5 3.2 %collective-permute-start.4 = (bf16[2304,128]{1,0:T(8,128)(2,1)}, bf16[2304,128]{1,0:T(8,128)(2,1)}, u32[]{:S(2)}, u32[]{:S(2)}) collective-permute-start(bf16[2304,128]{1,0:T(8,128)(2,1)} %collective-permute-done.3.refs_7_), channel_id=1, source_target_pairs={{0,224},{16,240},{32,0},{48,16},{64,32},{80,48},{96,64},{112,80},{... | collective-permute-start | bytes 1769480 | tf_op jit(solution)/shard_map/ppermute | solution.py:416
  36.7 7.6 %collective-permute-done.7.refs_2_ = bf16[2304,128]{1,0:T(8,128)(2,1)} collective-permute-done((bf16[2304,128]{1,0:T(8,128)(2,1)}, bf16[2304,128]{1,0:T(8,128)(2,1)}, u32[]{:S(2)}, u32[]{:S(2)}) %collective-permute-start.7) | collective-permute-done | bytes 589856 | tf_op jit(solution)/shard_map/ppermute | solution.py:416
  44.5 3.3 %plan.1 = (s32[6,13]{1,0:T(8,128)S(1)}, s32[6]{0:T(128)S(1)}, s32[8]{0:T(128)S(1)}) custom-call(s32[1]{0:T(128)} %bitcast.2.seq_ref, s32[48,18]{1,0:T(8,128)S(1)} %copy.11.list_ref, s32[48]{0:T(128)S(1)} %copy-done.3), custom_call_target="tpu_custom_call" | custom-call | flops 1000 | bytes 8000 | tf_op jit(solution)/shard_map/plan/pallas_call | solution.py:61
  47.8 3.4 %collective-permute-start.14 = (bf16[2304,128]{1,0:T(8,128)(2,1)}, bf16[2304,128]{1,0:T(8,128)(2,1)S(1)}, u32[]{:S(2)}, u32[]{:S(2)}) collective-permute-start(bf16[2304,128]{1,0:T(8,128)(2,1)} %collective-permute-done.4.refs_6_), channel_id=1, source_target_pairs={{0,224},{16,240},{32,0},{48,16},{64,32},{80,48},{96,64},{112,80},{... | collective-permute-start | bytes 1769480 | tf_op jit(solution)/shard_map/ppermute | solution.py:416
  51.2 3.2 %collective-permute-start.2 = (bf16[640,640]{1,0:T(8,128)(2,1)}, bf16[640,640]{1,0:T(8,128)(2,1)S(1)}, u32[]{:S(2)}, u32[]{:S(2)}) collective-permute-start(bf16[640,640]{1,0:T(8,128)(2,1)} %copy-done.4), channel_id=1, source_target_pairs={{0,8},{2,10},{4,12},{6,14},{8,0},{10,2},{12,4},{14,6},{1,9},{3,11}... | collective-permute-start | bytes 2457608 | tf_op jit(solution)/shard_map/ppermute | solution.py:441
  54.4 3.5 %collective-permute-done.10.refs_2_ = bf16[1536,128]{1,0:T(8,128)(2,1)} collective-permute-done((bf16[1536,128]{1,0:T(8,128)(2,1)}, bf16[1536,128]{1,0:T(8,128)(2,1)}, u32[]{:S(2)}, u32[]{:S(2)}) %collective-permute-start.10) | collective-permute-done | bytes 393248 | tf_op jit(solution)/shard_map/ppermute | solution.py:416
  57.9 0.5 collective-permute-start.13
  58.5 10.4 %collective-permute-done.8.refs_3_ = bf16[2304,128]{1,0:T(8,128)(2,1)} collective-permute-done((bf16[2304,128]{1,0:T(8,128)(2,1)}, bf16[2304,128]{1,0:T(8,128)(2,1)}, u32[]{:S(2)}, u32[]{:S(2)}) %collective-permute-start.8) | collective-permute-done | bytes 589856 | tf_op jit(solution)/shard_map/ppermute | solution.py:416
  68.8 3.4 %collective-permute-start.12 = (bf16[2304,128]{1,0:T(8,128)(2,1)}, bf16[2304,128]{1,0:T(8,128)(2,1)S(1)}, u32[]{:S(2)}, u32[]{:S(2)}) collective-permute-start(bf16[2304,128]{1,0:T(8,128)(2,1)} %collective-permute-done.8.refs_3_), channel_id=1, source_target_pairs={{0,32},{16,48},{32,64},{48,80},{64,96},{80,112},{96,128},{112,144}... | collective-permute-start | bytes 1769480 | tf_op jit(solution)/shard_map/ppermute | solution.py:416
  72.3 3.0 %collective-permute-start.19 = (bf16[1536,128]{1,0:T(8,128)(2,1)S(1)}, bf16[1536,128]{1,0:T(8,128)(2,1)S(1)}, u32[]{:S(2)}, u32[]{:S(2)}) collective-permute-start(bf16[1536,128]{1,0:T(8,128)(2,1)S(1)} %collective-permute-done.13.refs_6_), channel_id=1, source_target_pairs={{0,224},{16,240},{32,0},{48,16},{64,32},{80,48},{96,64},{112,80},{... | collective-permute-start | bytes 1179656 | tf_op jit(solution)/shard_map/ppermute | solution.py:416
  75.3 0.5 collective-permute-start.17
  75.8 6.1 %collective-permute-done.19.refs_5_ = bf16[1536,128]{1,0:T(8,128)(2,1)S(1)} collective-permute-done((bf16[1536,128]{1,0:T(8,128)(2,1)S(1)}, bf16[1536,128]{1,0:T(8,128)(2,1)S(1)}, u32[]{:S(2)}, u32[]{:S(2)}) %collective-permute-start.19) | collective-permute-done | bytes 393248 | tf_op jit(solution)/shard_map/ppermute | solution.py:416
  81.9 1.4 collective-permute-start.18
  83.3 2.3 %collective-permute-start.20 = (bf16[1536,128]{1,0:T(8,128)(2,1)S(1)}, bf16[1536,128]{1,0:T(8,128)(2,1)S(1)}, u32[]{:S(2)}, u32[]{:S(2)}) collective-permute-start(bf16[1536,128]{1,0:T(8,128)(2,1)S(1)} %collective-permute-done.19.refs_5_), channel_id=1, source_target_pairs={{0,224},{16,240},{32,0},{48,16},{64,32},{80,48},{96,64},{112,80},{... | collective-permute-start | bytes 1179656 | tf_op jit(solution)/shard_map/ppermute | solution.py:416
  85.6 1.0 copy-done.7
  86.6 13.8 %attend.2 = (f32[1152,128]{1,0:T(8,128)S(1)}, f32[1152,128]{1,0:T(8,128)S(1)}, bf16[1536,128]{1,0:T(8,128)(2,1)S(1)}) custom-call(s32[1]{0:T(128)} %bitcast.2.seq_ref, s32[8]{0:T(128)S(1)} %get-tuple-element.105.near_ref, s32[6,13]{1,0:T(8,128)S(1)} %get-tuple-element.78.blocks_ref, s32[6]{0:T(128)S(1)} %get-tuple-element.79.count_ref, ...), custom_call_target="tpu_custom_call" | custom-call | flops 13589544960 | bytes 4718592 | tf_op jit(solution)/shard_map/attend/pallas_call | solution.py:227
  100.7 10.5 %attend.3 = (f32[768,128]{1,0:T(8,128)S(1)}, f32[768,128]{1,0:T(8,128)S(1)}, bf16[1152,128]{1,0:T(8,128)(2,1)S(1)}) custom-call(s32[1]{0:T(128)} %bitcast.2.seq_ref, s32[8]{0:T(128)S(1)} %get-tuple-element.105.near_ref, s32[6,13]{1,0:T(8,128)S(1)} %get-tuple-element.78.blocks_ref, s32[6]{0:T(128)S(1)} %get-tuple-element.79.count_ref, ...), custom_call_target="tpu_custom_call" | custom-call | flops 9059696640 | bytes 3145728 | tf_op jit(solution)/shard_map/attend/pallas_call | solution.py:227
  111.3 0.9 collective-permute-done.25.refs_2_
  112.1 0.3 merge.3.refs_0_
  112.5 3.1 %collective-permute-start.26 = (bf16[384,384]{1,0:T(8,128)(2,1)S(1)}, bf16[384,384]{1,0:T(8,128)(2,1)S(1)}, u32[]{:S(2)}, u32[]{:S(2)}) collective-permute-start(bf16[384,384]{1,0:T(8,128)(2,1)S(1)} %merge.3.refs_0_), channel_id=1, source_target_pairs={{0,12},{2,14},{4,0},{6,2},{8,4},{10,6},{12,8},{14,10},{1,13},{3,15... | collective-permute-start | bytes 884744 | tf_op jit(solution)/shard_map/ppermute | solution.py:427
  115.6 0.6 collective-permute-start.27
  116.2 1.0 collective-permute-start.28
  117.2 3.5 %collective-permute-done.21.refs_2_ = bf16[1152,128]{1,0:T(8,128)(2,1)S(1)} collective-permute-done((bf16[1152,128]{1,0:T(8,128)(2,1)S(1)}, bf16[1152,128]{1,0:T(8,128)(2,1)S(1)}, u32[]{:S(2)}, u32[]{:S(2)}) %collective-permute-start.21) | collective-permute-done | bytes 294944 | tf_op jit(solution)/shard_map/ppermute | solution.py:396
  120.9 3.1 %collective-permute-start.22 = (bf16[384,256]{1,0:T(8,128)(2,1)S(1)}, bf16[384,256]{1,0:T(8,128)(2,1)S(1)}, u32[]{:S(2)}, u32[]{:S(2)}) collective-permute-start(bf16[384,256]{1,0:T(8,128)(2,1)S(1)} %merge.2.refs_1_), channel_id=1, source_target_pairs={{0,12},{2,14},{4,0},{6,2},{8,4},{10,6},{12,8},{14,10},{1,13},{3,15... | collective-permute-start | bytes 589832 | tf_op jit(solution)/shard_map/ppermute | solution.py:427
  124.0 0.6 collective-permute-start.23
  124.7 4.7 %collective-permute-done.26.refs_1_ = bf16[384,384]{1,0:T(8,128)(2,1)S(1)} collective-permute-done((bf16[384,384]{1,0:T(8,128)(2,1)S(1)}, bf16[384,384]{1,0:T(8,128)(2,1)S(1)}, u32[]{:S(2)}, u32[]{:S(2)}) %collective-permute-start.26) | collective-permute-done | bytes 294944 | tf_op jit(solution)/shard_map/ppermute | solution.py:427
  129.3 4.1 %collective-permute-done.28.refs_3_ = bf16[384,384]{1,0:T(8,128)(2,1)S(1)} collective-permute-done((bf16[384,384]{1,0:T(8,128)(2,1)S(1)}, bf16[384,384]{1,0:T(8,128)(2,1)S(1)}, u32[]{:S(2)}, u32[]{:S(2)}) %collective-permute-start.28) | collective-permute-done | bytes 294944 | tf_op jit(solution)/shard_map/ppermute | solution.py:427
  133.4 2.4 %project.2.refs_13_ = f32[2,384,640]{2,1,0:T(8,128)S(1)} custom-call(bf16[384,384]{1,0:T(8,128)(2,1)S(1)} %merge.3.refs_0_, bf16[384,384]{1,0:T(8,128)(2,1)S(1)} %collective-permute-done.26.refs_1_, bf16[384,384]{1,0:T(8,128)(2,1)S(1)} %collective-permute-done.27.refs_2_, bf16[384,384]{1,0:T(8,128)(2,1)S(1)} %collective-permute-done.28.refs_3_, ...), custom_call_target="tpu_custom_call" | custom-call | flops 1509949440 | bytes 5111808 | tf_op jit(solution)/shard_map/project/pallas_call | solution.py:371
  135.9 0.6 collective-permute-done.22.refs_2_
  136.4 1.2 collective-permute-done.23.refs_3_
  137.6 2.5 %collective-permute-done.24.refs_4_ = bf16[384,256]{1,0:T(8,128)(2,1)S(1)} collective-permute-done((bf16[384,256]{1,0:T(8,128)(2,1)S(1)}, bf16[384,256]{1,0:T(8,128)(2,1)S(1)}, u32[]{:S(2)}, u32[]{:S(2)}) %collective-permute-start.24) | collective-permute-done | bytes 196640 | tf_op jit(solution)/shard_map/ppermute | solution.py:427
  140.2 1.5 project.3
  141.7 0.6 collective-permute-start.29
  142.3 4.1 %cross.1 = bf16[384,640]{1,0:T(8,128)(2,1)} custom-call(bf16[384,640]{1,0:T(8,128)(2,1)S(1)} %copy-done.8, bf16[512,640]{1,0:T(8,128)(2,1)S(1)} %copy-done.5, bf16[512,640]{1,0:T(8,128)(2,1)S(1)} %copy-done.6), custom_call_target="tpu_custom_call" | custom-call | flops 5033164800 | bytes 983040 | tf_op jit(solution)/shard_map/cross/pallas_call | solution.py:333
  146.4 9.9 %collective-permute-done.29 = bf16[384,640]{1,0:T(8,128)(2,1)S(1)} collective-permute-done((bf16[384,640]{1,0:T(8,128)(2,1)S(1)}, bf16[384,640]{1,0:T(8,128)(2,1)S(1)}, u32[]{:S(2)}, u32[]{:S(2)}) %collective-permute-start.29) | collective-permute-done | bytes 491552 | tf_op jit(solution)/shard_map/ppermute | solution.py:465
  156.3 0.9 add_convert_fusion
  (44 shorter events, 0.6 us)
Async XLA Ops:
  0.6 1.0 copy-start.1
  1.7 1.0 copy-start.2
  2.7 41.7 %copy-start.9 = (s32[48,18]{0,1:T(8,128)S(1)}, s32[48,18]{0,1:T(8,128)}, u32[]{:S(2)}) copy-start(s32[48,18]{0,1:T(8,128)} %param.16) | copy-start | bytes 10372
  2.7 41.8 %copy-start.3 = (s32[48]{0:T(128)S(1)}, s32[48]{0:T(128)}, u32[]{:S(2)}) copy-start(s32[48]{0:T(128)} %count_ref.1) | copy-start | bytes 580
  3.8 20.3 %collective-permute-start = (bf16[2304,128]{1,0:T(8,128)(2,1)}, bf16[2304,128]{1,0:T(8,128)(2,1)}, u32[]{:S(2)}, u32[]{:S(2)}) collective-permute-start(bf16[2304,128]{1,0:T(8,128)(2,1)} %get-tuple-element.66.refs_0_), channel_id=1, source_target_pairs={{0,32},{16,48},{32,64},{48,80},{64,96},{80,112},{96,128},{112,144}... | collective-permute-start | bytes 1769480 | tf_op jit(solution)/shard_map/ppermute | solution.py:416
  5.7 24.7 %collective-permute-start.3 = (bf16[2304,128]{1,0:T(8,128)(2,1)}, bf16[2304,128]{1,0:T(8,128)(2,1)}, u32[]{:S(2)}, u32[]{:S(2)}) collective-permute-start(bf16[2304,128]{1,0:T(8,128)(2,1)} %get-tuple-element.66.refs_0_), channel_id=1, source_target_pairs={{0,224},{16,240},{32,0},{48,16},{64,32},{80,48},{96,64},{112,80},{... | collective-permute-start | bytes 1769480 | tf_op jit(solution)/shard_map/ppermute | solution.py:416
  9.7 23.8 %collective-permute-start.5 = (bf16[1536,128]{1,0:T(8,128)(2,1)}, bf16[1536,128]{1,0:T(8,128)(2,1)}, u32[]{:S(2)}, u32[]{:S(2)}) collective-permute-start(bf16[1536,128]{1,0:T(8,128)(2,1)} %get-tuple-element.73.refs_0_), channel_id=1, source_target_pairs={{0,224},{16,240},{32,0},{48,16},{64,32},{80,48},{96,64},{112,80},{... | collective-permute-start | bytes 1179656 | tf_op jit(solution)/shard_map/ppermute | solution.py:416
  11.7 25.0 %collective-permute-start.9 = (bf16[1536,128]{1,0:T(8,128)(2,1)}, bf16[1536,128]{1,0:T(8,128)(2,1)}, u32[]{:S(2)}, u32[]{:S(2)}) collective-permute-start(bf16[1536,128]{1,0:T(8,128)(2,1)} %get-tuple-element.73.refs_0_), channel_id=1, source_target_pairs={{0,32},{16,48},{32,64},{48,80},{64,96},{80,112},{96,128},{112,144}... | collective-permute-start | bytes 1179656 | tf_op jit(solution)/shard_map/ppermute | solution.py:416
  24.1 20.2 %collective-permute-start.7 = (bf16[2304,128]{1,0:T(8,128)(2,1)}, bf16[2304,128]{1,0:T(8,128)(2,1)}, u32[]{:S(2)}, u32[]{:S(2)}) collective-permute-start(bf16[2304,128]{1,0:T(8,128)(2,1)} %collective-permute-done.refs_1_), channel_id=1, source_target_pairs={{0,32},{16,48},{32,64},{48,80},{64,96},{80,112},{96,128},{112,144}... | collective-permute-start | bytes 1769480 | tf_op jit(solution)/shard_map/ppermute | solution.py:416
  24.1 20.2 %collective-permute-start.6 = (bf16[384,640]{1,0:T(8,128)(2,1)}, bf16[384,640]{1,0:T(8,128)(2,1)}, u32[]{:S(2)}, u32[]{:S(2)}) collective-permute-start(bf16[384,640]{1,0:T(8,128)(2,1)} %q_ref.4), channel_id=1, source_target_pairs={{0,16},{16,0},{32,48},{48,32},{64,80},{80,64},{96,112},{112,96},{1... | collective-permute-start | bytes 1474568 | tf_op jit(solution)/shard_map/ppermute | solution.py:396
  25.3 2.9 %copy-start = (bf16[640,5120]{1,0:T(8,128)(2,1)S(1)}, bf16[640,5120]{1,0:T(8,128)(2,1)}, u32[]{:S(2)}) copy-start(bf16[640,5120]{1,0:T(8,128)(2,1)} %weight_ref) | copy-start | bytes 19660804
  29.6 0.9 copy-start.4
  30.5 20.7 %collective-permute-start.1 = (bf16[640,640]{1,0:T(8,128)(2,1)}, bf16[640,640]{1,0:T(8,128)(2,1)S(1)}, u32[]{:S(2)}, u32[]{:S(2)}) collective-permute-start(bf16[640,640]{1,0:T(8,128)(2,1)} %get-tuple-element.68), channel_id=1, source_target_pairs={{0,12},{2,14},{4,0},{6,2},{8,4},{10,6},{12,8},{14,10},{1,13},{3,15... | collective-permute-start | bytes 2457608 | tf_op jit(solution)/shard_map/ppermute | solution.py:439
  33.5 14.3 %collective-permute-start.4 = (bf16[2304,128]{1,0:T(8,128)(2,1)}, bf16[2304,128]{1,0:T(8,128)(2,1)}, u32[]{:S(2)}, u32[]{:S(2)}) collective-permute-start(bf16[2304,128]{1,0:T(8,128)(2,1)} %collective-permute-done.3.refs_7_), channel_id=1, source_target_pairs={{0,224},{16,240},{32,0},{48,16},{64,32},{80,48},{96,64},{112,80},{... | collective-permute-start | bytes 1769480 | tf_op jit(solution)/shard_map/ppermute | solution.py:416
  36.7 32.1 %collective-permute-start.11 = (bf16[640,640]{1,0:T(8,128)(2,1)}, bf16[640,640]{1,0:T(8,128)(2,1)S(1)}, u32[]{:S(2)}, u32[]{:S(2)}) collective-permute-start(bf16[640,640]{1,0:T(8,128)(2,1)} %get-tuple-element.91), channel_id=1, source_target_pairs={{0,4},{2,6},{4,8},{6,10},{8,12},{10,14},{12,0},{14,2},{1,5},{3,7},... | collective-permute-start | bytes 2457608 | tf_op jit(solution)/shard_map/ppermute | solution.py:439
  44.4 13.6 %collective-permute-start.10 = (bf16[1536,128]{1,0:T(8,128)(2,1)}, bf16[1536,128]{1,0:T(8,128)(2,1)}, u32[]{:S(2)}, u32[]{:S(2)}) collective-permute-start(bf16[1536,128]{1,0:T(8,128)(2,1)} %collective-permute-done.9.refs_1_), channel_id=1, source_target_pairs={{0,32},{16,48},{32,64},{48,80},{64,96},{80,112},{96,128},{112,144}... | collective-permute-start | bytes 1179656 | tf_op jit(solution)/shard_map/ppermute | solution.py:416
  44.4 24.5 %collective-permute-start.8 = (bf16[2304,128]{1,0:T(8,128)(2,1)}, bf16[2304,128]{1,0:T(8,128)(2,1)}, u32[]{:S(2)}, u32[]{:S(2)}) collective-permute-start(bf16[2304,128]{1,0:T(8,128)(2,1)} %collective-permute-done.7.refs_2_), channel_id=1, source_target_pairs={{0,32},{16,48},{32,64},{48,80},{64,96},{80,112},{96,128},{112,144}... | collective-permute-start | bytes 1769480 | tf_op jit(solution)/shard_map/ppermute | solution.py:416
  47.8 24.4 %collective-permute-start.14 = (bf16[2304,128]{1,0:T(8,128)(2,1)}, bf16[2304,128]{1,0:T(8,128)(2,1)S(1)}, u32[]{:S(2)}, u32[]{:S(2)}) collective-permute-start(bf16[2304,128]{1,0:T(8,128)(2,1)} %collective-permute-done.4.refs_6_), channel_id=1, source_target_pairs={{0,224},{16,240},{32,0},{48,16},{64,32},{80,48},{96,64},{112,80},{... | collective-permute-start | bytes 1769480 | tf_op jit(solution)/shard_map/ppermute | solution.py:416
  51.2 32.1 %collective-permute-start.2 = (bf16[640,640]{1,0:T(8,128)(2,1)}, bf16[640,640]{1,0:T(8,128)(2,1)S(1)}, u32[]{:S(2)}, u32[]{:S(2)}) collective-permute-start(bf16[640,640]{1,0:T(8,128)(2,1)} %copy-done.4), channel_id=1, source_target_pairs={{0,8},{2,10},{4,12},{6,14},{8,0},{10,2},{12,4},{14,6},{1,9},{3,11}... | collective-permute-start | bytes 2457608 | tf_op jit(solution)/shard_map/ppermute | solution.py:441
  57.9 14.3 %collective-permute-start.13 = (bf16[1536,128]{1,0:T(8,128)(2,1)}, bf16[1536,128]{1,0:T(8,128)(2,1)S(1)}, u32[]{:S(2)}, u32[]{:S(2)}) collective-permute-start(bf16[1536,128]{1,0:T(8,128)(2,1)} %collective-permute-done.5.refs_7_), channel_id=1, source_target_pairs={{0,224},{16,240},{32,0},{48,16},{64,32},{80,48},{96,64},{112,80},{... | collective-permute-start | bytes 1179656 | tf_op jit(solution)/shard_map/ppermute | solution.py:416
  68.8 16.8 %collective-permute-start.12 = (bf16[2304,128]{1,0:T(8,128)(2,1)}, bf16[2304,128]{1,0:T(8,128)(2,1)S(1)}, u32[]{:S(2)}, u32[]{:S(2)}) collective-permute-start(bf16[2304,128]{1,0:T(8,128)(2,1)} %collective-permute-done.8.refs_3_), channel_id=1, source_target_pairs={{0,32},{16,48},{32,64},{48,80},{64,96},{80,112},{96,128},{112,144}... | collective-permute-start | bytes 1769480 | tf_op jit(solution)/shard_map/ppermute | solution.py:416
  72.3 9.6 %collective-permute-start.19 = (bf16[1536,128]{1,0:T(8,128)(2,1)S(1)}, bf16[1536,128]{1,0:T(8,128)(2,1)S(1)}, u32[]{:S(2)}, u32[]{:S(2)}) collective-permute-start(bf16[1536,128]{1,0:T(8,128)(2,1)S(1)} %collective-permute-done.13.refs_6_), channel_id=1, source_target_pairs={{0,224},{16,240},{32,0},{48,16},{64,32},{80,48},{96,64},{112,80},{... | collective-permute-start | bytes 1179656 | tf_op jit(solution)/shard_map/ppermute | solution.py:416
  75.3 25.2 %collective-permute-start.15 = (bf16[640,640]{1,0:T(8,128)(2,1)S(1)}, bf16[640,640]{1,0:T(8,128)(2,1)S(1)}, u32[]{:S(2)}, u32[]{:S(2)}) collective-permute-start(bf16[640,640]{1,0:T(8,128)(2,1)S(1)} %collective-permute-done.1.refs_6_.refs_7_), channel_id=1, source_target_pairs={{0,1},{1,0},{2,3},{3,2},{4,5},{5,4},{6,7},{7,6},{8,9},{9,8},{10,11... | collective-permute-start | bytes 2457608 | tf_op jit(solution)/shard_map/ppermute | solution.py:456
  75.3 25.3 %collective-permute-start.17 = (bf16[640,640]{1,0:T(8,128)(2,1)S(1)}, bf16[640,640]{1,0:T(8,128)(2,1)S(1)}, u32[]{:S(2)}, u32[]{:S(2)}) collective-permute-start(bf16[640,640]{1,0:T(8,128)(2,1)S(1)} %collective-permute-done.11.refs_10_.refs_11_), channel_id=1, source_target_pairs={{0,1},{1,0},{2,3},{3,2},{4,5},{5,4},{6,7},{7,6},{8,9},{9,8},{10,11... | collective-permute-start | bytes 2457608 | tf_op jit(solution)/shard_map/ppermute | solution.py:456
  81.9 18.7 %collective-permute-start.18 = (bf16[1536,128]{1,0:T(8,128)(2,1)}, bf16[1536,128]{1,0:T(8,128)(2,1)S(1)}, u32[]{:S(2)}, u32[]{:S(2)}) collective-permute-start(bf16[1536,128]{1,0:T(8,128)(2,1)} %collective-permute-done.10.refs_2_), channel_id=1, source_target_pairs={{0,32},{16,48},{32,64},{48,80},{64,96},{80,112},{96,128},{112,144}... | collective-permute-start | bytes 1179656 | tf_op jit(solution)/shard_map/ppermute | solution.py:416
  83.3 17.3 %collective-permute-start.20 = (bf16[1536,128]{1,0:T(8,128)(2,1)S(1)}, bf16[1536,128]{1,0:T(8,128)(2,1)S(1)}, u32[]{:S(2)}, u32[]{:S(2)}) collective-permute-start(bf16[1536,128]{1,0:T(8,128)(2,1)S(1)} %collective-permute-done.19.refs_5_), channel_id=1, source_target_pairs={{0,224},{16,240},{32,0},{48,16},{64,32},{80,48},{96,64},{112,80},{... | collective-permute-start | bytes 1179656 | tf_op jit(solution)/shard_map/ppermute | solution.py:416
  85.6 15.0 %collective-permute-start.16 = (bf16[640,640]{1,0:T(8,128)(2,1)S(1)}, bf16[640,640]{1,0:T(8,128)(2,1)S(1)}, u32[]{:S(2)}, u32[]{:S(2)}) collective-permute-start(bf16[640,640]{1,0:T(8,128)(2,1)S(1)} %collective-permute-done.2.refs_8_.refs_9_), channel_id=1, source_target_pairs={{0,1},{1,0},{2,3},{3,2},{4,5},{5,4},{6,7},{7,6},{8,9},{9,8},{10,11... | collective-permute-start | bytes 2457608 | tf_op jit(solution)/shard_map/ppermute | solution.py:456
  85.6 1.0 copy-start.7
  100.5 11.6 %collective-permute-start.25 = (bf16[1536,128]{1,0:T(8,128)(2,1)S(1)}, bf16[1536,128]{1,0:T(8,128)(2,1)S(1)}, u32[]{:S(2)}, u32[]{:S(2)}) collective-permute-start(bf16[1536,128]{1,0:T(8,128)(2,1)S(1)} %get-tuple-element.125), channel_id=1, source_target_pairs={{0,16},{16,0},{32,48},{48,32},{64,80},{80,64},{96,112},{112,96},{1... | collective-permute-start | bytes 1179656 | tf_op jit(solution)/shard_map/ppermute | solution.py:396
  111.2 9.5 %collective-permute-start.21 = (bf16[1152,128]{1,0:T(8,128)(2,1)S(1)}, bf16[1152,128]{1,0:T(8,128)(2,1)S(1)}, u32[]{:S(2)}, u32[]{:S(2)}) collective-permute-start(bf16[1152,128]{1,0:T(8,128)(2,1)S(1)} %get-tuple-element.114), channel_id=1, source_target_pairs={{0,16},{16,0},{32,48},{48,32},{64,80},{80,64},{96,112},{112,96},{1... | collective-permute-start | bytes 884744 | tf_op jit(solution)/shard_map/ppermute | solution.py:396
  112.5 16.8 %collective-permute-start.26 = (bf16[384,384]{1,0:T(8,128)(2,1)S(1)}, bf16[384,384]{1,0:T(8,128)(2,1)S(1)}, u32[]{:S(2)}, u32[]{:S(2)}) collective-permute-start(bf16[384,384]{1,0:T(8,128)(2,1)S(1)} %merge.3.refs_0_), channel_id=1, source_target_pairs={{0,12},{2,14},{4,0},{6,2},{8,4},{10,6},{12,8},{14,10},{1,13},{3,15... | collective-permute-start | bytes 884744 | tf_op jit(solution)/shard_map/ppermute | solution.py:427
  115.6 13.8 %collective-permute-start.27 = (bf16[384,384]{1,0:T(8,128)(2,1)S(1)}, bf16[384,384]{1,0:T(8,128)(2,1)S(1)}, u32[]{:S(2)}, u32[]{:S(2)}) collective-permute-start(bf16[384,384]{1,0:T(8,128)(2,1)S(1)} %merge.3.refs_0_), channel_id=1, source_target_pairs={{0,8},{2,10},{4,12},{6,14},{8,0},{10,2},{12,4},{14,6},{1,9},{3,11}... | collective-permute-start | bytes 884744 | tf_op jit(solution)/shard_map/ppermute | solution.py:427
  116.2 17.2 %collective-permute-start.28 = (bf16[384,384]{1,0:T(8,128)(2,1)S(1)}, bf16[384,384]{1,0:T(8,128)(2,1)S(1)}, u32[]{:S(2)}, u32[]{:S(2)}) collective-permute-start(bf16[384,384]{1,0:T(8,128)(2,1)S(1)} %merge.3.refs_0_), channel_id=1, source_target_pairs={{0,4},{2,6},{4,8},{6,10},{8,12},{10,14},{12,0},{14,2},{1,5},{3,7},... | collective-permute-start | bytes 884744 | tf_op jit(solution)/shard_map/ppermute | solution.py:427
  120.9 15.5 %collective-permute-start.22 = (bf16[384,256]{1,0:T(8,128)(2,1)S(1)}, bf16[384,256]{1,0:T(8,128)(2,1)S(1)}, u32[]{:S(2)}, u32[]{:S(2)}) collective-permute-start(bf16[384,256]{1,0:T(8,128)(2,1)S(1)} %merge.2.refs_1_), channel_id=1, source_target_pairs={{0,12},{2,14},{4,0},{6,2},{8,4},{10,6},{12,8},{14,10},{1,13},{3,15... | collective-permute-start | bytes 589832 | tf_op jit(solution)/shard_map/ppermute | solution.py:427
  124.0 13.6 %collective-permute-start.23 = (bf16[384,256]{1,0:T(8,128)(2,1)S(1)}, bf16[384,256]{1,0:T(8,128)(2,1)S(1)}, u32[]{:S(2)}, u32[]{:S(2)}) collective-permute-start(bf16[384,256]{1,0:T(8,128)(2,1)S(1)} %merge.2.refs_1_), channel_id=1, source_target_pairs={{0,8},{2,10},{4,12},{6,14},{8,0},{10,2},{12,4},{14,6},{1,9},{3,11}... | collective-permute-start | bytes 589832 | tf_op jit(solution)/shard_map/ppermute | solution.py:427
  129.3 10.8 %collective-permute-start.24 = (bf16[384,256]{1,0:T(8,128)(2,1)S(1)}, bf16[384,256]{1,0:T(8,128)(2,1)S(1)}, u32[]{:S(2)}, u32[]{:S(2)}) collective-permute-start(bf16[384,256]{1,0:T(8,128)(2,1)S(1)} %merge.2.refs_1_), channel_id=1, source_target_pairs={{0,4},{2,6},{4,8},{6,10},{8,12},{10,14},{12,0},{14,2},{1,5},{3,7},... | collective-permute-start | bytes 589832 | tf_op jit(solution)/shard_map/ppermute | solution.py:427
  135.8 6.4 %copy-start.5 = (bf16[512,640]{1,0:T(8,128)(2,1)S(1)}, bf16[512,640]{1,0:T(8,128)(2,1)}, u32[]{:S(2)}) copy-start(bf16[512,640]{1,0:T(8,128)(2,1)} %k_ref.3) | copy-start | bytes 1966084
  135.9 6.4 %copy-start.6 = (bf16[512,640]{1,0:T(8,128)(2,1)S(1)}, bf16[512,640]{1,0:T(8,128)(2,1)}, u32[]{:S(2)}) copy-start(bf16[512,640]{1,0:T(8,128)(2,1)} %v_ref.3) | copy-start | bytes 1966084
  135.9 6.4 %copy-start.8 = (bf16[384,640]{1,0:T(8,128)(2,1)S(1)}, bf16[384,640]{1,0:T(8,128)(2,1)}, u32[]{:S(2)}) copy-start(bf16[384,640]{1,0:T(8,128)(2,1)} %q_ref.5) | copy-start | bytes 1474564
  141.7 14.6 %collective-permute-start.29 = (bf16[384,640]{1,0:T(8,128)(2,1)S(1)}, bf16[384,640]{1,0:T(8,128)(2,1)S(1)}, u32[]{:S(2)}, u32[]{:S(2)}) collective-permute-start(bf16[384,640]{1,0:T(8,128)(2,1)S(1)} %get-tuple-element.127), channel_id=1, source_target_pairs={{0,2},{2,0},{4,6},{6,4},{8,10},{10,8},{12,14},{14,12},{1,3},{3,1},... | collective-permute-start | bytes 1474568 | tf_op jit(solution)/shard_map/ppermute | solution.py:465

commit v8 on v6

--- a/solution.py
+++ b/solution.py
@@ -431,7 +431,6 @@
         hop(-1, group, 1)
     queries_other = to_other(queries)
     early = list(plan(n_seq, seq, block_list, block_count))
-    out_weight, queries_other = lax.optimization_barrier((out_weight, queries_other))
     tiles = list(tile(lax.div(head, 2), pair, out_weight, n_y))
     early[0], tiles[0], queries_other = lax.optimization_barrier((early[0], tiles[0], queries_other))
     hop(1, 0, 2)

time: 154 us -> 146 us (0.948); the launches traced: 152 us -> 146 us
  local copies, waits for them, and re-layouts: 8.76 us -> 5.92 us
  waiting for transfers between devices: 68.5 us -> 66 us
    ppermute x14, waiting for transfers between devices: 39.5 us -> 45.9 us  [hop(): held[group][place] = lax.ppermute(array, 'seq', z_shift(way))]
    ppermute x3, waiting for transfers between devices: 9.41 us -> 5.17 us  [to_other(): return lax.ppermute(array, 'seq', swap)]
    ppermute x2, waiting for transfers between devices: 3 us -> 0.01 us  [body(): lax.ppermute(tiles[dy], 'head', y_shift(dy))]
    unnamed x25 -> x19, local copies, waits for them, and re-layouts: 8.76 us -> 5.92 us
    ppermute x6, waiting for transfers between devices: 10.8 us -> 9.21 us  [along_y(): lax.ppermute(array, 'head', y_shift(-dy))]
    ppermute x6, starting transfers between devices: 6.75 us -> 5.21 us  [along_y(): lax.ppermute(array, 'head', y_shift(-dy))]
  transfers between devices with their start and end apart: 30 -> 30, of which waited for: 13 -> 14; matrix products, arithmetic and copies ran while one was open for 0% -> 0% of each run, Pallas kernels for 21% -> 22%
where the time goes in v8:
time: 146 us
  waiting for transfers between devices  66 us (45%)
  starting transfers between devices  37.7 us (26%)
  Pallas kernels  34.6 us (24%)
  local copies, waits for them, and re-layouts  5.92 us (4%)
    ppermute x14, waiting for transfers between devices, hop(): held[group][place] = lax.ppermute(array, 'seq', z_shift(way))  45.9 us
    ppermute x14, starting transfers between devices, hop(): held[group][place] = lax.ppermute(array, 'seq', z_shift(way))  24.3 us
    pallas_call x2, Pallas kernels, attend(): pl.pallas_call(functools.partial(attend_kernel, heads, first, planes), ou...  20.9 us
    ppermute x6, waiting for transfers between devices, along_y(): lax.ppermute(array, 'head', y_shift(-dy))  9.21 us
    unnamed x19, local copies, waits for them, and re-layouts  5.92 us
    ppermute x1, waiting for transfers between devices, body(): got = lax.ppermute(send, 'head', [(g, g ^ 1) for g in range(n_head)])  5.71 us
    ppermute x6, starting transfers between devices, along_y(): lax.ppermute(array, 'head', y_shift(-dy))  5.21 us
    ppermute x3, waiting for transfers between devices, to_other(): return lax.ppermute(array, 'seq', swap)  5.17 us
  transfers between devices with their start and end apart: 30, of which 14 were waited for; matrix products, arithmetic and copies ran while one was open for 0% of the time, Pallas kernels for 22%

profile of v8, /device:TPU:4, one launch (start us, length us, event | category | flops | bytes accessed | tf_op | source)
XLA Modules:
  0.0 145.9 jit_solution(17161263519074475467)
XLA Ops:
  0.6 1.0 copy-done.1
  1.7 1.0 copy-done.2
  2.7 1.1 pack.1
  3.8 1.9 %collective-permute-start.6 = (bf16[2304,128]{1,0:T(8,128)(2,1)}, bf16[2304,128]{1,0:T(8,128)(2,1)}, u32[]{:S(2)}, u32[]{:S(2)}) collective-permute-start(bf16[2304,128]{1,0:T(8,128)(2,1)} %get-tuple-element.68.refs_0_), channel_id=1, source_target_pairs={{0,32},{16,48},{32,64},{48,80},{64,96},{80,112},{96,128},{112,144}... | collective-permute-start | bytes 1769480 | tf_op jit(solution)/shard_map/ppermute | solution.py:416
  5.7 2.9 %copy-done = bf16[640,5120]{1,0:T(8,128)(2,1)S(1)} copy-done((bf16[640,5120]{1,0:T(8,128)(2,1)S(1)}, bf16[640,5120]{1,0:T(8,128)(2,1)}, u32[]{:S(2)}) %copy-start) | copy-done | bytes 6553624
  8.6 0.6 tile.1
  9.2 0.9 copy-done.4
  10.1 3.0 %collective-permute-start = (bf16[640,640]{1,0:T(8,128)(2,1)S(1)}, bf16[640,640]{1,0:T(8,128)(2,1)S(1)}, u32[]{:S(2)}, u32[]{:S(2)}) collective-permute-start(bf16[640,640]{1,0:T(8,128)(2,1)S(1)} %get-tuple-element.64), channel_id=1, source_target_pairs={{0,12},{2,14},{4,0},{6,2},{8,4},{10,6},{12,8},{14,10},{1,13},{3,15... | collective-permute-start | bytes 2457608 | tf_op jit(solution)/shard_map/ppermute | solution.py:438
  13.1 3.9 %collective-permute-start.2 = (bf16[2304,128]{1,0:T(8,128)(2,1)}, bf16[2304,128]{1,0:T(8,128)(2,1)}, u32[]{:S(2)}, u32[]{:S(2)}) collective-permute-start(bf16[2304,128]{1,0:T(8,128)(2,1)} %get-tuple-element.68.refs_0_), channel_id=1, source_target_pairs={{0,224},{16,240},{32,0},{48,16},{64,32},{80,48},{96,64},{112,80},{... | collective-permute-start | bytes 1769480 | tf_op jit(solution)/shard_map/ppermute | solution.py:416
  17.0 6.3 %collective-permute-done.6.refs_1_ = bf16[2304,128]{1,0:T(8,128)(2,1)} collective-permute-done((bf16[2304,128]{1,0:T(8,128)(2,1)}, bf16[2304,128]{1,0:T(8,128)(2,1)}, u32[]{:S(2)}, u32[]{:S(2)}) %collective-permute-start.6) | collective-permute-done | bytes 589856 | tf_op jit(solution)/shard_map/ppermute | solution.py:416
  23.3 6.4 %collective-permute-done.2.refs_7_ = bf16[2304,128]{1,0:T(8,128)(2,1)} collective-permute-done((bf16[2304,128]{1,0:T(8,128)(2,1)}, bf16[2304,128]{1,0:T(8,128)(2,1)}, u32[]{:S(2)}, u32[]{:S(2)}) %collective-permute-start.2) | collective-permute-done | bytes 589856 | tf_op jit(solution)/shard_map/ppermute | solution.py:416
  29.7 3.7 %collective-permute-start.3 = (bf16[2304,128]{1,0:T(8,128)(2,1)}, bf16[2304,128]{1,0:T(8,128)(2,1)}, u32[]{:S(2)}, u32[]{:S(2)}) collective-permute-start(bf16[2304,128]{1,0:T(8,128)(2,1)} %collective-permute-done.2.refs_7_), channel_id=1, source_target_pairs={{0,224},{16,240},{32,0},{48,16},{64,32},{80,48},{96,64},{112,80},{... | collective-permute-start | bytes 1769480 | tf_op jit(solution)/shard_map/ppermute | solution.py:416
  33.4 1.2 collective-permute-start.5
  34.6 0.5 collective-permute-start.4
  35.1 4.3 %collective-permute-done.7.refs_2_ = bf16[2304,128]{1,0:T(8,128)(2,1)} collective-permute-done((bf16[2304,128]{1,0:T(8,128)(2,1)}, bf16[2304,128]{1,0:T(8,128)(2,1)}, u32[]{:S(2)}, u32[]{:S(2)}) %collective-permute-start.7) | collective-permute-done | bytes 589856 | tf_op jit(solution)/shard_map/ppermute | solution.py:416
  39.5 3.4 %plan.1 = (s32[6,13]{1,0:T(8,128)S(1)}, s32[6]{0:T(128)S(1)}, s32[8]{0:T(128)S(1)}) custom-call(s32[1]{0:T(128)} %bitcast.2.seq_ref, s32[48,18]{1,0:T(8,128)S(1)} %copy.11.list_ref, s32[48]{0:T(128)S(1)} %copy-done.3), custom_call_target="tpu_custom_call" | custom-call | flops 1000 | bytes 8000 | tf_op jit(solution)/shard_map/plan/pallas_call | solution.py:61
  42.8 2.3 %collective-permute-done.5.q_other_ref = bf16[384,640]{1,0:T(8,128)(2,1)} collective-permute-done((bf16[384,640]{1,0:T(8,128)(2,1)}, bf16[384,640]{1,0:T(8,128)(2,1)}, u32[]{:S(2)}, u32[]{:S(2)}) %collective-permute-start.5) | collective-permute-done | bytes 491552 | tf_op jit(solution)/shard_map/ppermute | solution.py:396
  45.2 8.3 %collective-permute-done.4.refs_7_ = bf16[1536,128]{1,0:T(8,128)(2,1)} collective-permute-done((bf16[1536,128]{1,0:T(8,128)(2,1)}, bf16[1536,128]{1,0:T(8,128)(2,1)}, u32[]{:S(2)}, u32[]{:S(2)}) %collective-permute-start.4) | collective-permute-done | bytes 393248 | tf_op jit(solution)/shard_map/ppermute | solution.py:416
  53.5 3.7 %collective-permute-start.14 = (bf16[2304,128]{1,0:T(8,128)(2,1)}, bf16[2304,128]{1,0:T(8,128)(2,1)S(1)}, u32[]{:S(2)}, u32[]{:S(2)}) collective-permute-start(bf16[2304,128]{1,0:T(8,128)(2,1)} %collective-permute-done.3.refs_6_), channel_id=1, source_target_pairs={{0,224},{16,240},{32,0},{48,16},{64,32},{80,48},{96,64},{112,80},{... | collective-permute-start | bytes 1769480 | tf_op jit(solution)/shard_map/ppermute | solution.py:416
  57.2 0.6 collective-permute-start.1
  57.8 3.2 %collective-permute-start.13 = (bf16[1536,128]{1,0:T(8,128)(2,1)}, bf16[1536,128]{1,0:T(8,128)(2,1)S(1)}, u32[]{:S(2)}, u32[]{:S(2)}) collective-permute-start(bf16[1536,128]{1,0:T(8,128)(2,1)} %collective-permute-done.4.refs_7_), channel_id=1, source_target_pairs={{0,224},{16,240},{32,0},{48,16},{64,32},{80,48},{96,64},{112,80},{... | collective-permute-start | bytes 1179656 | tf_op jit(solution)/shard_map/ppermute | solution.py:416
  61.1 10.1 %collective-permute-done.11.refs_2_ = bf16[1536,128]{1,0:T(8,128)(2,1)S(1)} collective-permute-done((bf16[1536,128]{1,0:T(8,128)(2,1)}, bf16[1536,128]{1,0:T(8,128)(2,1)S(1)}, u32[]{:S(2)}, u32[]{:S(2)}) %collective-permute-start.11) | collective-permute-done | bytes 393248 | tf_op jit(solution)/shard_map/ppermute | solution.py:416
  71.2 5.2 %collective-permute-done.13.refs_6_ = bf16[1536,128]{1,0:T(8,128)(2,1)S(1)} collective-permute-done((bf16[1536,128]{1,0:T(8,128)(2,1)}, bf16[1536,128]{1,0:T(8,128)(2,1)S(1)}, u32[]{:S(2)}, u32[]{:S(2)}) %collective-permute-start.13) | collective-permute-done | bytes 393248 | tf_op jit(solution)/shard_map/ppermute | solution.py:416
  76.4 3.6 %collective-permute-start.19 = (bf16[1536,128]{1,0:T(8,128)(2,1)S(1)}, bf16[1536,128]{1,0:T(8,128)(2,1)S(1)}, u32[]{:S(2)}, u32[]{:S(2)}) collective-permute-start(bf16[1536,128]{1,0:T(8,128)(2,1)S(1)} %collective-permute-done.13.refs_6_), channel_id=1, source_target_pairs={{0,224},{16,240},{32,0},{48,16},{64,32},{80,48},{96,64},{112,80},{... | collective-permute-start | bytes 1179656 | tf_op jit(solution)/shard_map/ppermute | solution.py:416
  80.0 0.5 collective-permute-start.17
  80.5 5.3 %collective-permute-done.19.refs_5_ = bf16[1536,128]{1,0:T(8,128)(2,1)S(1)} collective-permute-done((bf16[1536,128]{1,0:T(8,128)(2,1)S(1)}, bf16[1536,128]{1,0:T(8,128)(2,1)S(1)}, u32[]{:S(2)}, u32[]{:S(2)}) %collective-permute-start.19) | collective-permute-done | bytes 393248 | tf_op jit(solution)/shard_map/ppermute | solution.py:416
  85.9 3.7 %collective-permute-start.20 = (bf16[1536,128]{1,0:T(8,128)(2,1)S(1)}, bf16[1536,128]{1,0:T(8,128)(2,1)S(1)}, u32[]{:S(2)}, u32[]{:S(2)}) collective-permute-start(bf16[1536,128]{1,0:T(8,128)(2,1)S(1)} %collective-permute-done.19.refs_5_), channel_id=1, source_target_pairs={{0,224},{16,240},{32,0},{48,16},{64,32},{80,48},{96,64},{112,80},{... | collective-permute-start | bytes 1179656 | tf_op jit(solution)/shard_map/ppermute | solution.py:416
  89.6 12.0 %attend.2 = (f32[1152,128]{1,0:T(8,128)S(1)}, f32[1152,128]{1,0:T(8,128)S(1)}, bf16[1536,128]{1,0:T(8,128)(2,1)S(1)}) custom-call(s32[1]{0:T(128)} %bitcast.2.seq_ref, s32[8]{0:T(128)S(1)} %get-tuple-element.101.near_ref, s32[6,13]{1,0:T(8,128)S(1)} %get-tuple-element.75.blocks_ref, s32[6]{0:T(128)S(1)} %get-tuple-element.76.count_ref, ...), custom_call_target="tpu_custom_call" | custom-call | flops 13589544960 | bytes 4718592 | tf_op jit(solution)/shard_map/attend/pallas_call | solution.py:227
  101.6 1.4 collective-permute-start.25
  103.0 8.9 %attend.3 = (f32[768,128]{1,0:T(8,128)S(1)}, f32[768,128]{1,0:T(8,128)S(1)}, bf16[1152,128]{1,0:T(8,128)(2,1)S(1)}) custom-call(s32[1]{0:T(128)} %bitcast.2.seq_ref, s32[8]{0:T(128)S(1)} %get-tuple-element.101.near_ref, s32[6,13]{1,0:T(8,128)S(1)} %get-tuple-element.75.blocks_ref, s32[6]{0:T(128)S(1)} %get-tuple-element.76.count_ref, ...), custom_call_target="tpu_custom_call" | custom-call | flops 9059696640 | bytes 3145728 | tf_op jit(solution)/shard_map/attend/pallas_call | solution.py:227
  111.9 0.9 collective-permute-start.21
  113.2 0.9 collective-permute-start.26
  114.0 0.9 collective-permute-start.27
  114.9 1.0 collective-permute-start.28
  115.9 2.8 %collective-permute-done.21.refs_2_ = bf16[1152,128]{1,0:T(8,128)(2,1)S(1)} collective-permute-done((bf16[1152,128]{1,0:T(8,128)(2,1)S(1)}, bf16[1152,128]{1,0:T(8,128)(2,1)S(1)}, u32[]{:S(2)}, u32[]{:S(2)}) %collective-permute-start.21) | collective-permute-done | bytes 294944 | tf_op jit(solution)/shard_map/ppermute | solution.py:396
  119.0 0.9 collective-permute-start.22
  119.9 0.9 collective-permute-start.23
  120.8 2.4 %collective-permute-done.26.refs_1_ = bf16[384,384]{1,0:T(8,128)(2,1)S(1)} collective-permute-done((bf16[384,384]{1,0:T(8,128)(2,1)S(1)}, bf16[384,384]{1,0:T(8,128)(2,1)S(1)}, u32[]{:S(2)}, u32[]{:S(2)}) %collective-permute-start.26) | collective-permute-done | bytes 294944 | tf_op jit(solution)/shard_map/ppermute | solution.py:427
  123.2 0.6 collective-permute-start.24
  123.8 1.7 %collective-permute-done.27.refs_2_ = bf16[384,384]{1,0:T(8,128)(2,1)S(1)} collective-permute-done((bf16[384,384]{1,0:T(8,128)(2,1)S(1)}, bf16[384,384]{1,0:T(8,128)(2,1)S(1)}, u32[]{:S(2)}, u32[]{:S(2)}) %collective-permute-start.27) | collective-permute-done | bytes 294944 | tf_op jit(solution)/shard_map/ppermute | solution.py:427
  125.5 3.4 %collective-permute-done.28.refs_3_ = bf16[384,384]{1,0:T(8,128)(2,1)S(1)} collective-permute-done((bf16[384,384]{1,0:T(8,128)(2,1)S(1)}, bf16[384,384]{1,0:T(8,128)(2,1)S(1)}, u32[]{:S(2)}, u32[]{:S(2)}) %collective-permute-start.28) | collective-permute-done | bytes 294944 | tf_op jit(solution)/shard_map/ppermute | solution.py:427
  128.9 2.4 %project.2.refs_13_ = f32[2,384,640]{2,1,0:T(8,128)S(1)} custom-call(bf16[384,384]{1,0:T(8,128)(2,1)S(1)} %merge.3.refs_0_, bf16[384,384]{1,0:T(8,128)(2,1)S(1)} %collective-permute-done.26.refs_1_, bf16[384,384]{1,0:T(8,128)(2,1)S(1)} %collective-permute-done.27.refs_2_, bf16[384,384]{1,0:T(8,128)(2,1)S(1)} %collective-permute-done.28.refs_3_, ...), custom_call_target="tpu_custom_call" | custom-call | flops 1509949440 | bytes 5111808 | tf_op jit(solution)/shard_map/project/pallas_call | solution.py:371
  131.4 1.7 %collective-permute-done.24.refs_4_ = bf16[384,256]{1,0:T(8,128)(2,1)S(1)} collective-permute-done((bf16[384,256]{1,0:T(8,128)(2,1)S(1)}, bf16[384,256]{1,0:T(8,128)(2,1)S(1)}, u32[]{:S(2)}, u32[]{:S(2)}) %collective-permute-start.24) | collective-permute-done | bytes 196640 | tf_op jit(solution)/shard_map/ppermute | solution.py:427
  133.1 1.5 %project.3 = (f32[384,640]{1,0:T(8,128)S(1)}, bf16[384,640]{1,0:T(8,128)(2,1)S(1)}) custom-call(s32[1]{0:T(128)S(6)} %convert_element_type.9.refs_0_, bf16[384,256]{1,0:T(8,128)(2,1)S(1)} %merge.2.refs_1_, bf16[384,256]{1,0:T(8,128)(2,1)S(1)} %collective-permute-done.22.refs_2_, bf16[384,256]{1,0:T(8,128)(2,1)S(1)} %collective-permute-done.23.refs_3_, ...), custom_call_target="tpu_custom_call" | custom-call | flops 1006632960 | bytes 3407872 | tf_op jit(solution)/shard_map/project/pallas_call | solution.py:371
  134.6 0.6 collective-permute-start.29
  135.2 4.1 %cross.1 = bf16[384,640]{1,0:T(8,128)(2,1)} custom-call(bf16[384,640]{1,0:T(8,128)(2,1)S(1)} %copy-done.7, bf16[512,640]{1,0:T(8,128)(2,1)S(1)} %copy-done.5, bf16[512,640]{1,0:T(8,128)(2,1)S(1)} %copy-done.6), custom_call_target="tpu_custom_call" | custom-call | flops 5033164800 | bytes 983040 | tf_op jit(solution)/shard_map/cross/pallas_call | solution.py:333
  139.4 5.7 %collective-permute-done.29 = bf16[384,640]{1,0:T(8,128)(2,1)S(1)} collective-permute-done((bf16[384,640]{1,0:T(8,128)(2,1)S(1)}, bf16[384,640]{1,0:T(8,128)(2,1)S(1)}, u32[]{:S(2)}, u32[]{:S(2)}) %collective-permute-start.29) | collective-permute-done | bytes 491552 | tf_op jit(solution)/shard_map/ppermute | solution.py:464
  145.1 0.9 add_convert_fusion
  (42 shorter events, 0.8 us)
Async XLA Ops:
  0.6 1.0 copy-start.1
  1.7 1.0 copy-start.2
  2.7 36.7 %copy-start.8 = (s32[48,18]{0,1:T(8,128)S(1)}, s32[48,18]{0,1:T(8,128)}, u32[]{:S(2)}) copy-start(s32[48,18]{0,1:T(8,128)} %param.16) | copy-start | bytes 10372
  2.7 36.8 %copy-start.3 = (s32[48]{0:T(128)S(1)}, s32[48]{0:T(128)}, u32[]{:S(2)}) copy-start(s32[48]{0:T(128)} %count_ref.1) | copy-start | bytes 580
  3.8 19.5 %collective-permute-start.6 = (bf16[2304,128]{1,0:T(8,128)(2,1)}, bf16[2304,128]{1,0:T(8,128)(2,1)}, u32[]{:S(2)}, u32[]{:S(2)}) collective-permute-start(bf16[2304,128]{1,0:T(8,128)(2,1)} %get-tuple-element.68.refs_0_), channel_id=1, source_target_pairs={{0,32},{16,48},{32,64},{48,80},{64,96},{80,112},{96,128},{112,144}... | collective-permute-start | bytes 1769480 | tf_op jit(solution)/shard_map/ppermute | solution.py:416
  5.7 2.9 %copy-start = (bf16[640,5120]{1,0:T(8,128)(2,1)S(1)}, bf16[640,5120]{1,0:T(8,128)(2,1)}, u32[]{:S(2)}) copy-start(bf16[640,5120]{1,0:T(8,128)(2,1)} %weight_ref.1) | copy-start | bytes 19660804
  9.2 0.9 copy-start.4
  10.1 24.5 %collective-permute-start = (bf16[640,640]{1,0:T(8,128)(2,1)S(1)}, bf16[640,640]{1,0:T(8,128)(2,1)S(1)}, u32[]{:S(2)}, u32[]{:S(2)}) collective-permute-start(bf16[640,640]{1,0:T(8,128)(2,1)S(1)} %get-tuple-element.64), channel_id=1, source_target_pairs={{0,12},{2,14},{4,0},{6,2},{8,4},{10,6},{12,8},{14,10},{1,13},{3,15... | collective-permute-start | bytes 2457608 | tf_op jit(solution)/shard_map/ppermute | solution.py:438
  13.1 16.6 %collective-permute-start.2 = (bf16[2304,128]{1,0:T(8,128)(2,1)}, bf16[2304,128]{1,0:T(8,128)(2,1)}, u32[]{:S(2)}, u32[]{:S(2)}) collective-permute-start(bf16[2304,128]{1,0:T(8,128)(2,1)} %get-tuple-element.68.refs_0_), channel_id=1, source_target_pairs={{0,224},{16,240},{32,0},{48,16},{64,32},{80,48},{96,64},{112,80},{... | collective-permute-start | bytes 1769480 | tf_op jit(solution)/shard_map/ppermute | solution.py:416
  17.0 22.3 %collective-permute-start.8 = (bf16[640,640]{1,0:T(8,128)(2,1)S(1)}, bf16[640,640]{1,0:T(8,128)(2,1)S(1)}, u32[]{:S(2)}, u32[]{:S(2)}) collective-permute-start(bf16[640,640]{1,0:T(8,128)(2,1)S(1)} %get-tuple-element.83), channel_id=1, source_target_pairs={{0,4},{2,6},{4,8},{6,10},{8,12},{10,14},{12,0},{14,2},{1,5},{3,7},... | collective-permute-start | bytes 2457608 | tf_op jit(solution)/shard_map/ppermute | solution.py:438
  23.3 16.0 %collective-permute-start.7 = (bf16[2304,128]{1,0:T(8,128)(2,1)}, bf16[2304,128]{1,0:T(8,128)(2,1)}, u32[]{:S(2)}, u32[]{:S(2)}) collective-permute-start(bf16[2304,128]{1,0:T(8,128)(2,1)} %collective-permute-done.6.refs_1_), channel_id=1, source_target_pairs={{0,32},{16,48},{32,64},{48,80},{64,96},{80,112},{96,128},{112,144}... | collective-permute-start | bytes 1769480 | tf_op jit(solution)/shard_map/ppermute | solution.py:416
  29.7 23.8 %collective-permute-start.3 = (bf16[2304,128]{1,0:T(8,128)(2,1)}, bf16[2304,128]{1,0:T(8,128)(2,1)}, u32[]{:S(2)}, u32[]{:S(2)}) collective-permute-start(bf16[2304,128]{1,0:T(8,128)(2,1)} %collective-permute-done.2.refs_7_), channel_id=1, source_target_pairs={{0,224},{16,240},{32,0},{48,16},{64,32},{80,48},{96,64},{112,80},{... | collective-permute-start | bytes 1769480 | tf_op jit(solution)/shard_map/ppermute | solution.py:416
  33.4 11.8 %collective-permute-start.5 = (bf16[384,640]{1,0:T(8,128)(2,1)}, bf16[384,640]{1,0:T(8,128)(2,1)}, u32[]{:S(2)}, u32[]{:S(2)}) collective-permute-start(bf16[384,640]{1,0:T(8,128)(2,1)} %q_ref.4), channel_id=1, source_target_pairs={{0,16},{16,0},{32,48},{48,32},{64,80},{80,64},{96,112},{112,96},{1... | collective-permute-start | bytes 1474568 | tf_op jit(solution)/shard_map/ppermute | solution.py:396
  34.6 18.9 %collective-permute-start.4 = (bf16[1536,128]{1,0:T(8,128)(2,1)}, bf16[1536,128]{1,0:T(8,128)(2,1)}, u32[]{:S(2)}, u32[]{:S(2)}) collective-permute-start(bf16[1536,128]{1,0:T(8,128)(2,1)} %get-tuple-element.70.refs_0_), channel_id=1, source_target_pairs={{0,224},{16,240},{32,0},{48,16},{64,32},{80,48},{96,64},{112,80},{... | collective-permute-start | bytes 1179656 | tf_op jit(solution)/shard_map/ppermute | solution.py:416
  39.3 17.8 %collective-permute-start.10 = (bf16[1536,128]{1,0:T(8,128)(2,1)}, bf16[1536,128]{1,0:T(8,128)(2,1)}, u32[]{:S(2)}, u32[]{:S(2)}) collective-permute-start(bf16[1536,128]{1,0:T(8,128)(2,1)} %get-tuple-element.70.refs_0_), channel_id=1, source_target_pairs={{0,32},{16,48},{32,64},{48,80},{64,96},{80,112},{96,128},{112,144}... | collective-permute-start | bytes 1179656 | tf_op jit(solution)/shard_map/ppermute | solution.py:416
  39.4 31.9 %collective-permute-start.9 = (bf16[2304,128]{1,0:T(8,128)(2,1)}, bf16[2304,128]{1,0:T(8,128)(2,1)}, u32[]{:S(2)}, u32[]{:S(2)}) collective-permute-start(bf16[2304,128]{1,0:T(8,128)(2,1)} %collective-permute-done.7.refs_2_), channel_id=1, source_target_pairs={{0,32},{16,48},{32,64},{48,80},{64,96},{80,112},{96,128},{112,144}... | collective-permute-start | bytes 1769480 | tf_op jit(solution)/shard_map/ppermute | solution.py:416
  53.5 22.9 %collective-permute-start.14 = (bf16[2304,128]{1,0:T(8,128)(2,1)}, bf16[2304,128]{1,0:T(8,128)(2,1)S(1)}, u32[]{:S(2)}, u32[]{:S(2)}) collective-permute-start(bf16[2304,128]{1,0:T(8,128)(2,1)} %collective-permute-done.3.refs_6_), channel_id=1, source_target_pairs={{0,224},{16,240},{32,0},{48,16},{64,32},{80,48},{96,64},{112,80},{... | collective-permute-start | bytes 1769480 | tf_op jit(solution)/shard_map/ppermute | solution.py:416
  57.2 14.0 %collective-permute-start.11 = (bf16[1536,128]{1,0:T(8,128)(2,1)}, bf16[1536,128]{1,0:T(8,128)(2,1)S(1)}, u32[]{:S(2)}, u32[]{:S(2)}) collective-permute-start(bf16[1536,128]{1,0:T(8,128)(2,1)} %collective-permute-done.10.refs_1_), channel_id=1, source_target_pairs={{0,32},{16,48},{32,64},{48,80},{64,96},{80,112},{96,128},{112,144}... | collective-permute-start | bytes 1179656 | tf_op jit(solution)/shard_map/ppermute | solution.py:416
  57.2 23.3 %collective-permute-start.1 = (bf16[640,640]{1,0:T(8,128)(2,1)}, bf16[640,640]{1,0:T(8,128)(2,1)S(1)}, u32[]{:S(2)}, u32[]{:S(2)}) collective-permute-start(bf16[640,640]{1,0:T(8,128)(2,1)} %copy-done.4), channel_id=1, source_target_pairs={{0,8},{2,10},{4,12},{6,14},{8,0},{10,2},{12,4},{14,6},{1,9},{3,11}... | collective-permute-start | bytes 2457608 | tf_op jit(solution)/shard_map/ppermute | solution.py:440
  57.8 18.6 %collective-permute-start.13 = (bf16[1536,128]{1,0:T(8,128)(2,1)}, bf16[1536,128]{1,0:T(8,128)(2,1)S(1)}, u32[]{:S(2)}, u32[]{:S(2)}) collective-permute-start(bf16[1536,128]{1,0:T(8,128)(2,1)} %collective-permute-done.4.refs_7_), channel_id=1, source_target_pairs={{0,224},{16,240},{32,0},{48,16},{64,32},{80,48},{96,64},{112,80},{... | collective-permute-start | bytes 1179656 | tf_op jit(solution)/shard_map/ppermute | solution.py:416
  71.2 14.6 %collective-permute-start.12 = (bf16[2304,128]{1,0:T(8,128)(2,1)}, bf16[2304,128]{1,0:T(8,128)(2,1)S(1)}, u32[]{:S(2)}, u32[]{:S(2)}) collective-permute-start(bf16[2304,128]{1,0:T(8,128)(2,1)} %collective-permute-done.9.refs_3_), channel_id=1, source_target_pairs={{0,32},{16,48},{32,64},{48,80},{64,96},{80,112},{96,128},{112,144}... | collective-permute-start | bytes 1769480 | tf_op jit(solution)/shard_map/ppermute | solution.py:416
  76.4 9.4 %collective-permute-start.19 = (bf16[1536,128]{1,0:T(8,128)(2,1)S(1)}, bf16[1536,128]{1,0:T(8,128)(2,1)S(1)}, u32[]{:S(2)}, u32[]{:S(2)}) collective-permute-start(bf16[1536,128]{1,0:T(8,128)(2,1)S(1)} %collective-permute-done.13.refs_6_), channel_id=1, source_target_pairs={{0,224},{16,240},{32,0},{48,16},{64,32},{80,48},{96,64},{112,80},{... | collective-permute-start | bytes 1179656 | tf_op jit(solution)/shard_map/ppermute | solution.py:416
  80.0 21.6 %collective-permute-start.15 = (bf16[640,640]{1,0:T(8,128)(2,1)S(1)}, bf16[640,640]{1,0:T(8,128)(2,1)S(1)}, u32[]{:S(2)}, u32[]{:S(2)}) collective-permute-start(bf16[640,640]{1,0:T(8,128)(2,1)S(1)} %collective-permute-done.refs_6_.refs_7_), channel_id=1, source_target_pairs={{0,1},{1,0},{2,3},{3,2},{4,5},{5,4},{6,7},{7,6},{8,9},{9,8},{10,11... | collective-permute-start | bytes 2457608 | tf_op jit(solution)/shard_map/ppermute | solution.py:455
  80.0 23.0 %collective-permute-start.17 = (bf16[640,640]{1,0:T(8,128)(2,1)S(1)}, bf16[640,640]{1,0:T(8,128)(2,1)S(1)}, u32[]{:S(2)}, u32[]{:S(2)}) collective-permute-start(bf16[640,640]{1,0:T(8,128)(2,1)S(1)} %collective-permute-done.8.refs_10_.refs_11_), channel_id=1, source_target_pairs={{0,1},{1,0},{2,3},{3,2},{4,5},{5,4},{6,7},{7,6},{8,9},{9,8},{10,11... | collective-permute-start | bytes 2457608 | tf_op jit(solution)/shard_map/ppermute | solution.py:455
  80.5 22.5 %collective-permute-start.16 = (bf16[640,640]{1,0:T(8,128)(2,1)S(1)}, bf16[640,640]{1,0:T(8,128)(2,1)S(1)}, u32[]{:S(2)}, u32[]{:S(2)}) collective-permute-start(bf16[640,640]{1,0:T(8,128)(2,1)S(1)} %collective-permute-done.1.refs_8_.refs_9_), channel_id=1, source_target_pairs={{0,1},{1,0},{2,3},{3,2},{4,5},{5,4},{6,7},{7,6},{8,9},{9,8},{10,11... | collective-permute-start | bytes 2457608 | tf_op jit(solution)/shard_map/ppermute | solution.py:455
  85.9 17.1 %collective-permute-start.18 = (bf16[1536,128]{1,0:T(8,128)(2,1)S(1)}, bf16[1536,128]{1,0:T(8,128)(2,1)S(1)}, u32[]{:S(2)}, u32[]{:S(2)}) collective-permute-start(bf16[1536,128]{1,0:T(8,128)(2,1)S(1)} %collective-permute-done.11.refs_2_), channel_id=1, source_target_pairs={{0,32},{16,48},{32,64},{48,80},{64,96},{80,112},{96,128},{112,144}... | collective-permute-start | bytes 1179656 | tf_op jit(solution)/shard_map/ppermute | solution.py:416
  85.9 17.1 %collective-permute-start.20 = (bf16[1536,128]{1,0:T(8,128)(2,1)S(1)}, bf16[1536,128]{1,0:T(8,128)(2,1)S(1)}, u32[]{:S(2)}, u32[]{:S(2)}) collective-permute-start(bf16[1536,128]{1,0:T(8,128)(2,1)S(1)} %collective-permute-done.19.refs_5_), channel_id=1, source_target_pairs={{0,224},{16,240},{32,0},{48,16},{64,32},{80,48},{96,64},{112,80},{... | collective-permute-start | bytes 1179656 | tf_op jit(solution)/shard_map/ppermute | solution.py:416
  101.6 11.2 %collective-permute-start.25 = (bf16[1536,128]{1,0:T(8,128)(2,1)S(1)}, bf16[1536,128]{1,0:T(8,128)(2,1)S(1)}, u32[]{:S(2)}, u32[]{:S(2)}) collective-permute-start(bf16[1536,128]{1,0:T(8,128)(2,1)S(1)} %get-tuple-element.121), channel_id=1, source_target_pairs={{0,16},{16,0},{32,48},{48,32},{64,80},{80,64},{96,112},{112,96},{1... | collective-permute-start | bytes 1179656 | tf_op jit(solution)/shard_map/ppermute | solution.py:396
  111.9 6.8 %collective-permute-start.21 = (bf16[1152,128]{1,0:T(8,128)(2,1)S(1)}, bf16[1152,128]{1,0:T(8,128)(2,1)S(1)}, u32[]{:S(2)}, u32[]{:S(2)}) collective-permute-start(bf16[1152,128]{1,0:T(8,128)(2,1)S(1)} %get-tuple-element.110), channel_id=1, source_target_pairs={{0,16},{16,0},{32,48},{48,32},{64,80},{80,64},{96,112},{112,96},{1... | collective-permute-start | bytes 884744 | tf_op jit(solution)/shard_map/ppermute | solution.py:396
  113.2 10.0 %collective-permute-start.26 = (bf16[384,384]{1,0:T(8,128)(2,1)S(1)}, bf16[384,384]{1,0:T(8,128)(2,1)S(1)}, u32[]{:S(2)}, u32[]{:S(2)}) collective-permute-start(bf16[384,384]{1,0:T(8,128)(2,1)S(1)} %merge.3.refs_0_), channel_id=1, source_target_pairs={{0,12},{2,14},{4,0},{6,2},{8,4},{10,6},{12,8},{14,10},{1,13},{3,15... | collective-permute-start | bytes 884744 | tf_op jit(solution)/shard_map/ppermute | solution.py:427
  114.0 11.5 %collective-permute-start.27 = (bf16[384,384]{1,0:T(8,128)(2,1)S(1)}, bf16[384,384]{1,0:T(8,128)(2,1)S(1)}, u32[]{:S(2)}, u32[]{:S(2)}) collective-permute-start(bf16[384,384]{1,0:T(8,128)(2,1)S(1)} %merge.3.refs_0_), channel_id=1, source_target_pairs={{0,8},{2,10},{4,12},{6,14},{8,0},{10,2},{12,4},{14,6},{1,9},{3,11}... | collective-permute-start | bytes 884744 | tf_op jit(solution)/shard_map/ppermute | solution.py:427
  114.9 14.0 %collective-permute-start.28 = (bf16[384,384]{1,0:T(8,128)(2,1)S(1)}, bf16[384,384]{1,0:T(8,128)(2,1)S(1)}, u32[]{:S(2)}, u32[]{:S(2)}) collective-permute-start(bf16[384,384]{1,0:T(8,128)(2,1)S(1)} %merge.3.refs_0_), channel_id=1, source_target_pairs={{0,4},{2,6},{4,8},{6,10},{8,12},{10,14},{12,0},{14,2},{1,5},{3,7},... | collective-permute-start | bytes 884744 | tf_op jit(solution)/shard_map/ppermute | solution.py:427
  119.0 12.4 %collective-permute-start.22 = (bf16[384,256]{1,0:T(8,128)(2,1)S(1)}, bf16[384,256]{1,0:T(8,128)(2,1)S(1)}, u32[]{:S(2)}, u32[]{:S(2)}) collective-permute-start(bf16[384,256]{1,0:T(8,128)(2,1)S(1)} %merge.2.refs_1_), channel_id=1, source_target_pairs={{0,12},{2,14},{4,0},{6,2},{8,4},{10,6},{12,8},{14,10},{1,13},{3,15... | collective-permute-start | bytes 589832 | tf_op jit(solution)/shard_map/ppermute | solution.py:427
  119.9 11.5 %collective-permute-start.23 = (bf16[384,256]{1,0:T(8,128)(2,1)S(1)}, bf16[384,256]{1,0:T(8,128)(2,1)S(1)}, u32[]{:S(2)}, u32[]{:S(2)}) collective-permute-start(bf16[384,256]{1,0:T(8,128)(2,1)S(1)} %merge.2.refs_1_), channel_id=1, source_target_pairs={{0,8},{2,10},{4,12},{6,14},{8,0},{10,2},{12,4},{14,6},{1,9},{3,11}... | collective-permute-start | bytes 589832 | tf_op jit(solution)/shard_map/ppermute | solution.py:427
  123.2 9.9 %collective-permute-start.24 = (bf16[384,256]{1,0:T(8,128)(2,1)S(1)}, bf16[384,256]{1,0:T(8,128)(2,1)S(1)}, u32[]{:S(2)}, u32[]{:S(2)}) collective-permute-start(bf16[384,256]{1,0:T(8,128)(2,1)S(1)} %merge.2.refs_1_), channel_id=1, source_target_pairs={{0,4},{2,6},{4,8},{6,10},{8,12},{10,14},{12,0},{14,2},{1,5},{3,7},... | collective-permute-start | bytes 589832 | tf_op jit(solution)/shard_map/ppermute | solution.py:427
  131.3 3.9 %copy-start.5 = (bf16[512,640]{1,0:T(8,128)(2,1)S(1)}, bf16[512,640]{1,0:T(8,128)(2,1)}, u32[]{:S(2)}) copy-start(bf16[512,640]{1,0:T(8,128)(2,1)} %k_ref.3) | copy-start | bytes 1966084
  131.3 3.9 %copy-start.6 = (bf16[512,640]{1,0:T(8,128)(2,1)S(1)}, bf16[512,640]{1,0:T(8,128)(2,1)}, u32[]{:S(2)}) copy-start(bf16[512,640]{1,0:T(8,128)(2,1)} %v_ref.3) | copy-start | bytes 1966084
  131.4 3.9 %copy-start.7 = (bf16[384,640]{1,0:T(8,128)(2,1)S(1)}, bf16[384,640]{1,0:T(8,128)(2,1)}, u32[]{:S(2)}) copy-start(bf16[384,640]{1,0:T(8,128)(2,1)} %q_ref.5) | copy-start | bytes 1474564
  134.6 10.4 %collective-permute-start.29 = (bf16[384,640]{1,0:T(8,128)(2,1)S(1)}, bf16[384,640]{1,0:T(8,128)(2,1)S(1)}, u32[]{:S(2)}, u32[]{:S(2)}) collective-permute-start(bf16[384,640]{1,0:T(8,128)(2,1)S(1)} %get-tuple-element.123), channel_id=1, source_target_pairs={{0,2},{2,0},{4,6},{6,4},{8,10},{10,8},{12,14},{14,12},{1,3},{3,1},... | collective-permute-start | bytes 1474568 | tf_op jit(solution)/shard_map/ppermute | solution.py:464
